TPU v7x, 32 devices: a whole 2x2x4 slice. The times are simulated.
32 devices in a mesh: groups: 2 (over y), rows: 8 (over z, x), sub: 2 (over core).
Axes of the slice: x: 2, y: 2, z: 4, core: 2. Of those that a mesh axis runs over, the one named last changes fastest.
Arguments:
- coupling: bfloat16 [131072, 128], P(('groups', 'rows', 'sub')), parts along dimension 0, may hold values from 0.009 to 110
- tile_vals: bfloat16 [1024, 6, 128, 128], P(('groups', 'rows', 'sub')), parts along dimension 0, may hold values from -0.02734375 to 0.02734375
- tile_cols: int32 [1024, 6], P(('groups', 'rows', 'sub')), parts along dimension 0, may hold values from 0 to 511, as said below
- cluster_graph: int32 [256, 128], P('groups'), parts along dimension 0, may hold values from 0 to 3
- cluster_mass: float32 [256], P('groups'), parts along dimension 0, may hold values from 0.25 to 4
Outputs:
- log_coupling: float32 [131072, 128], P(('groups', 'rows', 'sub')), parts along dimension 0
There are 2 independent parts, one for each index of `groups`. A program takes and returns all parts, laid end to end along the dimension named above; each array names one. Nothing has to cross between parts.
Inputs may be any that keep to these rules, and one draw needn't show every extreme that they name: `tile_cols`: within each device's rows of 32 block rows, a slot below 4 names a column block held by the same device or by the device just before or after it along rows+sub. Over the slots from 4 on, the block rows of one device name column blocks held by any one device at most 4 times, and some device exactly 4 times.
All inputs are finite; a program needn't handle non-finite values.
Results may differ from a plain program's by a relative error of at most 0.0003.
Values may be sent and summed in bfloat16 or wider, within the bound.
No kernel may reach another device: no remote copies, remote signals or barrier semaphores. Data moves between devices by JAX's collectives and lax.ppermute only.
A program may use at most 128 MiB of HBM per device.

v0:
```python
import functools

import jax
import jax.numpy as jnp
from jax import lax
from jax.experimental import pallas as pl
from jax.experimental.pallas import tpu as pltpu
from jax.sharding import PartitionSpec as P


NEAR = 4
NODES = ("rows", "sub")

eta_step = 2.0
relax_power = 0.5

ANY = pl.BlockSpec(memory_space=pl.ANY)
VMEM = pl.BlockSpec(memory_space=pltpu.VMEM)
SMEM = pl.BlockSpec(memory_space=pltpu.SMEM)

f32, bf16, i32 = jnp.float32, jnp.bfloat16, jnp.int32


def on_chip(x):
    return pltpu.with_memory_space_constraint(x, pltpu.VMEM)


def in_hbm(x):
    return pltpu.with_memory_space_constraint(x, pltpu.HBM)


def params(mib):
    return pltpu.CompilerParams(vmem_limit_bytes=mib << 20)


def requests_kernel(nodes_total, cols_ref, coupling_ref, out_ref, rows, sems):
    slots, blocks_dev = cols_ref.shape
    shards = out_ref.shape[0]
    nodes, clusters = coupling_ref.shape
    parts = sems.shape[0]
    step = nodes // parts
    copies = [
        pltpu.make_async_copy(coupling_ref.at[pl.ds(i * step, step)], rows.at[pl.ds(i * step, step)], sems.at[i])
        for i in range(parts)
    ]
    for copy in copies:
        copy.start()

    owner = lax.broadcasted_iota(i32, (shards, blocks_dev), 0)
    place = lax.broadcasted_iota(i32, (clusters, blocks_dev), 0).astype(f32)
    before = (
        lax.broadcasted_iota(i32, (blocks_dev, blocks_dev), 0)
        < lax.broadcasted_iota(i32, (blocks_dev, blocks_dev), 1)
    ).astype(f32)
    count = jnp.zeros((shards, 1), f32)
    table = jnp.zeros((shards, clusters), f32)
    for slot_id in range(NEAR, slots):
        local = cols_ref[slot_id : slot_id + 1, :] - owner * blocks_dev
        hit = (local >= 0) & (local < blocks_dev)
        hits = hit.astype(f32)
        earlier = jnp.dot(hits, before, preferred_element_type=f32) + count
        rank = jnp.sum(earlier * hits, axis=0, keepdims=True)
        count = count + jnp.sum(hits, axis=1, keepdims=True)
        wanted = jnp.where(hit, local, 0).astype(f32)
        table = table + lax.dot_general(
            wanted,
            (rank == place).astype(f32),
            (((1,), (1,)), ((), ())),
            precision=lax.Precision.HIGHEST,
            preferred_element_type=f32,
        )
    out_ref[:, 0, clusters:] = table
    total = jnp.zeros((8, clusters), f32)
    for i in range(parts):
        copies[i].wait()
        part = rows[pl.ds(i * step, step), :].astype(f32)
        total = total + jnp.sum(part.reshape(step // 8, 8, clusters), axis=0)
    mass = jnp.sum(total, axis=0, keepdims=True) / nodes_total
    out_ref[:, 0, :clusters] = jnp.broadcast_to(mass, (shards, clusters))


def gather_kernel(cap, heard_ref, blocks_ref, out_ref, held, wanted_ref, wanted_smem, sems):
    clusters = blocks_ref.shape[2]
    fetch = pltpu.make_async_copy(blocks_ref, held, sems.at[0])
    fetch.start()
    wanted_ref[...] = heard_ref[:, 0, clusters:].astype(i32)
    copy = pltpu.make_async_copy(wanted_ref, wanted_smem, sems.at[1])
    copy.start()
    copy.wait()
    fetch.wait()

    @pl.loop(0, heard_ref.shape[0])
    def _(n):
        for j in range(cap):
            pltpu.make_async_copy(held.at[wanted_smem[n, j]], out_ref.at[n * cap + j], sems.at[2]).start()

    pltpu.make_async_copy(out_ref, out_ref, sems.at[2]).wait()


def split(x):
    high = x.astype(bf16)
    return jnp.concatenate([high, (x - high.astype(f32)).astype(bf16)], axis=1)


def near_kernel(
    group, cap, cols_ref, base_ref, left_ref, own_ref, right_ref, tiles_ref, graph_ref, mass_ref,
    part_ref, graph2_ref, where_ref, window, tiles, part, pull_ref, count_ref, sems, tile_sems, part_sems,
):
    blocks_dev, tile, clusters = own_ref.shape
    slots = tiles_ref.shape[1]
    shards = mass_ref.shape[0]
    steps = blocks_dev // group
    copies = [
        pltpu.make_async_copy(src, window.at[pl.ds(i * blocks_dev, blocks_dev)], sems.at[i])
        for i, src in enumerate((left_ref, own_ref, right_ref))
    ]
    for copy in copies:
        copy.start()

    def fetch(i):
        here = pl.ds(i * group, group)
        return pltpu.make_async_copy(tiles_ref.at[here, pl.ds(0, NEAR)], tiles.at[here], tile_sems.at[i])

    def store(i):
        here = pl.ds(pl.multiple_of(i * group * tile, group * tile), group * tile)
        return pltpu.make_async_copy(part.at[here], part_ref.at[here], part_sems.at[i])

    for i in range(steps):
        fetch(i).start()

    graph = graph_ref[...].astype(f32)
    colmass = jnp.sum(mass_ref[:, 0, :clusters], axis=0, keepdims=True)
    pull_ref[...] = (
        lax.dot_general(
            jnp.broadcast_to(colmass, (8, clusters)),
            graph * graph,
            (((1,), (1,)), ((), ())),
            precision=lax.Precision.HIGHEST,
            preferred_element_type=f32,
        )
        / clusters
    )
    turned = graph.T.astype(bf16)
    graph2_ref[:clusters, :] = turned
    graph2_ref[clusters:, :] = turned

    @pl.loop(0, shards)
    def _(o):
        count_ref[o] = 0

    for slot_id in range(NEAR, slots):

        @pl.loop(0, blocks_dev)
        def _(b):
            owner = cols_ref[slot_id, b] // blocks_dev
            rank = count_ref[owner]
            count_ref[owner] = rank + 1
            where_ref[b * (slots - NEAR) + slot_id - NEAR] = owner * cap + rank

    for copy in copies:
        copy.wait()

    scale = 2.0 * eta_step / clusters

    @pl.loop(0, steps)
    def _(step):
        fetch(step).wait()
        for i in range(group):
            b = step * group + i
            here = pl.ds(pl.multiple_of(b * tile, tile), tile)
            picked = [window[cols_ref[s, b] - base_ref[0]] for s in range(NEAR)]
            wide = jnp.concatenate([tiles[b, s] for s in range(NEAR)], axis=1)
            spread = jnp.dot(wide, jnp.concatenate(picked, axis=0), preferred_element_type=f32)
            affinity = jnp.dot(split(spread), graph2_ref[...], preferred_element_type=f32)
            part[here, :] = (
                jnp.log(window[blocks_dev + b].astype(f32)) - eta_step * pull_ref[0:1, :] + scale * affinity
            )
        store(step).start()

    @pl.loop(0, steps)
    def _(step):
        store(step).wait()


def far_kernel(
    group, nodes_total, where_ref, blocks_ref, tiles_ref, part_ref, graph2_ref,
    logits_ref, mass_ref, tiles, tile_sems, part_sems,
):
    tile, clusters = blocks_ref.shape[1:]
    blocks_dev, far_slots = tiles.shape[:2]
    steps = blocks_dev // group
    scale = 2.0 * eta_step / clusters

    def fetches(i):
        here = pl.ds(i * group, group)
        there = pl.ds(i * group * tile, group * tile)
        return (
            pltpu.make_async_copy(tiles_ref.at[here, pl.ds(NEAR, far_slots)], tiles.at[here], tile_sems.at[i]),
            pltpu.make_async_copy(part_ref.at[there], logits_ref.at[there], part_sems.at[i]),
        )

    for i in range(steps):
        for copy in fetches(i):
            copy.start()

    total = jnp.zeros((8, clusters), f32)
    for step in range(steps):
        for copy in fetches(step):
            copy.wait()
        spreads = []
        for i in range(group):
            b = step * group + i
            picked = [blocks_ref[where_ref[b * far_slots + s]] for s in range(far_slots)]
            wide = jnp.concatenate([tiles[b, s] for s in range(far_slots)], axis=1)
            spreads.append(split(jnp.dot(wide, jnp.concatenate(picked, axis=0), preferred_element_type=f32)))
        here = pl.ds(step * group * tile, group * tile)
        affinity = jnp.dot(jnp.concatenate(spreads, axis=0), graph2_ref[...], preferred_element_type=f32)
        logits = logits_ref[here, :] + scale * affinity
        logits_ref[here, :] = logits
        total = total + jnp.sum(jnp.exp(logits).reshape(group * tile // 8, 8, clusters), axis=0)

    mass_ref[...] = jnp.sum(total, axis=0, keepdims=True) / nodes_total


def last_kernel(parts, logits_ref, newmass_ref, more_ref, target_ref, out_ref, kept, sems):
    shift = relax_power * (jnp.log(target_ref[...]) - jnp.log(newmass_ref[...] + more_ref[...]))
    rows = logits_ref.shape[0]
    step = rows // parts
    copies = []
    for i in range(parts):
        here = pl.ds(i * step, step)
        shifted = logits_ref[here, :] + shift
        kept[here, :] = shifted - jnp.log(jnp.sum(jnp.exp(shifted), axis=1, keepdims=True))
        copies.append(pltpu.make_async_copy(kept.at[here], out_ref.at[here], sems.at[i]))
        copies[-1].start()
    for copy in copies:
        copy.wait()


def local(coupling, tile_vals, tile_cols, cluster_graph, cluster_mass):
    shards = lax.axis_size(NODES)
    my_index = lax.axis_index(NODES)
    blocks_dev, slots = tile_cols.shape
    tile = tile_vals.shape[2]
    rows, clusters = coupling.shape
    far_slots = slots - NEAR
    nodes_total = rows * shards
    far_count = blocks_dev * far_slots
    cap = (far_count + shards - 1) // shards
    blocks = coupling.reshape(blocks_dev, tile, clusters)
    cols = tile_cols.T
    group = 4
    steps = blocks_dev // group
    flops = 2 * rows * clusters

    ends = shards - 1
    left = lax.ppermute(blocks, NODES, [(i, i + 1) for i in range(ends)])
    right = lax.ppermute(blocks, NODES, [(i + 1, i) for i in range(ends)])

    asked = pl.pallas_call(
        functools.partial(requests_kernel, nodes_total),
        out_shape=pltpu.VMEM((shards, 1, 2 * clusters), f32),
        in_specs=[VMEM, ANY],
        out_specs=VMEM,
        scratch_shapes=[pltpu.VMEM((rows, clusters), bf16), pltpu.SemaphoreType.DMA((8,))],
        compiler_params=params(8),
        name="requests",
    )(cols, in_hbm(coupling))
    heard = lax.all_to_all(asked, NODES, split_axis=0, concat_axis=0, tiled=True)
    found = pl.pallas_call(
        functools.partial(gather_kernel, cap),
        out_shape=pltpu.HBM((shards * cap, tile, clusters), bf16),
        in_specs=[VMEM, ANY],
        out_specs=ANY,
        scratch_shapes=[
            pltpu.VMEM((blocks_dev, tile, clusters), bf16),
            pltpu.VMEM((shards, clusters), i32),
            pltpu.SMEM((shards, clusters), i32),
            pltpu.SemaphoreType.DMA((3,)),
        ],
        compiler_params=params(8),
        name="gather",
    )(on_chip(heard), in_hbm(blocks))
    fetched = lax.all_to_all(
        found.reshape(shards, cap, tile, clusters), NODES, split_axis=0, concat_axis=0, tiled=True
    ).reshape(shards * cap, tile, clusters)

    base = (my_index * blocks_dev - blocks_dev).astype(i32).reshape(1)
    part, graph2, where = pl.pallas_call(
        functools.partial(near_kernel, group, cap),
        out_shape=(
            pltpu.HBM((rows, clusters), f32),
            pltpu.VMEM((2 * clusters, clusters), bf16),
            jax.ShapeDtypeStruct((far_count,), i32),
        ),
        in_specs=[SMEM, SMEM, ANY, ANY, ANY, ANY, VMEM, VMEM],
        out_specs=(ANY, VMEM, SMEM),
        scratch_shapes=[
            pltpu.VMEM((3 * blocks_dev, tile, clusters), bf16),
            pltpu.VMEM((blocks_dev, NEAR, tile, tile), bf16),
            pltpu.VMEM((rows, clusters), f32),
            pltpu.VMEM((8, clusters), f32),
            pltpu.SMEM((shards,), i32),
            pltpu.SemaphoreType.DMA((3,)),
            pltpu.SemaphoreType.DMA((steps,)),
            pltpu.SemaphoreType.DMA((steps,)),
        ],
        compiler_params=params(20),
        cost_estimate=pl.CostEstimate(
            flops=flops * (NEAR * tile + 2 * clusters), bytes_accessed=16 << 20, transcendentals=rows * clusters
        ),
        name="near",
    )(cols, base, in_hbm(left), in_hbm(blocks), in_hbm(right), in_hbm(tile_vals), cluster_graph, on_chip(heard))

    logits, mass_part = pl.pallas_call(
        functools.partial(far_kernel, group, nodes_total),
        out_shape=(pltpu.VMEM((rows, clusters), f32), pltpu.VMEM((1, clusters), f32)),
        in_specs=[SMEM, VMEM, ANY, ANY, VMEM],
        out_specs=(VMEM, VMEM),
        scratch_shapes=[
            pltpu.VMEM((blocks_dev, far_slots, tile, tile), bf16),
            pltpu.SemaphoreType.DMA((steps,)),
            pltpu.SemaphoreType.DMA((steps,)),
        ],
        compiler_params=params(16),
        cost_estimate=pl.CostEstimate(
            flops=flops * (far_slots * tile + 2 * clusters), bytes_accessed=8 << 20, transcendentals=rows * clusters
        ),
        name="far",
    )(where, on_chip(fetched), in_hbm(tile_vals), in_hbm(part), on_chip(graph2))

    newmass, more = mass_part, jnp.zeros_like(mass_part)
    span = 1
    while span < shards:
        newmass = newmass + more if span > 1 else newmass
        more = lax.ppermute(newmass, NODES, [(i, i ^ span) for i in range(shards)])
        span *= 2

    return pl.pallas_call(
        functools.partial(last_kernel, 8),
        out_shape=jax.ShapeDtypeStruct((rows, clusters), f32),
        in_specs=[VMEM, VMEM, VMEM, VMEM],
        out_specs=ANY,
        scratch_shapes=[pltpu.VMEM((rows, clusters), f32), pltpu.SemaphoreType.DMA((8,))],
        compiler_params=params(8),
        name="last",
    )(on_chip(logits), on_chip(newmass), on_chip(more), cluster_mass.reshape(1, clusters))


def solution(mesh):
    return jax.shard_map(
        local,
        mesh=mesh,
        in_specs=(
            P(("groups", "rows", "sub"), None),
            P(("groups", "rows", "sub"), None, None, None),
            P(("groups", "rows", "sub"), None),
            P("groups", None),
            P("groups"),
        ),
        out_specs=P(("groups", "rows", "sub"), None),
        check_vma=False,
    )
```

profile of v0, /device:TPU:16, one launch (start us, length us, event | category | flops | bytes accessed | tf_op | source)
XLA Modules:
  0.0 110.9 jit_solution(4603756846836373684)
XLA Ops:
  0.0 0.0 copy-start.1
  0.0 0.7 copy-done.1
  0.7 1.5 %requests.1 = f32[16,1,256]{2,1,0:T(1,128)S(1)} custom-call(s32[6,32]{1,0:T(8,128)S(1)} %bitcast.7, bf16[4096,128]{1,0:T(8,128)(2,1)} %coupling_ref.1), custom_call_target="tpu_custom_call" | custom-call | tf_op jit(solution)/shard_map/requests/pallas_call | solution.py:260
  2.2 10.1 %all_to_all.10.mass_ref.heard_ref = f32[16,1,256]{2,1,0:T(1,128)S(1)} all-to-all(f32[16,1,256]{2,1,0:T(1,128)S(1)} %requests.1), channel_id=1, replica_groups=mesh['groups'=2,'rows'=8,'sub'=2] {'rows','sub'}, dimensions={0} | all-to-all | bytes 32768 | tf_op jit(solution)/shard_map/all_to_all | solution.py:269
  12.3 2.6 %gather.1 = bf16[64,128,128]{2,1,0:T(8,128)(2,1)} custom-call(f32[16,1,256]{2,1,0:T(1,128)S(1)} %all_to_all.10.mass_ref.heard_ref, bf16[32,128,128]{2,1,0:T(8,128)(2,1)} %bitcast.10), custom_call_target="tpu_custom_call" | custom-call | tf_op jit(solution)/shard_map/gather/pallas_call | solution.py:270
  14.9 0.0 copy-start.4
  14.9 0.0 copy-start
  15.0 0.0 copy-start.2
  15.0 6.1 %all-to-all-start.1 = ((bf16[16,4,128,128]{3,2,1,0:T(8,128)(2,1)}), bf16[16,4,128,128]{3,2,1,0:T(8,128)(2,1)S(1)}, u32[]{:S(2)}, u32[]{:S(2)}) async-start(bf16[16,4,128,128]{3,2,1,0:T(8,128)(2,1)} %bitcast.14), calls=%async_computation.1 | async-start | bytes 4194304 | tf_op jit(solution)/shard_map/all_to_all | solution.py:284
  21.1 0.0 copy-done.4
  21.1 3.1 %collective-permute-start.1 = (bf16[32,128,128]{2,1,0:T(8,128)(2,1)S(1)}, bf16[32,128,128]{2,1,0:T(8,128)(2,1)}, u32[]{:S(2)}, u32[]{:S(2)}) collective-permute-start(bf16[32,128,128]{2,1,0:T(8,128)(2,1)S(1)} %bitcast.12), channel_id=1, source_target_pairs={{1,0},{2,1},{3,2},{4,3},{5,4},{6,5},{7,6},{8,7},{9,8},{10,9},{11,1... | collective-permute-start | bytes 3145736 | tf_op jit(solution)/shard_map/ppermute | solution.py:258
  24.2 1.9 %collective-permute-start = (bf16[32,128,128]{2,1,0:T(8,128)(2,1)S(1)}, bf16[32,128,128]{2,1,0:T(8,128)(2,1)}, u32[]{:S(2)}, u32[]{:S(2)}) collective-permute-start(bf16[32,128,128]{2,1,0:T(8,128)(2,1)S(1)} %bitcast.13), channel_id=1, source_target_pairs={{0,1},{1,2},{2,3},{3,4},{4,5},{5,6},{6,7},{7,8},{8,9},{9,10},{10,1... | collective-permute-start | bytes 3145736 | tf_op jit(solution)/shard_map/ppermute | solution.py:257
  26.2 52.0 %collective-permute-done.1.right_ref = bf16[32,128,128]{2,1,0:T(8,128)(2,1)} collective-permute-done((bf16[32,128,128]{2,1,0:T(8,128)(2,1)S(1)}, bf16[32,128,128]{2,1,0:T(8,128)(2,1)}, u32[]{:S(2)}, u32[]{:S(2)}) %collective-permute-start.1) | collective-permute-done | bytes 1048608 | tf_op jit(solution)/shard_map/ppermute | solution.py:258
  78.2 2.0 %collective-permute-done.left_ref = bf16[32,128,128]{2,1,0:T(8,128)(2,1)} collective-permute-done((bf16[32,128,128]{2,1,0:T(8,128)(2,1)S(1)}, bf16[32,128,128]{2,1,0:T(8,128)(2,1)}, u32[]{:S(2)}, u32[]{:S(2)}) %collective-permute-start) | collective-permute-done | bytes 1048608 | tf_op jit(solution)/shard_map/ppermute | solution.py:257
  80.2 0.0 copy-done
  80.2 0.0 copy-done.2
  80.2 11.3 %near.1 = (f32[4096,128]{1,0:T(8,128)}, bf16[256,128]{1,0:T(8,128)(2,1)S(1)}, s32[64]{0:T(128)S(1)}) custom-call(s32[6,32]{1,0:T(8,128)S(1)} %bitcast.8, s32[1]{0:T(128)} %bitcast.1.base_ref, bf16[32,128,128]{2,1,0:T(8,128)(2,1)} %collective-permute-done.left_ref, bf16[32,128,128]{2,1,0:T(8,128)(2,1)} %bitcast.11, ...), custom_call_target="tpu_custom_call" | custom-call | flops 805306368 | bytes 16777216 | tf_op jit(solution)/shard_map/near/pallas_call | solution.py:289
  91.5 0.0 all-to-all-done.1
  91.5 0.0 copy-start.3
  91.5 5.0 %far.1 = (f32[4096,128]{1,0:T(8,128)S(1)}, f32[1,128]{1,0:T(1,128)S(1)}) custom-call(s32[64]{0:T(128)S(1)} %get-tuple-element.10.where_ref, bf16[64,128,128]{2,1,0:T(8,128)(2,1)S(1)} %bitcast.6, bf16[32,6,128,128]{3,2,1,0:T(8,128)(2,1)} %tiles_ref.3, f32[4096,128]{1,0:T(8,128)} %get-tuple-element.11.part_ref, bf16[256,128]{1,0:T(8,128)(2,1)S(1)} %get-tuple-element.12.graph2_ref), custom_call_target="tpu_custom_call" | custom-call | flops 536870912 | bytes 8388608 | tf_op jit(solution)/shard_map/far/pallas_call | solution.py:315
  96.5 0.1 collective-permute-start.2
  96.6 1.1 %collective-permute-done.2 = f32[1,128]{1,0:T(1,128)S(1)} collective-permute-done((f32[1,128]{1,0:T(1,128)S(1)}, f32[1,128]{1,0:T(1,128)S(1)}, u32[]{:S(2)}, u32[]{:S(2)}) %collective-permute-start.2) | collective-permute-done | bytes 544 | tf_op jit(solution)/shard_map/ppermute | solution.py:336
  97.7 0.0 collective-permute-start.3
  97.7 3.6 %collective-permute-done.3 = f32[1,128]{1,0:T(1,128)S(1)} collective-permute-done((f32[1,128]{1,0:T(1,128)S(1)}, f32[1,128]{1,0:T(1,128)S(1)}, u32[]{:S(2)}, u32[]{:S(2)}) %collective-permute-start.3) | collective-permute-done | bytes 544 | tf_op jit(solution)/shard_map/ppermute | solution.py:336
  101.3 0.0 collective-permute-start.4
  101.3 3.6 %collective-permute-done.4 = f32[1,128]{1,0:T(1,128)S(1)} collective-permute-done((f32[1,128]{1,0:T(1,128)S(1)}, f32[1,128]{1,0:T(1,128)S(1)}, u32[]{:S(2)}, u32[]{:S(2)}) %collective-permute-start.4) | collective-permute-done | bytes 544 | tf_op jit(solution)/shard_map/ppermute | solution.py:336
  104.9 0.0 collective-permute-start.5
  104.9 4.5 %collective-permute-done.5.more_ref = f32[1,128]{1,0:T(1,128)S(1)} collective-permute-done((f32[1,128]{1,0:T(1,128)S(1)}, f32[1,128]{1,0:T(1,128)S(1)}, u32[]{:S(2)}, u32[]{:S(2)}) %collective-permute-start.5) | collective-permute-done | bytes 544 | tf_op jit(solution)/shard_map/ppermute | solution.py:336
  109.3 0.0 copy-done.3
  109.3 1.5 %last.1 = f32[4096,128]{1,0:T(8,128)} custom-call(f32[4096,128]{1,0:T(8,128)S(1)} %get-tuple-element.13.logits_ref, f32[1,128]{1,0:T(1,128)S(1)} %add.16.newmass_ref, f32[1,128]{1,0:T(1,128)S(1)} %collective-permute-done.5.more_ref, f32[1,128]{1,0:T(1,128)S(1)} %bitcast.9), custom_call_target="tpu_custom_call" | custom-call | tf_op jit(solution)/shard_map/last/pallas_call | solution.py:339
  (3 shorter events, 0.0 us)
Async XLA Ops:
  0.0 0.7 copy-start.1
  14.9 6.2 %copy-start.4 = (bf16[4096,128]{1,0:T(8,128)(2,1)S(1)}, bf16[4096,128]{1,0:T(8,128)(2,1)}, u32[]{:S(2)}) copy-start(bf16[4096,128]{1,0:T(8,128)(2,1)} %coupling_ref.1) | copy-start | bytes 3145732
  14.9 65.2 %copy-start = (s32[128,128]{1,0:T(8,128)S(1)}, s32[128,128]{1,0:T(8,128)}, u32[]{:S(2)}) copy-start(s32[128,128]{1,0:T(8,128)} %graph_ref.1) | copy-start | bytes 196612
  15.0 65.2 %copy-start.2 = (s32[32,6]{0,1:T(8,128)S(1)}, s32[32,6]{0,1:T(8,128)}, u32[]{:S(2)}) copy-start(s32[32,6]{0,1:T(8,128)} %param.7) | copy-start | bytes 2308
  15.0 76.5 %all-to-all-start.1 = ((bf16[16,4,128,128]{3,2,1,0:T(8,128)(2,1)}), bf16[16,4,128,128]{3,2,1,0:T(8,128)(2,1)S(1)}, u32[]{:S(2)}, u32[]{:S(2)}) async-start(bf16[16,4,128,128]{3,2,1,0:T(8,128)(2,1)} %bitcast.14), calls=%async_computation.1 | async-start | bytes 4194304 | tf_op jit(solution)/shard_map/all_to_all | solution.py:284
  21.1 57.0 %collective-permute-start.1 = (bf16[32,128,128]{2,1,0:T(8,128)(2,1)S(1)}, bf16[32,128,128]{2,1,0:T(8,128)(2,1)}, u32[]{:S(2)}, u32[]{:S(2)}) collective-permute-start(bf16[32,128,128]{2,1,0:T(8,128)(2,1)S(1)} %bitcast.12), channel_id=1, source_target_pairs={{1,0},{2,1},{3,2},{4,3},{5,4},{6,5},{7,6},{8,7},{9,8},{10,9},{11,1... | collective-permute-start | bytes 3145736 | tf_op jit(solution)/shard_map/ppermute | solution.py:258
  24.2 55.9 %collective-permute-start = (bf16[32,128,128]{2,1,0:T(8,128)(2,1)S(1)}, bf16[32,128,128]{2,1,0:T(8,128)(2,1)}, u32[]{:S(2)}, u32[]{:S(2)}) collective-permute-start(bf16[32,128,128]{2,1,0:T(8,128)(2,1)S(1)} %bitcast.13), channel_id=1, source_target_pairs={{0,1},{1,2},{2,3},{3,4},{4,5},{5,6},{6,7},{7,8},{8,9},{9,10},{10,1... | collective-permute-start | bytes 3145736 | tf_op jit(solution)/shard_map/ppermute | solution.py:257
  91.5 17.8 %copy-start.3 = (f32[128]{0:T(128)S(1)}, f32[128]{0:T(128)}, u32[]{:S(2)}) copy-start(f32[128]{0:T(128)} %param.9) | copy-start | bytes 1540
  96.5 1.2 %collective-permute-start.2 = (f32[1,128]{1,0:T(1,128)S(1)}, f32[1,128]{1,0:T(1,128)S(1)}, u32[]{:S(2)}, u32[]{:S(2)}) collective-permute-start(f32[1,128]{1,0:T(1,128)S(1)} %get-tuple-element.14), channel_id=1, source_target_pairs={{0,1},{1,0},{2,3},{3,2},{4,5},{5,4},{6,7},{7,6},{8,9},{9,8},{10,11... | collective-permute-start | bytes 1544 | tf_op jit(solution)/shard_map/ppermute | solution.py:336
  97.7 3.6 %collective-permute-start.3 = (f32[1,128]{1,0:T(1,128)S(1)}, f32[1,128]{1,0:T(1,128)S(1)}, u32[]{:S(2)}, u32[]{:S(2)}) collective-permute-start(f32[1,128]{1,0:T(1,128)S(1)} %add.14), channel_id=1, source_target_pairs={{0,2},{1,3},{2,0},{3,1},{4,6},{5,7},{6,4},{7,5},{8,10},{9,11},{10,... | collective-permute-start | bytes 1544 | tf_op jit(solution)/shard_map/ppermute | solution.py:336
  101.3 3.6 %collective-permute-start.4 = (f32[1,128]{1,0:T(1,128)S(1)}, f32[1,128]{1,0:T(1,128)S(1)}, u32[]{:S(2)}, u32[]{:S(2)}) collective-permute-start(f32[1,128]{1,0:T(1,128)S(1)} %add.15), channel_id=1, source_target_pairs={{0,4},{1,5},{2,6},{3,7},{4,0},{5,1},{6,2},{7,3},{8,12},{9,13},{10,... | collective-permute-start | bytes 1544 | tf_op jit(solution)/shard_map/ppermute | solution.py:336
  104.9 4.5 %collective-permute-start.5 = (f32[1,128]{1,0:T(1,128)S(1)}, f32[1,128]{1,0:T(1,128)S(1)}, u32[]{:S(2)}, u32[]{:S(2)}) collective-permute-start(f32[1,128]{1,0:T(1,128)S(1)} %add.16.newmass_ref), channel_id=1, source_target_pairs={{0,8},{1,9},{2,10},{3,11},{4,12},{5,13},{6,14},{7,15},{8,0},{9,1},... | collective-permute-start | bytes 1544 | tf_op jit(solution)/shard_map/ppermute | solution.py:336
where the time goes:
time: 112 us; the launch traced here: 111 us
  waiting for transfers between devices  66.7 us (60%)
  Pallas kernels  22 us (20%)
  starting transfers between devices  11.2 us (10%)
  blocking collectives  10.1 us (9%)
    ppermute x1, waiting for transfers between devices, local(): right = lax.ppermute(blocks, NODES, [(i + 1, i) for i in range(ends)])  52 us
    ppermute x4, waiting for transfers between devices, local(): more = lax.ppermute(newmass, NODES, [(i, i ^ span) for i in range(shards)])  12.7 us
    pallas_call x1, Pallas kernels, local(): pl.pallas_call(functools.partial(near_kernel, group, cap), out_shape=(plt...  11.3 us
    all_to_all x1, blocking collectives, local(): lax.all_to_all(asked, NODES, split_axis=0, concat_axis=0, tiled=True)  10.1 us
    all_to_all x1, starting transfers between devices, local(): lax.all_to_all(found.reshape(shards, cap, tile, clusters), NODES, split_a...  6.15 us
    pallas_call x1, Pallas kernels, local(): pl.pallas_call(functools.partial(far_kernel, group, nodes_total), out_sha...  4.96 us
    ppermute x1, starting transfers between devices, local(): right = lax.ppermute(blocks, NODES, [(i + 1, i) for i in range(ends)])  3.08 us
    pallas_call x1, Pallas kernels, local(): pl.pallas_call(functools.partial(gather_kernel, cap), out_shape=pltpu.HBM...  2.59 us
  transfers between devices with their start and end apart: 7, of which 6 were waited for; matrix products, arithmetic and copies ran while one was open for 0% of the time, Pallas kernels for 10%

commit v1 on v0

--- a/solution.py
+++ b/solution.py
@@ -102,9 +102,25 @@
     return jnp.concatenate([high, (x - high.astype(f32)).astype(bf16)], axis=1)
 
 
+def logs_kernel(parts, coupling_ref, out_ref, rows, kept, in_sems, out_sems):
+    step = rows.shape[0] // parts
+    here = [pl.ds(i * step, step) for i in range(parts)]
+    loads = [pltpu.make_async_copy(coupling_ref.at[at], rows.at[at], in_sems.at[i]) for i, at in enumerate(here)]
+    stores = [pltpu.make_async_copy(kept.at[at], out_ref.at[at], out_sems.at[i]) for i, at in enumerate(here)]
+    for load in loads:
+        load.start()
+    for i, at in enumerate(here):
+        loads[i].wait()
+        kept[at, :] = jnp.log(rows[at, :].astype(f32))
+        stores[i].start()
+    for store in stores:
+        store.wait()
+
+
 def near_kernel(
     group, cap, cols_ref, base_ref, left_ref, own_ref, right_ref, tiles_ref, graph_ref, mass_ref,
-    part_ref, graph2_ref, where_ref, window, tiles, part, pull_ref, count_ref, sems, tile_sems, part_sems,
+    logs_ref, part_ref, graph2_ref, where_ref,
+    window, tiles, part, pull_ref, count_ref, sems, tile_sems, logs_sems, part_sems,
 ):
     blocks_dev, tile, clusters = own_ref.shape
     slots = tiles_ref.shape[1]
@@ -121,12 +137,17 @@
         here = pl.ds(i * group, group)
         return pltpu.make_async_copy(tiles_ref.at[here, pl.ds(0, NEAR)], tiles.at[here], tile_sems.at[i])
 
+    def logs(i):
+        here = pl.ds(pl.multiple_of(i * group * tile, group * tile), group * tile)
+        return pltpu.make_async_copy(logs_ref.at[here], part.at[here], logs_sems.at[i])
+
     def store(i):
         here = pl.ds(pl.multiple_of(i * group * tile, group * tile), group * tile)
         return pltpu.make_async_copy(part.at[here], part_ref.at[here], part_sems.at[i])
 
     for i in range(steps):
         fetch(i).start()
+        logs(i).start()
 
     graph = graph_ref[...].astype(f32)
     colmass = jnp.sum(mass_ref[:, 0, :clusters], axis=0, keepdims=True)
@@ -165,6 +186,7 @@
     @pl.loop(0, steps)
     def _(step):
         fetch(step).wait()
+        logs(step).wait()
         for i in range(group):
             b = step * group + i
             here = pl.ds(pl.multiple_of(b * tile, tile), tile)
@@ -172,9 +194,7 @@
             wide = jnp.concatenate([tiles[b, s] for s in range(NEAR)], axis=1)
             spread = jnp.dot(wide, jnp.concatenate(picked, axis=0), preferred_element_type=f32)
             affinity = jnp.dot(split(spread), graph2_ref[...], preferred_element_type=f32)
-            part[here, :] = (
-                jnp.log(window[blocks_dev + b].astype(f32)) - eta_step * pull_ref[0:1, :] + scale * affinity
-            )
+            part[here, :] = part[here, :] - eta_step * pull_ref[0:1, :] + scale * affinity
         store(step).start()
 
     @pl.loop(0, steps)
@@ -267,6 +287,20 @@
         name="requests",
     )(cols, in_hbm(coupling))
     heard = lax.all_to_all(asked, NODES, split_axis=0, concat_axis=0, tiled=True)
+    logs = pl.pallas_call(
+        functools.partial(logs_kernel, 8),
+        out_shape=pltpu.HBM((rows, clusters), f32),
+        in_specs=[ANY],
+        out_specs=ANY,
+        scratch_shapes=[
+            pltpu.VMEM((rows, clusters), bf16),
+            pltpu.VMEM((rows, clusters), f32),
+            pltpu.SemaphoreType.DMA((8,)),
+            pltpu.SemaphoreType.DMA((8,)),
+        ],
+        compiler_params=params(8),
+        name="logs",
+    )(in_hbm(coupling))
     found = pl.pallas_call(
         functools.partial(gather_kernel, cap),
         out_shape=pltpu.HBM((shards * cap, tile, clusters), bf16),
@@ -293,7 +327,7 @@
             pltpu.VMEM((2 * clusters, clusters), bf16),
             jax.ShapeDtypeStruct((far_count,), i32),
         ),
-        in_specs=[SMEM, SMEM, ANY, ANY, ANY, ANY, VMEM, VMEM],
+        in_specs=[SMEM, SMEM, ANY, ANY, ANY, ANY, VMEM, VMEM, ANY],
         out_specs=(ANY, VMEM, SMEM),
         scratch_shapes=[
             pltpu.VMEM((3 * blocks_dev, tile, clusters), bf16),
@@ -304,13 +338,14 @@
             pltpu.SemaphoreType.DMA((3,)),
             pltpu.SemaphoreType.DMA((steps,)),
             pltpu.SemaphoreType.DMA((steps,)),
+            pltpu.SemaphoreType.DMA((steps,)),
         ],
         compiler_params=params(20),
         cost_estimate=pl.CostEstimate(
             flops=flops * (NEAR * tile + 2 * clusters), bytes_accessed=16 << 20, transcendentals=rows * clusters
         ),
         name="near",
-    )(cols, base, in_hbm(left), in_hbm(blocks), in_hbm(right), in_hbm(tile_vals), cluster_graph, on_chip(heard))
+    )(cols, base, in_hbm(left), in_hbm(blocks), in_hbm(right), in_hbm(tile_vals), cluster_graph, on_chip(heard), in_hbm(logs))
 
     logits, mass_part = pl.pallas_call(
         functools.partial(far_kernel, group, nodes_total),

time: 112 us -> 113 us (level)
  waiting for transfers between devices: 66.7 us -> 62.7 us
  Pallas kernels: 22 us -> 24.9 us
  starting transfers between devices: 11.2 us -> 12.8 us
    ppermute x1, waiting for transfers between devices: 52 us -> 0.01 us  [local(): right = lax.ppermute(blocks, NODES, [(i + 1, i) for i in range(ends)])]
    ppermute x1, waiting for transfers between devices: 2 us -> 50 us  [local(): left = lax.ppermute(blocks, NODES, [(i, i + 1) for i in range(ends)])]
    pallas_call x0 -> x1, Pallas kernels: none -> 2.39 us  [local(): pl.pallas_call(functools.partial(logs_kernel, 8), out_shape=pltpu.HBM((ro...]
    ppermute x1, starting transfers between devices: 3.08 us -> 4.43 us  [local(): right = lax.ppermute(blocks, NODES, [(i + 1, i) for i in range(ends)])]
  transfers between devices with their start and end apart: 7 -> 7, of which waited for: 6 -> 5; matrix products, arithmetic and copies ran while one was open for 0% -> 0% of each run, Pallas kernels for 10% -> 13%
where the time goes in v1:
time: 113 us; the launch traced here: 111 us
  waiting for transfers between devices  62.7 us (55%)
  Pallas kernels  24.9 us (22%)
  starting transfers between devices  12.8 us (11%)
  blocking collectives  10.1 us (9%)
    ppermute x1, waiting for transfers between devices, local(): left = lax.ppermute(blocks, NODES, [(i, i + 1) for i in range(ends)])  50 us
    ppermute x4, waiting for transfers between devices, local(): more = lax.ppermute(newmass, NODES, [(i, i ^ span) for i in range(shards)])  12.7 us
    pallas_call x1, Pallas kernels, local(): pl.pallas_call(functools.partial(near_kernel, group, cap), out_shape=(plt...  11.9 us
    all_to_all x1, blocking collectives, local(): lax.all_to_all(asked, NODES, split_axis=0, concat_axis=0, tiled=True)  10.1 us
    all_to_all x1, starting transfers between devices, local(): lax.all_to_all(found.reshape(shards, cap, tile, clusters), NODES, split_a...  6.15 us
    pallas_call x1, Pallas kernels, local(): pl.pallas_call(functools.partial(far_kernel, group, nodes_total), out_sha...  4.95 us
    ppermute x1, starting transfers between devices, local(): right = lax.ppermute(blocks, NODES, [(i + 1, i) for i in range(ends)])  4.43 us
    pallas_call x1, Pallas kernels, local(): pl.pallas_call(functools.partial(gather_kernel, cap), out_shape=pltpu.HBM...  2.59 us
  transfers between devices with their start and end apart: 7, of which 5 were waited for; matrix products, arithmetic and copies ran while one was open for 0% of the time, Pallas kernels for 13%

profile of v1, /device:TPU:16, one launch (start us, length us, event | category | flops | bytes accessed | tf_op | source)
XLA Modules:
  0.0 111.4 jit_solution(2395843632332840412)
XLA Ops:
  0.0 0.0 copy-start.1
  0.0 0.7 copy-done.1
  0.7 1.5 %requests.1 = f32[16,1,256]{2,1,0:T(1,128)S(1)} custom-call(s32[6,32]{1,0:T(8,128)S(1)} %bitcast.7, bf16[4096,128]{1,0:T(8,128)(2,1)} %coupling_ref.3), custom_call_target="tpu_custom_call" | custom-call | tf_op jit(solution)/shard_map/requests/pallas_call | solution.py:280
  2.2 10.1 %all_to_all.10.mass_ref.heard_ref = f32[16,1,256]{2,1,0:T(1,128)S(1)} all-to-all(f32[16,1,256]{2,1,0:T(1,128)S(1)} %requests.1), channel_id=1, replica_groups=mesh['groups'=2,'rows'=8,'sub'=2] {'rows','sub'}, dimensions={0} | all-to-all | bytes 32768 | tf_op jit(solution)/shard_map/all_to_all | solution.py:289
  12.3 2.6 %gather.1 = bf16[64,128,128]{2,1,0:T(8,128)(2,1)} custom-call(f32[16,1,256]{2,1,0:T(1,128)S(1)} %all_to_all.10.mass_ref.heard_ref, bf16[32,128,128]{2,1,0:T(8,128)(2,1)} %bitcast.10), custom_call_target="tpu_custom_call" | custom-call | tf_op jit(solution)/shard_map/gather/pallas_call | solution.py:304
  14.9 0.0 copy-start.4
  14.9 6.1 %all-to-all-start.1 = ((bf16[16,4,128,128]{3,2,1,0:T(8,128)(2,1)}), bf16[16,4,128,128]{3,2,1,0:T(8,128)(2,1)S(1)}, u32[]{:S(2)}, u32[]{:S(2)}) async-start(bf16[16,4,128,128]{3,2,1,0:T(8,128)(2,1)} %bitcast.14), calls=%async_computation.1 | async-start | bytes 4194304 | tf_op jit(solution)/shard_map/all_to_all | solution.py:318
  21.1 0.0 copy-done.4
  21.1 0.0 copy-start
  21.1 0.0 copy-start.2
  21.1 2.2 %collective-permute-start = (bf16[32,128,128]{2,1,0:T(8,128)(2,1)S(1)}, bf16[32,128,128]{2,1,0:T(8,128)(2,1)}, u32[]{:S(2)}, u32[]{:S(2)}) collective-permute-start(bf16[32,128,128]{2,1,0:T(8,128)(2,1)S(1)} %bitcast.12), channel_id=1, source_target_pairs={{0,1},{1,2},{2,3},{3,4},{4,5},{5,6},{6,7},{7,8},{8,9},{9,10},{10,1... | collective-permute-start | bytes 3145736 | tf_op jit(solution)/shard_map/ppermute | solution.py:277
  23.3 4.4 %collective-permute-start.1 = (bf16[32,128,128]{2,1,0:T(8,128)(2,1)S(1)}, bf16[32,128,128]{2,1,0:T(8,128)(2,1)}, u32[]{:S(2)}, u32[]{:S(2)}) collective-permute-start(bf16[32,128,128]{2,1,0:T(8,128)(2,1)S(1)} %bitcast.13), channel_id=1, source_target_pairs={{1,0},{2,1},{3,2},{4,3},{5,4},{6,5},{7,6},{8,7},{9,8},{10,9},{11,1... | collective-permute-start | bytes 3145736 | tf_op jit(solution)/shard_map/ppermute | solution.py:278
  27.7 2.4 %logs.1.logs_ref = f32[4096,128]{1,0:T(8,128)} custom-call(bf16[4096,128]{1,0:T(8,128)(2,1)} %coupling_ref.3), custom_call_target="tpu_custom_call" | custom-call | tf_op jit(solution)/shard_map/logs/pallas_call | solution.py:290
  30.2 50.0 %collective-permute-done.left_ref = bf16[32,128,128]{2,1,0:T(8,128)(2,1)} collective-permute-done((bf16[32,128,128]{2,1,0:T(8,128)(2,1)S(1)}, bf16[32,128,128]{2,1,0:T(8,128)(2,1)}, u32[]{:S(2)}, u32[]{:S(2)}) %collective-permute-start) | collective-permute-done | bytes 1048608 | tf_op jit(solution)/shard_map/ppermute | solution.py:277
  80.1 0.0 collective-permute-done.1.right_ref
  80.1 0.0 copy-done
  80.1 0.0 copy-done.2
  80.1 11.9 %near.1 = (f32[4096,128]{1,0:T(8,128)}, bf16[256,128]{1,0:T(8,128)(2,1)S(1)}, s32[64]{0:T(128)S(1)}) custom-call(s32[6,32]{1,0:T(8,128)S(1)} %bitcast.8, s32[1]{0:T(128)} %bitcast.1.base_ref, bf16[32,128,128]{2,1,0:T(8,128)(2,1)} %collective-permute-done.left_ref, bf16[32,128,128]{2,1,0:T(8,128)(2,1)} %bitcast.11, ...), custom_call_target="tpu_custom_call" | custom-call | flops 805306368 | bytes 16777216 | tf_op jit(solution)/shard_map/near/pallas_call | solution.py:323
  92.1 0.0 all-to-all-done.1
  92.1 0.0 copy-start.3
  92.1 4.9 %far.1 = (f32[4096,128]{1,0:T(8,128)S(1)}, f32[1,128]{1,0:T(1,128)S(1)}) custom-call(s32[64]{0:T(128)S(1)} %get-tuple-element.10.where_ref, bf16[64,128,128]{2,1,0:T(8,128)(2,1)S(1)} %bitcast.6, bf16[32,6,128,128]{3,2,1,0:T(8,128)(2,1)} %tiles_ref.3, f32[4096,128]{1,0:T(8,128)} %get-tuple-element.11.part_ref, bf16[256,128]{1,0:T(8,128)(2,1)S(1)} %get-tuple-element.12.graph2_ref), custom_call_target="tpu_custom_call" | custom-call | flops 536870912 | bytes 8388608 | tf_op jit(solution)/shard_map/far/pallas_call | solution.py:350
  97.1 0.1 collective-permute-start.2
  97.1 1.1 %collective-permute-done.2 = f32[1,128]{1,0:T(1,128)S(1)} collective-permute-done((f32[1,128]{1,0:T(1,128)S(1)}, f32[1,128]{1,0:T(1,128)S(1)}, u32[]{:S(2)}, u32[]{:S(2)}) %collective-permute-start.2) | collective-permute-done | bytes 544 | tf_op jit(solution)/shard_map/ppermute | solution.py:371
  98.3 0.0 collective-permute-start.3
  98.3 3.6 %collective-permute-done.3 = f32[1,128]{1,0:T(1,128)S(1)} collective-permute-done((f32[1,128]{1,0:T(1,128)S(1)}, f32[1,128]{1,0:T(1,128)S(1)}, u32[]{:S(2)}, u32[]{:S(2)}) %collective-permute-start.3) | collective-permute-done | bytes 544 | tf_op jit(solution)/shard_map/ppermute | solution.py:371
  101.9 0.0 collective-permute-start.4
  101.9 3.6 %collective-permute-done.4 = f32[1,128]{1,0:T(1,128)S(1)} collective-permute-done((f32[1,128]{1,0:T(1,128)S(1)}, f32[1,128]{1,0:T(1,128)S(1)}, u32[]{:S(2)}, u32[]{:S(2)}) %collective-permute-start.4) | collective-permute-done | bytes 544 | tf_op jit(solution)/shard_map/ppermute | solution.py:371
  105.4 0.0 collective-permute-start.5
  105.4 4.5 %collective-permute-done.5.more_ref = f32[1,128]{1,0:T(1,128)S(1)} collective-permute-done((f32[1,128]{1,0:T(1,128)S(1)}, f32[1,128]{1,0:T(1,128)S(1)}, u32[]{:S(2)}, u32[]{:S(2)}) %collective-permute-start.5) | collective-permute-done | bytes 544 | tf_op jit(solution)/shard_map/ppermute | solution.py:371
  109.9 0.0 copy-done.3
  109.9 1.5 %last.1 = f32[4096,128]{1,0:T(8,128)} custom-call(f32[4096,128]{1,0:T(8,128)S(1)} %get-tuple-element.13.logits_ref, f32[1,128]{1,0:T(1,128)S(1)} %add.16.newmass_ref, f32[1,128]{1,0:T(1,128)S(1)} %collective-permute-done.5.more_ref, f32[1,128]{1,0:T(1,128)S(1)} %bitcast.9), custom_call_target="tpu_custom_call" | custom-call | tf_op jit(solution)/shard_map/last/pallas_call | solution.py:374
  (3 shorter events, 0.0 us)
Async XLA Ops:
  0.0 0.7 copy-start.1
  14.9 6.2 %copy-start.4 = (bf16[4096,128]{1,0:T(8,128)(2,1)S(1)}, bf16[4096,128]{1,0:T(8,128)(2,1)}, u32[]{:S(2)}) copy-start(bf16[4096,128]{1,0:T(8,128)(2,1)} %coupling_ref.3) | copy-start | bytes 3145732
  14.9 77.1 %all-to-all-start.1 = ((bf16[16,4,128,128]{3,2,1,0:T(8,128)(2,1)}), bf16[16,4,128,128]{3,2,1,0:T(8,128)(2,1)S(1)}, u32[]{:S(2)}, u32[]{:S(2)}) async-start(bf16[16,4,128,128]{3,2,1,0:T(8,128)(2,1)} %bitcast.14), calls=%async_computation.1 | async-start | bytes 4194304 | tf_op jit(solution)/shard_map/all_to_all | solution.py:318
  21.1 59.0 %copy-start = (s32[128,128]{1,0:T(8,128)S(1)}, s32[128,128]{1,0:T(8,128)}, u32[]{:S(2)}) copy-start(s32[128,128]{1,0:T(8,128)} %graph_ref.1) | copy-start | bytes 196612
  21.1 59.0 %copy-start.2 = (s32[32,6]{0,1:T(8,128)S(1)}, s32[32,6]{0,1:T(8,128)}, u32[]{:S(2)}) copy-start(s32[32,6]{0,1:T(8,128)} %param.7) | copy-start | bytes 2308
  21.1 59.0 %collective-permute-start = (bf16[32,128,128]{2,1,0:T(8,128)(2,1)S(1)}, bf16[32,128,128]{2,1,0:T(8,128)(2,1)}, u32[]{:S(2)}, u32[]{:S(2)}) collective-permute-start(bf16[32,128,128]{2,1,0:T(8,128)(2,1)S(1)} %bitcast.12), channel_id=1, source_target_pairs={{0,1},{1,2},{2,3},{3,4},{4,5},{5,6},{6,7},{7,8},{8,9},{9,10},{10,1... | collective-permute-start | bytes 3145736 | tf_op jit(solution)/shard_map/ppermute | solution.py:277
  23.3 56.8 %collective-permute-start.1 = (bf16[32,128,128]{2,1,0:T(8,128)(2,1)S(1)}, bf16[32,128,128]{2,1,0:T(8,128)(2,1)}, u32[]{:S(2)}, u32[]{:S(2)}) collective-permute-start(bf16[32,128,128]{2,1,0:T(8,128)(2,1)S(1)} %bitcast.13), channel_id=1, source_target_pairs={{1,0},{2,1},{3,2},{4,3},{5,4},{6,5},{7,6},{8,7},{9,8},{10,9},{11,1... | collective-permute-start | bytes 3145736 | tf_op jit(solution)/shard_map/ppermute | solution.py:278
  92.1 17.8 %copy-start.3 = (f32[128]{0:T(128)S(1)}, f32[128]{0:T(128)}, u32[]{:S(2)}) copy-start(f32[128]{0:T(128)} %param.9) | copy-start | bytes 1540
  97.1 1.2 %collective-permute-start.2 = (f32[1,128]{1,0:T(1,128)S(1)}, f32[1,128]{1,0:T(1,128)S(1)}, u32[]{:S(2)}, u32[]{:S(2)}) collective-permute-start(f32[1,128]{1,0:T(1,128)S(1)} %get-tuple-element.14), channel_id=1, source_target_pairs={{0,1},{1,0},{2,3},{3,2},{4,5},{5,4},{6,7},{7,6},{8,9},{9,8},{10,11... | collective-permute-start | bytes 1544 | tf_op jit(solution)/shard_map/ppermute | solution.py:371
  98.3 3.6 %collective-permute-start.3 = (f32[1,128]{1,0:T(1,128)S(1)}, f32[1,128]{1,0:T(1,128)S(1)}, u32[]{:S(2)}, u32[]{:S(2)}) collective-permute-start(f32[1,128]{1,0:T(1,128)S(1)} %add.14), channel_id=1, source_target_pairs={{0,2},{1,3},{2,0},{3,1},{4,6},{5,7},{6,4},{7,5},{8,10},{9,11},{10,... | collective-permute-start | bytes 1544 | tf_op jit(solution)/shard_map/ppermute | solution.py:371
  101.9 3.6 %collective-permute-start.4 = (f32[1,128]{1,0:T(1,128)S(1)}, f32[1,128]{1,0:T(1,128)S(1)}, u32[]{:S(2)}, u32[]{:S(2)}) collective-permute-start(f32[1,128]{1,0:T(1,128)S(1)} %add.15), channel_id=1, source_target_pairs={{0,4},{1,5},{2,6},{3,7},{4,0},{5,1},{6,2},{7,3},{8,12},{9,13},{10,... | collective-permute-start | bytes 1544 | tf_op jit(solution)/shard_map/ppermute | solution.py:371
  105.4 4.5 %collective-permute-start.5 = (f32[1,128]{1,0:T(1,128)S(1)}, f32[1,128]{1,0:T(1,128)S(1)}, u32[]{:S(2)}, u32[]{:S(2)}) collective-permute-start(f32[1,128]{1,0:T(1,128)S(1)} %add.16.newmass_ref), channel_id=1, source_target_pairs={{0,8},{1,9},{2,10},{3,11},{4,12},{5,13},{6,14},{7,15},{8,0},{9,1},... | collective-permute-start | bytes 1544 | tf_op jit(solution)/shard_map/ppermute | solution.py:371

commit v2 on v0

--- a/solution.py
+++ b/solution.py
@@ -79,22 +79,40 @@
     out_ref[:, 0, :clusters] = jnp.broadcast_to(mass, (shards, clusters))
 
 
-def gather_kernel(cap, heard_ref, blocks_ref, out_ref, held, wanted_ref, wanted_smem, sems):
+def gather_kernel(cap, heard_ref, blocks_ref, out_ref, wanted_ref, wanted_smem, sems):
     clusters = blocks_ref.shape[2]
-    fetch = pltpu.make_async_copy(blocks_ref, held, sems.at[0])
-    fetch.start()
     wanted_ref[...] = heard_ref[:, 0, clusters:].astype(i32)
-    copy = pltpu.make_async_copy(wanted_ref, wanted_smem, sems.at[1])
+    copy = pltpu.make_async_copy(wanted_ref, wanted_smem, sems.at[0])
     copy.start()
     copy.wait()
-    fetch.wait()
 
     @pl.loop(0, heard_ref.shape[0])
     def _(n):
         for j in range(cap):
-            pltpu.make_async_copy(held.at[wanted_smem[n, j]], out_ref.at[n * cap + j], sems.at[2]).start()
-
-    pltpu.make_async_copy(out_ref, out_ref, sems.at[2]).wait()
+            pltpu.make_async_copy(blocks_ref.at[wanted_smem[n, j]], out_ref.at[n * cap + j], sems.at[1]).start()
+
+    pltpu.make_async_copy(out_ref, out_ref, sems.at[1]).wait()
+
+
+def prep_kernel(cap, cols_ref, graph_ref, graph2_ref, where_ref, count_ref):
+    slots, blocks_dev = cols_ref.shape
+    clusters = graph_ref.shape[0]
+    turned = graph_ref[...].astype(f32).T.astype(bf16)
+    graph2_ref[:clusters, :] = turned
+    graph2_ref[clusters:, :] = turned
+
+    @pl.loop(0, count_ref.shape[0])
+    def _(o):
+        count_ref[o] = 0
+
+    for slot_id in range(NEAR, slots):
+
+        @pl.loop(0, blocks_dev)
+        def _(b):
+            owner = cols_ref[slot_id, b] // blocks_dev
+            rank = count_ref[owner]
+            count_ref[owner] = rank + 1
+            where_ref[b * (slots - NEAR) + slot_id - NEAR] = owner * cap + rank
 
 
 def split(x):
@@ -103,19 +121,26 @@
 
 
 def near_kernel(
-    group, cap, cols_ref, base_ref, left_ref, own_ref, right_ref, tiles_ref, graph_ref, mass_ref,
-    part_ref, graph2_ref, where_ref, window, tiles, part, pull_ref, count_ref, sems, tile_sems, part_sems,
+    group, middle, cols_ref, place_ref, left_ref, own_ref, right_ref, across_ref, tiles_ref, graph_ref, mass_ref,
+    graph2_ref, part_ref, window, tiles, part, pull_ref, sems, tile_sems, part_sems,
 ):
     blocks_dev, tile, clusters = own_ref.shape
-    slots = tiles_ref.shape[1]
-    shards = mass_ref.shape[0]
     steps = blocks_dev // group
-    copies = [
-        pltpu.make_async_copy(src, window.at[pl.ds(i * blocks_dev, blocks_dev)], sems.at[i])
-        for i, src in enumerate((left_ref, own_ref, right_ref))
-    ]
-    for copy in copies:
-        copy.start()
+    place = place_ref[0]
+
+    def take(src, i):
+        return pltpu.make_async_copy(src, window.at[pl.ds(i * blocks_dev, blocks_dev)], sems.at[i])
+
+    take(own_ref, 1).start()
+    for i, src, at in ((0, left_ref, middle), (2, right_ref, middle - 1)):
+
+        @pl.when(place == at)
+        def _():
+            take(across_ref, i).start()
+
+        @pl.when(place != at)
+        def _():
+            take(src, i).start()
 
     def fetch(i):
         here = pl.ds(i * group, group)
@@ -140,26 +165,10 @@
         )
         / clusters
     )
-    turned = graph.T.astype(bf16)
-    graph2_ref[:clusters, :] = turned
-    graph2_ref[clusters:, :] = turned
-
-    @pl.loop(0, shards)
-    def _(o):
-        count_ref[o] = 0
-
-    for slot_id in range(NEAR, slots):
-
-        @pl.loop(0, blocks_dev)
-        def _(b):
-            owner = cols_ref[slot_id, b] // blocks_dev
-            rank = count_ref[owner]
-            count_ref[owner] = rank + 1
-            where_ref[b * (slots - NEAR) + slot_id - NEAR] = owner * cap + rank
-
-    for copy in copies:
-        copy.wait()
-
+    for i, src in enumerate((left_ref, own_ref, right_ref)):
+        take(src, i).wait()
+
+    base = (place - 1) * blocks_dev
     scale = 2.0 * eta_step / clusters
 
     @pl.loop(0, steps)
@@ -168,7 +177,7 @@
         for i in range(group):
             b = step * group + i
             here = pl.ds(pl.multiple_of(b * tile, tile), tile)
-            picked = [window[cols_ref[s, b] - base_ref[0]] for s in range(NEAR)]
+            picked = [window[cols_ref[s, b] - base] for s in range(NEAR)]
             wide = jnp.concatenate([tiles[b, s] for s in range(NEAR)], axis=1)
             spread = jnp.dot(wide, jnp.concatenate(picked, axis=0), preferred_element_type=f32)
             affinity = jnp.dot(split(spread), graph2_ref[...], preferred_element_type=f32)
@@ -183,7 +192,7 @@
 
 
 def far_kernel(
-    group, nodes_total, where_ref, blocks_ref, tiles_ref, part_ref, graph2_ref,
+    group, chunk, nodes_total, where_ref, blocks_ref, tiles_ref, part_ref, graph2_ref,
     logits_ref, mass_ref, tiles, tile_sems, part_sems,
 ):
     tile, clusters = blocks_ref.shape[1:]
@@ -192,38 +201,48 @@
     scale = 2.0 * eta_step / clusters
 
     def fetches(i):
-        here = pl.ds(i * group, group)
-        there = pl.ds(i * group * tile, group * tile)
+        here = pl.ds(i * chunk, chunk)
+        there = pl.ds(i * chunk * tile, chunk * tile)
         return (
             pltpu.make_async_copy(tiles_ref.at[here, pl.ds(NEAR, far_slots)], tiles.at[here], tile_sems.at[i]),
             pltpu.make_async_copy(part_ref.at[there], logits_ref.at[there], part_sems.at[i]),
         )
 
-    for i in range(steps):
+    for i in range(blocks_dev // chunk):
         for copy in fetches(i):
             copy.start()
 
-    total = jnp.zeros((8, clusters), f32)
-    for step in range(steps):
-        for copy in fetches(step):
-            copy.wait()
+    def products(step):
+        first = step * group
+        if first % chunk == 0:
+            for copy in fetches(first // chunk):
+                copy.wait()
         spreads = []
-        for i in range(group):
-            b = step * group + i
+        for b in range(first, first + group):
             picked = [blocks_ref[where_ref[b * far_slots + s]] for s in range(far_slots)]
             wide = jnp.concatenate([tiles[b, s] for s in range(far_slots)], axis=1)
             spreads.append(split(jnp.dot(wide, jnp.concatenate(picked, axis=0), preferred_element_type=f32)))
+        return jnp.concatenate(spreads, axis=0)
+
+    total = jnp.zeros((8, clusters), f32)
+    ahead = products(0)
+    for step in range(steps):
+        spreads = ahead
+        if step + 1 < steps:
+            ahead = products(step + 1)
         here = pl.ds(step * group * tile, group * tile)
-        affinity = jnp.dot(jnp.concatenate(spreads, axis=0), graph2_ref[...], preferred_element_type=f32)
+        affinity = jnp.dot(spreads, graph2_ref[...], preferred_element_type=f32)
         logits = logits_ref[here, :] + scale * affinity
         logits_ref[here, :] = logits
         total = total + jnp.sum(jnp.exp(logits).reshape(group * tile // 8, 8, clusters), axis=0)
 
-    mass_ref[...] = jnp.sum(total, axis=0, keepdims=True) / nodes_total
-
-
-def last_kernel(parts, logits_ref, newmass_ref, more_ref, target_ref, out_ref, kept, sems):
-    shift = relax_power * (jnp.log(target_ref[...]) - jnp.log(newmass_ref[...] + more_ref[...]))
+    mass = jnp.sum(total, axis=0, keepdims=True) / nodes_total
+    mass_ref[:, 0, :] = jnp.broadcast_to(mass, (mass_ref.shape[0], clusters))
+
+
+def last_kernel(parts, logits_ref, mass_ref, target_ref, out_ref, kept, sems):
+    newmass = jnp.sum(mass_ref[:, 0, :], axis=0, keepdims=True)
+    shift = relax_power * (jnp.log(target_ref[...]) - jnp.log(newmass))
     rows = logits_ref.shape[0]
     step = rows // parts
     copies = []
@@ -253,54 +272,60 @@
     steps = blocks_dev // group
     flops = 2 * rows * clusters
 
-    ends = shards - 1
-    left = lax.ppermute(blocks, NODES, [(i, i + 1) for i in range(ends)])
-    right = lax.ppermute(blocks, NODES, [(i + 1, i) for i in range(ends)])
-
-    asked = pl.pallas_call(
+    middle = shards // 2
+    across = lax.ppermute(blocks, NODES, [(middle - 1, middle), (middle, middle - 1)])
+    left = lax.ppermute(blocks, NODES, [(i, i + 1) for i in range(shards - 1) if i + 1 != middle])
+    right = lax.ppermute(blocks, NODES, [(i + 1, i) for i in range(shards - 1) if i + 1 != middle])
+
+    asked, held = pl.pallas_call(
         functools.partial(requests_kernel, nodes_total),
-        out_shape=pltpu.VMEM((shards, 1, 2 * clusters), f32),
+        out_shape=(jax.ShapeDtypeStruct((shards, 1, 2 * clusters), f32), pltpu.VMEM((rows, clusters), bf16)),
         in_specs=[VMEM, ANY],
-        out_specs=VMEM,
-        scratch_shapes=[pltpu.VMEM((rows, clusters), bf16), pltpu.SemaphoreType.DMA((8,))],
+        out_specs=(VMEM, VMEM),
+        scratch_shapes=[pltpu.SemaphoreType.DMA((8,))],
         compiler_params=params(8),
         name="requests",
     )(cols, in_hbm(coupling))
     heard = lax.all_to_all(asked, NODES, split_axis=0, concat_axis=0, tiled=True)
+    graph2, where = pl.pallas_call(
+        functools.partial(prep_kernel, cap),
+        out_shape=(
+            jax.ShapeDtypeStruct((2 * clusters, clusters), bf16),
+            jax.ShapeDtypeStruct((far_count,), i32),
+        ),
+        in_specs=[SMEM, VMEM],
+        out_specs=(VMEM, SMEM),
+        scratch_shapes=[pltpu.SMEM((shards,), i32)],
+        compiler_params=params(4),
+        name="prep",
+    )(cols, cluster_graph)
     found = pl.pallas_call(
         functools.partial(gather_kernel, cap),
         out_shape=pltpu.HBM((shards * cap, tile, clusters), bf16),
-        in_specs=[VMEM, ANY],
+        in_specs=[VMEM, VMEM],
         out_specs=ANY,
         scratch_shapes=[
-            pltpu.VMEM((blocks_dev, tile, clusters), bf16),
             pltpu.VMEM((shards, clusters), i32),
             pltpu.SMEM((shards, clusters), i32),
-            pltpu.SemaphoreType.DMA((3,)),
+            pltpu.SemaphoreType.DMA((2,)),
         ],
         compiler_params=params(8),
         name="gather",
-    )(on_chip(heard), in_hbm(blocks))
+    )(on_chip(heard), on_chip(held.reshape(blocks.shape)))
     fetched = lax.all_to_all(
         found.reshape(shards, cap, tile, clusters), NODES, split_axis=0, concat_axis=0, tiled=True
     ).reshape(shards * cap, tile, clusters)
 
-    base = (my_index * blocks_dev - blocks_dev).astype(i32).reshape(1)
-    part, graph2, where = pl.pallas_call(
-        functools.partial(near_kernel, group, cap),
-        out_shape=(
-            pltpu.HBM((rows, clusters), f32),
-            pltpu.VMEM((2 * clusters, clusters), bf16),
-            jax.ShapeDtypeStruct((far_count,), i32),
-        ),
-        in_specs=[SMEM, SMEM, ANY, ANY, ANY, ANY, VMEM, VMEM],
-        out_specs=(ANY, VMEM, SMEM),
+    part = pl.pallas_call(
+        functools.partial(near_kernel, group, middle),
+        out_shape=pltpu.HBM((rows, clusters), f32),
+        in_specs=[SMEM, SMEM, ANY, ANY, ANY, ANY, ANY, VMEM, VMEM, VMEM],
+        out_specs=ANY,
         scratch_shapes=[
             pltpu.VMEM((3 * blocks_dev, tile, clusters), bf16),
             pltpu.VMEM((blocks_dev, NEAR, tile, tile), bf16),
             pltpu.VMEM((rows, clusters), f32),
             pltpu.VMEM((8, clusters), f32),
-            pltpu.SMEM((shards,), i32),
             pltpu.SemaphoreType.DMA((3,)),
             pltpu.SemaphoreType.DMA((steps,)),
             pltpu.SemaphoreType.DMA((steps,)),
@@ -310,17 +335,21 @@
             flops=flops * (NEAR * tile + 2 * clusters), bytes_accessed=16 << 20, transcendentals=rows * clusters
         ),
         name="near",
-    )(cols, base, in_hbm(left), in_hbm(blocks), in_hbm(right), in_hbm(tile_vals), cluster_graph, on_chip(heard))
-
-    logits, mass_part = pl.pallas_call(
-        functools.partial(far_kernel, group, nodes_total),
-        out_shape=(pltpu.VMEM((rows, clusters), f32), pltpu.VMEM((1, clusters), f32)),
+    )(
+        cols, my_index.astype(i32).reshape(1), in_hbm(left), in_hbm(blocks), in_hbm(right), in_hbm(across),
+        in_hbm(tile_vals), cluster_graph, on_chip(heard), on_chip(graph2),
+    )
+
+    chunk = min(16, blocks_dev)
+    logits, mass_parts = pl.pallas_call(
+        functools.partial(far_kernel, group, chunk, nodes_total),
+        out_shape=(pltpu.VMEM((rows, clusters), f32), pltpu.VMEM((shards, 1, clusters), f32)),
         in_specs=[SMEM, VMEM, ANY, ANY, VMEM],
         out_specs=(VMEM, VMEM),
         scratch_shapes=[
             pltpu.VMEM((blocks_dev, far_slots, tile, tile), bf16),
-            pltpu.SemaphoreType.DMA((steps,)),
-            pltpu.SemaphoreType.DMA((steps,)),
+            pltpu.SemaphoreType.DMA((blocks_dev // chunk,)),
+            pltpu.SemaphoreType.DMA((blocks_dev // chunk,)),
         ],
         compiler_params=params(16),
         cost_estimate=pl.CostEstimate(
@@ -329,22 +358,17 @@
         name="far",
     )(where, on_chip(fetched), in_hbm(tile_vals), in_hbm(part), on_chip(graph2))
 
-    newmass, more = mass_part, jnp.zeros_like(mass_part)
-    span = 1
-    while span < shards:
-        newmass = newmass + more if span > 1 else newmass
-        more = lax.ppermute(newmass, NODES, [(i, i ^ span) for i in range(shards)])
-        span *= 2
+    masses = lax.all_to_all(mass_parts, NODES, split_axis=0, concat_axis=0, tiled=True)
 
     return pl.pallas_call(
         functools.partial(last_kernel, 8),
         out_shape=jax.ShapeDtypeStruct((rows, clusters), f32),
-        in_specs=[VMEM, VMEM, VMEM, VMEM],
+        in_specs=[VMEM, VMEM, VMEM],
         out_specs=ANY,
         scratch_shapes=[pltpu.VMEM((rows, clusters), f32), pltpu.SemaphoreType.DMA((8,))],
         compiler_params=params(8),
         name="last",
-    )(on_chip(logits), on_chip(newmass), on_chip(more), cluster_mass.reshape(1, clusters))
+    )(on_chip(logits), on_chip(masses), cluster_mass.reshape(1, clusters))
 
 
 def solution(mesh):

time: 112 us -> 108 us (0.964)
  the two profiles are of different devices: /device:TPU:16 before, /device:TPU:0 now
where the time goes in v2:
time: 108 us; the launch traced here: 107 us
  blocking collectives  53 us (49%)
  Pallas kernels  22 us (20%)
  waiting for transfers between devices  20.8 us (19%)
  starting transfers between devices  10.8 us (10%)
    all_to_all x1, blocking collectives, local(): lax.all_to_all(mass_parts, NODES, split_axis=0, concat_axis=0, tiled=True)  39.3 us
    all_to_all x1, waiting for transfers between devices, local(): lax.all_to_all(found.reshape(shards, cap, tile, clusters), NODES, split_a...  20.8 us
    all_to_all x1, blocking collectives, local(): lax.all_to_all(asked, NODES, split_axis=0, concat_axis=0, tiled=True)  13.7 us
    pallas_call x1, Pallas kernels, local(): pl.pallas_call(functools.partial(near_kernel, group, middle), out_shape=p...  10.8 us
    ppermute x1, starting transfers between devices, local(): lax.ppermute(blocks, NODES, [(i, i + 1) for i in range(shards - 1) if i +...  4.02 us
    all_to_all x1, starting transfers between devices, local(): lax.all_to_all(found.reshape(shards, cap, tile, clusters), NODES, split_a...  3.86 us
    pallas_call x1, Pallas kernels, local(): pl.pallas_call(functools.partial(far_kernel, group, chunk, nodes_total),...  3.69 us
    pallas_call x1, Pallas kernels, local(): pl.pallas_call(functools.partial(prep_kernel, cap), out_shape=(jax.ShapeD...  2.39 us
  transfers between devices with their start and end apart: 4, of which 1 were waited for; matrix products, arithmetic and copies ran while one was open for 0% of the time, Pallas kernels for 12%

profile of v2, /device:TPU:0, one launch (start us, length us, event | category | flops | bytes accessed | tf_op | source)
XLA Modules:
  0.0 107.3 jit_solution(8932126491434328984)
XLA Ops:
  0.0 0.0 copy-start.1
  0.0 0.7 copy-done.1
  0.7 1.5 %requests.1 = (f32[16,1,256]{2,1,0:T(1,128)S(1)}, bf16[4096,128]{1,0:T(8,128)(2,1)S(1)}) custom-call(s32[6,32]{1,0:T(8,128)S(1)} %bitcast.9, bf16[4096,128]{1,0:T(8,128)(2,1)} %coupling_ref.1), custom_call_target="tpu_custom_call" | custom-call | tf_op jit(solution)/shard_map/requests/pallas_call | solution.py:280
  2.2 13.7 %all_to_all.15.heard_ref.mass_ref = f32[16,1,256]{2,1,0:T(1,128)S(1)} all-to-all(f32[16,1,256]{2,1,0:T(1,128)S(1)} %get-tuple-element.12), channel_id=1, replica_groups=mesh['groups'=2,'rows'=8,'sub'=2] {'rows','sub'}, dimensions={0} | all-to-all | bytes 32768 | tf_op jit(solution)/shard_map/all_to_all | solution.py:289
  15.9 2.0 %gather.1 = bf16[64,128,128]{2,1,0:T(8,128)(2,1)} custom-call(f32[16,1,256]{2,1,0:T(1,128)S(1)} %all_to_all.15.heard_ref.mass_ref, bf16[32,128,128]{2,1,0:T(8,128)(2,1)S(1)} %bitcast.8), custom_call_target="tpu_custom_call" | custom-call | tf_op jit(solution)/shard_map/gather/pallas_call | solution.py:302
  17.9 0.0 copy-start.4
  17.9 0.0 copy-start
  17.9 0.0 copy-start.2
  18.0 3.9 %all-to-all-start.1 = ((bf16[16,4,128,128]{3,2,1,0:T(8,128)(2,1)}), bf16[16,4,128,128]{3,2,1,0:T(8,128)(2,1)S(1)}, u32[]{:S(2)}, u32[]{:S(2)}) async-start(bf16[16,4,128,128]{3,2,1,0:T(8,128)(2,1)} %bitcast.13), calls=%async_computation.1 | async-start | bytes 4194304 | tf_op jit(solution)/shard_map/all_to_all | solution.py:315
  21.8 0.0 copy-done.4
  21.8 1.6 %collective-permute-start.2 = (bf16[32,128,128]{2,1,0:T(8,128)(2,1)S(1)}, bf16[32,128,128]{2,1,0:T(8,128)(2,1)}, u32[]{:S(2)}, u32[]{:S(2)}) collective-permute-start(bf16[32,128,128]{2,1,0:T(8,128)(2,1)S(1)} %bitcast.15), channel_id=1, source_target_pairs={{7,8},{8,7},{23,24},{24,23}} | collective-permute-start | bytes 3145736 | tf_op jit(solution)/shard_map/ppermute | solution.py:276
  23.5 1.3 %collective-permute-start.1 = (bf16[32,128,128]{2,1,0:T(8,128)(2,1)S(1)}, bf16[32,128,128]{2,1,0:T(8,128)(2,1)}, u32[]{:S(2)}, u32[]{:S(2)}) collective-permute-start(bf16[32,128,128]{2,1,0:T(8,128)(2,1)S(1)} %bitcast.16), channel_id=1, source_target_pairs={{1,0},{2,1},{3,2},{4,3},{5,4},{6,5},{7,6},{9,8},{10,9},{11,10},{12... | collective-permute-start | bytes 3145736 | tf_op jit(solution)/shard_map/ppermute | solution.py:278
  24.8 4.0 %collective-permute-start = (bf16[32,128,128]{2,1,0:T(8,128)(2,1)S(1)}, bf16[32,128,128]{2,1,0:T(8,128)(2,1)}, u32[]{:S(2)}, u32[]{:S(2)}) collective-permute-start(bf16[32,128,128]{2,1,0:T(8,128)(2,1)S(1)} %bitcast.17), channel_id=1, source_target_pairs={{0,1},{1,2},{2,3},{3,4},{4,5},{5,6},{6,7},{8,9},{9,10},{10,11},{11... | collective-permute-start | bytes 3145736 | tf_op jit(solution)/shard_map/ppermute | solution.py:277
  28.8 0.0 copy-done
  28.8 0.0 copy-done.2
  28.8 2.4 %prep.1 = (bf16[256,128]{1,0:T(8,128)(2,1)S(1)}, s32[64]{0:T(128)S(1)}) custom-call(s32[6,32]{1,0:T(8,128)S(1)} %bitcast.10, s32[128,128]{1,0:T(8,128)S(1)} %copy-done), custom_call_target="tpu_custom_call" | custom-call | tf_op jit(solution)/shard_map/prep/pallas_call | solution.py:290
  31.2 0.0 collective-permute-done.2.across_ref
  31.2 0.0 collective-permute-done.1.right_ref
  31.2 0.0 collective-permute-done.left_ref
  31.2 10.8 %near.1.part_ref = f32[4096,128]{1,0:T(8,128)} custom-call(s32[6,32]{1,0:T(8,128)S(1)} %bitcast.11, s32[1]{0:T(128)} %bitcast.4.place_ref, bf16[32,128,128]{2,1,0:T(8,128)(2,1)} %collective-permute-done.left_ref, bf16[32,128,128]{2,1,0:T(8,128)(2,1)} %bitcast.14, bf16[32,128,128]{2,1,0:T(8,128)(2,1)} %collective-permute-done.1.right_ref, ...), custom_call_target="tpu_custom_call" | custom-call | flops 805306368 | bytes 16777216 | tf_op jit(solution)/shard_map/near/pallas_call | solution.py:319
  42.0 20.8 %all-to-all-done.1 = bf16[16,4,128,128]{3,2,1,0:T(8,128)(2,1)S(1)} async-done(((bf16[16,4,128,128]{3,2,1,0:T(8,128)(2,1)}), bf16[16,4,128,128]{3,2,1,0:T(8,128)(2,1)S(1)}, u32[]{:S(2)}, u32[]{:S(2)}) %all-to-all-start.1) | async-done | bytes 2097184 | tf_op jit(solution)/shard_map/all_to_all | solution.py:315
  62.8 0.0 copy-start.3
  62.8 3.7 %far.1 = (f32[4096,128]{1,0:T(8,128)S(1)}, f32[16,1,128]{2,1,0:T(1,128)S(1)}) custom-call(s32[64]{0:T(128)S(1)} %get-tuple-element.11.where_ref, bf16[64,128,128]{2,1,0:T(8,128)(2,1)S(1)} %bitcast.7, bf16[32,6,128,128]{3,2,1,0:T(8,128)(2,1)} %tiles_ref.3, f32[4096,128]{1,0:T(8,128)} %near.1.part_ref, bf16[256,128]{1,0:T(8,128)(2,1)S(1)} %get-tuple-element.14.graph2_ref), custom_call_target="tpu_custom_call" | custom-call | flops 536870912 | bytes 8388608 | tf_op jit(solution)/shard_map/far/pallas_call | solution.py:344
  66.5 39.3 %all_to_all.16.mass_ref = f32[16,1,128]{2,1,0:T(1,128)S(1)} all-to-all(f32[16,1,128]{2,1,0:T(1,128)S(1)} %get-tuple-element.16), channel_id=1, replica_groups=mesh['groups'=2,'rows'=8,'sub'=2] {'rows','sub'}, dimensions={0} | all-to-all | bytes 16384 | tf_op jit(solution)/shard_map/all_to_all | solution.py:361
  105.8 0.0 copy-done.3
  105.8 1.6 %last.1 = f32[4096,128]{1,0:T(8,128)} custom-call(f32[4096,128]{1,0:T(8,128)S(1)} %get-tuple-element.15.logits_ref, f32[16,1,128]{2,1,0:T(1,128)S(1)} %all_to_all.16.mass_ref, f32[1,128]{1,0:T(1,128)S(1)} %bitcast.12), custom_call_target="tpu_custom_call" | custom-call | tf_op jit(solution)/shard_map/last/pallas_call | solution.py:363
Async XLA Ops:
  0.0 0.7 copy-start.1
  17.9 3.9 %copy-start.4 = (bf16[4096,128]{1,0:T(8,128)(2,1)S(1)}, bf16[4096,128]{1,0:T(8,128)(2,1)}, u32[]{:S(2)}) copy-start(bf16[4096,128]{1,0:T(8,128)(2,1)} %coupling_ref.1) | copy-start | bytes 3145732
  17.9 10.8 %copy-start = (s32[128,128]{1,0:T(8,128)S(1)}, s32[128,128]{1,0:T(8,128)}, u32[]{:S(2)}) copy-start(s32[128,128]{1,0:T(8,128)} %graph_ref.3) | copy-start | bytes 196612
  17.9 10.8 %copy-start.2 = (s32[32,6]{0,1:T(8,128)S(1)}, s32[32,6]{0,1:T(8,128)}, u32[]{:S(2)}) copy-start(s32[32,6]{0,1:T(8,128)} %param.7) | copy-start | bytes 2308
  18.0 44.8 %all-to-all-start.1 = ((bf16[16,4,128,128]{3,2,1,0:T(8,128)(2,1)}), bf16[16,4,128,128]{3,2,1,0:T(8,128)(2,1)S(1)}, u32[]{:S(2)}, u32[]{:S(2)}) async-start(bf16[16,4,128,128]{3,2,1,0:T(8,128)(2,1)} %bitcast.13), calls=%async_computation.1 | async-start | bytes 4194304 | tf_op jit(solution)/shard_map/all_to_all | solution.py:315
  21.8 9.4 %collective-permute-start.2 = (bf16[32,128,128]{2,1,0:T(8,128)(2,1)S(1)}, bf16[32,128,128]{2,1,0:T(8,128)(2,1)}, u32[]{:S(2)}, u32[]{:S(2)}) collective-permute-start(bf16[32,128,128]{2,1,0:T(8,128)(2,1)S(1)} %bitcast.15), channel_id=1, source_target_pairs={{7,8},{8,7},{23,24},{24,23}} | collective-permute-start | bytes 3145736 | tf_op jit(solution)/shard_map/ppermute | solution.py:276
  23.5 7.7 %collective-permute-start.1 = (bf16[32,128,128]{2,1,0:T(8,128)(2,1)S(1)}, bf16[32,128,128]{2,1,0:T(8,128)(2,1)}, u32[]{:S(2)}, u32[]{:S(2)}) collective-permute-start(bf16[32,128,128]{2,1,0:T(8,128)(2,1)S(1)} %bitcast.16), channel_id=1, source_target_pairs={{1,0},{2,1},{3,2},{4,3},{5,4},{6,5},{7,6},{9,8},{10,9},{11,10},{12... | collective-permute-start | bytes 3145736 | tf_op jit(solution)/shard_map/ppermute | solution.py:278
  24.8 6.5 %collective-permute-start = (bf16[32,128,128]{2,1,0:T(8,128)(2,1)S(1)}, bf16[32,128,128]{2,1,0:T(8,128)(2,1)}, u32[]{:S(2)}, u32[]{:S(2)}) collective-permute-start(bf16[32,128,128]{2,1,0:T(8,128)(2,1)S(1)} %bitcast.17), channel_id=1, source_target_pairs={{0,1},{1,2},{2,3},{3,4},{4,5},{5,6},{6,7},{8,9},{9,10},{10,11},{11... | collective-permute-start | bytes 3145736 | tf_op jit(solution)/shard_map/ppermute | solution.py:277
  62.8 43.0 %copy-start.3 = (f32[128]{0:T(128)S(1)}, f32[128]{0:T(128)}, u32[]{:S(2)}) copy-start(f32[128]{0:T(128)} %param.9) | copy-start | bytes 1540

commit v3 on v2

--- a/solution.py
+++ b/solution.py
@@ -94,53 +94,24 @@
     pltpu.make_async_copy(out_ref, out_ref, sems.at[1]).wait()
 
 
-def prep_kernel(cap, cols_ref, graph_ref, graph2_ref, where_ref, count_ref):
-    slots, blocks_dev = cols_ref.shape
-    clusters = graph_ref.shape[0]
-    turned = graph_ref[...].astype(f32).T.astype(bf16)
-    graph2_ref[:clusters, :] = turned
-    graph2_ref[clusters:, :] = turned
-
-    @pl.loop(0, count_ref.shape[0])
-    def _(o):
-        count_ref[o] = 0
-
-    for slot_id in range(NEAR, slots):
-
-        @pl.loop(0, blocks_dev)
-        def _(b):
-            owner = cols_ref[slot_id, b] // blocks_dev
-            rank = count_ref[owner]
-            count_ref[owner] = rank + 1
-            where_ref[b * (slots - NEAR) + slot_id - NEAR] = owner * cap + rank
-
-
 def split(x):
     high = x.astype(bf16)
     return jnp.concatenate([high, (x - high.astype(f32)).astype(bf16)], axis=1)
 
 
 def near_kernel(
-    group, middle, cols_ref, place_ref, left_ref, own_ref, right_ref, across_ref, tiles_ref, graph_ref, mass_ref,
-    graph2_ref, part_ref, window, tiles, part, pull_ref, sems, tile_sems, part_sems,
+    group, cap, cols_ref, place_ref, left_ref, own_ref, right_ref, tiles_ref, graph_ref, mass_ref,
+    part_ref, graph2_ref, where_ref, window, tiles, part, pull_ref, count_ref, sems, tile_sems, part_sems,
 ):
     blocks_dev, tile, clusters = own_ref.shape
+    slots = tiles_ref.shape[1]
     steps = blocks_dev // group
-    place = place_ref[0]
-
-    def take(src, i):
-        return pltpu.make_async_copy(src, window.at[pl.ds(i * blocks_dev, blocks_dev)], sems.at[i])
-
-    take(own_ref, 1).start()
-    for i, src, at in ((0, left_ref, middle), (2, right_ref, middle - 1)):
-
-        @pl.when(place == at)
-        def _():
-            take(across_ref, i).start()
-
-        @pl.when(place != at)
-        def _():
-            take(src, i).start()
+    copies = [
+        pltpu.make_async_copy(src, window.at[pl.ds(i * blocks_dev, blocks_dev)], sems.at[i])
+        for i, src in enumerate((left_ref, own_ref, right_ref))
+    ]
+    for copy in copies:
+        copy.start()
 
     def fetch(i):
         here = pl.ds(i * group, group)
@@ -165,10 +136,27 @@
         )
         / clusters
     )
-    for i, src in enumerate((left_ref, own_ref, right_ref)):
-        take(src, i).wait()
-
-    base = (place - 1) * blocks_dev
+    turned = graph.T.astype(bf16)
+    graph2_ref[:clusters, :] = turned
+    graph2_ref[clusters:, :] = turned
+
+    @pl.loop(0, count_ref.shape[0])
+    def _(o):
+        count_ref[o] = 0
+
+    for slot_id in range(NEAR, slots):
+
+        @pl.loop(0, blocks_dev)
+        def _(b):
+            owner = cols_ref[slot_id, b] // blocks_dev
+            rank = count_ref[owner]
+            count_ref[owner] = rank + 1
+            where_ref[b * (slots - NEAR) + slot_id - NEAR] = owner * cap + rank
+
+    for copy in copies:
+        copy.wait()
+
+    base = (place_ref[0] - 1) * blocks_dev
     scale = 2.0 * eta_step / clusters
 
     @pl.loop(0, steps)
@@ -272,10 +260,8 @@
     steps = blocks_dev // group
     flops = 2 * rows * clusters
 
-    middle = shards // 2
-    across = lax.ppermute(blocks, NODES, [(middle - 1, middle), (middle, middle - 1)])
-    left = lax.ppermute(blocks, NODES, [(i, i + 1) for i in range(shards - 1) if i + 1 != middle])
-    right = lax.ppermute(blocks, NODES, [(i + 1, i) for i in range(shards - 1) if i + 1 != middle])
+    left = lax.ppermute(blocks, NODES, [(i, i + 1) for i in range(shards - 1)])
+    right = lax.ppermute(blocks, NODES, [(i + 1, i) for i in range(shards - 1)])
 
     asked, held = pl.pallas_call(
         functools.partial(requests_kernel, nodes_total),
@@ -287,18 +273,6 @@
         name="requests",
     )(cols, in_hbm(coupling))
     heard = lax.all_to_all(asked, NODES, split_axis=0, concat_axis=0, tiled=True)
-    graph2, where = pl.pallas_call(
-        functools.partial(prep_kernel, cap),
-        out_shape=(
-            jax.ShapeDtypeStruct((2 * clusters, clusters), bf16),
-            jax.ShapeDtypeStruct((far_count,), i32),
-        ),
-        in_specs=[SMEM, VMEM],
-        out_specs=(VMEM, SMEM),
-        scratch_shapes=[pltpu.SMEM((shards,), i32)],
-        compiler_params=params(4),
-        name="prep",
-    )(cols, cluster_graph)
     found = pl.pallas_call(
         functools.partial(gather_kernel, cap),
         out_shape=pltpu.HBM((shards * cap, tile, clusters), bf16),
@@ -316,16 +290,21 @@
         found.reshape(shards, cap, tile, clusters), NODES, split_axis=0, concat_axis=0, tiled=True
     ).reshape(shards * cap, tile, clusters)
 
-    part = pl.pallas_call(
-        functools.partial(near_kernel, group, middle),
-        out_shape=pltpu.HBM((rows, clusters), f32),
-        in_specs=[SMEM, SMEM, ANY, ANY, ANY, ANY, ANY, VMEM, VMEM, VMEM],
-        out_specs=ANY,
+    part, graph2, where = pl.pallas_call(
+        functools.partial(near_kernel, group, cap),
+        out_shape=(
+            pltpu.HBM((rows, clusters), f32),
+            pltpu.VMEM((2 * clusters, clusters), bf16),
+            jax.ShapeDtypeStruct((far_count,), i32),
+        ),
+        in_specs=[SMEM, SMEM, ANY, ANY, ANY, ANY, VMEM, VMEM],
+        out_specs=(ANY, VMEM, SMEM),
         scratch_shapes=[
             pltpu.VMEM((3 * blocks_dev, tile, clusters), bf16),
             pltpu.VMEM((blocks_dev, NEAR, tile, tile), bf16),
             pltpu.VMEM((rows, clusters), f32),
             pltpu.VMEM((8, clusters), f32),
+            pltpu.SMEM((shards,), i32),
             pltpu.SemaphoreType.DMA((3,)),
             pltpu.SemaphoreType.DMA((steps,)),
             pltpu.SemaphoreType.DMA((steps,)),
@@ -336,8 +315,8 @@
         ),
         name="near",
     )(
-        cols, my_index.astype(i32).reshape(1), in_hbm(left), in_hbm(blocks), in_hbm(right), in_hbm(across),
-        in_hbm(tile_vals), cluster_graph, on_chip(heard), on_chip(graph2),
+        cols, my_index.astype(i32).reshape(1), in_hbm(left), in_hbm(blocks), in_hbm(right),
+        in_hbm(tile_vals), cluster_graph, on_chip(heard),
     )
 
     chunk = min(16, blocks_dev)

time: 108 us -> 108 us (level)
  waiting for transfers between devices: 20.8 us -> 24.3 us
  Pallas kernels: 22 us -> 20.2 us
  starting transfers between devices: 10.8 us -> 9.18 us
    all_to_all x1, waiting for transfers between devices: 20.8 us -> 22.8 us  [local(): lax.all_to_all(found.reshape(shards, cap, tile, clusters), NODES, split_a...]
    pallas_call x2 -> x1, Pallas kernels: 13.2 us -> 11.4 us  [local(): pl.pallas_call(functools.partial(near_kernel, group, cap), out_shape=(plt...]
    ppermute x3 -> x2, starting transfers between devices: 6.93 us -> 5.32 us  [the longest x1 4.03 us: local(): left = lax.ppermute(blocks, NODES, [(i, i + 1) for i in range(shards - 1)])]
    ppermute x3 -> x2, waiting for transfers between devices: 0.01 us -> 1.41 us  [the longest x1 1.41 us: local(): left = lax.ppermute(blocks, NODES, [(i, i + 1) for i in range(shards - 1)])]
  transfers between devices with their start and end apart: 4 -> 3, of which waited for: 1 -> 2; matrix products, arithmetic and copies ran while one was open for 0% -> 0% of each run, Pallas kernels for 12% -> 11%
where the time goes in v3:
time: 108 us
  blocking collectives  53.5 us (50%)
  waiting for transfers between devices  24.3 us (22%)
  Pallas kernels  20.2 us (19%)
  starting transfers between devices  9.18 us (8%)
    all_to_all x1, blocking collectives, local(): lax.all_to_all(mass_parts, NODES, split_axis=0, concat_axis=0, tiled=True)  39.8 us
    all_to_all x1, waiting for transfers between devices, local(): lax.all_to_all(found.reshape(shards, cap, tile, clusters), NODES, split_a...  22.8 us
    all_to_all x1, blocking collectives, local(): lax.all_to_all(asked, NODES, split_axis=0, concat_axis=0, tiled=True)  13.7 us
    pallas_call x1, Pallas kernels, local(): pl.pallas_call(functools.partial(near_kernel, group, cap), out_shape=(plt...  11.4 us
    ppermute x1, starting transfers between devices, local(): left = lax.ppermute(blocks, NODES, [(i, i + 1) for i in range(shards - 1)])  4.03 us
    all_to_all x1, starting transfers between devices, local(): lax.all_to_all(found.reshape(shards, cap, tile, clusters), NODES, split_a...  3.86 us
    pallas_call x1, Pallas kernels, local(): pl.pallas_call(functools.partial(far_kernel, group, chunk, nodes_total),...  3.69 us
  transfers between devices with their start and end apart: 3, of which 2 were waited for; matrix products, arithmetic and copies ran while one was open for 0% of the time, Pallas kernels for 11%

profile of v3, /device:TPU:0, one launch (start us, length us, event | category | flops | bytes accessed | tf_op | source)
XLA Modules:
  0.0 107.9 jit_solution(11119581106161200892)
XLA Ops:
  0.0 0.0 copy-start.1
  0.0 0.7 copy-done.1
  0.7 1.5 %requests.1 = (f32[16,1,256]{2,1,0:T(1,128)S(1)}, bf16[4096,128]{1,0:T(8,128)(2,1)S(1)}) custom-call(s32[6,32]{1,0:T(8,128)S(1)} %bitcast.9, bf16[4096,128]{1,0:T(8,128)(2,1)} %coupling_ref.1), custom_call_target="tpu_custom_call" | custom-call | tf_op jit(solution)/shard_map/requests/pallas_call | solution.py:266
  2.2 13.7 %all_to_all.15.mass_ref.heard_ref = f32[16,1,256]{2,1,0:T(1,128)S(1)} all-to-all(f32[16,1,256]{2,1,0:T(1,128)S(1)} %get-tuple-element.12), channel_id=1, replica_groups=mesh['groups'=2,'rows'=8,'sub'=2] {'rows','sub'}, dimensions={0} | all-to-all | bytes 32768 | tf_op jit(solution)/shard_map/all_to_all | solution.py:275
  15.9 2.0 %gather.1 = bf16[64,128,128]{2,1,0:T(8,128)(2,1)} custom-call(f32[16,1,256]{2,1,0:T(1,128)S(1)} %all_to_all.15.mass_ref.heard_ref, bf16[32,128,128]{2,1,0:T(8,128)(2,1)S(1)} %bitcast.8), custom_call_target="tpu_custom_call" | custom-call | tf_op jit(solution)/shard_map/gather/pallas_call | solution.py:276
  18.0 0.0 copy-start.4
  18.0 0.0 copy-start
  18.0 0.0 copy-start.2
  18.0 3.9 %all-to-all-start.1 = ((bf16[16,4,128,128]{3,2,1,0:T(8,128)(2,1)}), bf16[16,4,128,128]{3,2,1,0:T(8,128)(2,1)S(1)}, u32[]{:S(2)}, u32[]{:S(2)}) async-start(bf16[16,4,128,128]{3,2,1,0:T(8,128)(2,1)} %bitcast.12), calls=%async_computation.1 | async-start | bytes 4194304 | tf_op jit(solution)/shard_map/all_to_all | solution.py:289
  21.9 0.0 copy-done.4
  21.9 1.3 %collective-permute-start.1 = (bf16[32,128,128]{2,1,0:T(8,128)(2,1)S(1)}, bf16[32,128,128]{2,1,0:T(8,128)(2,1)}, u32[]{:S(2)}, u32[]{:S(2)}) collective-permute-start(bf16[32,128,128]{2,1,0:T(8,128)(2,1)S(1)} %bitcast.14), channel_id=1, source_target_pairs={{1,0},{2,1},{3,2},{4,3},{5,4},{6,5},{7,6},{8,7},{9,8},{10,9},{11,1... | collective-permute-start | bytes 3145736 | tf_op jit(solution)/shard_map/ppermute | solution.py:264
  23.2 4.0 %collective-permute-start = (bf16[32,128,128]{2,1,0:T(8,128)(2,1)S(1)}, bf16[32,128,128]{2,1,0:T(8,128)(2,1)}, u32[]{:S(2)}, u32[]{:S(2)}) collective-permute-start(bf16[32,128,128]{2,1,0:T(8,128)(2,1)S(1)} %bitcast.15), channel_id=1, source_target_pairs={{0,1},{1,2},{2,3},{3,4},{4,5},{5,6},{6,7},{7,8},{8,9},{9,10},{10,1... | collective-permute-start | bytes 3145736 | tf_op jit(solution)/shard_map/ppermute | solution.py:263
  27.2 0.0 collective-permute-done.1.right_ref
  27.2 1.4 %collective-permute-done.left_ref = bf16[32,128,128]{2,1,0:T(8,128)(2,1)} collective-permute-done((bf16[32,128,128]{2,1,0:T(8,128)(2,1)S(1)}, bf16[32,128,128]{2,1,0:T(8,128)(2,1)}, u32[]{:S(2)}, u32[]{:S(2)}) %collective-permute-start) | collective-permute-done | bytes 1048608 | tf_op jit(solution)/shard_map/ppermute | solution.py:263
  28.6 0.0 copy-done
  28.6 0.0 copy-done.2
  28.6 11.4 %near.1 = (f32[4096,128]{1,0:T(8,128)}, bf16[256,128]{1,0:T(8,128)(2,1)S(1)}, s32[64]{0:T(128)S(1)}) custom-call(s32[6,32]{1,0:T(8,128)S(1)} %bitcast.10, s32[1]{0:T(128)} %bitcast.1.place_ref, bf16[32,128,128]{2,1,0:T(8,128)(2,1)} %collective-permute-done.left_ref, bf16[32,128,128]{2,1,0:T(8,128)(2,1)} %bitcast.13, ...), custom_call_target="tpu_custom_call" | custom-call | flops 805306368 | bytes 16777216 | tf_op jit(solution)/shard_map/near/pallas_call | solution.py:293
  40.0 22.8 %all-to-all-done.1 = bf16[16,4,128,128]{3,2,1,0:T(8,128)(2,1)S(1)} async-done(((bf16[16,4,128,128]{3,2,1,0:T(8,128)(2,1)}), bf16[16,4,128,128]{3,2,1,0:T(8,128)(2,1)S(1)}, u32[]{:S(2)}, u32[]{:S(2)}) %all-to-all-start.1) | async-done | bytes 2097184 | tf_op jit(solution)/shard_map/all_to_all | solution.py:289
  62.8 0.0 copy-start.3
  62.8 3.7 %far.1 = (f32[4096,128]{1,0:T(8,128)S(1)}, f32[16,1,128]{2,1,0:T(1,128)S(1)}) custom-call(s32[64]{0:T(128)S(1)} %get-tuple-element.13.where_ref, bf16[64,128,128]{2,1,0:T(8,128)(2,1)S(1)} %bitcast.7, bf16[32,6,128,128]{3,2,1,0:T(8,128)(2,1)} %tiles_ref.3, f32[4096,128]{1,0:T(8,128)} %get-tuple-element.15.part_ref, ...), custom_call_target="tpu_custom_call" | custom-call | flops 536870912 | bytes 8388608 | tf_op jit(solution)/shard_map/far/pallas_call | solution.py:323
  66.5 39.8 %all_to_all.16.mass_ref = f32[16,1,128]{2,1,0:T(1,128)S(1)} all-to-all(f32[16,1,128]{2,1,0:T(1,128)S(1)} %get-tuple-element.18), channel_id=1, replica_groups=mesh['groups'=2,'rows'=8,'sub'=2] {'rows','sub'}, dimensions={0} | all-to-all | bytes 16384 | tf_op jit(solution)/shard_map/all_to_all | solution.py:340
  106.4 0.0 copy-done.3
  106.4 1.6 %last.1 = f32[4096,128]{1,0:T(8,128)} custom-call(f32[4096,128]{1,0:T(8,128)S(1)} %get-tuple-element.17.logits_ref, f32[16,1,128]{2,1,0:T(1,128)S(1)} %all_to_all.16.mass_ref, f32[1,128]{1,0:T(1,128)S(1)} %bitcast.11), custom_call_target="tpu_custom_call" | custom-call | tf_op jit(solution)/shard_map/last/pallas_call | solution.py:342
Async XLA Ops:
  0.0 0.7 copy-start.1
  18.0 3.9 %copy-start.4 = (bf16[4096,128]{1,0:T(8,128)(2,1)S(1)}, bf16[4096,128]{1,0:T(8,128)(2,1)}, u32[]{:S(2)}) copy-start(bf16[4096,128]{1,0:T(8,128)(2,1)} %coupling_ref.1) | copy-start | bytes 3145732
  18.0 10.6 %copy-start = (s32[128,128]{1,0:T(8,128)S(1)}, s32[128,128]{1,0:T(8,128)}, u32[]{:S(2)}) copy-start(s32[128,128]{1,0:T(8,128)} %graph_ref.1) | copy-start | bytes 196612
  18.0 10.6 %copy-start.2 = (s32[32,6]{0,1:T(8,128)S(1)}, s32[32,6]{0,1:T(8,128)}, u32[]{:S(2)}) copy-start(s32[32,6]{0,1:T(8,128)} %param.7) | copy-start | bytes 2308
  18.0 44.8 %all-to-all-start.1 = ((bf16[16,4,128,128]{3,2,1,0:T(8,128)(2,1)}), bf16[16,4,128,128]{3,2,1,0:T(8,128)(2,1)S(1)}, u32[]{:S(2)}, u32[]{:S(2)}) async-start(bf16[16,4,128,128]{3,2,1,0:T(8,128)(2,1)} %bitcast.12), calls=%async_computation.1 | async-start | bytes 4194304 | tf_op jit(solution)/shard_map/all_to_all | solution.py:289
  21.9 5.3 %collective-permute-start.1 = (bf16[32,128,128]{2,1,0:T(8,128)(2,1)S(1)}, bf16[32,128,128]{2,1,0:T(8,128)(2,1)}, u32[]{:S(2)}, u32[]{:S(2)}) collective-permute-start(bf16[32,128,128]{2,1,0:T(8,128)(2,1)S(1)} %bitcast.14), channel_id=1, source_target_pairs={{1,0},{2,1},{3,2},{4,3},{5,4},{6,5},{7,6},{8,7},{9,8},{10,9},{11,1... | collective-permute-start | bytes 3145736 | tf_op jit(solution)/shard_map/ppermute | solution.py:264
  23.2 5.4 %collective-permute-start = (bf16[32,128,128]{2,1,0:T(8,128)(2,1)S(1)}, bf16[32,128,128]{2,1,0:T(8,128)(2,1)}, u32[]{:S(2)}, u32[]{:S(2)}) collective-permute-start(bf16[32,128,128]{2,1,0:T(8,128)(2,1)S(1)} %bitcast.15), channel_id=1, source_target_pairs={{0,1},{1,2},{2,3},{3,4},{4,5},{5,6},{6,7},{7,8},{8,9},{9,10},{10,1... | collective-permute-start | bytes 3145736 | tf_op jit(solution)/shard_map/ppermute | solution.py:263
  62.8 43.5 %copy-start.3 = (f32[128]{0:T(128)S(1)}, f32[128]{0:T(128)}, u32[]{:S(2)}) copy-start(f32[128]{0:T(128)} %param.9) | copy-start | bytes 1540

commit v4 on v3

--- a/solution.py
+++ b/solution.py
@@ -100,18 +100,27 @@
 
 
 def near_kernel(
-    group, cap, cols_ref, place_ref, left_ref, own_ref, right_ref, tiles_ref, graph_ref, mass_ref,
+    group, cap, middle, cols_ref, place_ref, left_ref, own_ref, right_ref, across_ref, tiles_ref, graph_ref, mass_ref,
     part_ref, graph2_ref, where_ref, window, tiles, part, pull_ref, count_ref, sems, tile_sems, part_sems,
 ):
     blocks_dev, tile, clusters = own_ref.shape
     slots = tiles_ref.shape[1]
     steps = blocks_dev // group
-    copies = [
-        pltpu.make_async_copy(src, window.at[pl.ds(i * blocks_dev, blocks_dev)], sems.at[i])
-        for i, src in enumerate((left_ref, own_ref, right_ref))
-    ]
-    for copy in copies:
-        copy.start()
+    place = place_ref[0]
+
+    def take(src, i):
+        return pltpu.make_async_copy(src, window.at[pl.ds(i * blocks_dev, blocks_dev)], sems.at[i])
+
+    take(own_ref, 1).start()
+    for i, src, at in ((0, left_ref, middle), (2, right_ref, middle - 1)):
+
+        @pl.when(place == at)
+        def _():
+            take(across_ref, i).start()
+
+        @pl.when(place != at)
+        def _():
+            take(src, i).start()
 
     def fetch(i):
         here = pl.ds(i * group, group)
@@ -153,10 +162,10 @@
             count_ref[owner] = rank + 1
             where_ref[b * (slots - NEAR) + slot_id - NEAR] = owner * cap + rank
 
-    for copy in copies:
-        copy.wait()
-
-    base = (place_ref[0] - 1) * blocks_dev
+    for i, src in enumerate((left_ref, own_ref, right_ref)):
+        take(src, i).wait()
+
+    base = (place - 1) * blocks_dev
     scale = 2.0 * eta_step / clusters
 
     @pl.loop(0, steps)
@@ -260,8 +269,10 @@
     steps = blocks_dev // group
     flops = 2 * rows * clusters
 
-    left = lax.ppermute(blocks, NODES, [(i, i + 1) for i in range(shards - 1)])
-    right = lax.ppermute(blocks, NODES, [(i + 1, i) for i in range(shards - 1)])
+    middle = shards // 2
+    across = lax.ppermute(blocks, NODES, [(middle - 1, middle), (middle, middle - 1)])
+    left = lax.ppermute(blocks, NODES, [(i, i + 1) for i in range(shards - 1) if i + 1 != middle])
+    right = lax.ppermute(blocks, NODES, [(i + 1, i) for i in range(shards - 1) if i + 1 != middle])
 
     asked, held = pl.pallas_call(
         functools.partial(requests_kernel, nodes_total),
@@ -291,13 +302,13 @@
     ).reshape(shards * cap, tile, clusters)
 
     part, graph2, where = pl.pallas_call(
-        functools.partial(near_kernel, group, cap),
+        functools.partial(near_kernel, group, cap, middle),
         out_shape=(
             pltpu.HBM((rows, clusters), f32),
             pltpu.VMEM((2 * clusters, clusters), bf16),
             jax.ShapeDtypeStruct((far_count,), i32),
         ),
-        in_specs=[SMEM, SMEM, ANY, ANY, ANY, ANY, VMEM, VMEM],
+        in_specs=[SMEM, SMEM, ANY, ANY, ANY, ANY, ANY, VMEM, VMEM],
         out_specs=(ANY, VMEM, SMEM),
         scratch_shapes=[
             pltpu.VMEM((3 * blocks_dev, tile, clusters), bf16),
@@ -315,7 +326,7 @@
         ),
         name="near",
     )(
-        cols, my_index.astype(i32).reshape(1), in_hbm(left), in_hbm(blocks), in_hbm(right),
+        cols, my_index.astype(i32).reshape(1), in_hbm(left), in_hbm(blocks), in_hbm(right), in_hbm(across),
         in_hbm(tile_vals), cluster_graph, on_chip(heard),
     )
 

time: 108 us -> 108 us (level)
  waiting for transfers between devices: 24.3 us -> 22.6 us
  starting transfers between devices: 9.18 us -> 10.8 us
    all_to_all x1, waiting for transfers between devices: 22.8 us -> 21.2 us  [local(): lax.all_to_all(found.reshape(shards, cap, tile, clusters), NODES, split_a...]
    ppermute x2 -> x3, starting transfers between devices: 5.32 us -> 6.93 us  [the longest x1 4.02 us: local(): lax.ppermute(blocks, NODES, [(i, i + 1) for i in range(shards - 1) if i +...]
  transfers between devices with their start and end apart: 3 -> 4, of which waited for: 2 -> 2; matrix products, arithmetic and copies ran while one was open for 0% -> 0% of each run, Pallas kernels for 11% -> 11%
where the time goes in v4:
time: 108 us
  blocking collectives  53.6 us (50%)
  waiting for transfers between devices  22.6 us (21%)
  Pallas kernels  20.2 us (19%)
  starting transfers between devices  10.8 us (10%)
    all_to_all x1, blocking collectives, local(): lax.all_to_all(mass_parts, NODES, split_axis=0, concat_axis=0, tiled=True)  39.9 us
    all_to_all x1, waiting for transfers between devices, local(): lax.all_to_all(found.reshape(shards, cap, tile, clusters), NODES, split_a...  21.2 us
    all_to_all x1, blocking collectives, local(): lax.all_to_all(asked, NODES, split_axis=0, concat_axis=0, tiled=True)  13.7 us
    pallas_call x1, Pallas kernels, local(): pl.pallas_call(functools.partial(near_kernel, group, cap, middle), out_sh...  11.4 us
    ppermute x1, starting transfers between devices, local(): lax.ppermute(blocks, NODES, [(i, i + 1) for i in range(shards - 1) if i +...  4.02 us
    all_to_all x1, starting transfers between devices, local(): lax.all_to_all(found.reshape(shards, cap, tile, clusters), NODES, split_a...  3.86 us
    pallas_call x1, Pallas kernels, local(): pl.pallas_call(functools.partial(far_kernel, group, chunk, nodes_total),...  3.69 us
  transfers between devices with their start and end apart: 4, of which 2 were waited for; matrix products, arithmetic and copies ran while one was open for 0% of the time, Pallas kernels for 11%

profile of v4, /device:TPU:0, one launch (start us, length us, event | category | flops | bytes accessed | tf_op | source)
XLA Modules:
  0.0 108.0 jit_solution(14545319572850167472)
XLA Ops:
  0.0 0.0 copy-start.1
  0.0 0.7 copy-done.1
  0.7 1.5 %requests.1 = (f32[16,1,256]{2,1,0:T(1,128)S(1)}, bf16[4096,128]{1,0:T(8,128)(2,1)S(1)}) custom-call(s32[6,32]{1,0:T(8,128)S(1)} %bitcast.9, bf16[4096,128]{1,0:T(8,128)(2,1)} %coupling_ref.1), custom_call_target="tpu_custom_call" | custom-call | tf_op jit(solution)/shard_map/requests/pallas_call | solution.py:277
  2.2 13.7 %all_to_all.15.mass_ref.heard_ref = f32[16,1,256]{2,1,0:T(1,128)S(1)} all-to-all(f32[16,1,256]{2,1,0:T(1,128)S(1)} %get-tuple-element.12), channel_id=1, replica_groups=mesh['groups'=2,'rows'=8,'sub'=2] {'rows','sub'}, dimensions={0} | all-to-all | bytes 32768 | tf_op jit(solution)/shard_map/all_to_all | solution.py:286
  15.9 2.0 %gather.1 = bf16[64,128,128]{2,1,0:T(8,128)(2,1)} custom-call(f32[16,1,256]{2,1,0:T(1,128)S(1)} %all_to_all.15.mass_ref.heard_ref, bf16[32,128,128]{2,1,0:T(8,128)(2,1)S(1)} %bitcast.8), custom_call_target="tpu_custom_call" | custom-call | tf_op jit(solution)/shard_map/gather/pallas_call | solution.py:287
  18.0 0.0 copy-start.4
  18.0 0.0 copy-start
  18.0 0.0 copy-start.2
  18.0 3.9 %all-to-all-start.1 = ((bf16[16,4,128,128]{3,2,1,0:T(8,128)(2,1)}), bf16[16,4,128,128]{3,2,1,0:T(8,128)(2,1)S(1)}, u32[]{:S(2)}, u32[]{:S(2)}) async-start(bf16[16,4,128,128]{3,2,1,0:T(8,128)(2,1)} %bitcast.12), calls=%async_computation.1 | async-start | bytes 4194304 | tf_op jit(solution)/shard_map/all_to_all | solution.py:300
  21.9 0.0 copy-done.4
  21.9 1.6 %collective-permute-start.2 = (bf16[32,128,128]{2,1,0:T(8,128)(2,1)S(1)}, bf16[32,128,128]{2,1,0:T(8,128)(2,1)}, u32[]{:S(2)}, u32[]{:S(2)}) collective-permute-start(bf16[32,128,128]{2,1,0:T(8,128)(2,1)S(1)} %bitcast.14), channel_id=1, source_target_pairs={{7,8},{8,7},{23,24},{24,23}} | collective-permute-start | bytes 3145736 | tf_op jit(solution)/shard_map/ppermute | solution.py:273
  23.5 1.3 %collective-permute-start.1 = (bf16[32,128,128]{2,1,0:T(8,128)(2,1)S(1)}, bf16[32,128,128]{2,1,0:T(8,128)(2,1)}, u32[]{:S(2)}, u32[]{:S(2)}) collective-permute-start(bf16[32,128,128]{2,1,0:T(8,128)(2,1)S(1)} %bitcast.15), channel_id=1, source_target_pairs={{1,0},{2,1},{3,2},{4,3},{5,4},{6,5},{7,6},{9,8},{10,9},{11,10},{12... | collective-permute-start | bytes 3145736 | tf_op jit(solution)/shard_map/ppermute | solution.py:275
  24.8 4.0 %collective-permute-start = (bf16[32,128,128]{2,1,0:T(8,128)(2,1)S(1)}, bf16[32,128,128]{2,1,0:T(8,128)(2,1)}, u32[]{:S(2)}, u32[]{:S(2)}) collective-permute-start(bf16[32,128,128]{2,1,0:T(8,128)(2,1)S(1)} %bitcast.16), channel_id=1, source_target_pairs={{0,1},{1,2},{2,3},{3,4},{4,5},{5,6},{6,7},{8,9},{9,10},{10,11},{11... | collective-permute-start | bytes 3145736 | tf_op jit(solution)/shard_map/ppermute | solution.py:274
  28.8 0.0 collective-permute-done.2.across_ref
  28.8 0.0 collective-permute-done.1.right_ref
  28.8 1.4 %collective-permute-done.left_ref = bf16[32,128,128]{2,1,0:T(8,128)(2,1)} collective-permute-done((bf16[32,128,128]{2,1,0:T(8,128)(2,1)S(1)}, bf16[32,128,128]{2,1,0:T(8,128)(2,1)}, u32[]{:S(2)}, u32[]{:S(2)}) %collective-permute-start) | collective-permute-done | bytes 1048608 | tf_op jit(solution)/shard_map/ppermute | solution.py:274
  30.2 0.0 copy-done
  30.3 0.0 copy-done.2
  30.3 11.4 %near.1 = (f32[4096,128]{1,0:T(8,128)}, bf16[256,128]{1,0:T(8,128)(2,1)S(1)}, s32[64]{0:T(128)S(1)}) custom-call(s32[6,32]{1,0:T(8,128)S(1)} %bitcast.10, s32[1]{0:T(128)} %bitcast.1.place_ref, bf16[32,128,128]{2,1,0:T(8,128)(2,1)} %collective-permute-done.left_ref, bf16[32,128,128]{2,1,0:T(8,128)(2,1)} %bitcast.13, ...), custom_call_target="tpu_custom_call" | custom-call | flops 805306368 | bytes 16777216 | tf_op jit(solution)/shard_map/near/pallas_call | solution.py:304
  41.6 21.2 %all-to-all-done.1 = bf16[16,4,128,128]{3,2,1,0:T(8,128)(2,1)S(1)} async-done(((bf16[16,4,128,128]{3,2,1,0:T(8,128)(2,1)}), bf16[16,4,128,128]{3,2,1,0:T(8,128)(2,1)S(1)}, u32[]{:S(2)}, u32[]{:S(2)}) %all-to-all-start.1) | async-done | bytes 2097184 | tf_op jit(solution)/shard_map/all_to_all | solution.py:300
  62.8 0.0 copy-start.3
  62.8 3.7 %far.1 = (f32[4096,128]{1,0:T(8,128)S(1)}, f32[16,1,128]{2,1,0:T(1,128)S(1)}) custom-call(s32[64]{0:T(128)S(1)} %get-tuple-element.13.where_ref, bf16[64,128,128]{2,1,0:T(8,128)(2,1)S(1)} %bitcast.7, bf16[32,6,128,128]{3,2,1,0:T(8,128)(2,1)} %tiles_ref.3, f32[4096,128]{1,0:T(8,128)} %get-tuple-element.15.part_ref, ...), custom_call_target="tpu_custom_call" | custom-call | flops 536870912 | bytes 8388608 | tf_op jit(solution)/shard_map/far/pallas_call | solution.py:334
  66.5 39.9 %all_to_all.16.mass_ref = f32[16,1,128]{2,1,0:T(1,128)S(1)} all-to-all(f32[16,1,128]{2,1,0:T(1,128)S(1)} %get-tuple-element.18), channel_id=1, replica_groups=mesh['groups'=2,'rows'=8,'sub'=2] {'rows','sub'}, dimensions={0} | all-to-all | bytes 16384 | tf_op jit(solution)/shard_map/all_to_all | solution.py:351
  106.4 0.0 copy-done.3
  106.4 1.6 %last.1 = f32[4096,128]{1,0:T(8,128)} custom-call(f32[4096,128]{1,0:T(8,128)S(1)} %get-tuple-element.17.logits_ref, f32[16,1,128]{2,1,0:T(1,128)S(1)} %all_to_all.16.mass_ref, f32[1,128]{1,0:T(1,128)S(1)} %bitcast.11), custom_call_target="tpu_custom_call" | custom-call | tf_op jit(solution)/shard_map/last/pallas_call | solution.py:353
Async XLA Ops:
  0.0 0.7 copy-start.1
  18.0 3.9 %copy-start.4 = (bf16[4096,128]{1,0:T(8,128)(2,1)S(1)}, bf16[4096,128]{1,0:T(8,128)(2,1)}, u32[]{:S(2)}) copy-start(bf16[4096,128]{1,0:T(8,128)(2,1)} %coupling_ref.1) | copy-start | bytes 3145732
  18.0 12.3 %copy-start = (s32[128,128]{1,0:T(8,128)S(1)}, s32[128,128]{1,0:T(8,128)}, u32[]{:S(2)}) copy-start(s32[128,128]{1,0:T(8,128)} %graph_ref.1) | copy-start | bytes 196612
  18.0 12.3 %copy-start.2 = (s32[32,6]{0,1:T(8,128)S(1)}, s32[32,6]{0,1:T(8,128)}, u32[]{:S(2)}) copy-start(s32[32,6]{0,1:T(8,128)} %param.7) | copy-start | bytes 2308
  18.0 44.8 %all-to-all-start.1 = ((bf16[16,4,128,128]{3,2,1,0:T(8,128)(2,1)}), bf16[16,4,128,128]{3,2,1,0:T(8,128)(2,1)S(1)}, u32[]{:S(2)}, u32[]{:S(2)}) async-start(bf16[16,4,128,128]{3,2,1,0:T(8,128)(2,1)} %bitcast.12), calls=%async_computation.1 | async-start | bytes 4194304 | tf_op jit(solution)/shard_map/all_to_all | solution.py:300
  21.9 6.9 %collective-permute-start.2 = (bf16[32,128,128]{2,1,0:T(8,128)(2,1)S(1)}, bf16[32,128,128]{2,1,0:T(8,128)(2,1)}, u32[]{:S(2)}, u32[]{:S(2)}) collective-permute-start(bf16[32,128,128]{2,1,0:T(8,128)(2,1)S(1)} %bitcast.14), channel_id=1, source_target_pairs={{7,8},{8,7},{23,24},{24,23}} | collective-permute-start | bytes 3145736 | tf_op jit(solution)/shard_map/ppermute | solution.py:273
  23.5 5.3 %collective-permute-start.1 = (bf16[32,128,128]{2,1,0:T(8,128)(2,1)S(1)}, bf16[32,128,128]{2,1,0:T(8,128)(2,1)}, u32[]{:S(2)}, u32[]{:S(2)}) collective-permute-start(bf16[32,128,128]{2,1,0:T(8,128)(2,1)S(1)} %bitcast.15), channel_id=1, source_target_pairs={{1,0},{2,1},{3,2},{4,3},{5,4},{6,5},{7,6},{9,8},{10,9},{11,10},{12... | collective-permute-start | bytes 3145736 | tf_op jit(solution)/shard_map/ppermute | solution.py:275
  24.8 5.4 %collective-permute-start = (bf16[32,128,128]{2,1,0:T(8,128)(2,1)S(1)}, bf16[32,128,128]{2,1,0:T(8,128)(2,1)}, u32[]{:S(2)}, u32[]{:S(2)}) collective-permute-start(bf16[32,128,128]{2,1,0:T(8,128)(2,1)S(1)} %bitcast.16), channel_id=1, source_target_pairs={{0,1},{1,2},{2,3},{3,4},{4,5},{5,6},{6,7},{8,9},{9,10},{10,11},{11... | collective-permute-start | bytes 3145736 | tf_op jit(solution)/shard_map/ppermute | solution.py:274
  62.8 43.6 %copy-start.3 = (f32[128]{0:T(128)S(1)}, f32[128]{0:T(128)}, u32[]{:S(2)}) copy-start(f32[128]{0:T(128)} %param.9) | copy-start | bytes 1540

commit v5 on v4

--- a/solution.py
+++ b/solution.py
@@ -9,6 +9,7 @@
 
 
 NEAR = 4
+LEVEL = 4
 NODES = ("rows", "sub")
 
 eta_step = 2.0
@@ -33,9 +34,10 @@
     return pltpu.CompilerParams(vmem_limit_bytes=mib << 20)
 
 
-def requests_kernel(nodes_total, cols_ref, coupling_ref, out_ref, rows, sems):
+def requests_kernel(nodes_total, place_ref, cols_ref, coupling_ref, *refs):
+    *out_refs, own_ref, rows, table_ref, sems = refs
     slots, blocks_dev = cols_ref.shape
-    shards = out_ref.shape[0]
+    shards = table_ref.shape[0]
     nodes, clusters = coupling_ref.shape
     parts = sems.shape[0]
     step = nodes // parts
@@ -69,29 +71,38 @@
             precision=lax.Precision.HIGHEST,
             preferred_element_type=f32,
         )
-    out_ref[:, 0, clusters:] = table
+    table_ref[:, 0, :] = table
+    level = place_ref[0] // LEVEL
+    for dz, ref in enumerate((own_ref, *out_refs)):
+        for row in range(LEVEL):
+            ref[row] = table_ref[(level ^ dz) * LEVEL + row]
     total = jnp.zeros((8, clusters), f32)
     for i in range(parts):
         copies[i].wait()
         part = rows[pl.ds(i * step, step), :].astype(f32)
         total = total + jnp.sum(part.reshape(step // 8, 8, clusters), axis=0)
     mass = jnp.sum(total, axis=0, keepdims=True) / nodes_total
-    out_ref[:, 0, :clusters] = jnp.broadcast_to(mass, (shards, clusters))
-
-
-def gather_kernel(cap, heard_ref, blocks_ref, out_ref, wanted_ref, wanted_smem, sems):
-    clusters = blocks_ref.shape[2]
-    wanted_ref[...] = heard_ref[:, 0, clusters:].astype(i32)
+    for ref in (own_ref, *out_refs):
+        ref[LEVEL] = mass
+
+
+def gather_kernel(cap, stage, place_ref, *refs):
+    count = (len(refs) - 5) // 2
+    heard_refs, sources, out_refs = refs[:count], refs[count : count + 2], refs[count + 2 : 2 * count + 2]
+    wanted_ref, wanted_smem, sems = refs[2 * count + 2 :]
+    for n, heard in enumerate(heard_refs):
+        wanted_ref[n * 8 : n * 8 + LEVEL, :] = heard[:LEVEL, 0, :].astype(i32)
     copy = pltpu.make_async_copy(wanted_ref, wanted_smem, sems.at[0])
     copy.start()
     copy.wait()
-
-    @pl.loop(0, heard_ref.shape[0])
-    def _(n):
-        for j in range(cap):
-            pltpu.make_async_copy(blocks_ref.at[wanted_smem[n, j]], out_ref.at[n * cap + j], sems.at[1]).start()
-
-    pltpu.make_async_copy(out_ref, out_ref, sems.at[1]).wait()
+    spot = place_ref[0] % LEVEL
+    for n, out_ref in enumerate(out_refs):
+        for sub, src in enumerate(sources):
+            row = n * 8 + (spot ^ (2 * stage + sub))
+            for j in range(cap):
+                pltpu.make_async_copy(src.at[wanted_smem[row, j]], out_ref.at[sub * cap + j], sems.at[n + 1]).start()
+    for n, out_ref in enumerate(out_refs):
+        pltpu.make_async_copy(out_ref, out_ref, sems.at[n + 1]).wait()
 
 
 def split(x):
@@ -100,27 +111,33 @@
 
 
 def near_kernel(
-    group, cap, middle, cols_ref, place_ref, left_ref, own_ref, right_ref, across_ref, tiles_ref, graph_ref, mass_ref,
-    part_ref, graph2_ref, where_ref, window, tiles, part, pull_ref, count_ref, sems, tile_sems, part_sems,
+    group, cap, shards, place_ref, cols_ref, own_ref, chip_ref, level_ref, beyond_ref, across_ref, tiles_ref, graph_ref,
+    *refs,
 ):
+    *mass_refs, part_ref, graph2_ref, where_ref = refs[:-9]
+    window, tiles, part, pull_ref, count_ref, own_sem, sems, tile_sems, part_sems = refs[-9:]
     blocks_dev, tile, clusters = own_ref.shape
     slots = tiles_ref.shape[1]
     steps = blocks_dev // group
     place = place_ref[0]
-
-    def take(src, i):
-        return pltpu.make_async_copy(src, window.at[pl.ds(i * blocks_dev, blocks_dev)], sems.at[i])
-
-    take(own_ref, 1).start()
-    for i, src, at in ((0, left_ref, middle), (2, right_ref, middle - 1)):
-
-        @pl.when(place == at)
-        def _():
-            take(across_ref, i).start()
-
-        @pl.when(place != at)
-        def _():
-            take(src, i).start()
+    spot, level = place % LEVEL, place // LEVEL
+
+    def take(src, i, sem):
+        return pltpu.make_async_copy(src, window.at[pl.ds(i * blocks_dev, blocks_dev)], sem)
+
+    take(own_ref, 1, own_sem).start()
+    even = spot % 2 == 0
+    middle = shards // 2
+    split_here = (place == middle) | (place == middle - 1)
+    edge = ((spot == 0) | (spot == LEVEL - 1)) & jnp.logical_not(split_here)
+    inside = (spot != 0) & (spot != LEVEL - 1)
+    for flag, src in ((split_here, across_ref), (edge, beyond_ref), (inside, level_ref)):
+        for is_even, chip_at, other_at in ((True, 2, 0), (False, 0, 2)):
+
+            @pl.when(flag & (even == is_even))
+            def _():
+                take(chip_ref, chip_at, sems.at[0]).start()
+                take(src, other_at, sems.at[1]).start()
 
     def fetch(i):
         here = pl.ds(i * group, group)
@@ -134,7 +151,9 @@
         fetch(i).start()
 
     graph = graph_ref[...].astype(f32)
-    colmass = jnp.sum(mass_ref[:, 0, :clusters], axis=0, keepdims=True)
+    colmass = mass_refs[0][...]
+    for ref in mass_refs[1:]:
+        colmass = colmass + ref[...]
     pull_ref[...] = (
         lax.dot_general(
             jnp.broadcast_to(colmass, (8, clusters)),
@@ -160,10 +179,13 @@
             owner = cols_ref[slot_id, b] // blocks_dev
             rank = count_ref[owner]
             count_ref[owner] = rank + 1
-            where_ref[b * (slots - NEAR) + slot_id - NEAR] = owner * cap + rank
-
-    for i, src in enumerate((left_ref, own_ref, right_ref)):
-        take(src, i).wait()
+            turn = (owner % LEVEL) ^ spot
+            row = ((turn // 2) * (shards // LEVEL) + ((owner // LEVEL) ^ level)) * 2 + turn % 2
+            where_ref[b * (slots - NEAR) + slot_id - NEAR] = row * cap + rank
+
+    take(own_ref, 1, own_sem).wait()
+    take(chip_ref, 0, sems.at[0]).wait()
+    take(chip_ref, 2, sems.at[1]).wait()
 
     base = (place - 1) * blocks_dev
     scale = 2.0 * eta_step / clusters
@@ -189,13 +211,17 @@
 
 
 def far_kernel(
-    group, chunk, nodes_total, where_ref, blocks_ref, tiles_ref, part_ref, graph2_ref,
-    logits_ref, mass_ref, tiles, tile_sems, part_sems,
+    group, chunk, nodes_total, where_ref, tiles_ref, part_ref, graph2_ref, *refs
 ):
+    *found_refs, logits_ref, mass_ref = refs[:-5]
+    blocks_ref, tiles, block_sem, tile_sems, part_sems = refs[-5:]
     tile, clusters = blocks_ref.shape[1:]
     blocks_dev, far_slots = tiles.shape[:2]
     steps = blocks_dev // group
     scale = 2.0 * eta_step / clusters
+    width = found_refs[0].shape[0]
+    for i, found in enumerate(found_refs):
+        pltpu.make_async_copy(found, blocks_ref.at[pl.ds(i * width, width)], block_sem).start()
 
     def fetches(i):
         here = pl.ds(i * chunk, chunk)
@@ -221,6 +247,7 @@
             spreads.append(split(jnp.dot(wide, jnp.concatenate(picked, axis=0), preferred_element_type=f32)))
         return jnp.concatenate(spreads, axis=0)
 
+    pltpu.make_async_copy(blocks_ref, blocks_ref, block_sem).wait()
     total = jnp.zeros((8, clusters), f32)
     ahead = products(0)
     for step in range(steps):
@@ -269,46 +296,71 @@
     steps = blocks_dev // group
     flops = 2 * rows * clusters
 
+    levels = shards // LEVEL
+    others = range(1, levels)
+    place = my_index.astype(i32).reshape(1)
+
+    def swap(x, bits):
+        return lax.ppermute(x, NODES, [(i, i ^ bits) for i in range(shards)])
+
     middle = shards // 2
     across = lax.ppermute(blocks, NODES, [(middle - 1, middle), (middle, middle - 1)])
-    left = lax.ppermute(blocks, NODES, [(i, i + 1) for i in range(shards - 1) if i + 1 != middle])
-    right = lax.ppermute(blocks, NODES, [(i + 1, i) for i in range(shards - 1) if i + 1 != middle])
-
-    asked, held = pl.pallas_call(
+
+    *asked, mine, held = pl.pallas_call(
         functools.partial(requests_kernel, nodes_total),
-        out_shape=(jax.ShapeDtypeStruct((shards, 1, 2 * clusters), f32), pltpu.VMEM((rows, clusters), bf16)),
-        in_specs=[VMEM, ANY],
-        out_specs=(VMEM, VMEM),
-        scratch_shapes=[pltpu.SemaphoreType.DMA((8,))],
+        out_shape=(
+            *[pltpu.VMEM((LEVEL + 1, 1, clusters), f32)] * levels,
+            pltpu.VMEM((rows, clusters), bf16),
+        ),
+        in_specs=[SMEM, VMEM, ANY],
+        out_specs=[VMEM] * (levels + 1),
+        scratch_shapes=[pltpu.VMEM((shards, 1, clusters), f32), pltpu.SemaphoreType.DMA((8,))],
         compiler_params=params(8),
         name="requests",
-    )(cols, in_hbm(coupling))
-    heard = lax.all_to_all(asked, NODES, split_axis=0, concat_axis=0, tiled=True)
-    found = pl.pallas_call(
-        functools.partial(gather_kernel, cap),
-        out_shape=pltpu.HBM((shards * cap, tile, clusters), bf16),
-        in_specs=[VMEM, VMEM],
-        out_specs=ANY,
-        scratch_shapes=[
-            pltpu.VMEM((shards, clusters), i32),
-            pltpu.SMEM((shards, clusters), i32),
-            pltpu.SemaphoreType.DMA((2,)),
-        ],
-        compiler_params=params(8),
-        name="gather",
-    )(on_chip(heard), on_chip(held.reshape(blocks.shape)))
-    fetched = lax.all_to_all(
-        found.reshape(shards, cap, tile, clusters), NODES, split_axis=0, concat_axis=0, tiled=True
-    ).reshape(shards * cap, tile, clusters)
+    )(place, cols, in_hbm(coupling))
+    heard = [swap(x, dz * LEVEL) for dz, x in zip(others, asked)]
+    over = swap(blocks, 2)
+    chip = swap(blocks, 1)
+
+    def gather(stage, heard, sources):
+        return pl.pallas_call(
+            functools.partial(gather_kernel, cap, stage),
+            out_shape=[pltpu.HBM((2 * cap, tile, clusters), bf16)] * len(heard),
+            in_specs=[SMEM] + [VMEM] * (len(heard) + 2),
+            out_specs=[ANY] * len(heard),
+            scratch_shapes=[
+                pltpu.VMEM((8 * len(heard), clusters), i32),
+                pltpu.SMEM((8 * len(heard), clusters), i32),
+                pltpu.SemaphoreType.DMA((len(heard) + 1,)),
+            ],
+            compiler_params=params(8),
+        )(place, *[on_chip(x) for x in heard], *[on_chip(x) for x in sources])
+
+    found = gather(0, heard, (held.reshape(blocks.shape), chip))
+    fetched = [swap(x, dz * LEVEL) for dz, x in zip(others, found)]
+    over_chip = swap(over, 1)
+    edges = [z * LEVEL for z in range(1, levels) if z * LEVEL != middle]
+    beyond = lax.ppermute(over, NODES, [(i - LEVEL + 1, i) for i in edges] + [(i + LEVEL - 2, i - 1) for i in edges])
+    found = gather(1, (*heard, mine), (over, over_chip))
+    there = [swap(x, dz * LEVEL) for dz, x in zip(others, found)]
+    home_late = found[-1]
+    (home,) = gather(0, (mine,), (held.reshape(blocks.shape), chip))
+
+    mass = mine[LEVEL]
+    for x in heard:
+        mass = mass + x[LEVEL]
+    mass_chip = swap(mass, 1)
+    mass = mass + mass_chip
+    mass_over = swap(mass, 2)
 
     part, graph2, where = pl.pallas_call(
-        functools.partial(near_kernel, group, cap, middle),
+        functools.partial(near_kernel, group, cap, shards),
         out_shape=(
             pltpu.HBM((rows, clusters), f32),
             pltpu.VMEM((2 * clusters, clusters), bf16),
             jax.ShapeDtypeStruct((far_count,), i32),
         ),
-        in_specs=[SMEM, SMEM, ANY, ANY, ANY, ANY, ANY, VMEM, VMEM],
+        in_specs=[SMEM, SMEM, ANY, ANY, ANY, ANY, ANY, ANY, VMEM, VMEM, VMEM],
         out_specs=(ANY, VMEM, SMEM),
         scratch_shapes=[
             pltpu.VMEM((3 * blocks_dev, tile, clusters), bf16),
@@ -316,7 +368,8 @@
             pltpu.VMEM((rows, clusters), f32),
             pltpu.VMEM((8, clusters), f32),
             pltpu.SMEM((shards,), i32),
-            pltpu.SemaphoreType.DMA((3,)),
+            pltpu.SemaphoreType.DMA,
+            pltpu.SemaphoreType.DMA((2,)),
             pltpu.SemaphoreType.DMA((steps,)),
             pltpu.SemaphoreType.DMA((steps,)),
         ],
@@ -326,18 +379,21 @@
         ),
         name="near",
     )(
-        cols, my_index.astype(i32).reshape(1), in_hbm(left), in_hbm(blocks), in_hbm(right), in_hbm(across),
-        in_hbm(tile_vals), cluster_graph, on_chip(heard),
+        place, cols, in_hbm(blocks), in_hbm(chip), in_hbm(over_chip), in_hbm(beyond), in_hbm(across),
+        in_hbm(tile_vals), cluster_graph, mass, mass_over,
     )
 
     chunk = min(16, blocks_dev)
+    parts = [home, *fetched, home_late, *there]
     logits, mass_parts = pl.pallas_call(
         functools.partial(far_kernel, group, chunk, nodes_total),
         out_shape=(pltpu.VMEM((rows, clusters), f32), pltpu.VMEM((shards, 1, clusters), f32)),
-        in_specs=[SMEM, VMEM, ANY, ANY, VMEM],
+        in_specs=[SMEM, ANY, ANY, VMEM] + [ANY] * len(parts),
         out_specs=(VMEM, VMEM),
         scratch_shapes=[
+            pltpu.VMEM((2 * cap * len(parts), tile, clusters), bf16),
             pltpu.VMEM((blocks_dev, far_slots, tile, tile), bf16),
+            pltpu.SemaphoreType.DMA,
             pltpu.SemaphoreType.DMA((blocks_dev // chunk,)),
             pltpu.SemaphoreType.DMA((blocks_dev // chunk,)),
         ],
@@ -346,7 +402,7 @@
             flops=flops * (far_slots * tile + 2 * clusters), bytes_accessed=8 << 20, transcendentals=rows * clusters
         ),
         name="far",
-    )(where, on_chip(fetched), in_hbm(tile_vals), in_hbm(part), on_chip(graph2))
+    )(where, in_hbm(tile_vals), in_hbm(part), on_chip(graph2), *parts)
 
     masses = lax.all_to_all(mass_parts, NODES, split_axis=0, concat_axis=0, tiled=True)
 

time: 108 us -> 123 us (1.14)
  blocking collectives: 53.6 us -> 13.4 us
  waiting for transfers between devices: 22.6 us -> 58.7 us
  starting transfers between devices: 10.8 us -> 27.2 us
  Pallas kernels: 20.2 us -> 22.2 us
    ppermute x2 -> x15, waiting for transfers between devices: 1.42 us -> 58.7 us  [the longest x14 58.7 us: swap(): return lax.ppermute(x, NODES, [(i, i ^ bits) for i in range(shards)])]
    all_to_all x1, blocking collectives: 39.9 us -> 13.4 us  [local(): lax.all_to_all(mass_parts, NODES, split_axis=0, concat_axis=0, tiled=True)]
    all_to_all x1 -> x0, waiting for transfers between devices: 21.2 us -> none  [local(): lax.all_to_all(found.reshape(shards, cap, tile, clusters), NODES, split_a...]
    ppermute x2 -> x15, starting transfers between devices: 5.3 us -> 25.6 us  [the longest x14 24 us: swap(): return lax.ppermute(x, NODES, [(i, i ^ bits) for i in range(shards)])]
    all_to_all x1 -> x0, blocking collectives: 13.7 us -> none  [local(): lax.all_to_all(asked, NODES, split_axis=0, concat_axis=0, tiled=True)]
    all_to_all x1 -> x0, starting transfers between devices: 3.86 us -> none  [local(): lax.all_to_all(found.reshape(shards, cap, tile, clusters), NODES, split_a...]
    pallas_call x2 -> x4, Pallas kernels: 13.4 us -> 15.3 us  [the longest x1 10.4 us: local(): pl.pallas_call(functools.partial(near_kernel, group, cap, shards), out_sh...]
  transfers between devices with their start and end apart: 4 -> 16, of which waited for: 2 -> 7; matrix products, arithmetic and copies ran while one was open for 0% -> 0% of each run, Pallas kernels for 11% -> 14%
where the time goes in v5:
time: 123 us
  waiting for transfers between devices  58.7 us (48%)
  starting transfers between devices  27.2 us (22%)
  Pallas kernels  22.2 us (18%)
  blocking collectives  13.4 us (11%)
    ppermute x14, waiting for transfers between devices, swap(): return lax.ppermute(x, NODES, [(i, i ^ bits) for i in range(shards)])  58.7 us
    ppermute x14, starting transfers between devices, swap(): return lax.ppermute(x, NODES, [(i, i ^ bits) for i in range(shards)])  24 us
    all_to_all x1, blocking collectives, local(): lax.all_to_all(mass_parts, NODES, split_axis=0, concat_axis=0, tiled=True)  13.4 us
    pallas_call x1, Pallas kernels, local(): pl.pallas_call(functools.partial(near_kernel, group, cap, shards), out_sh...  10.4 us
    pallas_call x3, Pallas kernels, gather(): pl.pallas_call(functools.partial(gather_kernel, cap, stage), out_shape=[p...  4.93 us
    pallas_call x1, Pallas kernels, local(): pl.pallas_call(functools.partial(far_kernel, group, chunk, nodes_total),...  3.84 us
  transfers between devices with their start and end apart: 16, of which 7 were waited for; matrix products, arithmetic and copies ran while one was open for 0% of the time, Pallas kernels for 14%

profile of v5, /device:TPU:0, one launch (start us, length us, event | category | flops | bytes accessed | tf_op | source)
XLA Modules:
  0.0 122.5 jit_solution(1288851260471916922)
XLA Ops:
  0.0 3.0 %collective-permute-start.1 = (bf16[32,128,128]{2,1,0:T(8,128)(2,1)}, bf16[32,128,128]{2,1,0:T(8,128)(2,1)S(1)}, u32[]{:S(2)}, u32[]{:S(2)}) collective-permute-start(bf16[32,128,128]{2,1,0:T(8,128)(2,1)} %bitcast.12), channel_id=1, source_target_pairs={{0,2},{1,3},{2,0},{3,1},{4,6},{5,7},{6,4},{7,5},{8,10},{9,11},{10,... | collective-permute-start | bytes 3145736 | tf_op jit(solution)/shard_map/ppermute | solution.py:304
  3.0 0.0 collective-permute-start
  3.0 23.4 %collective-permute-done.1.refs_4_ = bf16[32,128,128]{2,1,0:T(8,128)(2,1)S(1)} collective-permute-done((bf16[32,128,128]{2,1,0:T(8,128)(2,1)}, bf16[32,128,128]{2,1,0:T(8,128)(2,1)S(1)}, u32[]{:S(2)}, u32[]{:S(2)}) %collective-permute-start.1) | collective-permute-done | bytes 1048608 | tf_op jit(solution)/shard_map/ppermute | solution.py:304
  26.3 0.0 collective-permute-start.2
  26.3 1.6 %collective-permute-start.4 = (bf16[32,128,128]{2,1,0:T(8,128)(2,1)}, bf16[32,128,128]{2,1,0:T(8,128)(2,1)}, u32[]{:S(2)}, u32[]{:S(2)}) collective-permute-start(bf16[32,128,128]{2,1,0:T(8,128)(2,1)} %bitcast.14), channel_id=1, source_target_pairs={{7,8},{8,7},{23,24},{24,23}} | collective-permute-start | bytes 3145736 | tf_op jit(solution)/shard_map/ppermute | solution.py:307
  28.0 1.6 %collective-permute-start.3 = (bf16[32,128,128]{2,1,0:T(8,128)(2,1)S(1)}, bf16[32,128,128]{2,1,0:T(8,128)(2,1)}, u32[]{:S(2)}, u32[]{:S(2)}) collective-permute-start(bf16[32,128,128]{2,1,0:T(8,128)(2,1)S(1)} %collective-permute-done.1.refs_4_), channel_id=1, source_target_pairs={{1,4},{9,12},{6,3},{14,11},{17,20},{25,28},{22,19},{30,27}} | collective-permute-start | bytes 3145736 | tf_op jit(solution)/shard_map/ppermute | solution.py:343
  29.6 0.7 copy-done.5
  30.3 1.5 %requests.1 = (f32[5,1,128]{2,1,0:T(1,128)S(1)}, f32[5,1,128]{2,1,0:T(1,128)S(1)}, f32[5,1,128]{2,1,0:T(1,128)S(1)}, f32[5,1,128]{2,1,0:T(1,128)S(1)}, bf16[4096,128]{1,0:T(8,128)(2,1)S(1)}) custom-call(s32[1]{0:T(128)} %bitcast.place_ref, s32[6,32]{1,0:T(8,128)S(1)} %bitcast.9, bf16[4096,128]{1,0:T(8,128)(2,1)} %coupling_ref.1), custom_call_target="tpu_custom_call" | custom-call | tf_op jit(solution)/shard_map/requests/pallas_call | solution.py:309
  31.8 1.6 %collective-permute-start.5 = (f32[5,1,128]{2,1,0:T(1,128)S(1)}, f32[5,1,128]{2,1,0:T(1,128)S(1)}, u32[]{:S(2)}, u32[]{:S(2)}) collective-permute-start(f32[5,1,128]{2,1,0:T(1,128)S(1)} %get-tuple-element.23), channel_id=1, source_target_pairs={{0,4},{1,5},{2,6},{3,7},{4,0},{5,1},{6,2},{7,3},{8,12},{9,13},{10,... | collective-permute-start | bytes 7688 | tf_op jit(solution)/shard_map/ppermute | solution.py:304
  33.4 2.1 %collective-permute-done.5.refs_0_ = f32[5,1,128]{2,1,0:T(1,128)S(1)} collective-permute-done((f32[5,1,128]{2,1,0:T(1,128)S(1)}, f32[5,1,128]{2,1,0:T(1,128)S(1)}, u32[]{:S(2)}, u32[]{:S(2)}) %collective-permute-start.5) | collective-permute-done | bytes 2592 | tf_op jit(solution)/shard_map/ppermute | solution.py:304
  35.5 4.6 %collective-permute-start.6 = (f32[5,1,128]{2,1,0:T(1,128)S(1)}, f32[5,1,128]{2,1,0:T(1,128)S(1)}, u32[]{:S(2)}, u32[]{:S(2)}) collective-permute-start(f32[5,1,128]{2,1,0:T(1,128)S(1)} %get-tuple-element.24), channel_id=1, source_target_pairs={{0,8},{1,9},{2,10},{3,11},{4,12},{5,13},{6,14},{7,15},{8,0},{9,1},... | collective-permute-start | bytes 7688 | tf_op jit(solution)/shard_map/ppermute | solution.py:304
  40.1 5.5 %collective-permute-done.6.refs_1_ = f32[5,1,128]{2,1,0:T(1,128)S(1)} collective-permute-done((f32[5,1,128]{2,1,0:T(1,128)S(1)}, f32[5,1,128]{2,1,0:T(1,128)S(1)}, u32[]{:S(2)}, u32[]{:S(2)}) %collective-permute-start.6) | collective-permute-done | bytes 2592 | tf_op jit(solution)/shard_map/ppermute | solution.py:304
  45.6 0.0 collective-permute-start.7
  45.6 5.4 %collective-permute-done.7.refs_2_ = f32[5,1,128]{2,1,0:T(1,128)S(1)} collective-permute-done((f32[5,1,128]{2,1,0:T(1,128)S(1)}, f32[5,1,128]{2,1,0:T(1,128)S(1)}, u32[]{:S(2)}, u32[]{:S(2)}) %collective-permute-start.7) | collective-permute-done | bytes 2592 | tf_op jit(solution)/shard_map/ppermute | solution.py:304
  51.0 0.0 collective-permute-done.chip_ref.refs_2_.refs_4_
  51.0 1.7 %shard_map.56 = (bf16[8,128,128]{2,1,0:T(8,128)(2,1)}, bf16[8,128,128]{2,1,0:T(8,128)(2,1)}, bf16[8,128,128]{2,1,0:T(8,128)(2,1)}) custom-call(s32[1]{0:T(128)} %bitcast.place_ref, f32[5,1,128]{2,1,0:T(1,128)S(1)} %collective-permute-done.5.refs_0_, f32[5,1,128]{2,1,0:T(1,128)S(1)} %collective-permute-done.6.refs_1_, ...), custom_call_target="tpu_custom_call" | custom-call | tf_op jit(solution)/shard_map/pallas_call | solution.py:326
  52.7 0.0 copy-start.8
  52.7 0.1 collective-permute-start.10
  52.8 1.3 %collective-permute-start.8 = (f32[1,128]{1,0:T(1,128)S(1)}, f32[1,128]{1,0:T(1,128)S(1)}, u32[]{:S(2)}, u32[]{:S(2)}) collective-permute-start(f32[1,128]{1,0:T(1,128)S(1)} %fusion), channel_id=1, source_target_pairs={{0,1},{1,0},{2,3},{3,2},{4,5},{5,4},{6,7},{7,6},{8,9},{9,8},{10,11... | collective-permute-start | bytes 1544 | tf_op jit(solution)/shard_map/ppermute | solution.py:304
  54.1 0.8 collective-permute-done.8
  55.0 4.6 %collective-permute-start.9 = (f32[1,128]{1,0:T(1,128)S(1)}, f32[1,128]{1,0:T(1,128)S(1)}, u32[]{:S(2)}, u32[]{:S(2)}) collective-permute-start(f32[1,128]{1,0:T(1,128)S(1)} %add.49.refs_0_), channel_id=1, source_target_pairs={{0,2},{1,3},{2,0},{3,1},{4,6},{5,7},{6,4},{7,5},{8,10},{9,11},{10,... | collective-permute-start | bytes 1544 | tf_op jit(solution)/shard_map/ppermute | solution.py:304
  59.6 0.0 collective-permute-done.2.level_ref.refs_5_
  59.6 2.2 %collective-permute-start.11 = (bf16[8,128,128]{2,1,0:T(8,128)(2,1)}, bf16[8,128,128]{2,1,0:T(8,128)(2,1)S(1)}, u32[]{:S(2)}, u32[]{:S(2)}) collective-permute-start(bf16[8,128,128]{2,1,0:T(8,128)(2,1)} %get-tuple-element.31), channel_id=1, source_target_pairs={{0,8},{1,9},{2,10},{3,11},{4,12},{5,13},{6,14},{7,15},{8,0},{9,1},... | collective-permute-start | bytes 786440 | tf_op jit(solution)/shard_map/ppermute | solution.py:304
  61.8 1.9 %shard_map.57 = (bf16[8,128,128]{2,1,0:T(8,128)(2,1)}, bf16[8,128,128]{2,1,0:T(8,128)(2,1)}, bf16[8,128,128]{2,1,0:T(8,128)(2,1)}, bf16[8,128,128]{2,1,0:T(8,128)(2,1)}) custom-call(s32[1]{0:T(128)} %bitcast.place_ref, f32[5,1,128]{2,1,0:T(1,128)S(1)} %collective-permute-done.5.refs_0_, f32[5,1,128]{2,1,0:T(1,128)S(1)} %collective-permute-done.6.refs_1_, ...), custom_call_target="tpu_custom_call" | custom-call | tf_op jit(solution)/shard_map/pallas_call | solution.py:326
  63.7 0.0 collective-permute-done.9.refs_1_
  63.7 0.0 copy-done.8
  63.7 2.2 %collective-permute-start.12 = (bf16[8,128,128]{2,1,0:T(8,128)(2,1)S(1)}, bf16[8,128,128]{2,1,0:T(8,128)(2,1)S(1)}, u32[]{:S(2)}, u32[]{:S(2)}) collective-permute-start(bf16[8,128,128]{2,1,0:T(8,128)(2,1)S(1)} %copy-done.8), channel_id=1, source_target_pairs={{0,12},{1,13},{2,14},{3,15},{4,8},{5,9},{6,10},{7,11},{8,4},{9,5},... | collective-permute-start | bytes 786440 | tf_op jit(solution)/shard_map/ppermute | solution.py:304
  65.9 0.0 collective-permute-done.4.across_ref
  65.9 0.0 collective-permute-start.13
  65.9 0.0 collective-permute-done.10.refs_1_
  65.9 2.2 %collective-permute-start.14 = (bf16[8,128,128]{2,1,0:T(8,128)(2,1)}, bf16[8,128,128]{2,1,0:T(8,128)(2,1)S(1)}, u32[]{:S(2)}, u32[]{:S(2)}) collective-permute-start(bf16[8,128,128]{2,1,0:T(8,128)(2,1)} %get-tuple-element.35), channel_id=1, source_target_pairs={{0,8},{1,9},{2,10},{3,11},{4,12},{5,13},{6,14},{7,15},{8,0},{9,1},... | collective-permute-start | bytes 786440 | tf_op jit(solution)/shard_map/ppermute | solution.py:304
  68.2 0.0 collective-permute-done.3.beyond_ref
  68.2 2.1 %collective-permute-start.15 = (bf16[8,128,128]{2,1,0:T(8,128)(2,1)}, bf16[8,128,128]{2,1,0:T(8,128)(2,1)S(1)}, u32[]{:S(2)}, u32[]{:S(2)}) collective-permute-start(bf16[8,128,128]{2,1,0:T(8,128)(2,1)} %get-tuple-element.36), channel_id=1, source_target_pairs={{0,12},{1,13},{2,14},{3,15},{4,8},{5,9},{6,10},{7,11},{8,4},{9,5},... | collective-permute-start | bytes 786440 | tf_op jit(solution)/shard_map/ppermute | solution.py:304
  70.3 0.0 copy-done
  70.3 1.3 %shard_map.55.refs_0_ = bf16[8,128,128]{2,1,0:T(8,128)(2,1)} custom-call(s32[1]{0:T(128)} %bitcast.place_ref, f32[5,1,128]{2,1,0:T(1,128)S(1)} %get-tuple-element.22.refs_0_.refs_3_, bf16[32,128,128]{2,1,0:T(8,128)(2,1)S(1)} %bitcast.8, bf16[32,128,128]{2,1,0:T(8,128)(2,1)S(1)} %collective-permute-done.chip_ref.refs_2_.refs_4_), custom_call_target="tpu_custom_call" | custom-call | tf_op jit(solution)/shard_map/pallas_call | solution.py:326
  71.7 0.0 copy-done.1
  71.7 10.4 %near.1 = (f32[4096,128]{1,0:T(8,128)}, bf16[256,128]{1,0:T(8,128)(2,1)S(1)}, s32[64]{0:T(128)S(1)}) custom-call(s32[1]{0:T(128)} %bitcast.place_ref, s32[6,32]{1,0:T(8,128)S(1)} %bitcast.10, bf16[32,128,128]{2,1,0:T(8,128)(2,1)} %bitcast.15, bf16[32,128,128]{2,1,0:T(8,128)(2,1)} %copy-done, bf16[32,128,128]{2,1,0:T(8,128)(2,1)} %copy-done.1, ...), custom_call_target="tpu_custom_call" | custom-call | flops 805306368 | bytes 16777216 | tf_op jit(solution)/shard_map/near/pallas_call | solution.py:356
  82.1 0.0 collective-permute-done.11.refs_2_
  82.1 0.0 collective-permute-done.12.refs_3_
  82.1 1.3 %collective-permute-done.13.refs_5_ = bf16[8,128,128]{2,1,0:T(8,128)(2,1)S(1)} collective-permute-done((bf16[8,128,128]{2,1,0:T(8,128)(2,1)}, bf16[8,128,128]{2,1,0:T(8,128)(2,1)S(1)}, u32[]{:S(2)}, u32[]{:S(2)}) %collective-permute-start.13) | collective-permute-done | bytes 262176 | tf_op jit(solution)/shard_map/ppermute | solution.py:304
  83.4 20.3 %collective-permute-done.14.refs_6_ = bf16[8,128,128]{2,1,0:T(8,128)(2,1)S(1)} collective-permute-done((bf16[8,128,128]{2,1,0:T(8,128)(2,1)}, bf16[8,128,128]{2,1,0:T(8,128)(2,1)S(1)}, u32[]{:S(2)}, u32[]{:S(2)}) %collective-permute-start.14) | collective-permute-done | bytes 262176 | tf_op jit(solution)/shard_map/ppermute | solution.py:304
  103.7 0.0 collective-permute-done.15.refs_7_
  103.7 0.0 copy-done.3
  103.7 0.0 copy-start.7
  103.7 3.8 %far.1 = (f32[4096,128]{1,0:T(8,128)S(1)}, f32[16,1,128]{2,1,0:T(1,128)S(1)}) custom-call(s32[64]{0:T(128)S(1)} %get-tuple-element.26.where_ref, bf16[32,6,128,128]{3,2,1,0:T(8,128)(2,1)} %tiles_ref.3, f32[4096,128]{1,0:T(8,128)} %get-tuple-element.27.part_ref, bf16[256,128]{1,0:T(8,128)(2,1)S(1)} %get-tuple-element.28.graph2_ref, ...), custom_call_target="tpu_custom_call" | custom-call | flops 536870912 | bytes 8388608 | tf_op jit(solution)/shard_map/far/pallas_call | solution.py:388
  107.6 13.4 %all_to_all.5.mass_ref = f32[16,1,128]{2,1,0:T(1,128)S(1)} all-to-all(f32[16,1,128]{2,1,0:T(1,128)S(1)} %get-tuple-element.38), channel_id=1, replica_groups=mesh['groups'=2,'rows'=8,'sub'=2] {'rows','sub'}, dimensions={0} | all-to-all | bytes 16384 | tf_op jit(solution)/shard_map/all_to_all | solution.py:407
  121.0 0.0 copy-done.7
  121.0 1.6 %last.1 = f32[4096,128]{1,0:T(8,128)} custom-call(f32[4096,128]{1,0:T(8,128)S(1)} %get-tuple-element.37.logits_ref, f32[16,1,128]{2,1,0:T(1,128)S(1)} %all_to_all.5.mass_ref, f32[1,128]{1,0:T(1,128)S(1)} %bitcast.11), custom_call_target="tpu_custom_call" | custom-call | tf_op jit(solution)/shard_map/last/pallas_call | solution.py:409
  (12 shorter events, 0.0 us)
Async XLA Ops:
  0.0 26.3 %collective-permute-start.1 = (bf16[32,128,128]{2,1,0:T(8,128)(2,1)}, bf16[32,128,128]{2,1,0:T(8,128)(2,1)S(1)}, u32[]{:S(2)}, u32[]{:S(2)}) collective-permute-start(bf16[32,128,128]{2,1,0:T(8,128)(2,1)} %bitcast.12), channel_id=1, source_target_pairs={{0,2},{1,3},{2,0},{3,1},{4,6},{5,7},{6,4},{7,5},{8,10},{9,11},{10,... | collective-permute-start | bytes 3145736 | tf_op jit(solution)/shard_map/ppermute | solution.py:304
  3.0 48.0 %collective-permute-start = (bf16[32,128,128]{2,1,0:T(8,128)(2,1)}, bf16[32,128,128]{2,1,0:T(8,128)(2,1)S(1)}, u32[]{:S(2)}, u32[]{:S(2)}) collective-permute-start(bf16[32,128,128]{2,1,0:T(8,128)(2,1)} %bitcast.13), channel_id=1, source_target_pairs={{0,1},{1,0},{2,3},{3,2},{4,5},{5,4},{6,7},{7,6},{8,9},{9,8},{10,11... | collective-permute-start | bytes 3145736 | tf_op jit(solution)/shard_map/ppermute | solution.py:304
  26.3 33.2 %collective-permute-start.2 = (bf16[32,128,128]{2,1,0:T(8,128)(2,1)S(1)}, bf16[32,128,128]{2,1,0:T(8,128)(2,1)S(1)}, u32[]{:S(2)}, u32[]{:S(2)}) collective-permute-start(bf16[32,128,128]{2,1,0:T(8,128)(2,1)S(1)} %collective-permute-done.1.refs_4_), channel_id=1, source_target_pairs={{0,1},{1,0},{2,3},{3,2},{4,5},{5,4},{6,7},{7,6},{8,9},{9,8},{10,11... | collective-permute-start | bytes 3145736 | tf_op jit(solution)/shard_map/ppermute | solution.py:304
  26.3 39.6 %collective-permute-start.4 = (bf16[32,128,128]{2,1,0:T(8,128)(2,1)}, bf16[32,128,128]{2,1,0:T(8,128)(2,1)}, u32[]{:S(2)}, u32[]{:S(2)}) collective-permute-start(bf16[32,128,128]{2,1,0:T(8,128)(2,1)} %bitcast.14), channel_id=1, source_target_pairs={{7,8},{8,7},{23,24},{24,23}} | collective-permute-start | bytes 3145736 | tf_op jit(solution)/shard_map/ppermute | solution.py:307
  28.0 40.2 %collective-permute-start.3 = (bf16[32,128,128]{2,1,0:T(8,128)(2,1)S(1)}, bf16[32,128,128]{2,1,0:T(8,128)(2,1)}, u32[]{:S(2)}, u32[]{:S(2)}) collective-permute-start(bf16[32,128,128]{2,1,0:T(8,128)(2,1)S(1)} %collective-permute-done.1.refs_4_), channel_id=1, source_target_pairs={{1,4},{9,12},{6,3},{14,11},{17,20},{25,28},{22,19},{30,27}} | collective-permute-start | bytes 3145736 | tf_op jit(solution)/shard_map/ppermute | solution.py:343
  29.6 0.7 copy-start.5
  31.8 3.7 %collective-permute-start.5 = (f32[5,1,128]{2,1,0:T(1,128)S(1)}, f32[5,1,128]{2,1,0:T(1,128)S(1)}, u32[]{:S(2)}, u32[]{:S(2)}) collective-permute-start(f32[5,1,128]{2,1,0:T(1,128)S(1)} %get-tuple-element.23), channel_id=1, source_target_pairs={{0,4},{1,5},{2,6},{3,7},{4,0},{5,1},{6,2},{7,3},{8,12},{9,13},{10,... | collective-permute-start | bytes 7688 | tf_op jit(solution)/shard_map/ppermute | solution.py:304
  35.5 10.1 %collective-permute-start.6 = (f32[5,1,128]{2,1,0:T(1,128)S(1)}, f32[5,1,128]{2,1,0:T(1,128)S(1)}, u32[]{:S(2)}, u32[]{:S(2)}) collective-permute-start(f32[5,1,128]{2,1,0:T(1,128)S(1)} %get-tuple-element.24), channel_id=1, source_target_pairs={{0,8},{1,9},{2,10},{3,11},{4,12},{5,13},{6,14},{7,15},{8,0},{9,1},... | collective-permute-start | bytes 7688 | tf_op jit(solution)/shard_map/ppermute | solution.py:304
  45.6 5.4 %collective-permute-start.7 = (f32[5,1,128]{2,1,0:T(1,128)S(1)}, f32[5,1,128]{2,1,0:T(1,128)S(1)}, u32[]{:S(2)}, u32[]{:S(2)}) collective-permute-start(f32[5,1,128]{2,1,0:T(1,128)S(1)} %get-tuple-element.25), channel_id=1, source_target_pairs={{0,12},{1,13},{2,14},{3,15},{4,8},{5,9},{6,10},{7,11},{8,4},{9,5},... | collective-permute-start | bytes 7688 | tf_op jit(solution)/shard_map/ppermute | solution.py:304
  51.0 19.3 %copy-start = (bf16[32,128,128]{2,1,0:T(8,128)(2,1)}, bf16[32,128,128]{2,1,0:T(8,128)(2,1)S(1)}, u32[]{:S(2)}) copy-start(bf16[32,128,128]{2,1,0:T(8,128)(2,1)S(1)} %collective-permute-done.chip_ref.refs_2_.refs_4_) | copy-start | bytes 3145732
  52.7 11.0 %copy-start.8 = (bf16[8,128,128]{2,1,0:T(8,128)(2,1)S(1)}, bf16[8,128,128]{2,1,0:T(8,128)(2,1)}, u32[]{:S(2)}) copy-start(bf16[8,128,128]{2,1,0:T(8,128)(2,1)} %get-tuple-element.32) | copy-start | bytes 786436
  52.7 13.2 %collective-permute-start.10 = (bf16[8,128,128]{2,1,0:T(8,128)(2,1)}, bf16[8,128,128]{2,1,0:T(8,128)(2,1)S(1)}, u32[]{:S(2)}, u32[]{:S(2)}) collective-permute-start(bf16[8,128,128]{2,1,0:T(8,128)(2,1)} %get-tuple-element.30), channel_id=1, source_target_pairs={{0,4},{1,5},{2,6},{3,7},{4,0},{5,1},{6,2},{7,3},{8,12},{9,13},{10,... | collective-permute-start | bytes 786440 | tf_op jit(solution)/shard_map/ppermute | solution.py:304
  52.8 2.2 %collective-permute-start.8 = (f32[1,128]{1,0:T(1,128)S(1)}, f32[1,128]{1,0:T(1,128)S(1)}, u32[]{:S(2)}, u32[]{:S(2)}) collective-permute-start(f32[1,128]{1,0:T(1,128)S(1)} %fusion), channel_id=1, source_target_pairs={{0,1},{1,0},{2,3},{3,2},{4,5},{5,4},{6,7},{7,6},{8,9},{9,8},{10,11... | collective-permute-start | bytes 1544 | tf_op jit(solution)/shard_map/ppermute | solution.py:304
  55.0 8.7 %collective-permute-start.9 = (f32[1,128]{1,0:T(1,128)S(1)}, f32[1,128]{1,0:T(1,128)S(1)}, u32[]{:S(2)}, u32[]{:S(2)}) collective-permute-start(f32[1,128]{1,0:T(1,128)S(1)} %add.49.refs_0_), channel_id=1, source_target_pairs={{0,2},{1,3},{2,0},{3,1},{4,6},{5,7},{6,4},{7,5},{8,10},{9,11},{10,... | collective-permute-start | bytes 1544 | tf_op jit(solution)/shard_map/ppermute | solution.py:304
  59.6 12.1 %copy-start.1 = (bf16[32,128,128]{2,1,0:T(8,128)(2,1)}, bf16[32,128,128]{2,1,0:T(8,128)(2,1)S(1)}, u32[]{:S(2)}) copy-start(bf16[32,128,128]{2,1,0:T(8,128)(2,1)S(1)} %collective-permute-done.2.level_ref.refs_5_) | copy-start | bytes 3145732
  59.6 12.1 %copy-start.4 = (s32[128,128]{1,0:T(8,128)S(1)}, s32[128,128]{1,0:T(8,128)}, u32[]{:S(2)}) copy-start(s32[128,128]{1,0:T(8,128)} %graph_ref.1) | copy-start | bytes 196612
  59.6 12.1 %copy-start.6 = (s32[32,6]{0,1:T(8,128)S(1)}, s32[32,6]{0,1:T(8,128)}, u32[]{:S(2)}) copy-start(s32[32,6]{0,1:T(8,128)} %param.7) | copy-start | bytes 2308
  59.6 22.5 %collective-permute-start.11 = (bf16[8,128,128]{2,1,0:T(8,128)(2,1)}, bf16[8,128,128]{2,1,0:T(8,128)(2,1)S(1)}, u32[]{:S(2)}, u32[]{:S(2)}) collective-permute-start(bf16[8,128,128]{2,1,0:T(8,128)(2,1)} %get-tuple-element.31), channel_id=1, source_target_pairs={{0,8},{1,9},{2,10},{3,11},{4,12},{5,13},{6,14},{7,15},{8,0},{9,1},... | collective-permute-start | bytes 786440 | tf_op jit(solution)/shard_map/ppermute | solution.py:304
  63.7 18.4 %collective-permute-start.12 = (bf16[8,128,128]{2,1,0:T(8,128)(2,1)S(1)}, bf16[8,128,128]{2,1,0:T(8,128)(2,1)S(1)}, u32[]{:S(2)}, u32[]{:S(2)}) collective-permute-start(bf16[8,128,128]{2,1,0:T(8,128)(2,1)S(1)} %copy-done.8), channel_id=1, source_target_pairs={{0,12},{1,13},{2,14},{3,15},{4,8},{5,9},{6,10},{7,11},{8,4},{9,5},... | collective-permute-start | bytes 786440 | tf_op jit(solution)/shard_map/ppermute | solution.py:304
  65.9 17.5 %collective-permute-start.13 = (bf16[8,128,128]{2,1,0:T(8,128)(2,1)}, bf16[8,128,128]{2,1,0:T(8,128)(2,1)S(1)}, u32[]{:S(2)}, u32[]{:S(2)}) collective-permute-start(bf16[8,128,128]{2,1,0:T(8,128)(2,1)} %get-tuple-element.34), channel_id=1, source_target_pairs={{0,4},{1,5},{2,6},{3,7},{4,0},{5,1},{6,2},{7,3},{8,12},{9,13},{10,... | collective-permute-start | bytes 786440 | tf_op jit(solution)/shard_map/ppermute | solution.py:304
  65.9 37.8 %collective-permute-start.14 = (bf16[8,128,128]{2,1,0:T(8,128)(2,1)}, bf16[8,128,128]{2,1,0:T(8,128)(2,1)S(1)}, u32[]{:S(2)}, u32[]{:S(2)}) collective-permute-start(bf16[8,128,128]{2,1,0:T(8,128)(2,1)} %get-tuple-element.35), channel_id=1, source_target_pairs={{0,8},{1,9},{2,10},{3,11},{4,12},{5,13},{6,14},{7,15},{8,0},{9,1},... | collective-permute-start | bytes 786440 | tf_op jit(solution)/shard_map/ppermute | solution.py:304
  68.2 35.5 %collective-permute-start.15 = (bf16[8,128,128]{2,1,0:T(8,128)(2,1)}, bf16[8,128,128]{2,1,0:T(8,128)(2,1)S(1)}, u32[]{:S(2)}, u32[]{:S(2)}) collective-permute-start(bf16[8,128,128]{2,1,0:T(8,128)(2,1)} %get-tuple-element.36), channel_id=1, source_target_pairs={{0,12},{1,13},{2,14},{3,15},{4,8},{5,9},{6,10},{7,11},{8,4},{9,5},... | collective-permute-start | bytes 786440 | tf_op jit(solution)/shard_map/ppermute | solution.py:304
  71.7 32.0 %copy-start.2 = (bf16[8,128,128]{2,1,0:T(8,128)(2,1)S(1)}, bf16[8,128,128]{2,1,0:T(8,128)(2,1)}, u32[]{:S(2)}) copy-start(bf16[8,128,128]{2,1,0:T(8,128)(2,1)} %shard_map.55.refs_0_) | copy-start | bytes 786436
  71.7 32.0 %copy-start.3 = (bf16[8,128,128]{2,1,0:T(8,128)(2,1)S(1)}, bf16[8,128,128]{2,1,0:T(8,128)(2,1)}, u32[]{:S(2)}) copy-start(bf16[8,128,128]{2,1,0:T(8,128)(2,1)} %get-tuple-element.33.refs_4_) | copy-start | bytes 786436
  103.7 17.3 %copy-start.7 = (f32[128]{0:T(128)S(1)}, f32[128]{0:T(128)}, u32[]{:S(2)}) copy-start(f32[128]{0:T(128)} %param.9) | copy-start | bytes 1540

commit v6 on v5

--- a/solution.py
+++ b/solution.py
@@ -34,9 +34,11 @@
     return pltpu.CompilerParams(vmem_limit_bytes=mib << 20)
 
 
-def requests_kernel(nodes_total, place_ref, cols_ref, coupling_ref, *refs):
-    *out_refs, own_ref, rows, table_ref, sems = refs
+def requests_kernel(nodes_total, place_ref, all_cols_ref, coupling_ref, *refs):
+    *out_refs, own_ref, rows, cols_ref, table_ref, cols_sem, sems = refs
     slots, blocks_dev = cols_ref.shape
+    cols_copy = pltpu.make_async_copy(all_cols_ref, cols_ref, cols_sem)
+    cols_copy.start()
     shards = table_ref.shape[0]
     nodes, clusters = coupling_ref.shape
     parts = sems.shape[0]
@@ -56,6 +58,7 @@
     ).astype(f32)
     count = jnp.zeros((shards, 1), f32)
     table = jnp.zeros((shards, clusters), f32)
+    cols_copy.wait()
     for slot_id in range(NEAR, slots):
         local = cols_ref[slot_id : slot_id + 1, :] - owner * blocks_dev
         hit = (local >= 0) & (local < blocks_dev)
@@ -110,46 +113,11 @@
     return jnp.concatenate([high, (x - high.astype(f32)).astype(bf16)], axis=1)
 
 
-def near_kernel(
-    group, cap, shards, place_ref, cols_ref, own_ref, chip_ref, level_ref, beyond_ref, across_ref, tiles_ref, graph_ref,
-    *refs,
-):
-    *mass_refs, part_ref, graph2_ref, where_ref = refs[:-9]
-    window, tiles, part, pull_ref, count_ref, own_sem, sems, tile_sems, part_sems = refs[-9:]
-    blocks_dev, tile, clusters = own_ref.shape
-    slots = tiles_ref.shape[1]
-    steps = blocks_dev // group
-    place = place_ref[0]
-    spot, level = place % LEVEL, place // LEVEL
-
-    def take(src, i, sem):
-        return pltpu.make_async_copy(src, window.at[pl.ds(i * blocks_dev, blocks_dev)], sem)
-
-    take(own_ref, 1, own_sem).start()
-    even = spot % 2 == 0
-    middle = shards // 2
-    split_here = (place == middle) | (place == middle - 1)
-    edge = ((spot == 0) | (spot == LEVEL - 1)) & jnp.logical_not(split_here)
-    inside = (spot != 0) & (spot != LEVEL - 1)
-    for flag, src in ((split_here, across_ref), (edge, beyond_ref), (inside, level_ref)):
-        for is_even, chip_at, other_at in ((True, 2, 0), (False, 0, 2)):
-
-            @pl.when(flag & (even == is_even))
-            def _():
-                take(chip_ref, chip_at, sems.at[0]).start()
-                take(src, other_at, sems.at[1]).start()
-
-    def fetch(i):
-        here = pl.ds(i * group, group)
-        return pltpu.make_async_copy(tiles_ref.at[here, pl.ds(0, NEAR)], tiles.at[here], tile_sems.at[i])
-
-    def store(i):
-        here = pl.ds(pl.multiple_of(i * group * tile, group * tile), group * tile)
-        return pltpu.make_async_copy(part.at[here], part_ref.at[here], part_sems.at[i])
-
-    for i in range(steps):
-        fetch(i).start()
-
+def prep_kernel(cap, shards, place_ref, cols_ref, graph_ref, *refs):
+    *mass_refs, graph2_ref, pull_ref, where_ref, count_ref = refs
+    slots, blocks_dev = cols_ref.shape
+    clusters = graph_ref.shape[0]
+    spot, level = place_ref[0] % LEVEL, place_ref[0] // LEVEL
     graph = graph_ref[...].astype(f32)
     colmass = mass_refs[0][...]
     for ref in mass_refs[1:]:
@@ -168,7 +136,7 @@
     graph2_ref[:clusters, :] = turned
     graph2_ref[clusters:, :] = turned
 
-    @pl.loop(0, count_ref.shape[0])
+    @pl.loop(0, shards)
     def _(o):
         count_ref[o] = 0
 
@@ -183,6 +151,43 @@
             row = ((turn // 2) * (shards // LEVEL) + ((owner // LEVEL) ^ level)) * 2 + turn % 2
             where_ref[b * (slots - NEAR) + slot_id - NEAR] = row * cap + rank
 
+
+def near_kernel(
+    group, chunk, shards, place_ref, cols_ref, own_ref, chip_ref, level_ref, beyond_ref, across_ref, tiles_ref,
+    graph2_ref, pull_ref, part_ref, window, tiles, part, own_sem, sems, tile_sems, part_sems,
+):
+    blocks_dev, tile, clusters = own_ref.shape
+    steps = blocks_dev // group
+    place = place_ref[0]
+    spot = place % LEVEL
+
+    def take(src, i, sem):
+        return pltpu.make_async_copy(src, window.at[pl.ds(i * blocks_dev, blocks_dev)], sem)
+
+    take(own_ref, 1, own_sem).start()
+    even = spot % 2 == 0
+    middle = shards // 2
+    split_here = (place == middle) | (place == middle - 1)
+    edge = ((spot == 0) | (spot == LEVEL - 1)) & jnp.logical_not(split_here)
+    inside = (spot != 0) & (spot != LEVEL - 1)
+    for flag, src in ((split_here, across_ref), (edge, beyond_ref), (inside, level_ref)):
+        for is_even, chip_at, other_at in ((True, 2, 0), (False, 0, 2)):
+
+            @pl.when(flag & (even == is_even))
+            def _():
+                take(chip_ref, chip_at, sems.at[0]).start()
+                take(src, other_at, sems.at[1]).start()
+
+    def fetch(i):
+        here = pl.ds(i * chunk, chunk)
+        return pltpu.make_async_copy(tiles_ref.at[here, pl.ds(0, NEAR)], tiles.at[here], tile_sems.at[i])
+
+    def store(i):
+        here = pl.ds(i * chunk * tile, chunk * tile)
+        return pltpu.make_async_copy(part.at[here], part_ref.at[here], part_sems.at[i])
+
+    for i in range(blocks_dev // chunk):
+        fetch(i).start()
     take(own_ref, 1, own_sem).wait()
     take(chip_ref, 0, sems.at[0]).wait()
     take(chip_ref, 2, sems.at[1]).wait()
@@ -190,24 +195,32 @@
     base = (place - 1) * blocks_dev
     scale = 2.0 * eta_step / clusters
 
-    @pl.loop(0, steps)
-    def _(step):
-        fetch(step).wait()
-        for i in range(group):
-            b = step * group + i
-            here = pl.ds(pl.multiple_of(b * tile, tile), tile)
+    def products(step):
+        first = step * group
+        if first % chunk == 0:
+            fetch(first // chunk).wait()
+        spreads = []
+        for b in range(first, first + group):
             picked = [window[cols_ref[s, b] - base] for s in range(NEAR)]
             wide = jnp.concatenate([tiles[b, s] for s in range(NEAR)], axis=1)
-            spread = jnp.dot(wide, jnp.concatenate(picked, axis=0), preferred_element_type=f32)
-            affinity = jnp.dot(split(spread), graph2_ref[...], preferred_element_type=f32)
-            part[here, :] = (
-                jnp.log(window[blocks_dev + b].astype(f32)) - eta_step * pull_ref[0:1, :] + scale * affinity
-            )
-        store(step).start()
-
-    @pl.loop(0, steps)
-    def _(step):
-        store(step).wait()
+            spreads.append(split(jnp.dot(wide, jnp.concatenate(picked, axis=0), preferred_element_type=f32)))
+        return jnp.concatenate(spreads, axis=0)
+
+    ahead = products(0)
+    for step in range(steps):
+        spreads = ahead
+        if step + 1 < steps:
+            ahead = products(step + 1)
+        first = step * group
+        affinity = jnp.dot(spreads, graph2_ref[...], preferred_element_type=f32)
+        own = window[blocks_dev + first : blocks_dev + first + group].reshape(group * tile, clusters)
+        part[first * tile : (first + group) * tile, :] = (
+            jnp.log(own.astype(f32)) - eta_step * pull_ref[0:1, :] + scale * affinity
+        )
+        if (first + group) % chunk == 0:
+            store(first // chunk).start()
+    for i in range(blocks_dev // chunk):
+        store(i).wait()
 
 
 def far_kernel(
@@ -304,7 +317,9 @@
         return lax.ppermute(x, NODES, [(i, i ^ bits) for i in range(shards)])
 
     middle = shards // 2
-    across = lax.ppermute(blocks, NODES, [(middle - 1, middle), (middle, middle - 1)])
+    over = swap(blocks, 2)
+    chip = swap(blocks, 1)
+    across = lax.ppermute(blocks, NODES, [(middle - 1, middle + 2), (middle, middle - 3)])
 
     *asked, mine, held = pl.pallas_call(
         functools.partial(requests_kernel, nodes_total),
@@ -312,15 +327,18 @@
             *[pltpu.VMEM((LEVEL + 1, 1, clusters), f32)] * levels,
             pltpu.VMEM((rows, clusters), bf16),
         ),
-        in_specs=[SMEM, VMEM, ANY],
+        in_specs=[SMEM, ANY, ANY],
         out_specs=[VMEM] * (levels + 1),
-        scratch_shapes=[pltpu.VMEM((shards, 1, clusters), f32), pltpu.SemaphoreType.DMA((8,))],
+        scratch_shapes=[
+            pltpu.VMEM((slots, blocks_dev), i32),
+            pltpu.VMEM((shards, 1, clusters), f32),
+            pltpu.SemaphoreType.DMA,
+            pltpu.SemaphoreType.DMA((8,)),
+        ],
         compiler_params=params(8),
         name="requests",
-    )(place, cols, in_hbm(coupling))
+    )(place, in_hbm(cols), in_hbm(coupling))
     heard = [swap(x, dz * LEVEL) for dz, x in zip(others, asked)]
-    over = swap(blocks, 2)
-    chip = swap(blocks, 1)
 
     def gather(stage, heard, sources):
         return pl.pallas_call(
@@ -341,6 +359,7 @@
     over_chip = swap(over, 1)
     edges = [z * LEVEL for z in range(1, levels) if z * LEVEL != middle]
     beyond = lax.ppermute(over, NODES, [(i - LEVEL + 1, i) for i in edges] + [(i + LEVEL - 2, i - 1) for i in edges])
+    across = lax.ppermute(across, NODES, [(middle + 2, middle), (middle - 3, middle - 1)])
     found = gather(1, (*heard, mine), (over, over_chip))
     there = [swap(x, dz * LEVEL) for dz, x in zip(others, found)]
     home_late = found[-1]
@@ -353,21 +372,30 @@
     mass = mass + mass_chip
     mass_over = swap(mass, 2)
 
-    part, graph2, where = pl.pallas_call(
-        functools.partial(near_kernel, group, cap, shards),
+    graph2, pull, where = pl.pallas_call(
+        functools.partial(prep_kernel, cap, shards),
         out_shape=(
-            pltpu.HBM((rows, clusters), f32),
             pltpu.VMEM((2 * clusters, clusters), bf16),
+            pltpu.VMEM((8, clusters), f32),
             jax.ShapeDtypeStruct((far_count,), i32),
         ),
-        in_specs=[SMEM, SMEM, ANY, ANY, ANY, ANY, ANY, ANY, VMEM, VMEM, VMEM],
-        out_specs=(ANY, VMEM, SMEM),
+        in_specs=[SMEM, SMEM, VMEM, VMEM, VMEM],
+        out_specs=(VMEM, VMEM, SMEM),
+        scratch_shapes=[pltpu.SMEM((shards,), i32)],
+        compiler_params=params(4),
+        name="prep",
+    )(place, cols, cluster_graph, mass, mass_over)
+
+    chunk = min(16, blocks_dev)
+    part = pl.pallas_call(
+        functools.partial(near_kernel, group, group, shards),
+        out_shape=pltpu.HBM((rows, clusters), f32),
+        in_specs=[SMEM, SMEM, ANY, ANY, ANY, ANY, ANY, ANY, VMEM, VMEM],
+        out_specs=ANY,
         scratch_shapes=[
             pltpu.VMEM((3 * blocks_dev, tile, clusters), bf16),
             pltpu.VMEM((blocks_dev, NEAR, tile, tile), bf16),
             pltpu.VMEM((rows, clusters), f32),
-            pltpu.VMEM((8, clusters), f32),
-            pltpu.SMEM((shards,), i32),
             pltpu.SemaphoreType.DMA,
             pltpu.SemaphoreType.DMA((2,)),
             pltpu.SemaphoreType.DMA((steps,)),
@@ -378,12 +406,8 @@
             flops=flops * (NEAR * tile + 2 * clusters), bytes_accessed=16 << 20, transcendentals=rows * clusters
         ),
         name="near",
-    )(
-        place, cols, in_hbm(blocks), in_hbm(chip), in_hbm(over_chip), in_hbm(beyond), in_hbm(across),
-        in_hbm(tile_vals), cluster_graph, mass, mass_over,
-    )
-
-    chunk = min(16, blocks_dev)
+    )(place, cols, in_hbm(blocks), chip, over_chip, beyond, across, in_hbm(tile_vals), on_chip(graph2), on_chip(pull))
+
     parts = [home, *fetched, home_late, *there]
     logits, mass_parts = pl.pallas_call(
         functools.partial(far_kernel, group, chunk, nodes_total),

time: 123 us -> 122 us (level)
  waiting for transfers between devices: 58.7 us -> 49.9 us
  starting transfers between devices: 27.2 us -> 35.4 us
    ppermute x14, waiting for transfers between devices: 58.7 us -> 49.9 us  [swap(): return lax.ppermute(x, NODES, [(i, i ^ bits) for i in range(shards)])]
    ppermute x14, starting transfers between devices: 24 us -> 31.4 us  [swap(): return lax.ppermute(x, NODES, [(i, i ^ bits) for i in range(shards)])]
    pallas_call x1 -> x2, Pallas kernels: 10.4 us -> 9.41 us  [the longest x1 6.19 us: local(): pl.pallas_call(functools.partial(near_kernel, group, group, shards), out_...]
  transfers between devices with their start and end apart: 16 -> 17, of which waited for: 7 -> 7; matrix products, arithmetic and copies ran while one was open for 0% -> 0% of each run, Pallas kernels for 14% -> 14%
where the time goes in v6:
time: 122 us
  waiting for transfers between devices  49.9 us (41%)
  starting transfers between devices  35.4 us (29%)
  Pallas kernels  23 us (19%)
  blocking collectives  13.3 us (11%)
    ppermute x14, waiting for transfers between devices, swap(): return lax.ppermute(x, NODES, [(i, i ^ bits) for i in range(shards)])  49.9 us
    ppermute x14, starting transfers between devices, swap(): return lax.ppermute(x, NODES, [(i, i ^ bits) for i in range(shards)])  31.4 us
    all_to_all x1, blocking collectives, local(): lax.all_to_all(mass_parts, NODES, split_axis=0, concat_axis=0, tiled=True)  13.3 us
    pallas_call x1, Pallas kernels, local(): pl.pallas_call(functools.partial(near_kernel, group, group, shards), out_...  6.19 us
    pallas_call x3, Pallas kernels, gather(): pl.pallas_call(functools.partial(gather_kernel, cap, stage), out_shape=[p...  6.03 us
    pallas_call x1, Pallas kernels, local(): pl.pallas_call(functools.partial(far_kernel, group, chunk, nodes_total),...  3.85 us
    pallas_call x1, Pallas kernels, local(): pl.pallas_call(functools.partial(prep_kernel, cap, shards), out_shape=(pl...  3.22 us
  transfers between devices with their start and end apart: 17, of which 7 were waited for; matrix products, arithmetic and copies ran while one was open for 0% of the time, Pallas kernels for 14%

profile of v6, /device:TPU:0, one launch (start us, length us, event | category | flops | bytes accessed | tf_op | source)
XLA Modules:
  0.0 121.8 jit_solution(2024426389665135901)
XLA Ops:
  0.0 3.0 %collective-permute-start.6 = (bf16[32,128,128]{2,1,0:T(8,128)(2,1)}, bf16[32,128,128]{2,1,0:T(8,128)(2,1)}, u32[]{:S(2)}, u32[]{:S(2)}) collective-permute-start(bf16[32,128,128]{2,1,0:T(8,128)(2,1)} %bitcast.13), channel_id=1, source_target_pairs={{0,2},{1,3},{2,0},{3,1},{4,6},{5,7},{6,4},{7,5},{8,10},{9,11},{10,... | collective-permute-start | bytes 3145736 | tf_op jit(solution)/shard_map/ppermute | solution.py:317
  3.0 1.7 %collective-permute-start.9 = (bf16[32,128,128]{2,1,0:T(8,128)(2,1)}, bf16[32,128,128]{2,1,0:T(8,128)(2,1)}, u32[]{:S(2)}, u32[]{:S(2)}) collective-permute-start(bf16[32,128,128]{2,1,0:T(8,128)(2,1)} %bitcast.14), channel_id=1, source_target_pairs={{7,10},{8,5},{23,26},{24,21}} | collective-permute-start | bytes 3145736 | tf_op jit(solution)/shard_map/ppermute | solution.py:322
  4.6 0.0 collective-permute-start.5
  4.6 21.8 %collective-permute-done.6.refs_4_ = bf16[32,128,128]{2,1,0:T(8,128)(2,1)} collective-permute-done((bf16[32,128,128]{2,1,0:T(8,128)(2,1)}, bf16[32,128,128]{2,1,0:T(8,128)(2,1)}, u32[]{:S(2)}, u32[]{:S(2)}) %collective-permute-start.6) | collective-permute-done | bytes 1048608 | tf_op jit(solution)/shard_map/ppermute | solution.py:317
  26.4 0.0 collective-permute-start.7
  26.4 0.0 collective-permute-done.9
  26.4 0.7 collective-permute-start.10
  27.2 1.6 %collective-permute-start.8 = (bf16[32,128,128]{2,1,0:T(8,128)(2,1)}, bf16[32,128,128]{2,1,0:T(8,128)(2,1)}, u32[]{:S(2)}, u32[]{:S(2)}) collective-permute-start(bf16[32,128,128]{2,1,0:T(8,128)(2,1)} %collective-permute-done.6.refs_4_), channel_id=1, source_target_pairs={{1,4},{9,12},{6,3},{14,11},{17,20},{25,28},{22,19},{30,27}} | collective-permute-start | bytes 3145736 | tf_op jit(solution)/shard_map/ppermute | solution.py:361
  28.8 2.2 %requests.1 = (f32[5,1,128]{2,1,0:T(1,128)S(1)}, f32[5,1,128]{2,1,0:T(1,128)S(1)}, f32[5,1,128]{2,1,0:T(1,128)S(1)}, f32[5,1,128]{2,1,0:T(1,128)S(1)}, bf16[4096,128]{1,0:T(8,128)(2,1)S(1)}) custom-call(s32[1]{0:T(128)} %bitcast.place_ref, s32[6,32]{1,0:T(8,128)} %bitcast.9, bf16[4096,128]{1,0:T(8,128)(2,1)} %coupling_ref.1), custom_call_target="tpu_custom_call" | custom-call | tf_op jit(solution)/shard_map/requests/pallas_call | solution.py:324
  31.0 1.6 %collective-permute-start = (f32[5,1,128]{2,1,0:T(1,128)S(1)}, f32[5,1,128]{2,1,0:T(1,128)S(1)}, u32[]{:S(2)}, u32[]{:S(2)}) collective-permute-start(f32[5,1,128]{2,1,0:T(1,128)S(1)} %get-tuple-element.23), channel_id=1, source_target_pairs={{0,4},{1,5},{2,6},{3,7},{4,0},{5,1},{6,2},{7,3},{8,12},{9,13},{10,... | collective-permute-start | bytes 7688 | tf_op jit(solution)/shard_map/ppermute | solution.py:317
  32.5 2.1 %collective-permute-done.refs_0_ = f32[5,1,128]{2,1,0:T(1,128)S(1)} collective-permute-done((f32[5,1,128]{2,1,0:T(1,128)S(1)}, f32[5,1,128]{2,1,0:T(1,128)S(1)}, u32[]{:S(2)}, u32[]{:S(2)}) %collective-permute-start) | collective-permute-done | bytes 2592 | tf_op jit(solution)/shard_map/ppermute | solution.py:317
  34.6 3.4 %collective-permute-start.1 = (f32[5,1,128]{2,1,0:T(1,128)S(1)}, f32[5,1,128]{2,1,0:T(1,128)S(1)}, u32[]{:S(2)}, u32[]{:S(2)}) collective-permute-start(f32[5,1,128]{2,1,0:T(1,128)S(1)} %get-tuple-element.24), channel_id=1, source_target_pairs={{0,8},{1,9},{2,10},{3,11},{4,12},{5,13},{6,14},{7,15},{8,0},{9,1},... | collective-permute-start | bytes 7688 | tf_op jit(solution)/shard_map/ppermute | solution.py:317
  38.0 1.6 %collective-permute-done.1.refs_1_ = f32[5,1,128]{2,1,0:T(1,128)S(1)} collective-permute-done((f32[5,1,128]{2,1,0:T(1,128)S(1)}, f32[5,1,128]{2,1,0:T(1,128)S(1)}, u32[]{:S(2)}, u32[]{:S(2)}) %collective-permute-start.1) | collective-permute-done | bytes 2592 | tf_op jit(solution)/shard_map/ppermute | solution.py:317
  39.6 3.2 %collective-permute-start.2 = (f32[5,1,128]{2,1,0:T(1,128)S(1)}, f32[5,1,128]{2,1,0:T(1,128)S(1)}, u32[]{:S(2)}, u32[]{:S(2)}) collective-permute-start(f32[5,1,128]{2,1,0:T(1,128)S(1)} %get-tuple-element.25), channel_id=1, source_target_pairs={{0,12},{1,13},{2,14},{3,15},{4,8},{5,9},{6,10},{7,11},{8,4},{9,5},... | collective-permute-start | bytes 7688 | tf_op jit(solution)/shard_map/ppermute | solution.py:317
  42.8 2.2 %collective-permute-done.2.refs_2_ = f32[5,1,128]{2,1,0:T(1,128)S(1)} collective-permute-done((f32[5,1,128]{2,1,0:T(1,128)S(1)}, f32[5,1,128]{2,1,0:T(1,128)S(1)}, u32[]{:S(2)}, u32[]{:S(2)}) %collective-permute-start.2) | collective-permute-done | bytes 2592 | tf_op jit(solution)/shard_map/ppermute | solution.py:317
  45.0 0.0 collective-permute-done.5.chip_ref.refs_2_.refs_4_
  45.0 1.6 %shard_map.56 = (bf16[8,128,128]{2,1,0:T(8,128)(2,1)}, bf16[8,128,128]{2,1,0:T(8,128)(2,1)}, bf16[8,128,128]{2,1,0:T(8,128)(2,1)}) custom-call(s32[1]{0:T(128)} %bitcast.place_ref, f32[5,1,128]{2,1,0:T(1,128)S(1)} %collective-permute-done.refs_0_, f32[5,1,128]{2,1,0:T(1,128)S(1)} %collective-permute-done.1.refs_1_, ...), custom_call_target="tpu_custom_call" | custom-call | tf_op jit(solution)/shard_map/pallas_call | solution.py:344
  46.6 0.0 copy-start.5
  46.6 0.1 collective-permute-start.11
  46.7 6.8 %collective-permute-start.3 = (f32[1,128]{1,0:T(1,128)S(1)}, f32[1,128]{1,0:T(1,128)S(1)}, u32[]{:S(2)}, u32[]{:S(2)}) collective-permute-start(f32[1,128]{1,0:T(1,128)S(1)} %fusion), channel_id=1, source_target_pairs={{0,1},{1,0},{2,3},{3,2},{4,5},{5,4},{6,7},{7,6},{8,9},{9,8},{10,11... | collective-permute-start | bytes 1544 | tf_op jit(solution)/shard_map/ppermute | solution.py:317
  53.5 0.8 collective-permute-done.3
  54.3 4.7 %collective-permute-start.4 = (f32[1,128]{1,0:T(1,128)S(1)}, f32[1,128]{1,0:T(1,128)S(1)}, u32[]{:S(2)}, u32[]{:S(2)}) collective-permute-start(f32[1,128]{1,0:T(1,128)S(1)} %add.49.refs_0_), channel_id=1, source_target_pairs={{0,2},{1,3},{2,0},{3,1},{4,6},{5,7},{6,4},{7,5},{8,10},{9,11},{10,... | collective-permute-start | bytes 1544 | tf_op jit(solution)/shard_map/ppermute | solution.py:317
  59.0 0.0 collective-permute-done.7.level_ref.refs_5_
  59.0 2.1 %collective-permute-start.12 = (bf16[8,128,128]{2,1,0:T(8,128)(2,1)}, bf16[8,128,128]{2,1,0:T(8,128)(2,1)S(1)}, u32[]{:S(2)}, u32[]{:S(2)}) collective-permute-start(bf16[8,128,128]{2,1,0:T(8,128)(2,1)} %get-tuple-element.31), channel_id=1, source_target_pairs={{0,8},{1,9},{2,10},{3,11},{4,12},{5,13},{6,14},{7,15},{8,0},{9,1},... | collective-permute-start | bytes 786440 | tf_op jit(solution)/shard_map/ppermute | solution.py:317
  61.1 3.1 %shard_map.57 = (bf16[8,128,128]{2,1,0:T(8,128)(2,1)}, bf16[8,128,128]{2,1,0:T(8,128)(2,1)}, bf16[8,128,128]{2,1,0:T(8,128)(2,1)}, bf16[8,128,128]{2,1,0:T(8,128)(2,1)}) custom-call(s32[1]{0:T(128)} %bitcast.place_ref, f32[5,1,128]{2,1,0:T(1,128)S(1)} %collective-permute-done.refs_0_, f32[5,1,128]{2,1,0:T(1,128)S(1)} %collective-permute-done.1.refs_1_, ...), custom_call_target="tpu_custom_call" | custom-call | tf_op jit(solution)/shard_map/pallas_call | solution.py:344
  64.2 0.0 collective-permute-done.4.refs_1_
  64.2 0.0 copy-done.5
  64.2 2.2 %collective-permute-start.13 = (bf16[8,128,128]{2,1,0:T(8,128)(2,1)S(1)}, bf16[8,128,128]{2,1,0:T(8,128)(2,1)S(1)}, u32[]{:S(2)}, u32[]{:S(2)}) collective-permute-start(bf16[8,128,128]{2,1,0:T(8,128)(2,1)S(1)} %copy-done.5), channel_id=1, source_target_pairs={{0,12},{1,13},{2,14},{3,15},{4,8},{5,9},{6,10},{7,11},{8,4},{9,5},... | collective-permute-start | bytes 786440 | tf_op jit(solution)/shard_map/ppermute | solution.py:317
  66.5 0.0 collective-permute-done.11.refs_1_
  66.5 0.0 collective-permute-start.14
  66.5 0.0 collective-permute-done.10.across_ref
  66.5 2.2 %collective-permute-start.15 = (bf16[8,128,128]{2,1,0:T(8,128)(2,1)}, bf16[8,128,128]{2,1,0:T(8,128)(2,1)S(1)}, u32[]{:S(2)}, u32[]{:S(2)}) collective-permute-start(bf16[8,128,128]{2,1,0:T(8,128)(2,1)} %get-tuple-element.35), channel_id=1, source_target_pairs={{0,8},{1,9},{2,10},{3,11},{4,12},{5,13},{6,14},{7,15},{8,0},{9,1},... | collective-permute-start | bytes 786440 | tf_op jit(solution)/shard_map/ppermute | solution.py:317
  68.7 0.0 collective-permute-done.8.beyond_ref
  68.7 2.2 %collective-permute-start.16 = (bf16[8,128,128]{2,1,0:T(8,128)(2,1)}, bf16[8,128,128]{2,1,0:T(8,128)(2,1)S(1)}, u32[]{:S(2)}, u32[]{:S(2)}) collective-permute-start(bf16[8,128,128]{2,1,0:T(8,128)(2,1)} %get-tuple-element.36), channel_id=1, source_target_pairs={{0,12},{1,13},{2,14},{3,15},{4,8},{5,9},{6,10},{7,11},{8,4},{9,5},... | collective-permute-start | bytes 786440 | tf_op jit(solution)/shard_map/ppermute | solution.py:317
  70.9 0.0 copy-done.2
  70.9 0.0 copy-done.3
  70.9 3.2 %prep.1 = (bf16[256,128]{1,0:T(8,128)(2,1)S(1)}, f32[8,128]{1,0:T(8,128)S(1)}, s32[64]{0:T(128)S(1)}) custom-call(s32[1]{0:T(128)} %bitcast.place_ref, s32[6,32]{1,0:T(8,128)S(1)} %bitcast.10, s32[128,128]{1,0:T(8,128)S(1)} %copy-done.2, f32[1,128]{1,0:T(1,128)S(1)} %add.49.refs_0_, f32[1,128]{1,0:T(1,128)S(1)} %collective-permute-done.4.refs_1_), custom_call_target="tpu_custom_call" | custom-call | tf_op jit(solution)/shard_map/prep/pallas_call | solution.py:375
  74.1 1.3 %shard_map.55.refs_0_ = bf16[8,128,128]{2,1,0:T(8,128)(2,1)} custom-call(s32[1]{0:T(128)} %bitcast.place_ref, f32[5,1,128]{2,1,0:T(1,128)S(1)} %get-tuple-element.22.refs_0_.refs_3_, bf16[32,128,128]{2,1,0:T(8,128)(2,1)S(1)} %bitcast.8, bf16[32,128,128]{2,1,0:T(8,128)(2,1)S(1)} %collective-permute-done.5.chip_ref.refs_2_.refs_4_), custom_call_target="tpu_custom_call" | custom-call | tf_op jit(solution)/shard_map/pallas_call | solution.py:344
  75.5 6.2 %near.1.part_ref = f32[4096,128]{1,0:T(8,128)} custom-call(s32[1]{0:T(128)} %bitcast.place_ref, s32[6,32]{1,0:T(8,128)S(1)} %bitcast.11, bf16[32,128,128]{2,1,0:T(8,128)(2,1)} %bitcast.16, bf16[32,128,128]{2,1,0:T(8,128)(2,1)S(1)} %collective-permute-done.5.chip_ref.refs_2_.refs_4_, bf16[32,128,128]{2,1,0:T(8,128)(2,1)S(1)} %collective-permute-done.7.level_ref.refs_5_, ...), custom_call_target="tpu_custom_call" | custom-call | flops 805306368 | bytes 16777216 | tf_op jit(solution)/shard_map/near/pallas_call | solution.py:390
  81.7 0.0 collective-permute-done.12.refs_2_
  81.7 0.0 collective-permute-done.13.refs_3_
  81.7 2.3 %collective-permute-done.14.refs_5_ = bf16[8,128,128]{2,1,0:T(8,128)(2,1)S(1)} collective-permute-done((bf16[8,128,128]{2,1,0:T(8,128)(2,1)}, bf16[8,128,128]{2,1,0:T(8,128)(2,1)S(1)}, u32[]{:S(2)}, u32[]{:S(2)}) %collective-permute-start.14) | collective-permute-done | bytes 262176 | tf_op jit(solution)/shard_map/ppermute | solution.py:317
  84.0 19.1 %collective-permute-done.15.refs_6_ = bf16[8,128,128]{2,1,0:T(8,128)(2,1)S(1)} collective-permute-done((bf16[8,128,128]{2,1,0:T(8,128)(2,1)}, bf16[8,128,128]{2,1,0:T(8,128)(2,1)S(1)}, u32[]{:S(2)}, u32[]{:S(2)}) %collective-permute-start.15) | collective-permute-done | bytes 262176 | tf_op jit(solution)/shard_map/ppermute | solution.py:317
  103.1 0.0 collective-permute-done.16.refs_7_
  103.1 0.0 copy-start.4
  103.1 3.9 %far.1 = (f32[4096,128]{1,0:T(8,128)S(1)}, f32[16,1,128]{2,1,0:T(1,128)S(1)}) custom-call(s32[64]{0:T(128)S(1)} %get-tuple-element.26.where_ref, bf16[32,6,128,128]{3,2,1,0:T(8,128)(2,1)} %tiles_ref.3, f32[4096,128]{1,0:T(8,128)} %near.1.part_ref, bf16[256,128]{1,0:T(8,128)(2,1)S(1)} %get-tuple-element.27.graph2_ref, bf16[8,128,128]{2,1,0:T(8,128)(2,1)S(1)} %copy-done, ...), custom_call_target="tpu_custom_call" | custom-call | flops 536870912 | bytes 8388608 | tf_op jit(solution)/shard_map/far/pallas_call | solution.py:412
  106.9 13.3 %all_to_all.5.mass_ref = f32[16,1,128]{2,1,0:T(1,128)S(1)} all-to-all(f32[16,1,128]{2,1,0:T(1,128)S(1)} %get-tuple-element.38), channel_id=1, replica_groups=mesh['groups'=2,'rows'=8,'sub'=2] {'rows','sub'}, dimensions={0} | all-to-all | bytes 16384 | tf_op jit(solution)/shard_map/all_to_all | solution.py:431
  120.2 1.6 %last.1 = f32[4096,128]{1,0:T(8,128)} custom-call(f32[4096,128]{1,0:T(8,128)S(1)} %get-tuple-element.37.logits_ref, f32[16,1,128]{2,1,0:T(1,128)S(1)} %all_to_all.5.mass_ref, f32[1,128]{1,0:T(1,128)S(1)} %bitcast.12), custom_call_target="tpu_custom_call" | custom-call | tf_op jit(solution)/shard_map/last/pallas_call | solution.py:433
  (9 shorter events, 0.0 us)
Async XLA Ops:
  0.0 26.4 %collective-permute-start.6 = (bf16[32,128,128]{2,1,0:T(8,128)(2,1)}, bf16[32,128,128]{2,1,0:T(8,128)(2,1)}, u32[]{:S(2)}, u32[]{:S(2)}) collective-permute-start(bf16[32,128,128]{2,1,0:T(8,128)(2,1)} %bitcast.13), channel_id=1, source_target_pairs={{0,2},{1,3},{2,0},{3,1},{4,6},{5,7},{6,4},{7,5},{8,10},{9,11},{10,... | collective-permute-start | bytes 3145736 | tf_op jit(solution)/shard_map/ppermute | solution.py:317
  3.0 23.5 %collective-permute-start.9 = (bf16[32,128,128]{2,1,0:T(8,128)(2,1)}, bf16[32,128,128]{2,1,0:T(8,128)(2,1)}, u32[]{:S(2)}, u32[]{:S(2)}) collective-permute-start(bf16[32,128,128]{2,1,0:T(8,128)(2,1)} %bitcast.14), channel_id=1, source_target_pairs={{7,10},{8,5},{23,26},{24,21}} | collective-permute-start | bytes 3145736 | tf_op jit(solution)/shard_map/ppermute | solution.py:322
  4.6 40.4 %collective-permute-start.5 = (bf16[32,128,128]{2,1,0:T(8,128)(2,1)}, bf16[32,128,128]{2,1,0:T(8,128)(2,1)S(1)}, u32[]{:S(2)}, u32[]{:S(2)}) collective-permute-start(bf16[32,128,128]{2,1,0:T(8,128)(2,1)} %bitcast.15), channel_id=1, source_target_pairs={{0,1},{1,0},{2,3},{3,2},{4,5},{5,4},{6,7},{7,6},{8,9},{9,8},{10,11... | collective-permute-start | bytes 3145736 | tf_op jit(solution)/shard_map/ppermute | solution.py:317
  26.4 32.6 %collective-permute-start.7 = (bf16[32,128,128]{2,1,0:T(8,128)(2,1)}, bf16[32,128,128]{2,1,0:T(8,128)(2,1)S(1)}, u32[]{:S(2)}, u32[]{:S(2)}) collective-permute-start(bf16[32,128,128]{2,1,0:T(8,128)(2,1)} %collective-permute-done.6.refs_4_), channel_id=1, source_target_pairs={{0,1},{1,0},{2,3},{3,2},{4,5},{5,4},{6,7},{7,6},{8,9},{9,8},{10,11... | collective-permute-start | bytes 3145736 | tf_op jit(solution)/shard_map/ppermute | solution.py:317
  26.4 40.0 %collective-permute-start.10 = (bf16[32,128,128]{2,1,0:T(8,128)(2,1)}, bf16[32,128,128]{2,1,0:T(8,128)(2,1)S(1)}, u32[]{:S(2)}, u32[]{:S(2)}) collective-permute-start(bf16[32,128,128]{2,1,0:T(8,128)(2,1)} %collective-permute-done.9), channel_id=1, source_target_pairs={{10,8},{5,7},{26,24},{21,23}} | collective-permute-start | bytes 3145736 | tf_op jit(solution)/shard_map/ppermute | solution.py:362
  27.2 41.5 %collective-permute-start.8 = (bf16[32,128,128]{2,1,0:T(8,128)(2,1)}, bf16[32,128,128]{2,1,0:T(8,128)(2,1)}, u32[]{:S(2)}, u32[]{:S(2)}) collective-permute-start(bf16[32,128,128]{2,1,0:T(8,128)(2,1)} %collective-permute-done.6.refs_4_), channel_id=1, source_target_pairs={{1,4},{9,12},{6,3},{14,11},{17,20},{25,28},{22,19},{30,27}} | collective-permute-start | bytes 3145736 | tf_op jit(solution)/shard_map/ppermute | solution.py:361
  31.0 3.7 %collective-permute-start = (f32[5,1,128]{2,1,0:T(1,128)S(1)}, f32[5,1,128]{2,1,0:T(1,128)S(1)}, u32[]{:S(2)}, u32[]{:S(2)}) collective-permute-start(f32[5,1,128]{2,1,0:T(1,128)S(1)} %get-tuple-element.23), channel_id=1, source_target_pairs={{0,4},{1,5},{2,6},{3,7},{4,0},{5,1},{6,2},{7,3},{8,12},{9,13},{10,... | collective-permute-start | bytes 7688 | tf_op jit(solution)/shard_map/ppermute | solution.py:317
  34.6 5.0 %collective-permute-start.1 = (f32[5,1,128]{2,1,0:T(1,128)S(1)}, f32[5,1,128]{2,1,0:T(1,128)S(1)}, u32[]{:S(2)}, u32[]{:S(2)}) collective-permute-start(f32[5,1,128]{2,1,0:T(1,128)S(1)} %get-tuple-element.24), channel_id=1, source_target_pairs={{0,8},{1,9},{2,10},{3,11},{4,12},{5,13},{6,14},{7,15},{8,0},{9,1},... | collective-permute-start | bytes 7688 | tf_op jit(solution)/shard_map/ppermute | solution.py:317
  39.6 5.4 %collective-permute-start.2 = (f32[5,1,128]{2,1,0:T(1,128)S(1)}, f32[5,1,128]{2,1,0:T(1,128)S(1)}, u32[]{:S(2)}, u32[]{:S(2)}) collective-permute-start(f32[5,1,128]{2,1,0:T(1,128)S(1)} %get-tuple-element.25), channel_id=1, source_target_pairs={{0,12},{1,13},{2,14},{3,15},{4,8},{5,9},{6,10},{7,11},{8,4},{9,5},... | collective-permute-start | bytes 7688 | tf_op jit(solution)/shard_map/ppermute | solution.py:317
  45.0 25.9 %copy-start.2 = (s32[128,128]{1,0:T(8,128)S(1)}, s32[128,128]{1,0:T(8,128)}, u32[]{:S(2)}) copy-start(s32[128,128]{1,0:T(8,128)} %graph_ref.1) | copy-start | bytes 196612
  45.0 25.9 %copy-start.3 = (s32[32,6]{0,1:T(8,128)S(1)}, s32[32,6]{0,1:T(8,128)}, u32[]{:S(2)}) copy-start(s32[32,6]{0,1:T(8,128)} %param.7) | copy-start | bytes 2308
  46.6 17.6 %copy-start.5 = (bf16[8,128,128]{2,1,0:T(8,128)(2,1)S(1)}, bf16[8,128,128]{2,1,0:T(8,128)(2,1)}, u32[]{:S(2)}) copy-start(bf16[8,128,128]{2,1,0:T(8,128)(2,1)} %get-tuple-element.32) | copy-start | bytes 786436
  46.6 19.8 %collective-permute-start.11 = (bf16[8,128,128]{2,1,0:T(8,128)(2,1)}, bf16[8,128,128]{2,1,0:T(8,128)(2,1)S(1)}, u32[]{:S(2)}, u32[]{:S(2)}) collective-permute-start(bf16[8,128,128]{2,1,0:T(8,128)(2,1)} %get-tuple-element.30), channel_id=1, source_target_pairs={{0,4},{1,5},{2,6},{3,7},{4,0},{5,1},{6,2},{7,3},{8,12},{9,13},{10,... | collective-permute-start | bytes 786440 | tf_op jit(solution)/shard_map/ppermute | solution.py:317
  46.7 7.6 %collective-permute-start.3 = (f32[1,128]{1,0:T(1,128)S(1)}, f32[1,128]{1,0:T(1,128)S(1)}, u32[]{:S(2)}, u32[]{:S(2)}) collective-permute-start(f32[1,128]{1,0:T(1,128)S(1)} %fusion), channel_id=1, source_target_pairs={{0,1},{1,0},{2,3},{3,2},{4,5},{5,4},{6,7},{7,6},{8,9},{9,8},{10,11... | collective-permute-start | bytes 1544 | tf_op jit(solution)/shard_map/ppermute | solution.py:317
  54.3 9.9 %collective-permute-start.4 = (f32[1,128]{1,0:T(1,128)S(1)}, f32[1,128]{1,0:T(1,128)S(1)}, u32[]{:S(2)}, u32[]{:S(2)}) collective-permute-start(f32[1,128]{1,0:T(1,128)S(1)} %add.49.refs_0_), channel_id=1, source_target_pairs={{0,2},{1,3},{2,0},{3,1},{4,6},{5,7},{6,4},{7,5},{8,10},{9,11},{10,... | collective-permute-start | bytes 1544 | tf_op jit(solution)/shard_map/ppermute | solution.py:317
  59.0 22.7 %collective-permute-start.12 = (bf16[8,128,128]{2,1,0:T(8,128)(2,1)}, bf16[8,128,128]{2,1,0:T(8,128)(2,1)S(1)}, u32[]{:S(2)}, u32[]{:S(2)}) collective-permute-start(bf16[8,128,128]{2,1,0:T(8,128)(2,1)} %get-tuple-element.31), channel_id=1, source_target_pairs={{0,8},{1,9},{2,10},{3,11},{4,12},{5,13},{6,14},{7,15},{8,0},{9,1},... | collective-permute-start | bytes 786440 | tf_op jit(solution)/shard_map/ppermute | solution.py:317
  64.2 17.4 %collective-permute-start.13 = (bf16[8,128,128]{2,1,0:T(8,128)(2,1)S(1)}, bf16[8,128,128]{2,1,0:T(8,128)(2,1)S(1)}, u32[]{:S(2)}, u32[]{:S(2)}) collective-permute-start(bf16[8,128,128]{2,1,0:T(8,128)(2,1)S(1)} %copy-done.5), channel_id=1, source_target_pairs={{0,12},{1,13},{2,14},{3,15},{4,8},{5,9},{6,10},{7,11},{8,4},{9,5},... | collective-permute-start | bytes 786440 | tf_op jit(solution)/shard_map/ppermute | solution.py:317
  66.5 17.5 %collective-permute-start.14 = (bf16[8,128,128]{2,1,0:T(8,128)(2,1)}, bf16[8,128,128]{2,1,0:T(8,128)(2,1)S(1)}, u32[]{:S(2)}, u32[]{:S(2)}) collective-permute-start(bf16[8,128,128]{2,1,0:T(8,128)(2,1)} %get-tuple-element.34), channel_id=1, source_target_pairs={{0,4},{1,5},{2,6},{3,7},{4,0},{5,1},{6,2},{7,3},{8,12},{9,13},{10,... | collective-permute-start | bytes 786440 | tf_op jit(solution)/shard_map/ppermute | solution.py:317
  66.5 36.6 %collective-permute-start.15 = (bf16[8,128,128]{2,1,0:T(8,128)(2,1)}, bf16[8,128,128]{2,1,0:T(8,128)(2,1)S(1)}, u32[]{:S(2)}, u32[]{:S(2)}) collective-permute-start(bf16[8,128,128]{2,1,0:T(8,128)(2,1)} %get-tuple-element.35), channel_id=1, source_target_pairs={{0,8},{1,9},{2,10},{3,11},{4,12},{5,13},{6,14},{7,15},{8,0},{9,1},... | collective-permute-start | bytes 786440 | tf_op jit(solution)/shard_map/ppermute | solution.py:317
  68.7 34.4 %collective-permute-start.16 = (bf16[8,128,128]{2,1,0:T(8,128)(2,1)}, bf16[8,128,128]{2,1,0:T(8,128)(2,1)S(1)}, u32[]{:S(2)}, u32[]{:S(2)}) collective-permute-start(bf16[8,128,128]{2,1,0:T(8,128)(2,1)} %get-tuple-element.36), channel_id=1, source_target_pairs={{0,12},{1,13},{2,14},{3,15},{4,8},{5,9},{6,10},{7,11},{8,4},{9,5},... | collective-permute-start | bytes 786440 | tf_op jit(solution)/shard_map/ppermute | solution.py:317
  75.4 27.6 %copy-start = (bf16[8,128,128]{2,1,0:T(8,128)(2,1)S(1)}, bf16[8,128,128]{2,1,0:T(8,128)(2,1)}, u32[]{:S(2)}) copy-start(bf16[8,128,128]{2,1,0:T(8,128)(2,1)} %shard_map.55.refs_0_) | copy-start | bytes 786436
  75.5 27.6 %copy-start.1 = (bf16[8,128,128]{2,1,0:T(8,128)(2,1)S(1)}, bf16[8,128,128]{2,1,0:T(8,128)(2,1)}, u32[]{:S(2)}) copy-start(bf16[8,128,128]{2,1,0:T(8,128)(2,1)} %get-tuple-element.33.refs_4_) | copy-start | bytes 786436
  103.1 17.2 %copy-start.4 = (f32[128]{0:T(128)S(1)}, f32[128]{0:T(128)}, u32[]{:S(2)}) copy-start(f32[128]{0:T(128)} %param.9) | copy-start | bytes 1540

commit v7 on v6

--- a/solution.py
+++ b/solution.py
@@ -153,8 +153,7 @@
 
 
 def near_kernel(
-    group, chunk, shards, place_ref, cols_ref, own_ref, chip_ref, level_ref, beyond_ref, across_ref, tiles_ref,
-    graph2_ref, pull_ref, part_ref, window, tiles, part, own_sem, sems, tile_sems, part_sems,
+    group, chunk, place_ref, cols_ref, own_ref, chip_ref, level_ref, edge_ref, tiles_ref, graph2_ref, pull_ref, part_ref, window, tiles, part, own_sem, sems, tile_sems, part_sems,
 ):
     blocks_dev, tile, clusters = own_ref.shape
     steps = blocks_dev // group
@@ -166,11 +165,8 @@
 
     take(own_ref, 1, own_sem).start()
     even = spot % 2 == 0
-    middle = shards // 2
-    split_here = (place == middle) | (place == middle - 1)
-    edge = ((spot == 0) | (spot == LEVEL - 1)) & jnp.logical_not(split_here)
-    inside = (spot != 0) & (spot != LEVEL - 1)
-    for flag, src in ((split_here, across_ref), (edge, beyond_ref), (inside, level_ref)):
+    edge = (spot == 0) | (spot == LEVEL - 1)
+    for flag, src in ((edge, edge_ref), (jnp.logical_not(edge), level_ref)):
         for is_even, chip_at, other_at in ((True, 2, 0), (False, 0, 2)):
 
             @pl.when(flag & (even == is_even))
@@ -316,10 +312,8 @@
     def swap(x, bits):
         return lax.ppermute(x, NODES, [(i, i ^ bits) for i in range(shards)])
 
-    middle = shards // 2
     over = swap(blocks, 2)
     chip = swap(blocks, 1)
-    across = lax.ppermute(blocks, NODES, [(middle - 1, middle + 2), (middle, middle - 3)])
 
     *asked, mine, held = pl.pallas_call(
         functools.partial(requests_kernel, nodes_total),
@@ -339,6 +333,8 @@
         name="requests",
     )(place, in_hbm(cols), in_hbm(coupling))
     heard = [swap(x, dz * LEVEL) for dz, x in zip(others, asked)]
+    edges = [z * LEVEL for z in range(1, levels)]
+    edge = lax.ppermute(blocks, NODES, [(i - 1, i + 2) for i in edges] + [(i, i - 3) for i in edges])
 
     def gather(stage, heard, sources):
         return pl.pallas_call(
@@ -357,9 +353,7 @@
     found = gather(0, heard, (held.reshape(blocks.shape), chip))
     fetched = [swap(x, dz * LEVEL) for dz, x in zip(others, found)]
     over_chip = swap(over, 1)
-    edges = [z * LEVEL for z in range(1, levels) if z * LEVEL != middle]
-    beyond = lax.ppermute(over, NODES, [(i - LEVEL + 1, i) for i in edges] + [(i + LEVEL - 2, i - 1) for i in edges])
-    across = lax.ppermute(across, NODES, [(middle + 2, middle), (middle - 3, middle - 1)])
+    edge = lax.ppermute(edge, NODES, [(i + 2, i) for i in edges] + [(i - 3, i - 1) for i in edges])
     found = gather(1, (*heard, mine), (over, over_chip))
     there = [swap(x, dz * LEVEL) for dz, x in zip(others, found)]
     home_late = found[-1]
@@ -388,9 +382,9 @@
 
     chunk = min(16, blocks_dev)
     part = pl.pallas_call(
-        functools.partial(near_kernel, group, group, shards),
+        functools.partial(near_kernel, group, group),
         out_shape=pltpu.HBM((rows, clusters), f32),
-        in_specs=[SMEM, SMEM, ANY, ANY, ANY, ANY, ANY, ANY, VMEM, VMEM],
+        in_specs=[SMEM, SMEM, ANY, ANY, ANY, ANY, ANY, VMEM, VMEM],
         out_specs=ANY,
         scratch_shapes=[
             pltpu.VMEM((3 * blocks_dev, tile, clusters), bf16),
@@ -406,7 +400,7 @@
             flops=flops * (NEAR * tile + 2 * clusters), bytes_accessed=16 << 20, transcendentals=rows * clusters
         ),
         name="near",
-    )(place, cols, in_hbm(blocks), chip, over_chip, beyond, across, in_hbm(tile_vals), on_chip(graph2), on_chip(pull))
+    )(place, cols, in_hbm(blocks), chip, over_chip, edge, in_hbm(tile_vals), on_chip(graph2), on_chip(pull))
 
     parts = [home, *fetched, home_late, *there]
     logits, mass_parts = pl.pallas_call(

time: 122 us -> 110 us (0.902)
  starting transfers between devices: 35.4 us -> 26.3 us
  waiting for transfers between devices: 49.9 us -> 48 us
    ppermute x14, starting transfers between devices: 31.4 us -> 23 us  [swap(): return lax.ppermute(x, NODES, [(i, i ^ bits) for i in range(shards)])]
    ppermute x14, waiting for transfers between devices: 49.9 us -> 48 us  [swap(): return lax.ppermute(x, NODES, [(i, i ^ bits) for i in range(shards)])]
    pallas_call x3, Pallas kernels: 6.03 us -> 4.79 us  [gather(): pl.pallas_call(functools.partial(gather_kernel, cap, stage), out_shape=[p...]
    ppermute x3 -> x2, starting transfers between devices: 3.99 us -> 3.29 us  [the longest x1 1.66 us: local(): lax.ppermute(edge, NODES, [(i + 2, i) for i in edges] + [(i - 3, i - 1) f...]
  transfers between devices with their start and end apart: 17 -> 16, of which waited for: 7 -> 6; matrix products, arithmetic and copies ran while one was open for 0% -> 0% of each run, Pallas kernels for 14% -> 15%
where the time goes in v7:
time: 110 us
  waiting for transfers between devices  48 us (44%)
  starting transfers between devices  26.3 us (24%)
  Pallas kernels  21.8 us (20%)
  blocking collectives  13.8 us (13%)
    ppermute x14, waiting for transfers between devices, swap(): return lax.ppermute(x, NODES, [(i, i ^ bits) for i in range(shards)])  48 us
    ppermute x14, starting transfers between devices, swap(): return lax.ppermute(x, NODES, [(i, i ^ bits) for i in range(shards)])  23 us
    all_to_all x1, blocking collectives, local(): lax.all_to_all(mass_parts, NODES, split_axis=0, concat_axis=0, tiled=True)  13.8 us
    pallas_call x1, Pallas kernels, local(): pl.pallas_call(functools.partial(near_kernel, group, group), out_shape=pl...  6.19 us
    pallas_call x3, Pallas kernels, gather(): pl.pallas_call(functools.partial(gather_kernel, cap, stage), out_shape=[p...  4.79 us
    pallas_call x1, Pallas kernels, local(): pl.pallas_call(functools.partial(far_kernel, group, chunk, nodes_total),...  3.85 us
    pallas_call x1, Pallas kernels, local(): pl.pallas_call(functools.partial(prep_kernel, cap, shards), out_shape=(pl...  3.22 us
  transfers between devices with their start and end apart: 16, of which 6 were waited for; matrix products, arithmetic and copies ran while one was open for 0% of the time, Pallas kernels for 15%

profile of v7, /device:TPU:0, one launch (start us, length us, event | category | flops | bytes accessed | tf_op | source)
XLA Modules:
  0.0 110.0 jit_solution(16665980022537726663)
XLA Ops:
  0.0 3.0 %collective-permute-start.6 = (bf16[32,128,128]{2,1,0:T(8,128)(2,1)}, bf16[32,128,128]{2,1,0:T(8,128)(2,1)S(1)}, u32[]{:S(2)}, u32[]{:S(2)}) collective-permute-start(bf16[32,128,128]{2,1,0:T(8,128)(2,1)} %bitcast.13), channel_id=1, source_target_pairs={{0,2},{1,3},{2,0},{3,1},{4,6},{5,7},{6,4},{7,5},{8,10},{9,11},{10,... | collective-permute-start | bytes 3145736 | tf_op jit(solution)/shard_map/ppermute | solution.py:313
  3.0 1.6 %collective-permute-start.8 = (bf16[32,128,128]{2,1,0:T(8,128)(2,1)}, bf16[32,128,128]{2,1,0:T(8,128)(2,1)}, u32[]{:S(2)}, u32[]{:S(2)}) collective-permute-start(bf16[32,128,128]{2,1,0:T(8,128)(2,1)} %bitcast.14), channel_id=1, source_target_pairs={{3,6},{7,10},{11,14},{4,1},{8,5},{12,9},{19,22},{23,26},{27,30},{2... | collective-permute-start | bytes 3145736 | tf_op jit(solution)/shard_map/ppermute | solution.py:337
  4.6 0.0 collective-permute-start.5
  4.6 21.7 %collective-permute-done.6.refs_4_ = bf16[32,128,128]{2,1,0:T(8,128)(2,1)S(1)} collective-permute-done((bf16[32,128,128]{2,1,0:T(8,128)(2,1)}, bf16[32,128,128]{2,1,0:T(8,128)(2,1)S(1)}, u32[]{:S(2)}, u32[]{:S(2)}) %collective-permute-start.6) | collective-permute-done | bytes 1048608 | tf_op jit(solution)/shard_map/ppermute | solution.py:313
  26.3 0.0 collective-permute-start.7
  26.3 0.0 collective-permute-done.8
  26.3 1.7 %collective-permute-start.9 = (bf16[32,128,128]{2,1,0:T(8,128)(2,1)}, bf16[32,128,128]{2,1,0:T(8,128)(2,1)}, u32[]{:S(2)}, u32[]{:S(2)}) collective-permute-start(bf16[32,128,128]{2,1,0:T(8,128)(2,1)} %collective-permute-done.8), channel_id=1, source_target_pairs={{6,4},{10,8},{14,12},{1,3},{5,7},{9,11},{22,20},{26,24},{30,28},{1... | collective-permute-start | bytes 3145736 | tf_op jit(solution)/shard_map/ppermute | solution.py:356
  28.0 2.2 %requests.1 = (f32[5,1,128]{2,1,0:T(1,128)S(1)}, f32[5,1,128]{2,1,0:T(1,128)S(1)}, f32[5,1,128]{2,1,0:T(1,128)S(1)}, f32[5,1,128]{2,1,0:T(1,128)S(1)}, bf16[4096,128]{1,0:T(8,128)(2,1)S(1)}) custom-call(s32[1]{0:T(128)} %bitcast.place_ref, s32[6,32]{1,0:T(8,128)} %bitcast.9, bf16[4096,128]{1,0:T(8,128)(2,1)} %coupling_ref.1), custom_call_target="tpu_custom_call" | custom-call | tf_op jit(solution)/shard_map/requests/pallas_call | solution.py:318
  30.2 1.5 %collective-permute-start = (f32[5,1,128]{2,1,0:T(1,128)S(1)}, f32[5,1,128]{2,1,0:T(1,128)S(1)}, u32[]{:S(2)}, u32[]{:S(2)}) collective-permute-start(f32[5,1,128]{2,1,0:T(1,128)S(1)} %get-tuple-element.23), channel_id=1, source_target_pairs={{0,4},{1,5},{2,6},{3,7},{4,0},{5,1},{6,2},{7,3},{8,12},{9,13},{10,... | collective-permute-start | bytes 7688 | tf_op jit(solution)/shard_map/ppermute | solution.py:313
  31.7 2.6 %collective-permute-start.1 = (f32[5,1,128]{2,1,0:T(1,128)S(1)}, f32[5,1,128]{2,1,0:T(1,128)S(1)}, u32[]{:S(2)}, u32[]{:S(2)}) collective-permute-start(f32[5,1,128]{2,1,0:T(1,128)S(1)} %get-tuple-element.24), channel_id=1, source_target_pairs={{0,8},{1,9},{2,10},{3,11},{4,12},{5,13},{6,14},{7,15},{8,0},{9,1},... | collective-permute-start | bytes 7688 | tf_op jit(solution)/shard_map/ppermute | solution.py:313
  34.3 0.0 collective-permute-done.refs_0_
  34.3 3.0 %collective-permute-start.2 = (f32[5,1,128]{2,1,0:T(1,128)S(1)}, f32[5,1,128]{2,1,0:T(1,128)S(1)}, u32[]{:S(2)}, u32[]{:S(2)}) collective-permute-start(f32[5,1,128]{2,1,0:T(1,128)S(1)} %get-tuple-element.25), channel_id=1, source_target_pairs={{0,12},{1,13},{2,14},{3,15},{4,8},{5,9},{6,10},{7,11},{8,4},{9,5},... | collective-permute-start | bytes 7688 | tf_op jit(solution)/shard_map/ppermute | solution.py:313
  37.3 0.0 collective-permute-done.1.refs_1_
  37.3 2.4 %collective-permute-done.2.refs_2_ = f32[5,1,128]{2,1,0:T(1,128)S(1)} collective-permute-done((f32[5,1,128]{2,1,0:T(1,128)S(1)}, f32[5,1,128]{2,1,0:T(1,128)S(1)}, u32[]{:S(2)}, u32[]{:S(2)}) %collective-permute-start.2) | collective-permute-done | bytes 2592 | tf_op jit(solution)/shard_map/ppermute | solution.py:313
  39.7 0.0 collective-permute-done.5.chip_ref.refs_2_.refs_4_
  39.7 1.6 %shard_map.56 = (bf16[8,128,128]{2,1,0:T(8,128)(2,1)}, bf16[8,128,128]{2,1,0:T(8,128)(2,1)}, bf16[8,128,128]{2,1,0:T(8,128)(2,1)}) custom-call(s32[1]{0:T(128)} %bitcast.place_ref, f32[5,1,128]{2,1,0:T(1,128)S(1)} %collective-permute-done.refs_0_, f32[5,1,128]{2,1,0:T(1,128)S(1)} %collective-permute-done.1.refs_1_, ...), custom_call_target="tpu_custom_call" | custom-call | tf_op jit(solution)/shard_map/pallas_call | solution.py:340
  41.3 0.1 collective-permute-start.10
  41.4 0.8 collective-permute-start.3
  42.2 0.8 collective-permute-done.3
  43.0 3.2 %collective-permute-start.4 = (f32[1,128]{1,0:T(1,128)S(1)}, f32[1,128]{1,0:T(1,128)S(1)}, u32[]{:S(2)}, u32[]{:S(2)}) collective-permute-start(f32[1,128]{1,0:T(1,128)S(1)} %add.49.refs_0_), channel_id=1, source_target_pairs={{0,2},{1,3},{2,0},{3,1},{4,6},{5,7},{6,4},{7,5},{8,10},{9,11},{10,... | collective-permute-start | bytes 1544 | tf_op jit(solution)/shard_map/ppermute | solution.py:313
  46.3 3.5 %collective-permute-start.11 = (bf16[8,128,128]{2,1,0:T(8,128)(2,1)}, bf16[8,128,128]{2,1,0:T(8,128)(2,1)S(1)}, u32[]{:S(2)}, u32[]{:S(2)}) collective-permute-start(bf16[8,128,128]{2,1,0:T(8,128)(2,1)} %get-tuple-element.31), channel_id=1, source_target_pairs={{0,8},{1,9},{2,10},{3,11},{4,12},{5,13},{6,14},{7,15},{8,0},{9,1},... | collective-permute-start | bytes 786440 | tf_op jit(solution)/shard_map/ppermute | solution.py:313
  49.8 0.0 collective-permute-done.7.level_ref.refs_5_
  49.8 0.8 collective-permute-start.12
  50.6 1.8 %shard_map.57 = (bf16[8,128,128]{2,1,0:T(8,128)(2,1)}, bf16[8,128,128]{2,1,0:T(8,128)(2,1)}, bf16[8,128,128]{2,1,0:T(8,128)(2,1)}, bf16[8,128,128]{2,1,0:T(8,128)(2,1)}) custom-call(s32[1]{0:T(128)} %bitcast.place_ref, f32[5,1,128]{2,1,0:T(1,128)S(1)} %collective-permute-done.refs_0_, f32[5,1,128]{2,1,0:T(1,128)S(1)} %collective-permute-done.1.refs_1_, ...), custom_call_target="tpu_custom_call" | custom-call | tf_op jit(solution)/shard_map/pallas_call | solution.py:340
  52.4 0.0 collective-permute-done.4.refs_1_
  52.4 0.1 collective-permute-start.13
  52.5 0.0 collective-permute-done.10.refs_1_
  52.5 3.6 %collective-permute-start.14 = (bf16[8,128,128]{2,1,0:T(8,128)(2,1)}, bf16[8,128,128]{2,1,0:T(8,128)(2,1)S(1)}, u32[]{:S(2)}, u32[]{:S(2)}) collective-permute-start(bf16[8,128,128]{2,1,0:T(8,128)(2,1)} %get-tuple-element.35), channel_id=1, source_target_pairs={{0,8},{1,9},{2,10},{3,11},{4,12},{5,13},{6,14},{7,15},{8,0},{9,1},... | collective-permute-start | bytes 786440 | tf_op jit(solution)/shard_map/ppermute | solution.py:313
  56.1 0.0 collective-permute-done.9.edge_ref
  56.1 0.8 collective-permute-start.15
  56.9 0.0 copy-done.2
  56.9 0.0 copy-done.3
  56.9 3.2 %prep.1 = (bf16[256,128]{1,0:T(8,128)(2,1)S(1)}, f32[8,128]{1,0:T(8,128)S(1)}, s32[64]{0:T(128)S(1)}) custom-call(s32[1]{0:T(128)} %bitcast.place_ref, s32[6,32]{1,0:T(8,128)S(1)} %bitcast.10, s32[128,128]{1,0:T(8,128)S(1)} %copy-done.2, f32[1,128]{1,0:T(1,128)S(1)} %add.49.refs_0_, f32[1,128]{1,0:T(1,128)S(1)} %collective-permute-done.4.refs_1_), custom_call_target="tpu_custom_call" | custom-call | tf_op jit(solution)/shard_map/prep/pallas_call | solution.py:369
  60.1 1.3 %shard_map.55.refs_0_ = bf16[8,128,128]{2,1,0:T(8,128)(2,1)} custom-call(s32[1]{0:T(128)} %bitcast.place_ref, f32[5,1,128]{2,1,0:T(1,128)S(1)} %get-tuple-element.22.refs_0_.refs_3_, bf16[32,128,128]{2,1,0:T(8,128)(2,1)S(1)} %bitcast.8, bf16[32,128,128]{2,1,0:T(8,128)(2,1)S(1)} %collective-permute-done.5.chip_ref.refs_2_.refs_4_), custom_call_target="tpu_custom_call" | custom-call | tf_op jit(solution)/shard_map/pallas_call | solution.py:340
  61.5 0.0 copy-start
  61.5 0.0 copy-start.1
  61.5 6.2 %near.1.part_ref = f32[4096,128]{1,0:T(8,128)} custom-call(s32[1]{0:T(128)} %bitcast.place_ref, s32[6,32]{1,0:T(8,128)S(1)} %bitcast.11, bf16[32,128,128]{2,1,0:T(8,128)(2,1)} %bitcast.16, bf16[32,128,128]{2,1,0:T(8,128)(2,1)S(1)} %collective-permute-done.5.chip_ref.refs_2_.refs_4_, bf16[32,128,128]{2,1,0:T(8,128)(2,1)S(1)} %collective-permute-done.7.level_ref.refs_5_, ...), custom_call_target="tpu_custom_call" | custom-call | flops 805306368 | bytes 16777216 | tf_op jit(solution)/shard_map/near/pallas_call | solution.py:384
  67.7 1.6 %collective-permute-done.11.refs_2_ = bf16[8,128,128]{2,1,0:T(8,128)(2,1)S(1)} collective-permute-done((bf16[8,128,128]{2,1,0:T(8,128)(2,1)}, bf16[8,128,128]{2,1,0:T(8,128)(2,1)S(1)}, u32[]{:S(2)}, u32[]{:S(2)}) %collective-permute-start.11) | collective-permute-done | bytes 262176 | tf_op jit(solution)/shard_map/ppermute | solution.py:313
  69.3 0.0 collective-permute-done.12.refs_3_
  69.3 1.5 %collective-permute-done.13.refs_5_ = bf16[8,128,128]{2,1,0:T(8,128)(2,1)S(1)} collective-permute-done((bf16[8,128,128]{2,1,0:T(8,128)(2,1)}, bf16[8,128,128]{2,1,0:T(8,128)(2,1)S(1)}, u32[]{:S(2)}, u32[]{:S(2)}) %collective-permute-start.13) | collective-permute-done | bytes 262176 | tf_op jit(solution)/shard_map/ppermute | solution.py:313
  70.8 19.9 %collective-permute-done.14.refs_6_ = bf16[8,128,128]{2,1,0:T(8,128)(2,1)S(1)} collective-permute-done((bf16[8,128,128]{2,1,0:T(8,128)(2,1)}, bf16[8,128,128]{2,1,0:T(8,128)(2,1)S(1)}, u32[]{:S(2)}, u32[]{:S(2)}) %collective-permute-start.14) | collective-permute-done | bytes 262176 | tf_op jit(solution)/shard_map/ppermute | solution.py:313
  90.8 0.0 collective-permute-done.15.refs_7_
  90.8 0.0 copy-done
  90.8 0.0 copy-done.1
  90.8 0.0 copy-start.4
  90.8 3.9 %far.1 = (f32[4096,128]{1,0:T(8,128)S(1)}, f32[16,1,128]{2,1,0:T(1,128)S(1)}) custom-call(s32[64]{0:T(128)S(1)} %get-tuple-element.26.where_ref, bf16[32,6,128,128]{3,2,1,0:T(8,128)(2,1)} %tiles_ref.3, f32[4096,128]{1,0:T(8,128)} %near.1.part_ref, bf16[256,128]{1,0:T(8,128)(2,1)S(1)} %get-tuple-element.27.graph2_ref, bf16[8,128,128]{2,1,0:T(8,128)(2,1)S(1)} %copy-done, ...), custom_call_target="tpu_custom_call" | custom-call | flops 536870912 | bytes 8388608 | tf_op jit(solution)/shard_map/far/pallas_call | solution.py:406
  94.6 13.8 %all_to_all.5.mass_ref = f32[16,1,128]{2,1,0:T(1,128)S(1)} all-to-all(f32[16,1,128]{2,1,0:T(1,128)S(1)} %get-tuple-element.38), channel_id=1, replica_groups=mesh['groups'=2,'rows'=8,'sub'=2] {'rows','sub'}, dimensions={0} | all-to-all | bytes 16384 | tf_op jit(solution)/shard_map/all_to_all | solution.py:425
  108.5 1.6 %last.1 = f32[4096,128]{1,0:T(8,128)} custom-call(f32[4096,128]{1,0:T(8,128)S(1)} %get-tuple-element.37.logits_ref, f32[16,1,128]{2,1,0:T(1,128)S(1)} %all_to_all.5.mass_ref, f32[1,128]{1,0:T(1,128)S(1)} %bitcast.12), custom_call_target="tpu_custom_call" | custom-call | tf_op jit(solution)/shard_map/last/pallas_call | solution.py:427
  (5 shorter events, 0.0 us)
Async XLA Ops:
  0.0 26.3 %collective-permute-start.6 = (bf16[32,128,128]{2,1,0:T(8,128)(2,1)}, bf16[32,128,128]{2,1,0:T(8,128)(2,1)S(1)}, u32[]{:S(2)}, u32[]{:S(2)}) collective-permute-start(bf16[32,128,128]{2,1,0:T(8,128)(2,1)} %bitcast.13), channel_id=1, source_target_pairs={{0,2},{1,3},{2,0},{3,1},{4,6},{5,7},{6,4},{7,5},{8,10},{9,11},{10,... | collective-permute-start | bytes 3145736 | tf_op jit(solution)/shard_map/ppermute | solution.py:313
  3.0 23.4 %collective-permute-start.8 = (bf16[32,128,128]{2,1,0:T(8,128)(2,1)}, bf16[32,128,128]{2,1,0:T(8,128)(2,1)}, u32[]{:S(2)}, u32[]{:S(2)}) collective-permute-start(bf16[32,128,128]{2,1,0:T(8,128)(2,1)} %bitcast.14), channel_id=1, source_target_pairs={{3,6},{7,10},{11,14},{4,1},{8,5},{12,9},{19,22},{23,26},{27,30},{2... | collective-permute-start | bytes 3145736 | tf_op jit(solution)/shard_map/ppermute | solution.py:337
  4.6 35.1 %collective-permute-start.5 = (bf16[32,128,128]{2,1,0:T(8,128)(2,1)}, bf16[32,128,128]{2,1,0:T(8,128)(2,1)S(1)}, u32[]{:S(2)}, u32[]{:S(2)}) collective-permute-start(bf16[32,128,128]{2,1,0:T(8,128)(2,1)} %bitcast.15), channel_id=1, source_target_pairs={{0,1},{1,0},{2,3},{3,2},{4,5},{5,4},{6,7},{7,6},{8,9},{9,8},{10,11... | collective-permute-start | bytes 3145736 | tf_op jit(solution)/shard_map/ppermute | solution.py:313
  26.3 23.5 %collective-permute-start.7 = (bf16[32,128,128]{2,1,0:T(8,128)(2,1)S(1)}, bf16[32,128,128]{2,1,0:T(8,128)(2,1)S(1)}, u32[]{:S(2)}, u32[]{:S(2)}) collective-permute-start(bf16[32,128,128]{2,1,0:T(8,128)(2,1)S(1)} %collective-permute-done.6.refs_4_), channel_id=1, source_target_pairs={{0,1},{1,0},{2,3},{3,2},{4,5},{5,4},{6,7},{7,6},{8,9},{9,8},{10,11... | collective-permute-start | bytes 3145736 | tf_op jit(solution)/shard_map/ppermute | solution.py:313
  26.3 29.8 %collective-permute-start.9 = (bf16[32,128,128]{2,1,0:T(8,128)(2,1)}, bf16[32,128,128]{2,1,0:T(8,128)(2,1)}, u32[]{:S(2)}, u32[]{:S(2)}) collective-permute-start(bf16[32,128,128]{2,1,0:T(8,128)(2,1)} %collective-permute-done.8), channel_id=1, source_target_pairs={{6,4},{10,8},{14,12},{1,3},{5,7},{9,11},{22,20},{26,24},{30,28},{1... | collective-permute-start | bytes 3145736 | tf_op jit(solution)/shard_map/ppermute | solution.py:356
  30.2 4.1 %collective-permute-start = (f32[5,1,128]{2,1,0:T(1,128)S(1)}, f32[5,1,128]{2,1,0:T(1,128)S(1)}, u32[]{:S(2)}, u32[]{:S(2)}) collective-permute-start(f32[5,1,128]{2,1,0:T(1,128)S(1)} %get-tuple-element.23), channel_id=1, source_target_pairs={{0,4},{1,5},{2,6},{3,7},{4,0},{5,1},{6,2},{7,3},{8,12},{9,13},{10,... | collective-permute-start | bytes 7688 | tf_op jit(solution)/shard_map/ppermute | solution.py:313
  31.7 5.6 %collective-permute-start.1 = (f32[5,1,128]{2,1,0:T(1,128)S(1)}, f32[5,1,128]{2,1,0:T(1,128)S(1)}, u32[]{:S(2)}, u32[]{:S(2)}) collective-permute-start(f32[5,1,128]{2,1,0:T(1,128)S(1)} %get-tuple-element.24), channel_id=1, source_target_pairs={{0,8},{1,9},{2,10},{3,11},{4,12},{5,13},{6,14},{7,15},{8,0},{9,1},... | collective-permute-start | bytes 7688 | tf_op jit(solution)/shard_map/ppermute | solution.py:313
  34.3 5.4 %collective-permute-start.2 = (f32[5,1,128]{2,1,0:T(1,128)S(1)}, f32[5,1,128]{2,1,0:T(1,128)S(1)}, u32[]{:S(2)}, u32[]{:S(2)}) collective-permute-start(f32[5,1,128]{2,1,0:T(1,128)S(1)} %get-tuple-element.25), channel_id=1, source_target_pairs={{0,12},{1,13},{2,14},{3,15},{4,8},{5,9},{6,10},{7,11},{8,4},{9,5},... | collective-permute-start | bytes 7688 | tf_op jit(solution)/shard_map/ppermute | solution.py:313
  39.7 17.2 %copy-start.2 = (s32[128,128]{1,0:T(8,128)S(1)}, s32[128,128]{1,0:T(8,128)}, u32[]{:S(2)}) copy-start(s32[128,128]{1,0:T(8,128)} %graph_ref.1) | copy-start | bytes 196612
  39.7 17.2 %copy-start.3 = (s32[32,6]{0,1:T(8,128)S(1)}, s32[32,6]{0,1:T(8,128)}, u32[]{:S(2)}) copy-start(s32[32,6]{0,1:T(8,128)} %param.7) | copy-start | bytes 2308
  41.3 11.2 %collective-permute-start.10 = (bf16[8,128,128]{2,1,0:T(8,128)(2,1)}, bf16[8,128,128]{2,1,0:T(8,128)(2,1)S(1)}, u32[]{:S(2)}, u32[]{:S(2)}) collective-permute-start(bf16[8,128,128]{2,1,0:T(8,128)(2,1)} %get-tuple-element.30), channel_id=1, source_target_pairs={{0,4},{1,5},{2,6},{3,7},{4,0},{5,1},{6,2},{7,3},{8,12},{9,13},{10,... | collective-permute-start | bytes 786440 | tf_op jit(solution)/shard_map/ppermute | solution.py:313
  41.4 1.6 %collective-permute-start.3 = (f32[1,128]{1,0:T(1,128)S(1)}, f32[1,128]{1,0:T(1,128)S(1)}, u32[]{:S(2)}, u32[]{:S(2)}) collective-permute-start(f32[1,128]{1,0:T(1,128)S(1)} %fusion), channel_id=1, source_target_pairs={{0,1},{1,0},{2,3},{3,2},{4,5},{5,4},{6,7},{7,6},{8,9},{9,8},{10,11... | collective-permute-start | bytes 1544 | tf_op jit(solution)/shard_map/ppermute | solution.py:313
  43.0 9.4 %collective-permute-start.4 = (f32[1,128]{1,0:T(1,128)S(1)}, f32[1,128]{1,0:T(1,128)S(1)}, u32[]{:S(2)}, u32[]{:S(2)}) collective-permute-start(f32[1,128]{1,0:T(1,128)S(1)} %add.49.refs_0_), channel_id=1, source_target_pairs={{0,2},{1,3},{2,0},{3,1},{4,6},{5,7},{6,4},{7,5},{8,10},{9,11},{10,... | collective-permute-start | bytes 1544 | tf_op jit(solution)/shard_map/ppermute | solution.py:313
  46.3 23.0 %collective-permute-start.11 = (bf16[8,128,128]{2,1,0:T(8,128)(2,1)}, bf16[8,128,128]{2,1,0:T(8,128)(2,1)S(1)}, u32[]{:S(2)}, u32[]{:S(2)}) collective-permute-start(bf16[8,128,128]{2,1,0:T(8,128)(2,1)} %get-tuple-element.31), channel_id=1, source_target_pairs={{0,8},{1,9},{2,10},{3,11},{4,12},{5,13},{6,14},{7,15},{8,0},{9,1},... | collective-permute-start | bytes 786440 | tf_op jit(solution)/shard_map/ppermute | solution.py:313
  49.8 19.5 %collective-permute-start.12 = (bf16[8,128,128]{2,1,0:T(8,128)(2,1)}, bf16[8,128,128]{2,1,0:T(8,128)(2,1)S(1)}, u32[]{:S(2)}, u32[]{:S(2)}) collective-permute-start(bf16[8,128,128]{2,1,0:T(8,128)(2,1)} %get-tuple-element.32), channel_id=1, source_target_pairs={{0,12},{1,13},{2,14},{3,15},{4,8},{5,9},{6,10},{7,11},{8,4},{9,5},... | collective-permute-start | bytes 786440 | tf_op jit(solution)/shard_map/ppermute | solution.py:313
  52.4 18.4 %collective-permute-start.13 = (bf16[8,128,128]{2,1,0:T(8,128)(2,1)}, bf16[8,128,128]{2,1,0:T(8,128)(2,1)S(1)}, u32[]{:S(2)}, u32[]{:S(2)}) collective-permute-start(bf16[8,128,128]{2,1,0:T(8,128)(2,1)} %get-tuple-element.34), channel_id=1, source_target_pairs={{0,4},{1,5},{2,6},{3,7},{4,0},{5,1},{6,2},{7,3},{8,12},{9,13},{10,... | collective-permute-start | bytes 786440 | tf_op jit(solution)/shard_map/ppermute | solution.py:313
  52.5 38.2 %collective-permute-start.14 = (bf16[8,128,128]{2,1,0:T(8,128)(2,1)}, bf16[8,128,128]{2,1,0:T(8,128)(2,1)S(1)}, u32[]{:S(2)}, u32[]{:S(2)}) collective-permute-start(bf16[8,128,128]{2,1,0:T(8,128)(2,1)} %get-tuple-element.35), channel_id=1, source_target_pairs={{0,8},{1,9},{2,10},{3,11},{4,12},{5,13},{6,14},{7,15},{8,0},{9,1},... | collective-permute-start | bytes 786440 | tf_op jit(solution)/shard_map/ppermute | solution.py:313
  56.1 34.7 %collective-permute-start.15 = (bf16[8,128,128]{2,1,0:T(8,128)(2,1)}, bf16[8,128,128]{2,1,0:T(8,128)(2,1)S(1)}, u32[]{:S(2)}, u32[]{:S(2)}) collective-permute-start(bf16[8,128,128]{2,1,0:T(8,128)(2,1)} %get-tuple-element.36), channel_id=1, source_target_pairs={{0,12},{1,13},{2,14},{3,15},{4,8},{5,9},{6,10},{7,11},{8,4},{9,5},... | collective-permute-start | bytes 786440 | tf_op jit(solution)/shard_map/ppermute | solution.py:313
  61.5 29.3 %copy-start = (bf16[8,128,128]{2,1,0:T(8,128)(2,1)S(1)}, bf16[8,128,128]{2,1,0:T(8,128)(2,1)}, u32[]{:S(2)}) copy-start(bf16[8,128,128]{2,1,0:T(8,128)(2,1)} %shard_map.55.refs_0_) | copy-start | bytes 786436
  61.5 29.3 %copy-start.1 = (bf16[8,128,128]{2,1,0:T(8,128)(2,1)S(1)}, bf16[8,128,128]{2,1,0:T(8,128)(2,1)}, u32[]{:S(2)}) copy-start(bf16[8,128,128]{2,1,0:T(8,128)(2,1)} %get-tuple-element.33.refs_4_) | copy-start | bytes 786436
  90.8 17.7 %copy-start.4 = (f32[128]{0:T(128)S(1)}, f32[128]{0:T(128)}, u32[]{:S(2)}) copy-start(f32[128]{0:T(128)} %param.9) | copy-start | bytes 1540

commit v8 on v7

--- a/solution.py
+++ b/solution.py
@@ -35,7 +35,7 @@
 
 
 def requests_kernel(nodes_total, place_ref, all_cols_ref, coupling_ref, *refs):
-    *out_refs, own_ref, rows, cols_ref, table_ref, cols_sem, sems = refs
+    *out_refs, own_ref, rows, half_ref, cols_ref, table_ref, cols_sem, half_sem, sems = refs
     slots, blocks_dev = cols_ref.shape
     cols_copy = pltpu.make_async_copy(all_cols_ref, cols_ref, cols_sem)
     cols_copy.start()
@@ -49,6 +49,8 @@
     ]
     for copy in copies:
         copy.start()
+    half_copy = pltpu.make_async_copy(coupling_ref.at[pl.ds(0, nodes // 2)], half_ref, half_sem)
+    half_copy.start()
 
     owner = lax.broadcasted_iota(i32, (shards, blocks_dev), 0)
     place = lax.broadcasted_iota(i32, (clusters, blocks_dev), 0).astype(f32)
@@ -87,6 +89,7 @@
     mass = jnp.sum(total, axis=0, keepdims=True) / nodes_total
     for ref in (own_ref, *out_refs):
         ref[LEVEL] = mass
+    half_copy.wait()
 
 
 def gather_kernel(cap, stage, place_ref, *refs):
@@ -153,7 +156,8 @@
 
 
 def near_kernel(
-    group, chunk, place_ref, cols_ref, own_ref, chip_ref, level_ref, edge_ref, tiles_ref, graph2_ref, pull_ref, part_ref, window, tiles, part, own_sem, sems, tile_sems, part_sems,
+    group, chunk, place_ref, cols_ref, own_ref, chip_ref, level_ref, edge_ref, beyond_ref, tiles_ref,
+    graph2_ref, pull_ref, part_ref, window, tiles, part, own_sem, sems, tile_sems, part_sems,
 ):
     blocks_dev, tile, clusters = own_ref.shape
     steps = blocks_dev // group
@@ -166,13 +170,23 @@
     take(own_ref, 1, own_sem).start()
     even = spot % 2 == 0
     edge = (spot == 0) | (spot == LEVEL - 1)
-    for flag, src in ((edge, edge_ref), (jnp.logical_not(edge), level_ref)):
-        for is_even, chip_at, other_at in ((True, 2, 0), (False, 0, 2)):
-
-            @pl.when(flag & (even == is_even))
-            def _():
-                take(chip_ref, chip_at, sems.at[0]).start()
-                take(src, other_at, sems.at[1]).start()
+    half = blocks_dev // 2
+    for is_even, chip_at, other_at in ((True, 2, 0), (False, 0, 2)):
+
+        @pl.when(even == is_even)
+        def _():
+            take(chip_ref, chip_at, sems.at[0]).start()
+
+        @pl.when((even == is_even) & jnp.logical_not(edge))
+        def _():
+            take(level_ref, other_at, sems.at[1]).start()
+
+        @pl.when((even == is_even) & edge)
+        def _():
+            low = window.at[pl.ds(other_at * blocks_dev, half)]
+            high = window.at[pl.ds(other_at * blocks_dev + half, half)]
+            pltpu.make_async_copy(edge_ref, low, sems.at[1]).start()
+            pltpu.make_async_copy(beyond_ref, high, sems.at[1]).start()
 
     def fetch(i):
         here = pl.ds(i * chunk, chunk)
@@ -315,17 +329,19 @@
     over = swap(blocks, 2)
     chip = swap(blocks, 1)
 
-    *asked, mine, held = pl.pallas_call(
+    *asked, mine, held, half = pl.pallas_call(
         functools.partial(requests_kernel, nodes_total),
         out_shape=(
             *[pltpu.VMEM((LEVEL + 1, 1, clusters), f32)] * levels,
             pltpu.VMEM((rows, clusters), bf16),
+            pltpu.VMEM((rows // 2, clusters), bf16),
         ),
         in_specs=[SMEM, ANY, ANY],
-        out_specs=[VMEM] * (levels + 1),
+        out_specs=[VMEM] * (levels + 2),
         scratch_shapes=[
             pltpu.VMEM((slots, blocks_dev), i32),
             pltpu.VMEM((shards, 1, clusters), f32),
+            pltpu.SemaphoreType.DMA,
             pltpu.SemaphoreType.DMA,
             pltpu.SemaphoreType.DMA((8,)),
         ],
@@ -334,7 +350,7 @@
     )(place, in_hbm(cols), in_hbm(coupling))
     heard = [swap(x, dz * LEVEL) for dz, x in zip(others, asked)]
     edges = [z * LEVEL for z in range(1, levels)]
-    edge = lax.ppermute(blocks, NODES, [(i - 1, i + 2) for i in edges] + [(i, i - 3) for i in edges])
+    edge = lax.ppermute(half, NODES, [(i - 1, i + 2) for i in edges] + [(i, i - 3) for i in edges])
 
     def gather(stage, heard, sources):
         return pl.pallas_call(
@@ -353,6 +369,7 @@
     found = gather(0, heard, (held.reshape(blocks.shape), chip))
     fetched = [swap(x, dz * LEVEL) for dz, x in zip(others, found)]
     over_chip = swap(over, 1)
+    beyond = lax.ppermute(over[blocks_dev // 2 :], NODES, [(i - 3, i) for i in edges] + [(i + 2, i - 1) for i in edges])
     edge = lax.ppermute(edge, NODES, [(i + 2, i) for i in edges] + [(i - 3, i - 1) for i in edges])
     found = gather(1, (*heard, mine), (over, over_chip))
     there = [swap(x, dz * LEVEL) for dz, x in zip(others, found)]
@@ -384,7 +401,7 @@
     part = pl.pallas_call(
         functools.partial(near_kernel, group, group),
         out_shape=pltpu.HBM((rows, clusters), f32),
-        in_specs=[SMEM, SMEM, ANY, ANY, ANY, ANY, ANY, VMEM, VMEM],
+        in_specs=[SMEM, SMEM, ANY, ANY, ANY, ANY, ANY, ANY, VMEM, VMEM],
         out_specs=ANY,
         scratch_shapes=[
             pltpu.VMEM((3 * blocks_dev, tile, clusters), bf16),
@@ -400,7 +417,10 @@
             flops=flops * (NEAR * tile + 2 * clusters), bytes_accessed=16 << 20, transcendentals=rows * clusters
         ),
         name="near",
-    )(place, cols, in_hbm(blocks), chip, over_chip, edge, in_hbm(tile_vals), on_chip(graph2), on_chip(pull))
+    )(
+        place, cols, in_hbm(blocks), chip, over_chip, edge.reshape(blocks_dev // 2, tile, clusters), beyond,
+        in_hbm(tile_vals), on_chip(graph2), on_chip(pull),
+    )
 
     parts = [home, *fetched, home_late, *there]
     logits, mass_parts = pl.pallas_call(

time: 110 us -> 128 us (1.16)
  starting transfers between devices: 26.3 us -> 41 us
  waiting for transfers between devices: 48 us -> 51.8 us
    ppermute x14, starting transfers between devices: 23 us -> 38.9 us  [swap(): return lax.ppermute(x, NODES, [(i, i ^ bits) for i in range(shards)])]
    ppermute x14, waiting for transfers between devices: 48 us -> 51.8 us  [swap(): return lax.ppermute(x, NODES, [(i, i ^ bits) for i in range(shards)])]
  transfers between devices with their start and end apart: 16 -> 17, of which waited for: 6 -> 8; matrix products, arithmetic and copies ran while one was open for 0% -> 0% of each run, Pallas kernels for 15% -> 13%
where the time goes in v8:
time: 128 us
  waiting for transfers between devices  51.8 us (40%)
  starting transfers between devices  41 us (32%)
  Pallas kernels  21.5 us (17%)
  blocking collectives  13.5 us (11%)
    ppermute x14, waiting for transfers between devices, swap(): return lax.ppermute(x, NODES, [(i, i ^ bits) for i in range(shards)])  51.8 us
    ppermute x14, starting transfers between devices, swap(): return lax.ppermute(x, NODES, [(i, i ^ bits) for i in range(shards)])  38.9 us
    all_to_all x1, blocking collectives, local(): lax.all_to_all(mass_parts, NODES, split_axis=0, concat_axis=0, tiled=True)  13.5 us
    pallas_call x1, Pallas kernels, local(): pl.pallas_call(functools.partial(near_kernel, group, group), out_shape=pl...  5.89 us
    pallas_call x3, Pallas kernels, gather(): pl.pallas_call(functools.partial(gather_kernel, cap, stage), out_shape=[p...  4.8 us
    pallas_call x1, Pallas kernels, local(): pl.pallas_call(functools.partial(far_kernel, group, chunk, nodes_total),...  3.85 us
    pallas_call x1, Pallas kernels, local(): pl.pallas_call(functools.partial(prep_kernel, cap, shards), out_shape=(pl...  3.22 us
  transfers between devices with their start and end apart: 17, of which 8 were waited for; matrix products, arithmetic and copies ran while one was open for 0% of the time, Pallas kernels for 13%

profile of v8, /device:TPU:0, one launch (start us, length us, event | category | flops | bytes accessed | tf_op | source)
XLA Modules:
  0.0 128.0 jit_solution(7289267930700253532)
XLA Ops:
  0.0 3.0 %collective-permute-start.6 = (bf16[32,128,128]{2,1,0:T(8,128)(2,1)}, bf16[32,128,128]{2,1,0:T(8,128)(2,1)S(1)}, u32[]{:S(2)}, u32[]{:S(2)}) collective-permute-start(bf16[32,128,128]{2,1,0:T(8,128)(2,1)} %bitcast.15), channel_id=1, source_target_pairs={{0,2},{1,3},{2,0},{3,1},{4,6},{5,7},{6,4},{7,5},{8,10},{9,11},{10,... | collective-permute-start | bytes 3145736 | tf_op jit(solution)/shard_map/ppermute | solution.py:327
  3.0 0.0 collective-permute-start.5
  3.0 23.4 %collective-permute-done.6.refs_4_ = bf16[32,128,128]{2,1,0:T(8,128)(2,1)S(1)} collective-permute-done((bf16[32,128,128]{2,1,0:T(8,128)(2,1)}, bf16[32,128,128]{2,1,0:T(8,128)(2,1)S(1)}, u32[]{:S(2)}, u32[]{:S(2)}) %collective-permute-start.6) | collective-permute-done | bytes 1048608 | tf_op jit(solution)/shard_map/ppermute | solution.py:327
  26.3 0.0 collective-permute-start.7
  26.3 2.2 %requests.1 = (f32[5,1,128]{2,1,0:T(1,128)S(1)}, f32[5,1,128]{2,1,0:T(1,128)S(1)}, f32[5,1,128]{2,1,0:T(1,128)S(1)}, f32[5,1,128]{2,1,0:T(1,128)S(1)}, bf16[4096...) custom-call(s32[1]{0:T(128)} %bitcast.place_ref, s32[6,32]{1,0:T(8,128)} %bitcast.11, bf16[4096,128]{1,0:T(8,128)(2,1)} %coupling_ref.1), custom_call_target="tpu_custom_call" | custom-call | tf_op jit(solution)/shard_map/requests/pallas_call | solution.py:332
  28.5 0.7 collective-permute-start.8
  29.2 0.0 collective-permute-done.8
  29.2 0.7 collective-permute-start.9
  30.0 0.7 collective-permute-start.10
  30.7 11.3 %collective-permute-start = (f32[5,1,128]{2,1,0:T(1,128)S(1)}, f32[5,1,128]{2,1,0:T(1,128)S(1)}, u32[]{:S(2)}, u32[]{:S(2)}) collective-permute-start(f32[5,1,128]{2,1,0:T(1,128)S(1)} %get-tuple-element.24), channel_id=1, source_target_pairs={{0,4},{1,5},{2,6},{3,7},{4,0},{5,1},{6,2},{7,3},{8,12},{9,13},{10,... | collective-permute-start | bytes 7688 | tf_op jit(solution)/shard_map/ppermute | solution.py:327
  41.9 1.6 %collective-permute-done.refs_0_ = f32[5,1,128]{2,1,0:T(1,128)S(1)} collective-permute-done((f32[5,1,128]{2,1,0:T(1,128)S(1)}, f32[5,1,128]{2,1,0:T(1,128)S(1)}, u32[]{:S(2)}, u32[]{:S(2)}) %collective-permute-start) | collective-permute-done | bytes 2592 | tf_op jit(solution)/shard_map/ppermute | solution.py:327
  43.5 3.3 %collective-permute-start.1 = (f32[5,1,128]{2,1,0:T(1,128)S(1)}, f32[5,1,128]{2,1,0:T(1,128)S(1)}, u32[]{:S(2)}, u32[]{:S(2)}) collective-permute-start(f32[5,1,128]{2,1,0:T(1,128)S(1)} %get-tuple-element.25), channel_id=1, source_target_pairs={{0,8},{1,9},{2,10},{3,11},{4,12},{5,13},{6,14},{7,15},{8,0},{9,1},... | collective-permute-start | bytes 7688 | tf_op jit(solution)/shard_map/ppermute | solution.py:327
  46.8 1.6 %collective-permute-done.1.refs_1_ = f32[5,1,128]{2,1,0:T(1,128)S(1)} collective-permute-done((f32[5,1,128]{2,1,0:T(1,128)S(1)}, f32[5,1,128]{2,1,0:T(1,128)S(1)}, u32[]{:S(2)}, u32[]{:S(2)}) %collective-permute-start.1) | collective-permute-done | bytes 2592 | tf_op jit(solution)/shard_map/ppermute | solution.py:327
  48.4 4.0 %collective-permute-start.2 = (f32[5,1,128]{2,1,0:T(1,128)S(1)}, f32[5,1,128]{2,1,0:T(1,128)S(1)}, u32[]{:S(2)}, u32[]{:S(2)}) collective-permute-start(f32[5,1,128]{2,1,0:T(1,128)S(1)} %get-tuple-element.26), channel_id=1, source_target_pairs={{0,12},{1,13},{2,14},{3,15},{4,8},{5,9},{6,10},{7,11},{8,4},{9,5},... | collective-permute-start | bytes 7688 | tf_op jit(solution)/shard_map/ppermute | solution.py:327
  52.3 1.6 %collective-permute-done.2.refs_2_ = f32[5,1,128]{2,1,0:T(1,128)S(1)} collective-permute-done((f32[5,1,128]{2,1,0:T(1,128)S(1)}, f32[5,1,128]{2,1,0:T(1,128)S(1)}, u32[]{:S(2)}, u32[]{:S(2)}) %collective-permute-start.2) | collective-permute-done | bytes 2592 | tf_op jit(solution)/shard_map/ppermute | solution.py:327
  53.9 0.0 collective-permute-done.5.chip_ref.refs_2_.refs_4_
  53.9 1.6 %shard_map.56 = (bf16[8,128,128]{2,1,0:T(8,128)(2,1)}, bf16[8,128,128]{2,1,0:T(8,128)(2,1)}, bf16[8,128,128]{2,1,0:T(8,128)(2,1)}) custom-call(s32[1]{0:T(128)} %bitcast.place_ref, f32[5,1,128]{2,1,0:T(1,128)S(1)} %collective-permute-done.refs_0_, f32[5,1,128]{2,1,0:T(1,128)S(1)} %collective-permute-done.1.refs_1_, ...), custom_call_target="tpu_custom_call" | custom-call | tf_op jit(solution)/shard_map/pallas_call | solution.py:356
  55.5 0.0 copy-start.5
  55.6 0.1 collective-permute-start.11
  55.7 3.8 %collective-permute-start.3 = (f32[1,128]{1,0:T(1,128)S(1)}, f32[1,128]{1,0:T(1,128)S(1)}, u32[]{:S(2)}, u32[]{:S(2)}) collective-permute-start(f32[1,128]{1,0:T(1,128)S(1)} %fusion), channel_id=1, source_target_pairs={{0,1},{1,0},{2,3},{3,2},{4,5},{5,4},{6,7},{7,6},{8,9},{9,8},{10,11... | collective-permute-start | bytes 1544 | tf_op jit(solution)/shard_map/ppermute | solution.py:327
  59.5 0.8 collective-permute-done.3
  60.3 4.8 %collective-permute-start.4 = (f32[1,128]{1,0:T(1,128)S(1)}, f32[1,128]{1,0:T(1,128)S(1)}, u32[]{:S(2)}, u32[]{:S(2)}) collective-permute-start(f32[1,128]{1,0:T(1,128)S(1)} %add.49.refs_0_), channel_id=1, source_target_pairs={{0,2},{1,3},{2,0},{3,1},{4,6},{5,7},{6,4},{7,5},{8,10},{9,11},{10,... | collective-permute-start | bytes 1544 | tf_op jit(solution)/shard_map/ppermute | solution.py:327
  65.0 0.0 collective-permute-done.7.level_ref.refs_5_
  65.1 2.1 %collective-permute-start.12 = (bf16[8,128,128]{2,1,0:T(8,128)(2,1)}, bf16[8,128,128]{2,1,0:T(8,128)(2,1)S(1)}, u32[]{:S(2)}, u32[]{:S(2)}) collective-permute-start(bf16[8,128,128]{2,1,0:T(8,128)(2,1)} %get-tuple-element.33), channel_id=1, source_target_pairs={{0,8},{1,9},{2,10},{3,11},{4,12},{5,13},{6,14},{7,15},{8,0},{9,1},... | collective-permute-start | bytes 786440 | tf_op jit(solution)/shard_map/ppermute | solution.py:327
  67.1 1.8 %shard_map.57 = (bf16[8,128,128]{2,1,0:T(8,128)(2,1)}, bf16[8,128,128]{2,1,0:T(8,128)(2,1)}, bf16[8,128,128]{2,1,0:T(8,128)(2,1)}, bf16[8,128,128]{2,1,0:T(8,128)(2,1)}) custom-call(s32[1]{0:T(128)} %bitcast.place_ref, f32[5,1,128]{2,1,0:T(1,128)S(1)} %collective-permute-done.refs_0_, f32[5,1,128]{2,1,0:T(1,128)S(1)} %collective-permute-done.1.refs_1_, ...), custom_call_target="tpu_custom_call" | custom-call | tf_op jit(solution)/shard_map/pallas_call | solution.py:356
  69.0 0.0 collective-permute-done.4.refs_1_
  69.0 0.0 copy-done.5
  69.0 2.3 %collective-permute-start.13 = (bf16[8,128,128]{2,1,0:T(8,128)(2,1)S(1)}, bf16[8,128,128]{2,1,0:T(8,128)(2,1)S(1)}, u32[]{:S(2)}, u32[]{:S(2)}) collective-permute-start(bf16[8,128,128]{2,1,0:T(8,128)(2,1)S(1)} %copy-done.5), channel_id=1, source_target_pairs={{0,12},{1,13},{2,14},{3,15},{4,8},{5,9},{6,10},{7,11},{8,4},{9,5},... | collective-permute-start | bytes 786440 | tf_op jit(solution)/shard_map/ppermute | solution.py:327
  71.3 0.0 collective-permute-done.9
  71.3 0.0 collective-permute-start.14
  71.3 0.0 collective-permute-done.11.refs_1_
  71.3 2.2 %collective-permute-start.15 = (bf16[8,128,128]{2,1,0:T(8,128)(2,1)}, bf16[8,128,128]{2,1,0:T(8,128)(2,1)S(1)}, u32[]{:S(2)}, u32[]{:S(2)}) collective-permute-start(bf16[8,128,128]{2,1,0:T(8,128)(2,1)} %get-tuple-element.37), channel_id=1, source_target_pairs={{0,8},{1,9},{2,10},{3,11},{4,12},{5,13},{6,14},{7,15},{8,0},{9,1},... | collective-permute-start | bytes 786440 | tf_op jit(solution)/shard_map/ppermute | solution.py:327
  73.5 0.0 collective-permute-done.10.beyond_ref
  73.5 2.2 %collective-permute-start.16 = (bf16[8,128,128]{2,1,0:T(8,128)(2,1)}, bf16[8,128,128]{2,1,0:T(8,128)(2,1)S(1)}, u32[]{:S(2)}, u32[]{:S(2)}) collective-permute-start(bf16[8,128,128]{2,1,0:T(8,128)(2,1)} %get-tuple-element.38), channel_id=1, source_target_pairs={{0,12},{1,13},{2,14},{3,15},{4,8},{5,9},{6,10},{7,11},{8,4},{9,5},... | collective-permute-start | bytes 786440 | tf_op jit(solution)/shard_map/ppermute | solution.py:327
  75.7 0.0 copy-done.2
  75.7 0.0 copy-done.3
  75.7 3.2 %prep.1 = (bf16[256,128]{1,0:T(8,128)(2,1)S(1)}, f32[8,128]{1,0:T(8,128)S(1)}, s32[64]{0:T(128)S(1)}) custom-call(s32[1]{0:T(128)} %bitcast.place_ref, s32[6,32]{1,0:T(8,128)S(1)} %bitcast.12, s32[128,128]{1,0:T(8,128)S(1)} %copy-done.2, f32[1,128]{1,0:T(1,128)S(1)} %add.49.refs_0_, f32[1,128]{1,0:T(1,128)S(1)} %collective-permute-done.4.refs_1_), custom_call_target="tpu_custom_call" | custom-call | tf_op jit(solution)/shard_map/prep/pallas_call | solution.py:386
  78.9 1.3 %shard_map.55.refs_0_ = bf16[8,128,128]{2,1,0:T(8,128)(2,1)} custom-call(s32[1]{0:T(128)} %bitcast.place_ref, f32[5,1,128]{2,1,0:T(1,128)S(1)} %get-tuple-element.23.refs_0_.refs_3_, bf16[32,128,128]{2,1,0:T(8,128)(2,1)S(1)} %bitcast.9, bf16[32,128,128]{2,1,0:T(8,128)(2,1)S(1)} %collective-permute-done.5.chip_ref.refs_2_.refs_4_), custom_call_target="tpu_custom_call" | custom-call | tf_op jit(solution)/shard_map/pallas_call | solution.py:356
  80.3 5.9 %near.1.part_ref = f32[4096,128]{1,0:T(8,128)} custom-call(s32[1]{0:T(128)} %bitcast.place_ref, s32[6,32]{1,0:T(8,128)S(1)} %bitcast.13, bf16[32,128,128]{2,1,0:T(8,128)(2,1)} %bitcast.17, bf16[32,128,128]{2,1,0:T(8,128)(2,1)S(1)} %collective-permute-done.5.chip_ref.refs_2_.refs_4_, bf16[32,128,128]{2,1,0:T(8,128)(2,1)S(1)} %collective-permute-done.7.level_ref.refs_5_, ...), custom_call_target="tpu_custom_call" | custom-call | flops 805306368 | bytes 16777216 | tf_op jit(solution)/shard_map/near/pallas_call | solution.py:401
  86.2 1.1 collective-permute-done.12.refs_2_
  87.3 0.0 collective-permute-done.13.refs_3_
  87.3 1.5 %collective-permute-done.14.refs_5_ = bf16[8,128,128]{2,1,0:T(8,128)(2,1)S(1)} collective-permute-done((bf16[8,128,128]{2,1,0:T(8,128)(2,1)}, bf16[8,128,128]{2,1,0:T(8,128)(2,1)S(1)}, u32[]{:S(2)}, u32[]{:S(2)}) %collective-permute-start.14) | collective-permute-done | bytes 262176 | tf_op jit(solution)/shard_map/ppermute | solution.py:327
  88.8 20.3 %collective-permute-done.15.refs_6_ = bf16[8,128,128]{2,1,0:T(8,128)(2,1)S(1)} collective-permute-done((bf16[8,128,128]{2,1,0:T(8,128)(2,1)}, bf16[8,128,128]{2,1,0:T(8,128)(2,1)S(1)}, u32[]{:S(2)}, u32[]{:S(2)}) %collective-permute-start.15) | collective-permute-done | bytes 262176 | tf_op jit(solution)/shard_map/ppermute | solution.py:327
  109.1 0.0 collective-permute-done.16.refs_7_
  109.1 0.0 copy-start.4
  109.1 3.9 %far.1 = (f32[4096,128]{1,0:T(8,128)S(1)}, f32[16,1,128]{2,1,0:T(1,128)S(1)}) custom-call(s32[64]{0:T(128)S(1)} %get-tuple-element.27.where_ref, bf16[32,6,128,128]{3,2,1,0:T(8,128)(2,1)} %tiles_ref.3, f32[4096,128]{1,0:T(8,128)} %near.1.part_ref, bf16[256,128]{1,0:T(8,128)(2,1)S(1)} %get-tuple-element.29.graph2_ref, bf16[8,128,128]{2,1,0:T(8,128)(2,1)S(1)} %copy-done, ...), custom_call_target="tpu_custom_call" | custom-call | flops 536870912 | bytes 8388608 | tf_op jit(solution)/shard_map/far/pallas_call | solution.py:426
  113.0 13.5 %all_to_all.5.mass_ref = f32[16,1,128]{2,1,0:T(1,128)S(1)} all-to-all(f32[16,1,128]{2,1,0:T(1,128)S(1)} %get-tuple-element.40), channel_id=1, replica_groups=mesh['groups'=2,'rows'=8,'sub'=2] {'rows','sub'}, dimensions={0} | all-to-all | bytes 16384 | tf_op jit(solution)/shard_map/all_to_all | solution.py:445
  126.4 1.6 %last.1 = f32[4096,128]{1,0:T(8,128)} custom-call(f32[4096,128]{1,0:T(8,128)S(1)} %get-tuple-element.39.logits_ref, f32[16,1,128]{2,1,0:T(1,128)S(1)} %all_to_all.5.mass_ref, f32[1,128]{1,0:T(1,128)S(1)} %bitcast.14), custom_call_target="tpu_custom_call" | custom-call | tf_op jit(solution)/shard_map/last/pallas_call | solution.py:447
  (10 shorter events, 0.1 us)
Async XLA Ops:
  0.0 26.3 %collective-permute-start.6 = (bf16[32,128,128]{2,1,0:T(8,128)(2,1)}, bf16[32,128,128]{2,1,0:T(8,128)(2,1)S(1)}, u32[]{:S(2)}, u32[]{:S(2)}) collective-permute-start(bf16[32,128,128]{2,1,0:T(8,128)(2,1)} %bitcast.15), channel_id=1, source_target_pairs={{0,2},{1,3},{2,0},{3,1},{4,6},{5,7},{6,4},{7,5},{8,10},{9,11},{10,... | collective-permute-start | bytes 3145736 | tf_op jit(solution)/shard_map/ppermute | solution.py:327
  3.0 50.9 %collective-permute-start.5 = (bf16[32,128,128]{2,1,0:T(8,128)(2,1)}, bf16[32,128,128]{2,1,0:T(8,128)(2,1)S(1)}, u32[]{:S(2)}, u32[]{:S(2)}) collective-permute-start(bf16[32,128,128]{2,1,0:T(8,128)(2,1)} %bitcast.16), channel_id=1, source_target_pairs={{0,1},{1,0},{2,3},{3,2},{4,5},{5,4},{6,7},{7,6},{8,9},{9,8},{10,11... | collective-permute-start | bytes 3145736 | tf_op jit(solution)/shard_map/ppermute | solution.py:327
  26.3 38.7 %collective-permute-start.7 = (bf16[32,128,128]{2,1,0:T(8,128)(2,1)S(1)}, bf16[32,128,128]{2,1,0:T(8,128)(2,1)S(1)}, u32[]{:S(2)}, u32[]{:S(2)}) collective-permute-start(bf16[32,128,128]{2,1,0:T(8,128)(2,1)S(1)} %collective-permute-done.6.refs_4_), channel_id=1, source_target_pairs={{0,1},{1,0},{2,3},{3,2},{4,5},{5,4},{6,7},{7,6},{8,9},{9,8},{10,11... | collective-permute-start | bytes 3145736 | tf_op jit(solution)/shard_map/ppermute | solution.py:327
  28.5 0.7 collective-permute-start.8
  29.2 42.1 %collective-permute-start.9 = (bf16[2048,128]{1,0:T(8,128)(2,1)S(1)}, bf16[2048,128]{1,0:T(8,128)(2,1)S(1)}, u32[]{:S(2)}, u32[]{:S(2)}) collective-permute-start(bf16[2048,128]{1,0:T(8,128)(2,1)S(1)} %collective-permute-done.8), channel_id=1, source_target_pairs={{6,4},{10,8},{14,12},{1,3},{5,7},{9,11},{22,20},{26,24},{30,28},{1... | collective-permute-start | bytes 1572872 | tf_op jit(solution)/shard_map/ppermute | solution.py:373
  30.0 43.5 %collective-permute-start.10 = (bf16[16,128,128]{2,1,0:T(8,128)(2,1)S(1)}, bf16[16,128,128]{2,1,0:T(8,128)(2,1)S(1)}, u32[]{:S(2)}, u32[]{:S(2)}) collective-permute-start(bf16[16,128,128]{2,1,0:T(8,128)(2,1)S(1)} %slice.23), channel_id=1, source_target_pairs={{1,4},{5,8},{9,12},{6,3},{10,7},{14,11},{17,20},{21,24},{25,28},{2... | collective-permute-start | bytes 1572872 | tf_op jit(solution)/shard_map/ppermute | solution.py:372
  30.7 12.8 %collective-permute-start = (f32[5,1,128]{2,1,0:T(1,128)S(1)}, f32[5,1,128]{2,1,0:T(1,128)S(1)}, u32[]{:S(2)}, u32[]{:S(2)}) collective-permute-start(f32[5,1,128]{2,1,0:T(1,128)S(1)} %get-tuple-element.24), channel_id=1, source_target_pairs={{0,4},{1,5},{2,6},{3,7},{4,0},{5,1},{6,2},{7,3},{8,12},{9,13},{10,... | collective-permute-start | bytes 7688 | tf_op jit(solution)/shard_map/ppermute | solution.py:327
  43.5 4.9 %collective-permute-start.1 = (f32[5,1,128]{2,1,0:T(1,128)S(1)}, f32[5,1,128]{2,1,0:T(1,128)S(1)}, u32[]{:S(2)}, u32[]{:S(2)}) collective-permute-start(f32[5,1,128]{2,1,0:T(1,128)S(1)} %get-tuple-element.25), channel_id=1, source_target_pairs={{0,8},{1,9},{2,10},{3,11},{4,12},{5,13},{6,14},{7,15},{8,0},{9,1},... | collective-permute-start | bytes 7688 | tf_op jit(solution)/shard_map/ppermute | solution.py:327
  48.4 5.5 %collective-permute-start.2 = (f32[5,1,128]{2,1,0:T(1,128)S(1)}, f32[5,1,128]{2,1,0:T(1,128)S(1)}, u32[]{:S(2)}, u32[]{:S(2)}) collective-permute-start(f32[5,1,128]{2,1,0:T(1,128)S(1)} %get-tuple-element.26), channel_id=1, source_target_pairs={{0,12},{1,13},{2,14},{3,15},{4,8},{5,9},{6,10},{7,11},{8,4},{9,5},... | collective-permute-start | bytes 7688 | tf_op jit(solution)/shard_map/ppermute | solution.py:327
  53.9 21.8 %copy-start.2 = (s32[128,128]{1,0:T(8,128)S(1)}, s32[128,128]{1,0:T(8,128)}, u32[]{:S(2)}) copy-start(s32[128,128]{1,0:T(8,128)} %graph_ref.1) | copy-start | bytes 196612
  53.9 21.8 %copy-start.3 = (s32[32,6]{0,1:T(8,128)S(1)}, s32[32,6]{0,1:T(8,128)}, u32[]{:S(2)}) copy-start(s32[32,6]{0,1:T(8,128)} %param.7) | copy-start | bytes 2308
  55.5 13.4 %copy-start.5 = (bf16[8,128,128]{2,1,0:T(8,128)(2,1)S(1)}, bf16[8,128,128]{2,1,0:T(8,128)(2,1)}, u32[]{:S(2)}) copy-start(bf16[8,128,128]{2,1,0:T(8,128)(2,1)} %get-tuple-element.34) | copy-start | bytes 786436
  55.6 15.7 %collective-permute-start.11 = (bf16[8,128,128]{2,1,0:T(8,128)(2,1)}, bf16[8,128,128]{2,1,0:T(8,128)(2,1)S(1)}, u32[]{:S(2)}, u32[]{:S(2)}) collective-permute-start(bf16[8,128,128]{2,1,0:T(8,128)(2,1)} %get-tuple-element.32), channel_id=1, source_target_pairs={{0,4},{1,5},{2,6},{3,7},{4,0},{5,1},{6,2},{7,3},{8,12},{9,13},{10,... | collective-permute-start | bytes 786440 | tf_op jit(solution)/shard_map/ppermute | solution.py:327
  55.7 4.6 %collective-permute-start.3 = (f32[1,128]{1,0:T(1,128)S(1)}, f32[1,128]{1,0:T(1,128)S(1)}, u32[]{:S(2)}, u32[]{:S(2)}) collective-permute-start(f32[1,128]{1,0:T(1,128)S(1)} %fusion), channel_id=1, source_target_pairs={{0,1},{1,0},{2,3},{3,2},{4,5},{5,4},{6,7},{7,6},{8,9},{9,8},{10,11... | collective-permute-start | bytes 1544 | tf_op jit(solution)/shard_map/ppermute | solution.py:327
  60.3 8.7 %collective-permute-start.4 = (f32[1,128]{1,0:T(1,128)S(1)}, f32[1,128]{1,0:T(1,128)S(1)}, u32[]{:S(2)}, u32[]{:S(2)}) collective-permute-start(f32[1,128]{1,0:T(1,128)S(1)} %add.49.refs_0_), channel_id=1, source_target_pairs={{0,2},{1,3},{2,0},{3,1},{4,6},{5,7},{6,4},{7,5},{8,10},{9,11},{10,... | collective-permute-start | bytes 1544 | tf_op jit(solution)/shard_map/ppermute | solution.py:327
  65.1 22.3 %collective-permute-start.12 = (bf16[8,128,128]{2,1,0:T(8,128)(2,1)}, bf16[8,128,128]{2,1,0:T(8,128)(2,1)S(1)}, u32[]{:S(2)}, u32[]{:S(2)}) collective-permute-start(bf16[8,128,128]{2,1,0:T(8,128)(2,1)} %get-tuple-element.33), channel_id=1, source_target_pairs={{0,8},{1,9},{2,10},{3,11},{4,12},{5,13},{6,14},{7,15},{8,0},{9,1},... | collective-permute-start | bytes 786440 | tf_op jit(solution)/shard_map/ppermute | solution.py:327
  69.0 18.3 %collective-permute-start.13 = (bf16[8,128,128]{2,1,0:T(8,128)(2,1)S(1)}, bf16[8,128,128]{2,1,0:T(8,128)(2,1)S(1)}, u32[]{:S(2)}, u32[]{:S(2)}) collective-permute-start(bf16[8,128,128]{2,1,0:T(8,128)(2,1)S(1)} %copy-done.5), channel_id=1, source_target_pairs={{0,12},{1,13},{2,14},{3,15},{4,8},{5,9},{6,10},{7,11},{8,4},{9,5},... | collective-permute-start | bytes 786440 | tf_op jit(solution)/shard_map/ppermute | solution.py:327
  71.3 17.5 %collective-permute-start.14 = (bf16[8,128,128]{2,1,0:T(8,128)(2,1)}, bf16[8,128,128]{2,1,0:T(8,128)(2,1)S(1)}, u32[]{:S(2)}, u32[]{:S(2)}) collective-permute-start(bf16[8,128,128]{2,1,0:T(8,128)(2,1)} %get-tuple-element.36), channel_id=1, source_target_pairs={{0,4},{1,5},{2,6},{3,7},{4,0},{5,1},{6,2},{7,3},{8,12},{9,13},{10,... | collective-permute-start | bytes 786440 | tf_op jit(solution)/shard_map/ppermute | solution.py:327
  71.3 37.8 %collective-permute-start.15 = (bf16[8,128,128]{2,1,0:T(8,128)(2,1)}, bf16[8,128,128]{2,1,0:T(8,128)(2,1)S(1)}, u32[]{:S(2)}, u32[]{:S(2)}) collective-permute-start(bf16[8,128,128]{2,1,0:T(8,128)(2,1)} %get-tuple-element.37), channel_id=1, source_target_pairs={{0,8},{1,9},{2,10},{3,11},{4,12},{5,13},{6,14},{7,15},{8,0},{9,1},... | collective-permute-start | bytes 786440 | tf_op jit(solution)/shard_map/ppermute | solution.py:327
  73.5 35.6 %collective-permute-start.16 = (bf16[8,128,128]{2,1,0:T(8,128)(2,1)}, bf16[8,128,128]{2,1,0:T(8,128)(2,1)S(1)}, u32[]{:S(2)}, u32[]{:S(2)}) collective-permute-start(bf16[8,128,128]{2,1,0:T(8,128)(2,1)} %get-tuple-element.38), channel_id=1, source_target_pairs={{0,12},{1,13},{2,14},{3,15},{4,8},{5,9},{6,10},{7,11},{8,4},{9,5},... | collective-permute-start | bytes 786440 | tf_op jit(solution)/shard_map/ppermute | solution.py:327
  80.3 28.8 %copy-start = (bf16[8,128,128]{2,1,0:T(8,128)(2,1)S(1)}, bf16[8,128,128]{2,1,0:T(8,128)(2,1)}, u32[]{:S(2)}) copy-start(bf16[8,128,128]{2,1,0:T(8,128)(2,1)} %shard_map.55.refs_0_) | copy-start | bytes 786436
  80.3 28.8 %copy-start.1 = (bf16[8,128,128]{2,1,0:T(8,128)(2,1)S(1)}, bf16[8,128,128]{2,1,0:T(8,128)(2,1)}, u32[]{:S(2)}) copy-start(bf16[8,128,128]{2,1,0:T(8,128)(2,1)} %get-tuple-element.35.refs_4_) | copy-start | bytes 786436
  109.1 17.3 %copy-start.4 = (f32[128]{0:T(128)S(1)}, f32[128]{0:T(128)}, u32[]{:S(2)}) copy-start(f32[128]{0:T(128)} %param.9) | copy-start | bytes 1540

commit v9 on v8

--- a/solution.py
+++ b/solution.py
@@ -22,6 +22,10 @@
 f32, bf16, i32 = jnp.float32, jnp.bfloat16, jnp.int32
 
 
+def order_of(levels):
+    return [*range(levels // 2, levels), *range(1, levels // 2)]
+
+
 def on_chip(x):
     return pltpu.with_memory_space_constraint(x, pltpu.VMEM)
 
@@ -35,21 +39,15 @@
 
 
 def requests_kernel(nodes_total, place_ref, all_cols_ref, coupling_ref, *refs):
-    *out_refs, own_ref, rows, half_ref, cols_ref, table_ref, cols_sem, half_sem, sems = refs
+    *out_refs, own_ref, rows, half_ref, cols_ref, table_ref, cols_sem, half_sem, sem = refs
     slots, blocks_dev = cols_ref.shape
     cols_copy = pltpu.make_async_copy(all_cols_ref, cols_ref, cols_sem)
     cols_copy.start()
     shards = table_ref.shape[0]
     nodes, clusters = coupling_ref.shape
-    parts = sems.shape[0]
-    step = nodes // parts
-    copies = [
-        pltpu.make_async_copy(coupling_ref.at[pl.ds(i * step, step)], rows.at[pl.ds(i * step, step)], sems.at[i])
-        for i in range(parts)
-    ]
-    for copy in copies:
-        copy.start()
-    half_copy = pltpu.make_async_copy(coupling_ref.at[pl.ds(0, nodes // 2)], half_ref, half_sem)
+    coupling_copy = pltpu.make_async_copy(coupling_ref, rows, sem)
+    coupling_copy.start()
+    half_copy = pltpu.make_async_copy(coupling_ref.at[pl.ds(0, half_ref.shape[0])], half_ref, half_sem)
     half_copy.start()
 
     owner = lax.broadcasted_iota(i32, (shards, blocks_dev), 0)
@@ -61,6 +59,7 @@
     count = jnp.zeros((shards, 1), f32)
     table = jnp.zeros((shards, clusters), f32)
     cols_copy.wait()
+    coupling_copy.wait()
     for slot_id in range(NEAR, slots):
         local = cols_ref[slot_id : slot_id + 1, :] - owner * blocks_dev
         hit = (local >= 0) & (local < blocks_dev)
@@ -81,12 +80,8 @@
     for dz, ref in enumerate((own_ref, *out_refs)):
         for row in range(LEVEL):
             ref[row] = table_ref[(level ^ dz) * LEVEL + row]
-    total = jnp.zeros((8, clusters), f32)
-    for i in range(parts):
-        copies[i].wait()
-        part = rows[pl.ds(i * step, step), :].astype(f32)
-        total = total + jnp.sum(part.reshape(step // 8, 8, clusters), axis=0)
-    mass = jnp.sum(total, axis=0, keepdims=True) / nodes_total
+    part = rows[...].astype(f32)
+    mass = jnp.sum(jnp.sum(part.reshape(nodes // 8, 8, clusters), axis=0), axis=0, keepdims=True) / nodes_total
     for ref in (own_ref, *out_refs):
         ref[LEVEL] = mass
     half_copy.wait()
@@ -157,7 +152,7 @@
 
 def near_kernel(
     group, chunk, place_ref, cols_ref, own_ref, chip_ref, level_ref, edge_ref, beyond_ref, tiles_ref,
-    graph2_ref, pull_ref, part_ref, window, tiles, part, own_sem, sems, tile_sems, part_sems,
+    graph2_ref, pull_ref, part_ref, far_tiles_ref, window, tiles, own_sem, far_sem, sems, tile_sems,
 ):
     blocks_dev, tile, clusters = own_ref.shape
     steps = blocks_dev // group
@@ -170,7 +165,7 @@
     take(own_ref, 1, own_sem).start()
     even = spot % 2 == 0
     edge = (spot == 0) | (spot == LEVEL - 1)
-    half = blocks_dev // 2
+    early, late = edge_ref.shape[0], beyond_ref.shape[0]
     for is_even, chip_at, other_at in ((True, 2, 0), (False, 0, 2)):
 
         @pl.when(even == is_even)
@@ -183,8 +178,8 @@
 
         @pl.when((even == is_even) & edge)
         def _():
-            low = window.at[pl.ds(other_at * blocks_dev, half)]
-            high = window.at[pl.ds(other_at * blocks_dev + half, half)]
+            low = window.at[pl.ds(other_at * blocks_dev, early)]
+            high = window.at[pl.ds(other_at * blocks_dev + early, late)]
             pltpu.make_async_copy(edge_ref, low, sems.at[1]).start()
             pltpu.make_async_copy(beyond_ref, high, sems.at[1]).start()
 
@@ -192,12 +187,10 @@
         here = pl.ds(i * chunk, chunk)
         return pltpu.make_async_copy(tiles_ref.at[here, pl.ds(0, NEAR)], tiles.at[here], tile_sems.at[i])
 
-    def store(i):
-        here = pl.ds(i * chunk * tile, chunk * tile)
-        return pltpu.make_async_copy(part.at[here], part_ref.at[here], part_sems.at[i])
-
     for i in range(blocks_dev // chunk):
         fetch(i).start()
+    far_tiles = pltpu.make_async_copy(tiles_ref.at[:, pl.ds(NEAR, far_tiles_ref.shape[1])], far_tiles_ref, far_sem)
+    far_tiles.start()
     take(own_ref, 1, own_sem).wait()
     take(chip_ref, 0, sems.at[0]).wait()
     take(chip_ref, 2, sems.at[1]).wait()
@@ -224,53 +217,31 @@
         first = step * group
         affinity = jnp.dot(spreads, graph2_ref[...], preferred_element_type=f32)
         own = window[blocks_dev + first : blocks_dev + first + group].reshape(group * tile, clusters)
-        part[first * tile : (first + group) * tile, :] = (
+        part_ref[first * tile : (first + group) * tile, :] = (
             jnp.log(own.astype(f32)) - eta_step * pull_ref[0:1, :] + scale * affinity
         )
-        if (first + group) % chunk == 0:
-            store(first // chunk).start()
-    for i in range(blocks_dev // chunk):
-        store(i).wait()
-
-
-def far_kernel(
-    group, chunk, nodes_total, where_ref, tiles_ref, part_ref, graph2_ref, *refs
-):
-    *found_refs, logits_ref, mass_ref = refs[:-5]
-    blocks_ref, tiles, block_sem, tile_sems, part_sems = refs[-5:]
+    far_tiles.wait()
+
+
+def far_kernel(group, nodes_total, where_ref, tiles_ref, part_ref, graph2_ref, *refs):
+    *found_refs, logits_ref, mass_ref, blocks_ref, sem = refs
     tile, clusters = blocks_ref.shape[1:]
-    blocks_dev, far_slots = tiles.shape[:2]
+    blocks_dev, far_slots = tiles_ref.shape[:2]
     steps = blocks_dev // group
     scale = 2.0 * eta_step / clusters
     width = found_refs[0].shape[0]
     for i, found in enumerate(found_refs):
-        pltpu.make_async_copy(found, blocks_ref.at[pl.ds(i * width, width)], block_sem).start()
-
-    def fetches(i):
-        here = pl.ds(i * chunk, chunk)
-        there = pl.ds(i * chunk * tile, chunk * tile)
-        return (
-            pltpu.make_async_copy(tiles_ref.at[here, pl.ds(NEAR, far_slots)], tiles.at[here], tile_sems.at[i]),
-            pltpu.make_async_copy(part_ref.at[there], logits_ref.at[there], part_sems.at[i]),
-        )
-
-    for i in range(blocks_dev // chunk):
-        for copy in fetches(i):
-            copy.start()
+        pltpu.make_async_copy(found, blocks_ref.at[pl.ds(i * width, width)], sem).start()
+    pltpu.make_async_copy(blocks_ref, blocks_ref, sem).wait()
 
     def products(step):
-        first = step * group
-        if first % chunk == 0:
-            for copy in fetches(first // chunk):
-                copy.wait()
         spreads = []
-        for b in range(first, first + group):
+        for b in range(step * group, (step + 1) * group):
             picked = [blocks_ref[where_ref[b * far_slots + s]] for s in range(far_slots)]
-            wide = jnp.concatenate([tiles[b, s] for s in range(far_slots)], axis=1)
+            wide = jnp.concatenate([tiles_ref[b, s] for s in range(far_slots)], axis=1)
             spreads.append(split(jnp.dot(wide, jnp.concatenate(picked, axis=0), preferred_element_type=f32)))
         return jnp.concatenate(spreads, axis=0)
 
-    pltpu.make_async_copy(blocks_ref, blocks_ref, block_sem).wait()
     total = jnp.zeros((8, clusters), f32)
     ahead = products(0)
     for step in range(steps):
@@ -279,7 +250,7 @@
             ahead = products(step + 1)
         here = pl.ds(step * group * tile, group * tile)
         affinity = jnp.dot(spreads, graph2_ref[...], preferred_element_type=f32)
-        logits = logits_ref[here, :] + scale * affinity
+        logits = part_ref[here, :] + scale * affinity
         logits_ref[here, :] = logits
         total = total + jnp.sum(jnp.exp(logits).reshape(group * tile // 8, 8, clusters), axis=0)
 
@@ -320,7 +291,8 @@
     flops = 2 * rows * clusters
 
     levels = shards // LEVEL
-    others = range(1, levels)
+    others = order_of(levels)
+    early = blocks_dev - blocks_dev * 3 // 8
     place = my_index.astype(i32).reshape(1)
 
     def swap(x, bits):
@@ -334,7 +306,7 @@
         out_shape=(
             *[pltpu.VMEM((LEVEL + 1, 1, clusters), f32)] * levels,
             pltpu.VMEM((rows, clusters), bf16),
-            pltpu.VMEM((rows // 2, clusters), bf16),
+            pltpu.VMEM((early * tile, clusters), bf16),
         ),
         in_specs=[SMEM, ANY, ANY],
         out_specs=[VMEM] * (levels + 2),
@@ -343,12 +315,12 @@
             pltpu.VMEM((shards, 1, clusters), f32),
             pltpu.SemaphoreType.DMA,
             pltpu.SemaphoreType.DMA,
-            pltpu.SemaphoreType.DMA((8,)),
+            pltpu.SemaphoreType.DMA,
         ],
         compiler_params=params(8),
         name="requests",
     )(place, in_hbm(cols), in_hbm(coupling))
-    heard = [swap(x, dz * LEVEL) for dz, x in zip(others, asked)]
+    heard = [swap(x, dz * LEVEL) for dz, x in ((dz, asked[dz - 1]) for dz in others)]
     edges = [z * LEVEL for z in range(1, levels)]
     edge = lax.ppermute(half, NODES, [(i - 1, i + 2) for i in edges] + [(i, i - 3) for i in edges])
 
@@ -369,7 +341,9 @@
     found = gather(0, heard, (held.reshape(blocks.shape), chip))
     fetched = [swap(x, dz * LEVEL) for dz, x in zip(others, found)]
     over_chip = swap(over, 1)
-    beyond = lax.ppermute(over[blocks_dev // 2 :], NODES, [(i - 3, i) for i in edges] + [(i + 2, i - 1) for i in edges])
+    beyond = lax.ppermute(
+        over[early:], NODES, [(i - 3, i) for i in edges] + [(i + 2, i - 1) for i in edges]
+    )
     edge = lax.ppermute(edge, NODES, [(i + 2, i) for i in edges] + [(i - 3, i - 1) for i in edges])
     found = gather(1, (*heard, mine), (over, over_chip))
     there = [swap(x, dz * LEVEL) for dz, x in zip(others, found)]
@@ -397,19 +371,20 @@
         name="prep",
     )(place, cols, cluster_graph, mass, mass_over)
 
-    chunk = min(16, blocks_dev)
-    part = pl.pallas_call(
+    part, far_tiles = pl.pallas_call(
         functools.partial(near_kernel, group, group),
-        out_shape=pltpu.HBM((rows, clusters), f32),
+        out_shape=(
+            pltpu.VMEM((rows, clusters), f32),
+            pltpu.VMEM((blocks_dev, far_slots, tile, tile), bf16),
+        ),
         in_specs=[SMEM, SMEM, ANY, ANY, ANY, ANY, ANY, ANY, VMEM, VMEM],
-        out_specs=ANY,
+        out_specs=(VMEM, VMEM),
         scratch_shapes=[
             pltpu.VMEM((3 * blocks_dev, tile, clusters), bf16),
             pltpu.VMEM((blocks_dev, NEAR, tile, tile), bf16),
-            pltpu.VMEM((rows, clusters), f32),
+            pltpu.SemaphoreType.DMA,
             pltpu.SemaphoreType.DMA,
             pltpu.SemaphoreType.DMA((2,)),
-            pltpu.SemaphoreType.DMA((steps,)),
             pltpu.SemaphoreType.DMA((steps,)),
         ],
         compiler_params=params(20),
@@ -418,29 +393,24 @@
         ),
         name="near",
     )(
-        place, cols, in_hbm(blocks), chip, over_chip, edge.reshape(blocks_dev // 2, tile, clusters), beyond,
+        place, cols, in_hbm(blocks), chip, over_chip, edge.reshape(early, tile, clusters), beyond,
         in_hbm(tile_vals), on_chip(graph2), on_chip(pull),
     )
 
-    parts = [home, *fetched, home_late, *there]
+    at = [others.index(dz) for dz in range(1, levels)]
+    parts = [home, *[fetched[i] for i in at], home_late, *[there[i] for i in at]]
     logits, mass_parts = pl.pallas_call(
-        functools.partial(far_kernel, group, chunk, nodes_total),
+        functools.partial(far_kernel, group, nodes_total),
         out_shape=(pltpu.VMEM((rows, clusters), f32), pltpu.VMEM((shards, 1, clusters), f32)),
-        in_specs=[SMEM, ANY, ANY, VMEM] + [ANY] * len(parts),
+        in_specs=[SMEM, VMEM, VMEM, VMEM] + [ANY] * len(parts),
         out_specs=(VMEM, VMEM),
-        scratch_shapes=[
-            pltpu.VMEM((2 * cap * len(parts), tile, clusters), bf16),
-            pltpu.VMEM((blocks_dev, far_slots, tile, tile), bf16),
-            pltpu.SemaphoreType.DMA,
-            pltpu.SemaphoreType.DMA((blocks_dev // chunk,)),
-            pltpu.SemaphoreType.DMA((blocks_dev // chunk,)),
-        ],
+        scratch_shapes=[pltpu.VMEM((2 * cap * len(parts), tile, clusters), bf16), pltpu.SemaphoreType.DMA],
         compiler_params=params(16),
         cost_estimate=pl.CostEstimate(
             flops=flops * (far_slots * tile + 2 * clusters), bytes_accessed=8 << 20, transcendentals=rows * clusters
         ),
         name="far",
-    )(where, in_hbm(tile_vals), in_hbm(part), on_chip(graph2), *parts)
+    )(where, on_chip(far_tiles), on_chip(part), on_chip(graph2), *parts)
 
     masses = lax.all_to_all(mass_parts, NODES, split_axis=0, concat_axis=0, tiled=True)
 

time: 128 us -> 113 us (0.88)
  starting transfers between devices: 41 us -> 29.1 us
  Pallas kernels: 21.5 us -> 18.8 us
    ppermute x14, starting transfers between devices: 38.9 us -> 27 us  [swap(): return lax.ppermute(x, NODES, [(i, i ^ bits) for i in range(shards)])]
    pallas_call x2, Pallas kernels: 9.74 us -> 7.33 us  [the longest x1 5.31 us: local(): pl.pallas_call(functools.partial(near_kernel, group, group), out_shape=(p...]
where the time goes in v9:
time: 113 us
  waiting for transfers between devices  51.9 us (46%)
  starting transfers between devices  29.1 us (26%)
  Pallas kernels  18.8 us (17%)
  blocking collectives  12.9 us (11%)
    ppermute x14, waiting for transfers between devices, swap(): return lax.ppermute(x, NODES, [(i, i ^ bits) for i in range(shards)])  51.9 us
    ppermute x14, starting transfers between devices, swap(): return lax.ppermute(x, NODES, [(i, i ^ bits) for i in range(shards)])  27 us
    all_to_all x1, blocking collectives, local(): lax.all_to_all(mass_parts, NODES, split_axis=0, concat_axis=0, tiled=True)  12.9 us
    pallas_call x1, Pallas kernels, local(): pl.pallas_call(functools.partial(near_kernel, group, group), out_shape=(p...  5.31 us
    pallas_call x3, Pallas kernels, gather(): pl.pallas_call(functools.partial(gather_kernel, cap, stage), out_shape=[p...  4.82 us
    pallas_call x1, Pallas kernels, local(): pl.pallas_call(functools.partial(prep_kernel, cap, shards), out_shape=(pl...  3.22 us
  transfers between devices with their start and end apart: 17, of which 8 were waited for; matrix products, arithmetic and copies ran while one was open for 0% of the time, Pallas kernels for 13%

profile of v9, /device:TPU:0, one launch (start us, length us, event | category | flops | bytes accessed | tf_op | source)
XLA Modules:
  0.0 112.8 jit_solution(1119598467339668106)
XLA Ops:
  0.0 3.0 %collective-permute-start.6 = (bf16[32,128,128]{2,1,0:T(8,128)(2,1)}, bf16[32,128,128]{2,1,0:T(8,128)(2,1)S(1)}, u32[]{:S(2)}, u32[]{:S(2)}) collective-permute-start(bf16[32,128,128]{2,1,0:T(8,128)(2,1)} %bitcast.15), channel_id=1, source_target_pairs={{0,2},{1,3},{2,0},{3,1},{4,6},{5,7},{6,4},{7,5},{8,10},{9,11},{10,... | collective-permute-start | bytes 3145736 | tf_op jit(solution)/shard_map/ppermute | solution.py:299
  3.0 0.0 collective-permute-start.5
  3.0 1.8 %requests.1 = (f32[5,1,128]{2,1,0:T(1,128)S(1)}, f32[5,1,128]{2,1,0:T(1,128)S(1)}, f32[5,1,128]{2,1,0:T(1,128)S(1)}, f32[5,1,128]{2,1,0:T(1,128)S(1)}, bf16[4096...) custom-call(s32[1]{0:T(128)} %bitcast.place_ref, s32[6,32]{1,0:T(8,128)} %bitcast.11, bf16[4096,128]{1,0:T(8,128)(2,1)} %coupling_ref.1), custom_call_target="tpu_custom_call" | custom-call | tf_op jit(solution)/shard_map/requests/pallas_call | solution.py:304
  4.8 0.7 collective-permute-start.8
  5.5 20.8 %collective-permute-done.6.refs_4_ = bf16[32,128,128]{2,1,0:T(8,128)(2,1)S(1)} collective-permute-done((bf16[32,128,128]{2,1,0:T(8,128)(2,1)}, bf16[32,128,128]{2,1,0:T(8,128)(2,1)S(1)}, u32[]{:S(2)}, u32[]{:S(2)}) %collective-permute-start.6) | collective-permute-done | bytes 1048608 | tf_op jit(solution)/shard_map/ppermute | solution.py:299
  26.3 0.0 collective-permute-start.7
  26.3 0.0 collective-permute-done.8
  26.3 0.7 collective-permute-start.9
  27.1 0.7 collective-permute-start.10
  27.8 4.1 %collective-permute-start = (f32[5,1,128]{2,1,0:T(1,128)S(1)}, f32[5,1,128]{2,1,0:T(1,128)S(1)}, u32[]{:S(2)}, u32[]{:S(2)}) collective-permute-start(f32[5,1,128]{2,1,0:T(1,128)S(1)} %get-tuple-element.26), channel_id=1, source_target_pairs={{0,8},{1,9},{2,10},{3,11},{4,12},{5,13},{6,14},{7,15},{8,0},{9,1},... | collective-permute-start | bytes 7688 | tf_op jit(solution)/shard_map/ppermute | solution.py:299
  31.9 1.6 %collective-permute-done.refs_0_ = f32[5,1,128]{2,1,0:T(1,128)S(1)} collective-permute-done((f32[5,1,128]{2,1,0:T(1,128)S(1)}, f32[5,1,128]{2,1,0:T(1,128)S(1)}, u32[]{:S(2)}, u32[]{:S(2)}) %collective-permute-start) | collective-permute-done | bytes 2592 | tf_op jit(solution)/shard_map/ppermute | solution.py:299
  33.4 4.0 %collective-permute-start.1 = (f32[5,1,128]{2,1,0:T(1,128)S(1)}, f32[5,1,128]{2,1,0:T(1,128)S(1)}, u32[]{:S(2)}, u32[]{:S(2)}) collective-permute-start(f32[5,1,128]{2,1,0:T(1,128)S(1)} %get-tuple-element.27), channel_id=1, source_target_pairs={{0,12},{1,13},{2,14},{3,15},{4,8},{5,9},{6,10},{7,11},{8,4},{9,5},... | collective-permute-start | bytes 7688 | tf_op jit(solution)/shard_map/ppermute | solution.py:299
  37.4 1.6 %collective-permute-done.1.refs_1_ = f32[5,1,128]{2,1,0:T(1,128)S(1)} collective-permute-done((f32[5,1,128]{2,1,0:T(1,128)S(1)}, f32[5,1,128]{2,1,0:T(1,128)S(1)}, u32[]{:S(2)}, u32[]{:S(2)}) %collective-permute-start.1) | collective-permute-done | bytes 2592 | tf_op jit(solution)/shard_map/ppermute | solution.py:299
  39.0 0.0 collective-permute-start.2
  39.0 3.6 %collective-permute-done.2.refs_2_ = f32[5,1,128]{2,1,0:T(1,128)S(1)} collective-permute-done((f32[5,1,128]{2,1,0:T(1,128)S(1)}, f32[5,1,128]{2,1,0:T(1,128)S(1)}, u32[]{:S(2)}, u32[]{:S(2)}) %collective-permute-start.2) | collective-permute-done | bytes 2592 | tf_op jit(solution)/shard_map/ppermute | solution.py:299
  42.6 0.0 collective-permute-done.5.chip_ref.refs_2_.refs_4_
  42.6 1.6 %shard_map.56 = (bf16[8,128,128]{2,1,0:T(8,128)(2,1)}, bf16[8,128,128]{2,1,0:T(8,128)(2,1)}, bf16[8,128,128]{2,1,0:T(8,128)(2,1)}) custom-call(s32[1]{0:T(128)} %bitcast.place_ref, f32[5,1,128]{2,1,0:T(1,128)S(1)} %collective-permute-done.refs_0_, f32[5,1,128]{2,1,0:T(1,128)S(1)} %collective-permute-done.1.refs_1_, ...), custom_call_target="tpu_custom_call" | custom-call | tf_op jit(solution)/shard_map/pallas_call | solution.py:328
  44.2 0.0 copy-start.5
  44.2 0.1 collective-permute-start.11
  44.3 1.2 %collective-permute-start.3 = (f32[1,128]{1,0:T(1,128)S(1)}, f32[1,128]{1,0:T(1,128)S(1)}, u32[]{:S(2)}, u32[]{:S(2)}) collective-permute-start(f32[1,128]{1,0:T(1,128)S(1)} %fusion), channel_id=1, source_target_pairs={{0,1},{1,0},{2,3},{3,2},{4,5},{5,4},{6,7},{7,6},{8,9},{9,8},{10,11... | collective-permute-start | bytes 1544 | tf_op jit(solution)/shard_map/ppermute | solution.py:299
  45.5 0.8 collective-permute-done.3
  46.4 5.9 %collective-permute-start.4 = (f32[1,128]{1,0:T(1,128)S(1)}, f32[1,128]{1,0:T(1,128)S(1)}, u32[]{:S(2)}, u32[]{:S(2)}) collective-permute-start(f32[1,128]{1,0:T(1,128)S(1)} %add.49.refs_0_), channel_id=1, source_target_pairs={{0,2},{1,3},{2,0},{3,1},{4,6},{5,7},{6,4},{7,5},{8,10},{9,11},{10,... | collective-permute-start | bytes 1544 | tf_op jit(solution)/shard_map/ppermute | solution.py:299
  52.3 0.0 collective-permute-done.7.level_ref.refs_5_
  52.3 1.0 collective-permute-start.12
  53.3 1.9 %shard_map.57 = (bf16[8,128,128]{2,1,0:T(8,128)(2,1)}, bf16[8,128,128]{2,1,0:T(8,128)(2,1)}, bf16[8,128,128]{2,1,0:T(8,128)(2,1)}, bf16[8,128,128]{2,1,0:T(8,128)(2,1)}) custom-call(s32[1]{0:T(128)} %bitcast.place_ref, f32[5,1,128]{2,1,0:T(1,128)S(1)} %collective-permute-done.refs_0_, f32[5,1,128]{2,1,0:T(1,128)S(1)} %collective-permute-done.1.refs_1_, ...), custom_call_target="tpu_custom_call" | custom-call | tf_op jit(solution)/shard_map/pallas_call | solution.py:328
  55.2 0.0 collective-permute-done.4.refs_1_
  55.2 0.0 copy-done.5
  55.2 3.3 %collective-permute-start.13 = (bf16[8,128,128]{2,1,0:T(8,128)(2,1)S(1)}, bf16[8,128,128]{2,1,0:T(8,128)(2,1)S(1)}, u32[]{:S(2)}, u32[]{:S(2)}) collective-permute-start(bf16[8,128,128]{2,1,0:T(8,128)(2,1)S(1)} %copy-done.5), channel_id=1, source_target_pairs={{0,12},{1,13},{2,14},{3,15},{4,8},{5,9},{6,10},{7,11},{8,4},{9,5},... | collective-permute-start | bytes 786440 | tf_op jit(solution)/shard_map/ppermute | solution.py:299
  58.5 0.0 collective-permute-done.11.refs_1_
  58.5 0.0 collective-permute-start.14
  58.5 0.0 collective-permute-done.9
  58.5 1.1 collective-permute-start.15
  59.7 0.0 collective-permute-done.10.beyond_ref
  59.7 3.3 %collective-permute-start.16 = (bf16[8,128,128]{2,1,0:T(8,128)(2,1)}, bf16[8,128,128]{2,1,0:T(8,128)(2,1)S(1)}, u32[]{:S(2)}, u32[]{:S(2)}) collective-permute-start(bf16[8,128,128]{2,1,0:T(8,128)(2,1)} %get-tuple-element.42), channel_id=1, source_target_pairs={{0,12},{1,13},{2,14},{3,15},{4,8},{5,9},{6,10},{7,11},{8,4},{9,5},... | collective-permute-start | bytes 786440 | tf_op jit(solution)/shard_map/ppermute | solution.py:299
  62.9 0.0 copy-done.2
  62.9 3.2 %prep.1 = (bf16[256,128]{1,0:T(8,128)(2,1)S(1)}, f32[8,128]{1,0:T(8,128)S(1)}, s32[64]{0:T(128)S(1)}) custom-call(s32[1]{0:T(128)} %bitcast.place_ref, s32[6,32]{1,0:T(8,128)S(1)} %bitcast.12, s32[128,128]{1,0:T(8,128)S(1)} %copy-done.2, f32[1,128]{1,0:T(1,128)S(1)} %add.49.refs_0_, f32[1,128]{1,0:T(1,128)S(1)} %collective-permute-done.4.refs_1_), custom_call_target="tpu_custom_call" | custom-call | tf_op jit(solution)/shard_map/prep/pallas_call | solution.py:360
  66.2 1.3 %shard_map.55.refs_0_ = bf16[8,128,128]{2,1,0:T(8,128)(2,1)} custom-call(s32[1]{0:T(128)} %bitcast.place_ref, f32[5,1,128]{2,1,0:T(1,128)S(1)} %get-tuple-element.25.refs_0_.refs_3_, bf16[32,128,128]{2,1,0:T(8,128)(2,1)S(1)} %bitcast.9, bf16[32,128,128]{2,1,0:T(8,128)(2,1)S(1)} %collective-permute-done.5.chip_ref.refs_2_.refs_4_), custom_call_target="tpu_custom_call" | custom-call | tf_op jit(solution)/shard_map/pallas_call | solution.py:328
  67.5 0.0 copy-start
  67.5 5.3 %near.1 = (f32[4096,128]{1,0:T(8,128)S(1)}, bf16[32,2,128,128]{3,2,1,0:T(8,128)(2,1)S(1)}) custom-call(s32[1]{0:T(128)} %bitcast.place_ref, s32[6,32]{1,0:T(8,128)S(1)} %bitcast.13, bf16[32,128,128]{2,1,0:T(8,128)(2,1)} %bitcast.17, bf16[32,128,128]{2,1,0:T(8,128)(2,1)S(1)} %collective-permute-done.5.chip_ref.refs_2_.refs_4_, ...), custom_call_target="tpu_custom_call" | custom-call | flops 805306368 | bytes 16777216 | tf_op jit(solution)/shard_map/near/pallas_call | solution.py:374
  72.8 1.7 %collective-permute-done.12.refs_2_ = bf16[8,128,128]{2,1,0:T(8,128)(2,1)S(1)} collective-permute-done((bf16[8,128,128]{2,1,0:T(8,128)(2,1)}, bf16[8,128,128]{2,1,0:T(8,128)(2,1)S(1)}, u32[]{:S(2)}, u32[]{:S(2)}) %collective-permute-start.12) | collective-permute-done | bytes 262176 | tf_op jit(solution)/shard_map/ppermute | solution.py:299
  74.5 0.0 collective-permute-done.13.refs_3_
  74.6 1.5 %collective-permute-done.14.refs_5_ = bf16[8,128,128]{2,1,0:T(8,128)(2,1)S(1)} collective-permute-done((bf16[8,128,128]{2,1,0:T(8,128)(2,1)}, bf16[8,128,128]{2,1,0:T(8,128)(2,1)S(1)}, u32[]{:S(2)}, u32[]{:S(2)}) %collective-permute-start.14) | collective-permute-done | bytes 262176 | tf_op jit(solution)/shard_map/ppermute | solution.py:299
  76.0 20.3 %collective-permute-done.15.refs_6_ = bf16[8,128,128]{2,1,0:T(8,128)(2,1)S(1)} collective-permute-done((bf16[8,128,128]{2,1,0:T(8,128)(2,1)}, bf16[8,128,128]{2,1,0:T(8,128)(2,1)S(1)}, u32[]{:S(2)}, u32[]{:S(2)}) %collective-permute-start.15) | collective-permute-done | bytes 262176 | tf_op jit(solution)/shard_map/ppermute | solution.py:299
  96.3 0.0 collective-permute-done.16.refs_7_
  96.3 0.0 copy-start.4
  96.3 2.0 %far.1 = (f32[4096,128]{1,0:T(8,128)S(1)}, f32[16,1,128]{2,1,0:T(1,128)S(1)}) custom-call(s32[64]{0:T(128)S(1)} %get-tuple-element.29.where_ref, bf16[32,2,128,128]{3,2,1,0:T(8,128)(2,1)S(1)} %get-tuple-element.33.tiles_ref, f32[4096,128]{1,0:T(8,128)S(1)} %get-tuple-element.34.part_ref, bf16[256,128]{1,0:T(8,128)(2,1)S(1)} %get-tuple-element.31.graph2_ref, ...), custom_call_target="tpu_custom_call" | custom-call | flops 536870912 | bytes 8388608 | tf_op jit(solution)/shard_map/far/pallas_call | solution.py:402
  98.4 12.9 %all_to_all.5.mass_ref = f32[16,1,128]{2,1,0:T(1,128)S(1)} all-to-all(f32[16,1,128]{2,1,0:T(1,128)S(1)} %get-tuple-element.44), channel_id=1, replica_groups=mesh['groups'=2,'rows'=8,'sub'=2] {'rows','sub'}, dimensions={0} | all-to-all | bytes 16384 | tf_op jit(solution)/shard_map/all_to_all | solution.py:415
  111.3 1.6 %last.1 = f32[4096,128]{1,0:T(8,128)} custom-call(f32[4096,128]{1,0:T(8,128)S(1)} %get-tuple-element.43.logits_ref, f32[16,1,128]{2,1,0:T(1,128)S(1)} %all_to_all.5.mass_ref, f32[1,128]{1,0:T(1,128)S(1)} %bitcast.14), custom_call_target="tpu_custom_call" | custom-call | tf_op jit(solution)/shard_map/last/pallas_call | solution.py:417
  (10 shorter events, 0.1 us)
Async XLA Ops:
  0.0 26.3 %collective-permute-start.6 = (bf16[32,128,128]{2,1,0:T(8,128)(2,1)}, bf16[32,128,128]{2,1,0:T(8,128)(2,1)S(1)}, u32[]{:S(2)}, u32[]{:S(2)}) collective-permute-start(bf16[32,128,128]{2,1,0:T(8,128)(2,1)} %bitcast.15), channel_id=1, source_target_pairs={{0,2},{1,3},{2,0},{3,1},{4,6},{5,7},{6,4},{7,5},{8,10},{9,11},{10,... | collective-permute-start | bytes 3145736 | tf_op jit(solution)/shard_map/ppermute | solution.py:299
  3.0 39.6 %collective-permute-start.5 = (bf16[32,128,128]{2,1,0:T(8,128)(2,1)}, bf16[32,128,128]{2,1,0:T(8,128)(2,1)S(1)}, u32[]{:S(2)}, u32[]{:S(2)}) collective-permute-start(bf16[32,128,128]{2,1,0:T(8,128)(2,1)} %bitcast.16), channel_id=1, source_target_pairs={{0,1},{1,0},{2,3},{3,2},{4,5},{5,4},{6,7},{7,6},{8,9},{9,8},{10,11... | collective-permute-start | bytes 3145736 | tf_op jit(solution)/shard_map/ppermute | solution.py:299
  4.8 21.5 %collective-permute-start.8 = (bf16[2560,128]{1,0:T(8,128)(2,1)S(1)}, bf16[2560,128]{1,0:T(8,128)(2,1)S(1)}, u32[]{:S(2)}, u32[]{:S(2)}) collective-permute-start(bf16[2560,128]{1,0:T(8,128)(2,1)S(1)} %get-tuple-element.30), channel_id=1, source_target_pairs={{3,6},{7,10},{11,14},{4,1},{8,5},{12,9},{19,22},{23,26},{27,30},{2... | collective-permute-start | bytes 1966088 | tf_op jit(solution)/shard_map/ppermute | solution.py:325
  26.3 25.9 %collective-permute-start.7 = (bf16[32,128,128]{2,1,0:T(8,128)(2,1)S(1)}, bf16[32,128,128]{2,1,0:T(8,128)(2,1)S(1)}, u32[]{:S(2)}, u32[]{:S(2)}) collective-permute-start(bf16[32,128,128]{2,1,0:T(8,128)(2,1)S(1)} %collective-permute-done.6.refs_4_), channel_id=1, source_target_pairs={{0,1},{1,0},{2,3},{3,2},{4,5},{5,4},{6,7},{7,6},{8,9},{9,8},{10,11... | collective-permute-start | bytes 3145736 | tf_op jit(solution)/shard_map/ppermute | solution.py:299
  26.3 32.2 %collective-permute-start.9 = (bf16[2560,128]{1,0:T(8,128)(2,1)S(1)}, bf16[2560,128]{1,0:T(8,128)(2,1)S(1)}, u32[]{:S(2)}, u32[]{:S(2)}) collective-permute-start(bf16[2560,128]{1,0:T(8,128)(2,1)S(1)} %collective-permute-done.8), channel_id=1, source_target_pairs={{6,4},{10,8},{14,12},{1,3},{5,7},{9,11},{22,20},{26,24},{30,28},{1... | collective-permute-start | bytes 1966088 | tf_op jit(solution)/shard_map/ppermute | solution.py:347
  27.1 32.6 %collective-permute-start.10 = (bf16[12,128,128]{2,1,0:T(8,128)(2,1)S(1)}, bf16[12,128,128]{2,1,0:T(8,128)(2,1)S(1)}, u32[]{:S(2)}, u32[]{:S(2)}) collective-permute-start(bf16[12,128,128]{2,1,0:T(8,128)(2,1)S(1)} %slice.23), channel_id=1, source_target_pairs={{1,4},{5,8},{9,12},{6,3},{10,7},{14,11},{17,20},{21,24},{25,28},{2... | collective-permute-start | bytes 1179656 | tf_op jit(solution)/shard_map/ppermute | solution.py:344
  27.8 5.7 %collective-permute-start = (f32[5,1,128]{2,1,0:T(1,128)S(1)}, f32[5,1,128]{2,1,0:T(1,128)S(1)}, u32[]{:S(2)}, u32[]{:S(2)}) collective-permute-start(f32[5,1,128]{2,1,0:T(1,128)S(1)} %get-tuple-element.26), channel_id=1, source_target_pairs={{0,8},{1,9},{2,10},{3,11},{4,12},{5,13},{6,14},{7,15},{8,0},{9,1},... | collective-permute-start | bytes 7688 | tf_op jit(solution)/shard_map/ppermute | solution.py:299
  33.4 5.5 %collective-permute-start.1 = (f32[5,1,128]{2,1,0:T(1,128)S(1)}, f32[5,1,128]{2,1,0:T(1,128)S(1)}, u32[]{:S(2)}, u32[]{:S(2)}) collective-permute-start(f32[5,1,128]{2,1,0:T(1,128)S(1)} %get-tuple-element.27), channel_id=1, source_target_pairs={{0,12},{1,13},{2,14},{3,15},{4,8},{5,9},{6,10},{7,11},{8,4},{9,5},... | collective-permute-start | bytes 7688 | tf_op jit(solution)/shard_map/ppermute | solution.py:299
  39.0 3.6 %collective-permute-start.2 = (f32[5,1,128]{2,1,0:T(1,128)S(1)}, f32[5,1,128]{2,1,0:T(1,128)S(1)}, u32[]{:S(2)}, u32[]{:S(2)}) collective-permute-start(f32[5,1,128]{2,1,0:T(1,128)S(1)} %get-tuple-element.28), channel_id=1, source_target_pairs={{0,4},{1,5},{2,6},{3,7},{4,0},{5,1},{6,2},{7,3},{8,12},{9,13},{10,... | collective-permute-start | bytes 7688 | tf_op jit(solution)/shard_map/ppermute | solution.py:299
  42.6 20.4 %copy-start.2 = (s32[128,128]{1,0:T(8,128)S(1)}, s32[128,128]{1,0:T(8,128)}, u32[]{:S(2)}) copy-start(s32[128,128]{1,0:T(8,128)} %graph_ref.1) | copy-start | bytes 196612
  42.6 20.4 %copy-start.3 = (s32[32,6]{0,1:T(8,128)S(1)}, s32[32,6]{0,1:T(8,128)}, u32[]{:S(2)}) copy-start(s32[32,6]{0,1:T(8,128)} %param.7) | copy-start | bytes 2308
  44.2 11.0 %copy-start.5 = (bf16[8,128,128]{2,1,0:T(8,128)(2,1)S(1)}, bf16[8,128,128]{2,1,0:T(8,128)(2,1)}, u32[]{:S(2)}) copy-start(bf16[8,128,128]{2,1,0:T(8,128)(2,1)} %get-tuple-element.38) | copy-start | bytes 786436
  44.2 14.3 %collective-permute-start.11 = (bf16[8,128,128]{2,1,0:T(8,128)(2,1)}, bf16[8,128,128]{2,1,0:T(8,128)(2,1)S(1)}, u32[]{:S(2)}, u32[]{:S(2)}) collective-permute-start(bf16[8,128,128]{2,1,0:T(8,128)(2,1)} %get-tuple-element.36), channel_id=1, source_target_pairs={{0,4},{1,5},{2,6},{3,7},{4,0},{5,1},{6,2},{7,3},{8,12},{9,13},{10,... | collective-permute-start | bytes 786440 | tf_op jit(solution)/shard_map/ppermute | solution.py:299
  44.3 2.0 %collective-permute-start.3 = (f32[1,128]{1,0:T(1,128)S(1)}, f32[1,128]{1,0:T(1,128)S(1)}, u32[]{:S(2)}, u32[]{:S(2)}) collective-permute-start(f32[1,128]{1,0:T(1,128)S(1)} %fusion), channel_id=1, source_target_pairs={{0,1},{1,0},{2,3},{3,2},{4,5},{5,4},{6,7},{7,6},{8,9},{9,8},{10,11... | collective-permute-start | bytes 1544 | tf_op jit(solution)/shard_map/ppermute | solution.py:299
  46.4 8.8 %collective-permute-start.4 = (f32[1,128]{1,0:T(1,128)S(1)}, f32[1,128]{1,0:T(1,128)S(1)}, u32[]{:S(2)}, u32[]{:S(2)}) collective-permute-start(f32[1,128]{1,0:T(1,128)S(1)} %add.49.refs_0_), channel_id=1, source_target_pairs={{0,2},{1,3},{2,0},{3,1},{4,6},{5,7},{6,4},{7,5},{8,10},{9,11},{10,... | collective-permute-start | bytes 1544 | tf_op jit(solution)/shard_map/ppermute | solution.py:299
  52.3 22.3 %collective-permute-start.12 = (bf16[8,128,128]{2,1,0:T(8,128)(2,1)}, bf16[8,128,128]{2,1,0:T(8,128)(2,1)S(1)}, u32[]{:S(2)}, u32[]{:S(2)}) collective-permute-start(bf16[8,128,128]{2,1,0:T(8,128)(2,1)} %get-tuple-element.37), channel_id=1, source_target_pairs={{0,8},{1,9},{2,10},{3,11},{4,12},{5,13},{6,14},{7,15},{8,0},{9,1},... | collective-permute-start | bytes 786440 | tf_op jit(solution)/shard_map/ppermute | solution.py:299
  55.2 19.4 %collective-permute-start.13 = (bf16[8,128,128]{2,1,0:T(8,128)(2,1)S(1)}, bf16[8,128,128]{2,1,0:T(8,128)(2,1)S(1)}, u32[]{:S(2)}, u32[]{:S(2)}) collective-permute-start(bf16[8,128,128]{2,1,0:T(8,128)(2,1)S(1)} %copy-done.5), channel_id=1, source_target_pairs={{0,12},{1,13},{2,14},{3,15},{4,8},{5,9},{6,10},{7,11},{8,4},{9,5},... | collective-permute-start | bytes 786440 | tf_op jit(solution)/shard_map/ppermute | solution.py:299
  58.5 17.5 %collective-permute-start.14 = (bf16[8,128,128]{2,1,0:T(8,128)(2,1)}, bf16[8,128,128]{2,1,0:T(8,128)(2,1)S(1)}, u32[]{:S(2)}, u32[]{:S(2)}) collective-permute-start(bf16[8,128,128]{2,1,0:T(8,128)(2,1)} %get-tuple-element.40), channel_id=1, source_target_pairs={{0,4},{1,5},{2,6},{3,7},{4,0},{5,1},{6,2},{7,3},{8,12},{9,13},{10,... | collective-permute-start | bytes 786440 | tf_op jit(solution)/shard_map/ppermute | solution.py:299
  58.5 37.8 %collective-permute-start.15 = (bf16[8,128,128]{2,1,0:T(8,128)(2,1)}, bf16[8,128,128]{2,1,0:T(8,128)(2,1)S(1)}, u32[]{:S(2)}, u32[]{:S(2)}) collective-permute-start(bf16[8,128,128]{2,1,0:T(8,128)(2,1)} %get-tuple-element.41), channel_id=1, source_target_pairs={{0,8},{1,9},{2,10},{3,11},{4,12},{5,13},{6,14},{7,15},{8,0},{9,1},... | collective-permute-start | bytes 786440 | tf_op jit(solution)/shard_map/ppermute | solution.py:299
  59.7 36.7 %collective-permute-start.16 = (bf16[8,128,128]{2,1,0:T(8,128)(2,1)}, bf16[8,128,128]{2,1,0:T(8,128)(2,1)S(1)}, u32[]{:S(2)}, u32[]{:S(2)}) collective-permute-start(bf16[8,128,128]{2,1,0:T(8,128)(2,1)} %get-tuple-element.42), channel_id=1, source_target_pairs={{0,12},{1,13},{2,14},{3,15},{4,8},{5,9},{6,10},{7,11},{8,4},{9,5},... | collective-permute-start | bytes 786440 | tf_op jit(solution)/shard_map/ppermute | solution.py:299
  67.5 28.8 %copy-start = (bf16[8,128,128]{2,1,0:T(8,128)(2,1)S(1)}, bf16[8,128,128]{2,1,0:T(8,128)(2,1)}, u32[]{:S(2)}) copy-start(bf16[8,128,128]{2,1,0:T(8,128)(2,1)} %shard_map.55.refs_0_) | copy-start | bytes 786436
  67.5 28.8 %copy-start.1 = (bf16[8,128,128]{2,1,0:T(8,128)(2,1)S(1)}, bf16[8,128,128]{2,1,0:T(8,128)(2,1)}, u32[]{:S(2)}) copy-start(bf16[8,128,128]{2,1,0:T(8,128)(2,1)} %get-tuple-element.39.refs_4_) | copy-start | bytes 786436
  96.3 14.9 %copy-start.4 = (f32[128]{0:T(128)S(1)}, f32[128]{0:T(128)}, u32[]{:S(2)}) copy-start(f32[128]{0:T(128)} %param.9) | copy-start | bytes 1540

commit v10 on v9

--- a/solution.py
+++ b/solution.py
@@ -50,31 +50,28 @@
     half_copy = pltpu.make_async_copy(coupling_ref.at[pl.ds(0, half_ref.shape[0])], half_ref, half_sem)
     half_copy.start()
 
-    owner = lax.broadcasted_iota(i32, (shards, blocks_dev), 0)
-    place = lax.broadcasted_iota(i32, (clusters, blocks_dev), 0).astype(f32)
+    count = (slots - NEAR) * blocks_dev
+    exact = bf16 if blocks_dev <= 256 else f32
+    owner = lax.broadcasted_iota(i32, (shards, count), 0)
+    place = lax.broadcasted_iota(i32, (clusters, count), 0).astype(f32)
     before = (
-        lax.broadcasted_iota(i32, (blocks_dev, blocks_dev), 0)
-        < lax.broadcasted_iota(i32, (blocks_dev, blocks_dev), 1)
-    ).astype(f32)
-    count = jnp.zeros((shards, 1), f32)
-    table = jnp.zeros((shards, clusters), f32)
+        lax.broadcasted_iota(i32, (count, count), 0) < lax.broadcasted_iota(i32, (count, count), 1)
+    ).astype(bf16)
     cols_copy.wait()
     coupling_copy.wait()
-    for slot_id in range(NEAR, slots):
-        local = cols_ref[slot_id : slot_id + 1, :] - owner * blocks_dev
-        hit = (local >= 0) & (local < blocks_dev)
-        hits = hit.astype(f32)
-        earlier = jnp.dot(hits, before, preferred_element_type=f32) + count
-        rank = jnp.sum(earlier * hits, axis=0, keepdims=True)
-        count = count + jnp.sum(hits, axis=1, keepdims=True)
-        wanted = jnp.where(hit, local, 0).astype(f32)
-        table = table + lax.dot_general(
-            wanted,
-            (rank == place).astype(f32),
-            (((1,), (1,)), ((), ())),
-            precision=lax.Precision.HIGHEST,
-            preferred_element_type=f32,
-        )
+    far_cols = jnp.concatenate([cols_ref[s : s + 1, :] for s in range(NEAR, slots)], axis=1)
+    local = far_cols - owner * blocks_dev
+    hit = (local >= 0) & (local < blocks_dev)
+    hits = hit.astype(f32)
+    earlier = jnp.dot(hits.astype(bf16), before, preferred_element_type=f32)
+    rank = jnp.sum(earlier * hits, axis=0, keepdims=True)
+    table = lax.dot_general(
+        jnp.where(hit, local, 0).astype(f32).astype(exact),
+        (rank == place).astype(f32).astype(exact),
+        (((1,), (1,)), ((), ())),
+        precision=None if exact == bf16 else lax.Precision.HIGHEST,
+        preferred_element_type=f32,
+    )
     table_ref[:, 0, :] = table
     level = place_ref[0] // LEVEL
     for dz, ref in enumerate((own_ref, *out_refs)):
@@ -90,10 +87,10 @@
 def gather_kernel(cap, stage, place_ref, *refs):
     count = (len(refs) - 5) // 2
     heard_refs, sources, out_refs = refs[:count], refs[count : count + 2], refs[count + 2 : 2 * count + 2]
-    wanted_ref, wanted_smem, sems = refs[2 * count + 2 :]
+    wanted_ref, wanted_smem, sem = refs[2 * count + 2 :]
     for n, heard in enumerate(heard_refs):
         wanted_ref[n * 8 : n * 8 + LEVEL, :] = heard[:LEVEL, 0, :].astype(i32)
-    copy = pltpu.make_async_copy(wanted_ref, wanted_smem, sems.at[0])
+    copy = pltpu.make_async_copy(wanted_ref, wanted_smem, sem)
     copy.start()
     copy.wait()
     spot = place_ref[0] % LEVEL
@@ -101,9 +98,7 @@
         for sub, src in enumerate(sources):
             row = n * 8 + (spot ^ (2 * stage + sub))
             for j in range(cap):
-                pltpu.make_async_copy(src.at[wanted_smem[row, j]], out_ref.at[sub * cap + j], sems.at[n + 1]).start()
-    for n, out_ref in enumerate(out_refs):
-        pltpu.make_async_copy(out_ref, out_ref, sems.at[n + 1]).wait()
+                out_ref[sub * cap + j] = src[wanted_smem[row, j]]
 
 
 def split(x):
@@ -111,8 +106,10 @@
     return jnp.concatenate([high, (x - high.astype(f32)).astype(bf16)], axis=1)
 
 
-def prep_kernel(cap, shards, place_ref, cols_ref, graph_ref, *refs):
-    *mass_refs, graph2_ref, pull_ref, where_ref, count_ref = refs
+def prep_kernel(cap, shards, place_ref, cols_ref, graph_ref, all_tiles_ref, *refs):
+    *mass_refs, graph2_ref, pull_ref, where_ref, tiles_ref, count_ref, sem = refs
+    tiles_copy = pltpu.make_async_copy(all_tiles_ref, tiles_ref, sem)
+    tiles_copy.start()
     slots, blocks_dev = cols_ref.shape
     clusters = graph_ref.shape[0]
     spot, level = place_ref[0] % LEVEL, place_ref[0] // LEVEL
@@ -149,10 +146,12 @@
             row = ((turn // 2) * (shards // LEVEL) + ((owner // LEVEL) ^ level)) * 2 + turn % 2
             where_ref[b * (slots - NEAR) + slot_id - NEAR] = row * cap + rank
 
+    tiles_copy.wait()
+
 
 def near_kernel(
-    group, chunk, place_ref, cols_ref, own_ref, chip_ref, level_ref, edge_ref, beyond_ref, tiles_ref,
-    graph2_ref, pull_ref, part_ref, far_tiles_ref, window, tiles, own_sem, far_sem, sems, tile_sems,
+    group, place_ref, cols_ref, own_ref, chip_ref, level_ref, edge_ref, beyond_ref, tiles_ref,
+    graph2_ref, pull_ref, part_ref, window, own_sem, sems,
 ):
     blocks_dev, tile, clusters = own_ref.shape
     steps = blocks_dev // group
@@ -183,14 +182,6 @@
             pltpu.make_async_copy(edge_ref, low, sems.at[1]).start()
             pltpu.make_async_copy(beyond_ref, high, sems.at[1]).start()
 
-    def fetch(i):
-        here = pl.ds(i * chunk, chunk)
-        return pltpu.make_async_copy(tiles_ref.at[here, pl.ds(0, NEAR)], tiles.at[here], tile_sems.at[i])
-
-    for i in range(blocks_dev // chunk):
-        fetch(i).start()
-    far_tiles = pltpu.make_async_copy(tiles_ref.at[:, pl.ds(NEAR, far_tiles_ref.shape[1])], far_tiles_ref, far_sem)
-    far_tiles.start()
     take(own_ref, 1, own_sem).wait()
     take(chip_ref, 0, sems.at[0]).wait()
     take(chip_ref, 2, sems.at[1]).wait()
@@ -199,13 +190,10 @@
     scale = 2.0 * eta_step / clusters
 
     def products(step):
-        first = step * group
-        if first % chunk == 0:
-            fetch(first // chunk).wait()
         spreads = []
-        for b in range(first, first + group):
+        for b in range(step * group, (step + 1) * group):
             picked = [window[cols_ref[s, b] - base] for s in range(NEAR)]
-            wide = jnp.concatenate([tiles[b, s] for s in range(NEAR)], axis=1)
+            wide = jnp.concatenate([tiles_ref[b, s] for s in range(NEAR)], axis=1)
             spreads.append(split(jnp.dot(wide, jnp.concatenate(picked, axis=0), preferred_element_type=f32)))
         return jnp.concatenate(spreads, axis=0)
 
@@ -220,13 +208,13 @@
         part_ref[first * tile : (first + group) * tile, :] = (
             jnp.log(own.astype(f32)) - eta_step * pull_ref[0:1, :] + scale * affinity
         )
-    far_tiles.wait()
 
 
 def far_kernel(group, nodes_total, where_ref, tiles_ref, part_ref, graph2_ref, *refs):
     *found_refs, logits_ref, mass_ref, blocks_ref, sem = refs
     tile, clusters = blocks_ref.shape[1:]
-    blocks_dev, far_slots = tiles_ref.shape[:2]
+    blocks_dev, slots = tiles_ref.shape[:2]
+    far_slots = slots - NEAR
     steps = blocks_dev // group
     scale = 2.0 * eta_step / clusters
     width = found_refs[0].shape[0]
@@ -238,7 +226,7 @@
         spreads = []
         for b in range(step * group, (step + 1) * group):
             picked = [blocks_ref[where_ref[b * far_slots + s]] for s in range(far_slots)]
-            wide = jnp.concatenate([tiles_ref[b, s] for s in range(far_slots)], axis=1)
+            wide = jnp.concatenate([tiles_ref[b, s] for s in range(NEAR, slots)], axis=1)
             spreads.append(split(jnp.dot(wide, jnp.concatenate(picked, axis=0), preferred_element_type=f32)))
         return jnp.concatenate(spreads, axis=0)
 
@@ -287,12 +275,11 @@
     blocks = coupling.reshape(blocks_dev, tile, clusters)
     cols = tile_cols.T
     group = 4
-    steps = blocks_dev // group
     flops = 2 * rows * clusters
 
     levels = shards // LEVEL
     others = order_of(levels)
-    early = blocks_dev - blocks_dev * 3 // 8
+    early = blocks_dev - blocks_dev * 7 // 16
     place = my_index.astype(i32).reshape(1)
 
     def swap(x, bits):
@@ -300,7 +287,6 @@
 
     over = swap(blocks, 2)
     chip = swap(blocks, 1)
-
     *asked, mine, held, half = pl.pallas_call(
         functools.partial(requests_kernel, nodes_total),
         out_shape=(
@@ -327,13 +313,13 @@
     def gather(stage, heard, sources):
         return pl.pallas_call(
             functools.partial(gather_kernel, cap, stage),
-            out_shape=[pltpu.HBM((2 * cap, tile, clusters), bf16)] * len(heard),
+            out_shape=[pltpu.VMEM((2 * cap, tile, clusters), bf16)] * len(heard),
             in_specs=[SMEM] + [VMEM] * (len(heard) + 2),
-            out_specs=[ANY] * len(heard),
+            out_specs=[VMEM] * len(heard),
             scratch_shapes=[
                 pltpu.VMEM((8 * len(heard), clusters), i32),
                 pltpu.SMEM((8 * len(heard), clusters), i32),
-                pltpu.SemaphoreType.DMA((len(heard) + 1,)),
+                pltpu.SemaphoreType.DMA,
             ],
             compiler_params=params(8),
         )(place, *[on_chip(x) for x in heard], *[on_chip(x) for x in sources])
@@ -357,44 +343,39 @@
     mass = mass + mass_chip
     mass_over = swap(mass, 2)
 
-    graph2, pull, where = pl.pallas_call(
+    graph2, pull, where, tiles = pl.pallas_call(
         functools.partial(prep_kernel, cap, shards),
         out_shape=(
             pltpu.VMEM((2 * clusters, clusters), bf16),
             pltpu.VMEM((8, clusters), f32),
             jax.ShapeDtypeStruct((far_count,), i32),
+            pltpu.VMEM(tile_vals.shape, bf16),
         ),
-        in_specs=[SMEM, SMEM, VMEM, VMEM, VMEM],
-        out_specs=(VMEM, VMEM, SMEM),
-        scratch_shapes=[pltpu.SMEM((shards,), i32)],
+        in_specs=[SMEM, SMEM, VMEM, ANY, VMEM, VMEM],
+        out_specs=(VMEM, VMEM, SMEM, VMEM),
+        scratch_shapes=[pltpu.SMEM((shards,), i32), pltpu.SemaphoreType.DMA],
         compiler_params=params(4),
         name="prep",
-    )(place, cols, cluster_graph, mass, mass_over)
-
-    part, far_tiles = pl.pallas_call(
-        functools.partial(near_kernel, group, group),
-        out_shape=(
-            pltpu.VMEM((rows, clusters), f32),
-            pltpu.VMEM((blocks_dev, far_slots, tile, tile), bf16),
-        ),
-        in_specs=[SMEM, SMEM, ANY, ANY, ANY, ANY, ANY, ANY, VMEM, VMEM],
-        out_specs=(VMEM, VMEM),
+    )(place, cols, cluster_graph, in_hbm(tile_vals), mass, mass_over)
+
+    part = pl.pallas_call(
+        functools.partial(near_kernel, group),
+        out_shape=pltpu.VMEM((rows, clusters), f32),
+        in_specs=[SMEM, SMEM, ANY, ANY, ANY, ANY, ANY, VMEM, VMEM, VMEM],
+        out_specs=VMEM,
         scratch_shapes=[
             pltpu.VMEM((3 * blocks_dev, tile, clusters), bf16),
-            pltpu.VMEM((blocks_dev, NEAR, tile, tile), bf16),
-            pltpu.SemaphoreType.DMA,
             pltpu.SemaphoreType.DMA,
             pltpu.SemaphoreType.DMA((2,)),
-            pltpu.SemaphoreType.DMA((steps,)),
         ],
-        compiler_params=params(20),
+        compiler_params=params(8),
         cost_estimate=pl.CostEstimate(
             flops=flops * (NEAR * tile + 2 * clusters), bytes_accessed=16 << 20, transcendentals=rows * clusters
         ),
         name="near",
     )(
-        place, cols, in_hbm(blocks), chip, over_chip, edge.reshape(early, tile, clusters), beyond,
-        in_hbm(tile_vals), on_chip(graph2), on_chip(pull),
+        place, cols, held.reshape(blocks.shape), chip, over_chip, edge.reshape(early, tile, clusters), beyond,
+        on_chip(tiles), on_chip(graph2), on_chip(pull),
     )
 
     at = [others.index(dz) for dz in range(1, levels)]
@@ -405,12 +386,12 @@
         in_specs=[SMEM, VMEM, VMEM, VMEM] + [ANY] * len(parts),
         out_specs=(VMEM, VMEM),
         scratch_shapes=[pltpu.VMEM((2 * cap * len(parts), tile, clusters), bf16), pltpu.SemaphoreType.DMA],
-        compiler_params=params(16),
+        compiler_params=params(8),
         cost_estimate=pl.CostEstimate(
             flops=flops * (far_slots * tile + 2 * clusters), bytes_accessed=8 << 20, transcendentals=rows * clusters
         ),
         name="far",
-    )(where, on_chip(far_tiles), on_chip(part), on_chip(graph2), *parts)
+    )(where, on_chip(tiles), on_chip(part), on_chip(graph2), *parts)
 
     masses = lax.all_to_all(mass_parts, NODES, split_axis=0, concat_axis=0, tiled=True)
 

time: 113 us -> 113 us (level)
  Pallas kernels: 18.8 us -> 14.9 us
  waiting for transfers between devices: 51.9 us -> 54.7 us
    ppermute x14, waiting for transfers between devices: 51.9 us -> 54.7 us  [swap(): return lax.ppermute(x, NODES, [(i, i ^ bits) for i in range(shards)])]
    pallas_call x3, Pallas kernels: 4.82 us -> 2.36 us  [gather(): pl.pallas_call(functools.partial(gather_kernel, cap, stage), out_shape=[p...]
    pallas_call x1, Pallas kernels: 5.31 us -> 3.06 us  [local(): pl.pallas_call(functools.partial(near_kernel, group), out_shape=pltpu.VME...]
  transfers between devices with their start and end apart: 17 -> 17, of which waited for: 8 -> 8; matrix products, arithmetic and copies ran while one was open for 0% -> 0% of each run, Pallas kernels for 13% -> 10%
where the time goes in v10:
time: 113 us
  waiting for transfers between devices  54.7 us (48%)
  starting transfers between devices  29.9 us (26%)
  Pallas kernels  14.9 us (13%)
  blocking collectives  13.3 us (12%)
    ppermute x14, waiting for transfers between devices, swap(): return lax.ppermute(x, NODES, [(i, i ^ bits) for i in range(shards)])  54.7 us
    ppermute x14, starting transfers between devices, swap(): return lax.ppermute(x, NODES, [(i, i ^ bits) for i in range(shards)])  27.8 us
    all_to_all x1, blocking collectives, local(): lax.all_to_all(mass_parts, NODES, split_axis=0, concat_axis=0, tiled=True)  13.3 us
    pallas_call x1, Pallas kernels, local(): pl.pallas_call(functools.partial(prep_kernel, cap, shards), out_shape=(pl...  3.99 us
    pallas_call x1, Pallas kernels, local(): pl.pallas_call(functools.partial(near_kernel, group), out_shape=pltpu.VME...  3.06 us
    pallas_call x3, Pallas kernels, gather(): pl.pallas_call(functools.partial(gather_kernel, cap, stage), out_shape=[p...  2.36 us
  transfers between devices with their start and end apart: 17, of which 8 were waited for; matrix products, arithmetic and copies ran while one was open for 0% of the time, Pallas kernels for 10%

profile of v10, /device:TPU:0, one launch (start us, length us, event | category | flops | bytes accessed | tf_op | source)
XLA Modules:
  0.0 112.9 jit_solution(4904224441594489279)
XLA Ops:
  0.0 3.0 %collective-permute-start.6 = (bf16[32,128,128]{2,1,0:T(8,128)(2,1)}, bf16[32,128,128]{2,1,0:T(8,128)(2,1)S(1)}, u32[]{:S(2)}, u32[]{:S(2)}) collective-permute-start(bf16[32,128,128]{2,1,0:T(8,128)(2,1)} %bitcast.16), channel_id=1, source_target_pairs={{0,2},{1,3},{2,0},{3,1},{4,6},{5,7},{6,4},{7,5},{8,10},{9,11},{10,... | collective-permute-start | bytes 3145736 | tf_op jit(solution)/shard_map/ppermute | solution.py:286
  3.0 0.0 collective-permute-start.5
  3.0 1.9 %requests.1 = (f32[5,1,128]{2,1,0:T(1,128)S(1)}, f32[5,1,128]{2,1,0:T(1,128)S(1)}, f32[5,1,128]{2,1,0:T(1,128)S(1)}, f32[5,1,128]{2,1,0:T(1,128)S(1)}, bf16[4096...) custom-call(s32[1]{0:T(128)} %bitcast.place_ref, s32[6,32]{1,0:T(8,128)} %bitcast.12, bf16[4096,128]{1,0:T(8,128)(2,1)} %coupling_ref.1), custom_call_target="tpu_custom_call" | custom-call | tf_op jit(solution)/shard_map/requests/pallas_call | solution.py:290
  4.8 0.7 collective-permute-start.8
  5.5 20.8 %collective-permute-done.6.refs_4_ = bf16[32,128,128]{2,1,0:T(8,128)(2,1)S(1)} collective-permute-done((bf16[32,128,128]{2,1,0:T(8,128)(2,1)}, bf16[32,128,128]{2,1,0:T(8,128)(2,1)S(1)}, u32[]{:S(2)}, u32[]{:S(2)}) %collective-permute-start.6) | collective-permute-done | bytes 1048608 | tf_op jit(solution)/shard_map/ppermute | solution.py:286
  26.3 0.0 collective-permute-start.7
  26.3 0.0 collective-permute-done.8
  26.3 0.7 collective-permute-start.9
  27.1 0.7 collective-permute-start.10
  27.8 3.1 %collective-permute-start.2 = (f32[5,1,128]{2,1,0:T(1,128)S(1)}, f32[5,1,128]{2,1,0:T(1,128)S(1)}, u32[]{:S(2)}, u32[]{:S(2)}) collective-permute-start(f32[5,1,128]{2,1,0:T(1,128)S(1)} %get-tuple-element.27), channel_id=1, source_target_pairs={{0,4},{1,5},{2,6},{3,7},{4,0},{5,1},{6,2},{7,3},{8,12},{9,13},{10,... | collective-permute-start | bytes 7688 | tf_op jit(solution)/shard_map/ppermute | solution.py:286
  30.9 1.6 %collective-permute-done.2.refs_2_ = f32[5,1,128]{2,1,0:T(1,128)S(1)} collective-permute-done((f32[5,1,128]{2,1,0:T(1,128)S(1)}, f32[5,1,128]{2,1,0:T(1,128)S(1)}, u32[]{:S(2)}, u32[]{:S(2)}) %collective-permute-start.2) | collective-permute-done | bytes 2592 | tf_op jit(solution)/shard_map/ppermute | solution.py:286
  32.4 4.1 %collective-permute-start.1 = (f32[5,1,128]{2,1,0:T(1,128)S(1)}, f32[5,1,128]{2,1,0:T(1,128)S(1)}, u32[]{:S(2)}, u32[]{:S(2)}) collective-permute-start(f32[5,1,128]{2,1,0:T(1,128)S(1)} %get-tuple-element.26), channel_id=1, source_target_pairs={{0,12},{1,13},{2,14},{3,15},{4,8},{5,9},{6,10},{7,11},{8,4},{9,5},... | collective-permute-start | bytes 7688 | tf_op jit(solution)/shard_map/ppermute | solution.py:286
  36.5 1.6 %collective-permute-done.1.refs_1_ = f32[5,1,128]{2,1,0:T(1,128)S(1)} collective-permute-done((f32[5,1,128]{2,1,0:T(1,128)S(1)}, f32[5,1,128]{2,1,0:T(1,128)S(1)}, u32[]{:S(2)}, u32[]{:S(2)}) %collective-permute-start.1) | collective-permute-done | bytes 2592 | tf_op jit(solution)/shard_map/ppermute | solution.py:286
  38.1 1.0 collective-permute-start
  39.1 3.5 %collective-permute-done.refs_0_ = f32[5,1,128]{2,1,0:T(1,128)S(1)} collective-permute-done((f32[5,1,128]{2,1,0:T(1,128)S(1)}, f32[5,1,128]{2,1,0:T(1,128)S(1)}, u32[]{:S(2)}, u32[]{:S(2)}) %collective-permute-start) | collective-permute-done | bytes 2592 | tf_op jit(solution)/shard_map/ppermute | solution.py:286
  42.6 0.0 collective-permute-done.5.chip_ref.refs_2_.refs_4_
  42.6 0.0 copy-start
  42.6 0.0 copy-start.1
  42.6 0.8 shard_map.56
  43.4 1.5 %collective-permute-start.11 = (bf16[8,128,128]{2,1,0:T(8,128)(2,1)S(1)}, bf16[8,128,128]{2,1,0:T(8,128)(2,1)S(1)}, u32[]{:S(2)}, u32[]{:S(2)}) collective-permute-start(bf16[8,128,128]{2,1,0:T(8,128)(2,1)S(1)} %get-tuple-element.34), channel_id=1, source_target_pairs={{0,4},{1,5},{2,6},{3,7},{4,0},{5,1},{6,2},{7,3},{8,12},{9,13},{10,... | collective-permute-start | bytes 786440 | tf_op jit(solution)/shard_map/ppermute | solution.py:286
  44.9 2.7 %collective-permute-start.3 = (f32[1,128]{1,0:T(1,128)S(1)}, f32[1,128]{1,0:T(1,128)S(1)}, u32[]{:S(2)}, u32[]{:S(2)}) collective-permute-start(f32[1,128]{1,0:T(1,128)S(1)} %fusion), channel_id=1, source_target_pairs={{0,1},{1,0},{2,3},{3,2},{4,5},{5,4},{6,7},{7,6},{8,9},{9,8},{10,11... | collective-permute-start | bytes 1544 | tf_op jit(solution)/shard_map/ppermute | solution.py:286
  47.7 0.8 collective-permute-done.3
  48.5 3.6 %collective-permute-start.4 = (f32[1,128]{1,0:T(1,128)S(1)}, f32[1,128]{1,0:T(1,128)S(1)}, u32[]{:S(2)}, u32[]{:S(2)}) collective-permute-start(f32[1,128]{1,0:T(1,128)S(1)} %add.49.refs_0_), channel_id=1, source_target_pairs={{0,2},{1,3},{2,0},{3,1},{4,6},{5,7},{6,4},{7,5},{8,10},{9,11},{10,... | collective-permute-start | bytes 1544 | tf_op jit(solution)/shard_map/ppermute | solution.py:286
  52.1 0.0 collective-permute-done.7.level_ref.refs_5_
  52.1 2.0 %collective-permute-start.12 = (bf16[8,128,128]{2,1,0:T(8,128)(2,1)S(1)}, bf16[8,128,128]{2,1,0:T(8,128)(2,1)S(1)}, u32[]{:S(2)}, u32[]{:S(2)}) collective-permute-start(bf16[8,128,128]{2,1,0:T(8,128)(2,1)S(1)} %get-tuple-element.35), channel_id=1, source_target_pairs={{0,8},{1,9},{2,10},{3,11},{4,12},{5,13},{6,14},{7,15},{8,0},{9,1},... | collective-permute-start | bytes 786440 | tf_op jit(solution)/shard_map/ppermute | solution.py:286
  54.1 0.9 shard_map.57
  55.0 0.0 collective-permute-done.4.refs_1_
  55.0 2.4 %collective-permute-start.13 = (bf16[8,128,128]{2,1,0:T(8,128)(2,1)S(1)}, bf16[8,128,128]{2,1,0:T(8,128)(2,1)S(1)}, u32[]{:S(2)}, u32[]{:S(2)}) collective-permute-start(bf16[8,128,128]{2,1,0:T(8,128)(2,1)S(1)} %get-tuple-element.36), channel_id=1, source_target_pairs={{0,12},{1,13},{2,14},{3,15},{4,8},{5,9},{6,10},{7,11},{8,4},{9,5},... | collective-permute-start | bytes 786440 | tf_op jit(solution)/shard_map/ppermute | solution.py:286
  57.4 0.0 collective-permute-done.9
  57.4 0.0 collective-permute-start.14
  57.4 0.0 collective-permute-done.11.refs_1_
  57.4 2.1 %collective-permute-start.15 = (bf16[8,128,128]{2,1,0:T(8,128)(2,1)S(1)}, bf16[8,128,128]{2,1,0:T(8,128)(2,1)S(1)}, u32[]{:S(2)}, u32[]{:S(2)}) collective-permute-start(bf16[8,128,128]{2,1,0:T(8,128)(2,1)S(1)} %get-tuple-element.39), channel_id=1, source_target_pairs={{0,8},{1,9},{2,10},{3,11},{4,12},{5,13},{6,14},{7,15},{8,0},{9,1},... | collective-permute-start | bytes 786440 | tf_op jit(solution)/shard_map/ppermute | solution.py:286
  59.5 0.0 collective-permute-done.10.beyond_ref
  59.5 2.3 %collective-permute-start.16 = (bf16[8,128,128]{2,1,0:T(8,128)(2,1)S(1)}, bf16[8,128,128]{2,1,0:T(8,128)(2,1)S(1)}, u32[]{:S(2)}, u32[]{:S(2)}) collective-permute-start(bf16[8,128,128]{2,1,0:T(8,128)(2,1)S(1)} %get-tuple-element.40), channel_id=1, source_target_pairs={{0,12},{1,13},{2,14},{3,15},{4,8},{5,9},{6,10},{7,11},{8,4},{9,5},... | collective-permute-start | bytes 786440 | tf_op jit(solution)/shard_map/ppermute | solution.py:286
  61.8 0.0 copy-done
  61.8 0.0 copy-done.1
  61.8 4.0 %prep.1 = (bf16[256,128]{1,0:T(8,128)(2,1)S(1)}, f32[8,128]{1,0:T(8,128)S(1)}, s32[64]{0:T(128)S(1)}, bf16[32,6,128,128]{3,2,1,0:T(8,128)(2,1)S(1)}) custom-call(s32[1]{0:T(128)} %bitcast.place_ref, s32[6,32]{1,0:T(8,128)S(1)} %bitcast.13, s32[128,128]{1,0:T(8,128)S(1)} %copy-done, bf16[32,6,128,128]{3,2,1,0:T(8,128)(2,1)} %all_tiles_ref.1, ...), custom_call_target="tpu_custom_call" | custom-call | tf_op jit(solution)/shard_map/prep/pallas_call | solution.py:346
  65.8 0.6 shard_map.55.refs_0_
  66.4 3.1 %near.1.part_ref = f32[4096,128]{1,0:T(8,128)S(1)} custom-call(s32[1]{0:T(128)} %bitcast.place_ref, s32[6,32]{1,0:T(8,128)S(1)} %bitcast.14, bf16[32,128,128]{2,1,0:T(8,128)(2,1)S(1)} %bitcast.10, bf16[32,128,128]{2,1,0:T(8,128)(2,1)S(1)} %collective-permute-done.5.chip_ref.refs_2_.refs_4_, ...), custom_call_target="tpu_custom_call" | custom-call | flops 805306368 | bytes 16777216 | tf_op jit(solution)/shard_map/near/pallas_call | solution.py:361
  69.5 4.7 %collective-permute-done.12.refs_2_ = bf16[8,128,128]{2,1,0:T(8,128)(2,1)S(1)} collective-permute-done((bf16[8,128,128]{2,1,0:T(8,128)(2,1)S(1)}, bf16[8,128,128]{2,1,0:T(8,128)(2,1)S(1)}, u32[]{:S(2)}, u32[]{:S(2)}) %collective-permute-start.12) | collective-permute-done | bytes 262176 | tf_op jit(solution)/shard_map/ppermute | solution.py:286
  74.2 0.0 collective-permute-done.13.refs_3_
  74.2 0.5 collective-permute-done.14.refs_5_
  74.7 21.2 %collective-permute-done.15.refs_6_ = bf16[8,128,128]{2,1,0:T(8,128)(2,1)S(1)} collective-permute-done((bf16[8,128,128]{2,1,0:T(8,128)(2,1)S(1)}, bf16[8,128,128]{2,1,0:T(8,128)(2,1)S(1)}, u32[]{:S(2)}, u32[]{:S(2)}) %collective-permute-start.15) | collective-permute-done | bytes 262176 | tf_op jit(solution)/shard_map/ppermute | solution.py:286
  95.9 0.0 collective-permute-done.16.refs_7_
  95.9 2.0 %far.1 = (f32[4096,128]{1,0:T(8,128)S(1)}, f32[16,1,128]{2,1,0:T(1,128)S(1)}) custom-call(s32[64]{0:T(128)S(1)} %get-tuple-element.28.where_ref, bf16[32,6,128,128]{3,2,1,0:T(8,128)(2,1)S(1)} %get-tuple-element.29.tiles_ref, f32[4096,128]{1,0:T(8,128)S(1)} %near.1.part_ref, bf16[256,128]{1,0:T(8,128)(2,1)S(1)} %get-tuple-element.32.graph2_ref, ...), custom_call_target="tpu_custom_call" | custom-call | flops 536870912 | bytes 8388608 | tf_op jit(solution)/shard_map/far/pallas_call | solution.py:383
  98.0 13.3 %all_to_all.5.mass_ref = f32[16,1,128]{2,1,0:T(1,128)S(1)} all-to-all(f32[16,1,128]{2,1,0:T(1,128)S(1)} %get-tuple-element.42), channel_id=1, replica_groups=mesh['groups'=2,'rows'=8,'sub'=2] {'rows','sub'}, dimensions={0} | all-to-all | bytes 16384 | tf_op jit(solution)/shard_map/all_to_all | solution.py:396
  111.3 0.0 copy-done.2
  111.3 1.6 %last.1 = f32[4096,128]{1,0:T(8,128)} custom-call(f32[4096,128]{1,0:T(8,128)S(1)} %get-tuple-element.41.logits_ref, f32[16,1,128]{2,1,0:T(1,128)S(1)} %all_to_all.5.mass_ref, f32[1,128]{1,0:T(1,128)S(1)} %bitcast.15), custom_call_target="tpu_custom_call" | custom-call | tf_op jit(solution)/shard_map/last/pallas_call | solution.py:398
  (4 shorter events, 0.0 us)
Async XLA Ops:
  0.0 26.3 %collective-permute-start.6 = (bf16[32,128,128]{2,1,0:T(8,128)(2,1)}, bf16[32,128,128]{2,1,0:T(8,128)(2,1)S(1)}, u32[]{:S(2)}, u32[]{:S(2)}) collective-permute-start(bf16[32,128,128]{2,1,0:T(8,128)(2,1)} %bitcast.16), channel_id=1, source_target_pairs={{0,2},{1,3},{2,0},{3,1},{4,6},{5,7},{6,4},{7,5},{8,10},{9,11},{10,... | collective-permute-start | bytes 3145736 | tf_op jit(solution)/shard_map/ppermute | solution.py:286
  3.0 39.6 %collective-permute-start.5 = (bf16[32,128,128]{2,1,0:T(8,128)(2,1)}, bf16[32,128,128]{2,1,0:T(8,128)(2,1)S(1)}, u32[]{:S(2)}, u32[]{:S(2)}) collective-permute-start(bf16[32,128,128]{2,1,0:T(8,128)(2,1)} %bitcast.17), channel_id=1, source_target_pairs={{0,1},{1,0},{2,3},{3,2},{4,5},{5,4},{6,7},{7,6},{8,9},{9,8},{10,11... | collective-permute-start | bytes 3145736 | tf_op jit(solution)/shard_map/ppermute | solution.py:286
  4.8 21.5 %collective-permute-start.8 = (bf16[2304,128]{1,0:T(8,128)(2,1)S(1)}, bf16[2304,128]{1,0:T(8,128)(2,1)S(1)}, u32[]{:S(2)}, u32[]{:S(2)}) collective-permute-start(bf16[2304,128]{1,0:T(8,128)(2,1)S(1)} %get-tuple-element.31), channel_id=1, source_target_pairs={{3,6},{7,10},{11,14},{4,1},{8,5},{12,9},{19,22},{23,26},{27,30},{2... | collective-permute-start | bytes 1769480 | tf_op jit(solution)/shard_map/ppermute | solution.py:311
  26.3 25.8 %collective-permute-start.7 = (bf16[32,128,128]{2,1,0:T(8,128)(2,1)S(1)}, bf16[32,128,128]{2,1,0:T(8,128)(2,1)S(1)}, u32[]{:S(2)}, u32[]{:S(2)}) collective-permute-start(bf16[32,128,128]{2,1,0:T(8,128)(2,1)S(1)} %collective-permute-done.6.refs_4_), channel_id=1, source_target_pairs={{0,1},{1,0},{2,3},{3,2},{4,5},{5,4},{6,7},{7,6},{8,9},{9,8},{10,11... | collective-permute-start | bytes 3145736 | tf_op jit(solution)/shard_map/ppermute | solution.py:286
  26.3 31.1 %collective-permute-start.9 = (bf16[2304,128]{1,0:T(8,128)(2,1)S(1)}, bf16[2304,128]{1,0:T(8,128)(2,1)S(1)}, u32[]{:S(2)}, u32[]{:S(2)}) collective-permute-start(bf16[2304,128]{1,0:T(8,128)(2,1)S(1)} %collective-permute-done.8), channel_id=1, source_target_pairs={{6,4},{10,8},{14,12},{1,3},{5,7},{9,11},{22,20},{26,24},{30,28},{1... | collective-permute-start | bytes 1769480 | tf_op jit(solution)/shard_map/ppermute | solution.py:333
  27.1 32.4 %collective-permute-start.10 = (bf16[14,128,128]{2,1,0:T(8,128)(2,1)S(1)}, bf16[14,128,128]{2,1,0:T(8,128)(2,1)S(1)}, u32[]{:S(2)}, u32[]{:S(2)}) collective-permute-start(bf16[14,128,128]{2,1,0:T(8,128)(2,1)S(1)} %slice.23), channel_id=1, source_target_pairs={{1,4},{5,8},{9,12},{6,3},{10,7},{14,11},{17,20},{21,24},{25,28},{2... | collective-permute-start | bytes 1376264 | tf_op jit(solution)/shard_map/ppermute | solution.py:330
  27.8 4.7 %collective-permute-start.2 = (f32[5,1,128]{2,1,0:T(1,128)S(1)}, f32[5,1,128]{2,1,0:T(1,128)S(1)}, u32[]{:S(2)}, u32[]{:S(2)}) collective-permute-start(f32[5,1,128]{2,1,0:T(1,128)S(1)} %get-tuple-element.27), channel_id=1, source_target_pairs={{0,4},{1,5},{2,6},{3,7},{4,0},{5,1},{6,2},{7,3},{8,12},{9,13},{10,... | collective-permute-start | bytes 7688 | tf_op jit(solution)/shard_map/ppermute | solution.py:286
  32.4 5.6 %collective-permute-start.1 = (f32[5,1,128]{2,1,0:T(1,128)S(1)}, f32[5,1,128]{2,1,0:T(1,128)S(1)}, u32[]{:S(2)}, u32[]{:S(2)}) collective-permute-start(f32[5,1,128]{2,1,0:T(1,128)S(1)} %get-tuple-element.26), channel_id=1, source_target_pairs={{0,12},{1,13},{2,14},{3,15},{4,8},{5,9},{6,10},{7,11},{8,4},{9,5},... | collective-permute-start | bytes 7688 | tf_op jit(solution)/shard_map/ppermute | solution.py:286
  38.1 4.5 %collective-permute-start = (f32[5,1,128]{2,1,0:T(1,128)S(1)}, f32[5,1,128]{2,1,0:T(1,128)S(1)}, u32[]{:S(2)}, u32[]{:S(2)}) collective-permute-start(f32[5,1,128]{2,1,0:T(1,128)S(1)} %get-tuple-element.25), channel_id=1, source_target_pairs={{0,8},{1,9},{2,10},{3,11},{4,12},{5,13},{6,14},{7,15},{8,0},{9,1},... | collective-permute-start | bytes 7688 | tf_op jit(solution)/shard_map/ppermute | solution.py:286
  42.6 19.2 %copy-start = (s32[128,128]{1,0:T(8,128)S(1)}, s32[128,128]{1,0:T(8,128)}, u32[]{:S(2)}) copy-start(s32[128,128]{1,0:T(8,128)} %graph_ref.1) | copy-start | bytes 196612
  42.6 19.2 %copy-start.1 = (s32[32,6]{0,1:T(8,128)S(1)}, s32[32,6]{0,1:T(8,128)}, u32[]{:S(2)}) copy-start(s32[32,6]{0,1:T(8,128)} %param.7) | copy-start | bytes 2308
  43.4 14.0 %collective-permute-start.11 = (bf16[8,128,128]{2,1,0:T(8,128)(2,1)S(1)}, bf16[8,128,128]{2,1,0:T(8,128)(2,1)S(1)}, u32[]{:S(2)}, u32[]{:S(2)}) collective-permute-start(bf16[8,128,128]{2,1,0:T(8,128)(2,1)S(1)} %get-tuple-element.34), channel_id=1, source_target_pairs={{0,4},{1,5},{2,6},{3,7},{4,0},{5,1},{6,2},{7,3},{8,12},{9,13},{10,... | collective-permute-start | bytes 786440 | tf_op jit(solution)/shard_map/ppermute | solution.py:286
  44.9 3.6 %collective-permute-start.3 = (f32[1,128]{1,0:T(1,128)S(1)}, f32[1,128]{1,0:T(1,128)S(1)}, u32[]{:S(2)}, u32[]{:S(2)}) collective-permute-start(f32[1,128]{1,0:T(1,128)S(1)} %fusion), channel_id=1, source_target_pairs={{0,1},{1,0},{2,3},{3,2},{4,5},{5,4},{6,7},{7,6},{8,9},{9,8},{10,11... | collective-permute-start | bytes 1544 | tf_op jit(solution)/shard_map/ppermute | solution.py:286
  48.5 6.5 %collective-permute-start.4 = (f32[1,128]{1,0:T(1,128)S(1)}, f32[1,128]{1,0:T(1,128)S(1)}, u32[]{:S(2)}, u32[]{:S(2)}) collective-permute-start(f32[1,128]{1,0:T(1,128)S(1)} %add.49.refs_0_), channel_id=1, source_target_pairs={{0,2},{1,3},{2,0},{3,1},{4,6},{5,7},{6,4},{7,5},{8,10},{9,11},{10,... | collective-permute-start | bytes 1544 | tf_op jit(solution)/shard_map/ppermute | solution.py:286
  52.1 22.1 %collective-permute-start.12 = (bf16[8,128,128]{2,1,0:T(8,128)(2,1)S(1)}, bf16[8,128,128]{2,1,0:T(8,128)(2,1)S(1)}, u32[]{:S(2)}, u32[]{:S(2)}) collective-permute-start(bf16[8,128,128]{2,1,0:T(8,128)(2,1)S(1)} %get-tuple-element.35), channel_id=1, source_target_pairs={{0,8},{1,9},{2,10},{3,11},{4,12},{5,13},{6,14},{7,15},{8,0},{9,1},... | collective-permute-start | bytes 786440 | tf_op jit(solution)/shard_map/ppermute | solution.py:286
  55.0 19.2 %collective-permute-start.13 = (bf16[8,128,128]{2,1,0:T(8,128)(2,1)S(1)}, bf16[8,128,128]{2,1,0:T(8,128)(2,1)S(1)}, u32[]{:S(2)}, u32[]{:S(2)}) collective-permute-start(bf16[8,128,128]{2,1,0:T(8,128)(2,1)S(1)} %get-tuple-element.36), channel_id=1, source_target_pairs={{0,12},{1,13},{2,14},{3,15},{4,8},{5,9},{6,10},{7,11},{8,4},{9,5},... | collective-permute-start | bytes 786440 | tf_op jit(solution)/shard_map/ppermute | solution.py:286
  57.4 17.3 %collective-permute-start.14 = (bf16[8,128,128]{2,1,0:T(8,128)(2,1)S(1)}, bf16[8,128,128]{2,1,0:T(8,128)(2,1)S(1)}, u32[]{:S(2)}, u32[]{:S(2)}) collective-permute-start(bf16[8,128,128]{2,1,0:T(8,128)(2,1)S(1)} %get-tuple-element.38), channel_id=1, source_target_pairs={{0,4},{1,5},{2,6},{3,7},{4,0},{5,1},{6,2},{7,3},{8,12},{9,13},{10,... | collective-permute-start | bytes 786440 | tf_op jit(solution)/shard_map/ppermute | solution.py:286
  57.4 38.5 %collective-permute-start.15 = (bf16[8,128,128]{2,1,0:T(8,128)(2,1)S(1)}, bf16[8,128,128]{2,1,0:T(8,128)(2,1)S(1)}, u32[]{:S(2)}, u32[]{:S(2)}) collective-permute-start(bf16[8,128,128]{2,1,0:T(8,128)(2,1)S(1)} %get-tuple-element.39), channel_id=1, source_target_pairs={{0,8},{1,9},{2,10},{3,11},{4,12},{5,13},{6,14},{7,15},{8,0},{9,1},... | collective-permute-start | bytes 786440 | tf_op jit(solution)/shard_map/ppermute | solution.py:286
  59.5 36.5 %collective-permute-start.16 = (bf16[8,128,128]{2,1,0:T(8,128)(2,1)S(1)}, bf16[8,128,128]{2,1,0:T(8,128)(2,1)S(1)}, u32[]{:S(2)}, u32[]{:S(2)}) collective-permute-start(bf16[8,128,128]{2,1,0:T(8,128)(2,1)S(1)} %get-tuple-element.40), channel_id=1, source_target_pairs={{0,12},{1,13},{2,14},{3,15},{4,8},{5,9},{6,10},{7,11},{8,4},{9,5},... | collective-permute-start | bytes 786440 | tf_op jit(solution)/shard_map/ppermute | solution.py:286
  95.9 15.4 %copy-start.2 = (f32[128]{0:T(128)S(1)}, f32[128]{0:T(128)}, u32[]{:S(2)}) copy-start(f32[128]{0:T(128)} %param.9) | copy-start | bytes 1540

commit v11 on v10

--- a/solution.py
+++ b/solution.py
@@ -279,7 +279,7 @@
 
     levels = shards // LEVEL
     others = order_of(levels)
-    early = blocks_dev - blocks_dev * 7 // 16
+    early = blocks_dev - blocks_dev * 3 // 8
     place = my_index.astype(i32).reshape(1)
 
     def swap(x, bits):
@@ -324,7 +324,11 @@
             compiler_params=params(8),
         )(place, *[on_chip(x) for x in heard], *[on_chip(x) for x in sources])
 
-    found = gather(0, heard, (held.reshape(blocks.shape), chip))
+    far_levels = levels - levels // 2
+    own_chip = (held.reshape(blocks.shape), chip)
+    found = [*gather(0, heard[:far_levels], own_chip)]
+    if far_levels < len(others):
+        found += gather(0, heard[far_levels:], own_chip)
     fetched = [swap(x, dz * LEVEL) for dz, x in zip(others, found)]
     over_chip = swap(over, 1)
     beyond = lax.ppermute(

time: 113 us -> 117 us (1.035)
  waiting for transfers between devices: 54.7 us -> 58.5 us
  starting transfers between devices: 29.9 us -> 27.8 us
  blocking collectives: 13.3 us -> 14.9 us
    ppermute x14, waiting for transfers between devices: 54.7 us -> 58.5 us  [swap(): return lax.ppermute(x, NODES, [(i, i ^ bits) for i in range(shards)])]
    ppermute x14, starting transfers between devices: 27.8 us -> 25.7 us  [swap(): return lax.ppermute(x, NODES, [(i, i ^ bits) for i in range(shards)])]
    all_to_all x1, blocking collectives: 13.3 us -> 14.9 us  [local(): lax.all_to_all(mass_parts, NODES, split_axis=0, concat_axis=0, tiled=True)]
    pallas_call x3 -> x4, Pallas kernels: 2.36 us -> 2.91 us  [gather(): pl.pallas_call(functools.partial(gather_kernel, cap, stage), out_shape=[p...]
where the time goes in v11:
time: 117 us
  waiting for transfers between devices  58.5 us (50%)
  starting transfers between devices  27.8 us (24%)
  Pallas kernels  15.4 us (13%)
  blocking collectives  14.9 us (13%)
    ppermute x14, waiting for transfers between devices, swap(): return lax.ppermute(x, NODES, [(i, i ^ bits) for i in range(shards)])  58.5 us
    ppermute x14, starting transfers between devices, swap(): return lax.ppermute(x, NODES, [(i, i ^ bits) for i in range(shards)])  25.7 us
    all_to_all x1, blocking collectives, local(): lax.all_to_all(mass_parts, NODES, split_axis=0, concat_axis=0, tiled=True)  14.9 us
    pallas_call x1, Pallas kernels, local(): pl.pallas_call(functools.partial(prep_kernel, cap, shards), out_shape=(pl...  3.99 us
    pallas_call x1, Pallas kernels, local(): pl.pallas_call(functools.partial(near_kernel, group), out_shape=pltpu.VME...  3.06 us
    pallas_call x4, Pallas kernels, gather(): pl.pallas_call(functools.partial(gather_kernel, cap, stage), out_shape=[p...  2.91 us
  transfers between devices with their start and end apart: 17, of which 8 were waited for; matrix products, arithmetic and copies ran while one was open for 0% of the time, Pallas kernels for 10%

profile of v11, /device:TPU:0, one launch (start us, length us, event | category | flops | bytes accessed | tf_op | source)
XLA Modules:
  0.0 116.7 jit_solution(11112580959808879498)
XLA Ops:
  0.0 3.0 %collective-permute-start.6 = (bf16[32,128,128]{2,1,0:T(8,128)(2,1)}, bf16[32,128,128]{2,1,0:T(8,128)(2,1)S(1)}, u32[]{:S(2)}, u32[]{:S(2)}) collective-permute-start(bf16[32,128,128]{2,1,0:T(8,128)(2,1)} %bitcast.17), channel_id=1, source_target_pairs={{0,2},{1,3},{2,0},{3,1},{4,6},{5,7},{6,4},{7,5},{8,10},{9,11},{10,... | collective-permute-start | bytes 3145736 | tf_op jit(solution)/shard_map/ppermute | solution.py:286
  3.0 1.9 %requests.1 = (f32[5,1,128]{2,1,0:T(1,128)S(1)}, f32[5,1,128]{2,1,0:T(1,128)S(1)}, f32[5,1,128]{2,1,0:T(1,128)S(1)}, f32[5,1,128]{2,1,0:T(1,128)S(1)}, bf16[4096...) custom-call(s32[1]{0:T(128)} %bitcast.place_ref, s32[6,32]{1,0:T(8,128)} %bitcast.13, bf16[4096,128]{1,0:T(8,128)(2,1)} %coupling_ref.1), custom_call_target="tpu_custom_call" | custom-call | tf_op jit(solution)/shard_map/requests/pallas_call | solution.py:290
  4.8 0.7 collective-permute-start.8
  5.5 0.2 collective-permute-start.5
  5.8 20.6 %collective-permute-done.6.refs_4_ = bf16[32,128,128]{2,1,0:T(8,128)(2,1)S(1)} collective-permute-done((bf16[32,128,128]{2,1,0:T(8,128)(2,1)}, bf16[32,128,128]{2,1,0:T(8,128)(2,1)S(1)}, u32[]{:S(2)}, u32[]{:S(2)}) %collective-permute-start.6) | collective-permute-done | bytes 1048608 | tf_op jit(solution)/shard_map/ppermute | solution.py:286
  26.3 0.0 collective-permute-start.7
  26.3 0.0 collective-permute-done.8
  26.3 0.7 collective-permute-start.9
  27.1 0.7 collective-permute-start.10
  27.8 3.1 %collective-permute-start.2 = (f32[5,1,128]{2,1,0:T(1,128)S(1)}, f32[5,1,128]{2,1,0:T(1,128)S(1)}, u32[]{:S(2)}, u32[]{:S(2)}) collective-permute-start(f32[5,1,128]{2,1,0:T(1,128)S(1)} %get-tuple-element.26), channel_id=1, source_target_pairs={{0,4},{1,5},{2,6},{3,7},{4,0},{5,1},{6,2},{7,3},{8,12},{9,13},{10,... | collective-permute-start | bytes 7688 | tf_op jit(solution)/shard_map/ppermute | solution.py:286
  30.9 1.6 %collective-permute-done.2.refs_0_.refs_2_ = f32[5,1,128]{2,1,0:T(1,128)S(1)} collective-permute-done((f32[5,1,128]{2,1,0:T(1,128)S(1)}, f32[5,1,128]{2,1,0:T(1,128)S(1)}, u32[]{:S(2)}, u32[]{:S(2)}) %collective-permute-start.2) | collective-permute-done | bytes 2592 | tf_op jit(solution)/shard_map/ppermute | solution.py:286
  32.4 0.0 collective-permute-done.5.chip_ref.refs_2_.refs_3_
  32.4 0.6 shard_map.56
  33.1 2.1 %collective-permute-start.11 = (bf16[8,128,128]{2,1,0:T(8,128)(2,1)S(1)}, bf16[8,128,128]{2,1,0:T(8,128)(2,1)S(1)}, u32[]{:S(2)}, u32[]{:S(2)}) collective-permute-start(bf16[8,128,128]{2,1,0:T(8,128)(2,1)S(1)} %shard_map.56), channel_id=1, source_target_pairs={{0,4},{1,5},{2,6},{3,7},{4,0},{5,1},{6,2},{7,3},{8,12},{9,13},{10,... | collective-permute-start | bytes 786440 | tf_op jit(solution)/shard_map/ppermute | solution.py:286
  35.2 2.5 %collective-permute-start.1 = (f32[5,1,128]{2,1,0:T(1,128)S(1)}, f32[5,1,128]{2,1,0:T(1,128)S(1)}, u32[]{:S(2)}, u32[]{:S(2)}) collective-permute-start(f32[5,1,128]{2,1,0:T(1,128)S(1)} %get-tuple-element.25), channel_id=1, source_target_pairs={{0,12},{1,13},{2,14},{3,15},{4,8},{5,9},{6,10},{7,11},{8,4},{9,5},... | collective-permute-start | bytes 7688 | tf_op jit(solution)/shard_map/ppermute | solution.py:286
  37.6 4.5 %collective-permute-done.1.refs_1_ = f32[5,1,128]{2,1,0:T(1,128)S(1)} collective-permute-done((f32[5,1,128]{2,1,0:T(1,128)S(1)}, f32[5,1,128]{2,1,0:T(1,128)S(1)}, u32[]{:S(2)}, u32[]{:S(2)}) %collective-permute-start.1) | collective-permute-done | bytes 2592 | tf_op jit(solution)/shard_map/ppermute | solution.py:286
  42.1 0.0 collective-permute-start
  42.1 4.5 %collective-permute-done.refs_0_ = f32[5,1,128]{2,1,0:T(1,128)S(1)} collective-permute-done((f32[5,1,128]{2,1,0:T(1,128)S(1)}, f32[5,1,128]{2,1,0:T(1,128)S(1)}, u32[]{:S(2)}, u32[]{:S(2)}) %collective-permute-start) | collective-permute-done | bytes 2592 | tf_op jit(solution)/shard_map/ppermute | solution.py:286
  46.6 1.8 %collective-permute-start.3 = (f32[1,128]{1,0:T(1,128)S(1)}, f32[1,128]{1,0:T(1,128)S(1)}, u32[]{:S(2)}, u32[]{:S(2)}) collective-permute-start(f32[1,128]{1,0:T(1,128)S(1)} %fusion), channel_id=1, source_target_pairs={{0,1},{1,0},{2,3},{3,2},{4,5},{5,4},{6,7},{7,6},{8,9},{9,8},{10,11... | collective-permute-start | bytes 1544 | tf_op jit(solution)/shard_map/ppermute | solution.py:286
  48.4 0.8 collective-permute-done.3
  49.3 0.0 copy-start.1
  49.3 7.0 %collective-permute-start.4 = (f32[1,128]{1,0:T(1,128)S(1)}, f32[1,128]{1,0:T(1,128)S(1)}, u32[]{:S(2)}, u32[]{:S(2)}) collective-permute-start(f32[1,128]{1,0:T(1,128)S(1)} %add.49.refs_0_), channel_id=1, source_target_pairs={{0,2},{1,3},{2,0},{3,1},{4,6},{5,7},{6,4},{7,5},{8,10},{9,11},{10,... | collective-permute-start | bytes 1544 | tf_op jit(solution)/shard_map/ppermute | solution.py:286
  56.3 0.7 shard_map.57
  57.0 0.0 collective-permute-done.7.level_ref.refs_5_
  57.0 0.1 collective-permute-start.12
  57.1 0.9 shard_map.58
  58.0 0.0 collective-permute-done.4.refs_1_
  58.0 1.1 collective-permute-start.13
  59.1 0.0 collective-permute-done.9
  59.1 2.5 %collective-permute-start.14 = (bf16[8,128,128]{2,1,0:T(8,128)(2,1)S(1)}, bf16[8,128,128]{2,1,0:T(8,128)(2,1)S(1)}, u32[]{:S(2)}, u32[]{:S(2)}) collective-permute-start(bf16[8,128,128]{2,1,0:T(8,128)(2,1)S(1)} %get-tuple-element.36), channel_id=1, source_target_pairs={{0,4},{1,5},{2,6},{3,7},{4,0},{5,1},{6,2},{7,3},{8,12},{9,13},{10,... | collective-permute-start | bytes 786440 | tf_op jit(solution)/shard_map/ppermute | solution.py:286
  61.6 0.0 collective-permute-done.11.refs_1_
  61.6 0.9 collective-permute-start.15
  62.5 0.0 collective-permute-done.10.beyond_ref
  62.5 1.5 %collective-permute-start.16 = (bf16[8,128,128]{2,1,0:T(8,128)(2,1)S(1)}, bf16[8,128,128]{2,1,0:T(8,128)(2,1)S(1)}, u32[]{:S(2)}, u32[]{:S(2)}) collective-permute-start(bf16[8,128,128]{2,1,0:T(8,128)(2,1)S(1)} %get-tuple-element.38), channel_id=1, source_target_pairs={{0,12},{1,13},{2,14},{3,15},{4,8},{5,9},{6,10},{7,11},{8,4},{9,5},... | collective-permute-start | bytes 786440 | tf_op jit(solution)/shard_map/ppermute | solution.py:286
  64.0 0.0 copy-done
  64.0 0.0 copy-done.1
  64.0 4.0 %prep.1 = (bf16[256,128]{1,0:T(8,128)(2,1)S(1)}, f32[8,128]{1,0:T(8,128)S(1)}, s32[64]{0:T(128)S(1)}, bf16[32,6,128,128]{3,2,1,0:T(8,128)(2,1)S(1)}) custom-call(s32[1]{0:T(128)} %bitcast.place_ref, s32[6,32]{1,0:T(8,128)S(1)} %bitcast.14, s32[128,128]{1,0:T(8,128)S(1)} %copy-done, bf16[32,6,128,128]{3,2,1,0:T(8,128)(2,1)} %all_tiles_ref.1, ...), custom_call_target="tpu_custom_call" | custom-call | tf_op jit(solution)/shard_map/prep/pallas_call | solution.py:350
  68.0 0.6 shard_map.55.refs_0_
  68.7 3.1 %near.1.part_ref = f32[4096,128]{1,0:T(8,128)S(1)} custom-call(s32[1]{0:T(128)} %bitcast.place_ref, s32[6,32]{1,0:T(8,128)S(1)} %bitcast.15, bf16[32,128,128]{2,1,0:T(8,128)(2,1)S(1)} %bitcast.11, bf16[32,128,128]{2,1,0:T(8,128)(2,1)S(1)} %collective-permute-done.5.chip_ref.refs_2_.refs_3_, ...), custom_call_target="tpu_custom_call" | custom-call | flops 805306368 | bytes 16777216 | tf_op jit(solution)/shard_map/near/pallas_call | solution.py:365
  71.7 4.9 %collective-permute-done.12.refs_2_ = bf16[8,128,128]{2,1,0:T(8,128)(2,1)S(1)} collective-permute-done((bf16[8,128,128]{2,1,0:T(8,128)(2,1)S(1)}, bf16[8,128,128]{2,1,0:T(8,128)(2,1)S(1)}, u32[]{:S(2)}, u32[]{:S(2)}) %collective-permute-start.12) | collective-permute-done | bytes 262176 | tf_op jit(solution)/shard_map/ppermute | solution.py:286
  76.7 0.0 collective-permute-done.13.refs_3_
  76.7 1.8 %collective-permute-done.14.refs_5_ = bf16[8,128,128]{2,1,0:T(8,128)(2,1)S(1)} collective-permute-done((bf16[8,128,128]{2,1,0:T(8,128)(2,1)S(1)}, bf16[8,128,128]{2,1,0:T(8,128)(2,1)S(1)}, u32[]{:S(2)}, u32[]{:S(2)}) %collective-permute-start.14) | collective-permute-done | bytes 262176 | tf_op jit(solution)/shard_map/ppermute | solution.py:286
  78.5 19.8 %collective-permute-done.15.refs_6_ = bf16[8,128,128]{2,1,0:T(8,128)(2,1)S(1)} collective-permute-done((bf16[8,128,128]{2,1,0:T(8,128)(2,1)S(1)}, bf16[8,128,128]{2,1,0:T(8,128)(2,1)S(1)}, u32[]{:S(2)}, u32[]{:S(2)}) %collective-permute-start.15) | collective-permute-done | bytes 262176 | tf_op jit(solution)/shard_map/ppermute | solution.py:286
  98.3 0.0 collective-permute-done.16.refs_7_
  98.3 2.0 %far.1 = (f32[4096,128]{1,0:T(8,128)S(1)}, f32[16,1,128]{2,1,0:T(1,128)S(1)}) custom-call(s32[64]{0:T(128)S(1)} %get-tuple-element.27.where_ref, bf16[32,6,128,128]{3,2,1,0:T(8,128)(2,1)S(1)} %get-tuple-element.28.tiles_ref, f32[4096,128]{1,0:T(8,128)S(1)} %near.1.part_ref, bf16[256,128]{1,0:T(8,128)(2,1)S(1)} %get-tuple-element.31.graph2_ref, ...), custom_call_target="tpu_custom_call" | custom-call | flops 536870912 | bytes 8388608 | tf_op jit(solution)/shard_map/far/pallas_call | solution.py:387
  100.3 14.9 %all_to_all.5.mass_ref = f32[16,1,128]{2,1,0:T(1,128)S(1)} all-to-all(f32[16,1,128]{2,1,0:T(1,128)S(1)} %get-tuple-element.40), channel_id=1, replica_groups=mesh['groups'=2,'rows'=8,'sub'=2] {'rows','sub'}, dimensions={0} | all-to-all | bytes 16384 | tf_op jit(solution)/shard_map/all_to_all | solution.py:400
  115.2 0.0 copy-done.2
  115.2 1.6 %last.1 = f32[4096,128]{1,0:T(8,128)} custom-call(f32[4096,128]{1,0:T(8,128)S(1)} %get-tuple-element.39.logits_ref, f32[16,1,128]{2,1,0:T(1,128)S(1)} %all_to_all.5.mass_ref, f32[1,128]{1,0:T(1,128)S(1)} %bitcast.16), custom_call_target="tpu_custom_call" | custom-call | tf_op jit(solution)/shard_map/last/pallas_call | solution.py:402
  (5 shorter events, 0.0 us)
Async XLA Ops:
  0.0 26.3 %collective-permute-start.6 = (bf16[32,128,128]{2,1,0:T(8,128)(2,1)}, bf16[32,128,128]{2,1,0:T(8,128)(2,1)S(1)}, u32[]{:S(2)}, u32[]{:S(2)}) collective-permute-start(bf16[32,128,128]{2,1,0:T(8,128)(2,1)} %bitcast.17), channel_id=1, source_target_pairs={{0,2},{1,3},{2,0},{3,1},{4,6},{5,7},{6,4},{7,5},{8,10},{9,11},{10,... | collective-permute-start | bytes 3145736 | tf_op jit(solution)/shard_map/ppermute | solution.py:286
  4.8 21.5 %collective-permute-start.8 = (bf16[2560,128]{1,0:T(8,128)(2,1)S(1)}, bf16[2560,128]{1,0:T(8,128)(2,1)S(1)}, u32[]{:S(2)}, u32[]{:S(2)}) collective-permute-start(bf16[2560,128]{1,0:T(8,128)(2,1)S(1)} %get-tuple-element.30), channel_id=1, source_target_pairs={{3,6},{7,10},{11,14},{4,1},{8,5},{12,9},{19,22},{23,26},{27,30},{2... | collective-permute-start | bytes 1966088 | tf_op jit(solution)/shard_map/ppermute | solution.py:311
  5.5 26.9 %collective-permute-start.5 = (bf16[32,128,128]{2,1,0:T(8,128)(2,1)}, bf16[32,128,128]{2,1,0:T(8,128)(2,1)S(1)}, u32[]{:S(2)}, u32[]{:S(2)}) collective-permute-start(bf16[32,128,128]{2,1,0:T(8,128)(2,1)} %bitcast.18), channel_id=1, source_target_pairs={{0,1},{1,0},{2,3},{3,2},{4,5},{5,4},{6,7},{7,6},{8,9},{9,8},{10,11... | collective-permute-start | bytes 3145736 | tf_op jit(solution)/shard_map/ppermute | solution.py:286
  26.3 30.7 %collective-permute-start.7 = (bf16[32,128,128]{2,1,0:T(8,128)(2,1)S(1)}, bf16[32,128,128]{2,1,0:T(8,128)(2,1)S(1)}, u32[]{:S(2)}, u32[]{:S(2)}) collective-permute-start(bf16[32,128,128]{2,1,0:T(8,128)(2,1)S(1)} %collective-permute-done.6.refs_4_), channel_id=1, source_target_pairs={{0,1},{1,0},{2,3},{3,2},{4,5},{5,4},{6,7},{7,6},{8,9},{9,8},{10,11... | collective-permute-start | bytes 3145736 | tf_op jit(solution)/shard_map/ppermute | solution.py:286
  26.3 32.8 %collective-permute-start.9 = (bf16[2560,128]{1,0:T(8,128)(2,1)S(1)}, bf16[2560,128]{1,0:T(8,128)(2,1)S(1)}, u32[]{:S(2)}, u32[]{:S(2)}) collective-permute-start(bf16[2560,128]{1,0:T(8,128)(2,1)S(1)} %collective-permute-done.8), channel_id=1, source_target_pairs={{6,4},{10,8},{14,12},{1,3},{5,7},{9,11},{22,20},{26,24},{30,28},{1... | collective-permute-start | bytes 1966088 | tf_op jit(solution)/shard_map/ppermute | solution.py:337
  27.1 35.4 %collective-permute-start.10 = (bf16[12,128,128]{2,1,0:T(8,128)(2,1)S(1)}, bf16[12,128,128]{2,1,0:T(8,128)(2,1)S(1)}, u32[]{:S(2)}, u32[]{:S(2)}) collective-permute-start(bf16[12,128,128]{2,1,0:T(8,128)(2,1)S(1)} %slice.23), channel_id=1, source_target_pairs={{1,4},{5,8},{9,12},{6,3},{10,7},{14,11},{17,20},{21,24},{25,28},{2... | collective-permute-start | bytes 1179656 | tf_op jit(solution)/shard_map/ppermute | solution.py:334
  27.8 4.7 %collective-permute-start.2 = (f32[5,1,128]{2,1,0:T(1,128)S(1)}, f32[5,1,128]{2,1,0:T(1,128)S(1)}, u32[]{:S(2)}, u32[]{:S(2)}) collective-permute-start(f32[5,1,128]{2,1,0:T(1,128)S(1)} %get-tuple-element.26), channel_id=1, source_target_pairs={{0,4},{1,5},{2,6},{3,7},{4,0},{5,1},{6,2},{7,3},{8,12},{9,13},{10,... | collective-permute-start | bytes 7688 | tf_op jit(solution)/shard_map/ppermute | solution.py:286
  33.1 28.5 %collective-permute-start.11 = (bf16[8,128,128]{2,1,0:T(8,128)(2,1)S(1)}, bf16[8,128,128]{2,1,0:T(8,128)(2,1)S(1)}, u32[]{:S(2)}, u32[]{:S(2)}) collective-permute-start(bf16[8,128,128]{2,1,0:T(8,128)(2,1)S(1)} %shard_map.56), channel_id=1, source_target_pairs={{0,4},{1,5},{2,6},{3,7},{4,0},{5,1},{6,2},{7,3},{8,12},{9,13},{10,... | collective-permute-start | bytes 786440 | tf_op jit(solution)/shard_map/ppermute | solution.py:286
  35.2 6.9 %collective-permute-start.1 = (f32[5,1,128]{2,1,0:T(1,128)S(1)}, f32[5,1,128]{2,1,0:T(1,128)S(1)}, u32[]{:S(2)}, u32[]{:S(2)}) collective-permute-start(f32[5,1,128]{2,1,0:T(1,128)S(1)} %get-tuple-element.25), channel_id=1, source_target_pairs={{0,12},{1,13},{2,14},{3,15},{4,8},{5,9},{6,10},{7,11},{8,4},{9,5},... | collective-permute-start | bytes 7688 | tf_op jit(solution)/shard_map/ppermute | solution.py:286
  42.1 4.5 %collective-permute-start = (f32[5,1,128]{2,1,0:T(1,128)S(1)}, f32[5,1,128]{2,1,0:T(1,128)S(1)}, u32[]{:S(2)}, u32[]{:S(2)}) collective-permute-start(f32[5,1,128]{2,1,0:T(1,128)S(1)} %get-tuple-element.24), channel_id=1, source_target_pairs={{0,8},{1,9},{2,10},{3,11},{4,12},{5,13},{6,14},{7,15},{8,0},{9,1},... | collective-permute-start | bytes 7688 | tf_op jit(solution)/shard_map/ppermute | solution.py:286
  46.6 2.6 %collective-permute-start.3 = (f32[1,128]{1,0:T(1,128)S(1)}, f32[1,128]{1,0:T(1,128)S(1)}, u32[]{:S(2)}, u32[]{:S(2)}) collective-permute-start(f32[1,128]{1,0:T(1,128)S(1)} %fusion), channel_id=1, source_target_pairs={{0,1},{1,0},{2,3},{3,2},{4,5},{5,4},{6,7},{7,6},{8,9},{9,8},{10,11... | collective-permute-start | bytes 1544 | tf_op jit(solution)/shard_map/ppermute | solution.py:286
  49.3 14.8 %copy-start = (s32[128,128]{1,0:T(8,128)S(1)}, s32[128,128]{1,0:T(8,128)}, u32[]{:S(2)}) copy-start(s32[128,128]{1,0:T(8,128)} %graph_ref.1) | copy-start | bytes 196612
  49.3 14.8 %copy-start.1 = (s32[32,6]{0,1:T(8,128)S(1)}, s32[32,6]{0,1:T(8,128)}, u32[]{:S(2)}) copy-start(s32[32,6]{0,1:T(8,128)} %param.7) | copy-start | bytes 2308
  49.3 8.8 %collective-permute-start.4 = (f32[1,128]{1,0:T(1,128)S(1)}, f32[1,128]{1,0:T(1,128)S(1)}, u32[]{:S(2)}, u32[]{:S(2)}) collective-permute-start(f32[1,128]{1,0:T(1,128)S(1)} %add.49.refs_0_), channel_id=1, source_target_pairs={{0,2},{1,3},{2,0},{3,1},{4,6},{5,7},{6,4},{7,5},{8,10},{9,11},{10,... | collective-permute-start | bytes 1544 | tf_op jit(solution)/shard_map/ppermute | solution.py:286
  57.0 19.6 %collective-permute-start.12 = (bf16[8,128,128]{2,1,0:T(8,128)(2,1)S(1)}, bf16[8,128,128]{2,1,0:T(8,128)(2,1)S(1)}, u32[]{:S(2)}, u32[]{:S(2)}) collective-permute-start(bf16[8,128,128]{2,1,0:T(8,128)(2,1)S(1)} %get-tuple-element.33), channel_id=1, source_target_pairs={{0,8},{1,9},{2,10},{3,11},{4,12},{5,13},{6,14},{7,15},{8,0},{9,1},... | collective-permute-start | bytes 786440 | tf_op jit(solution)/shard_map/ppermute | solution.py:286
  58.0 18.6 %collective-permute-start.13 = (bf16[8,128,128]{2,1,0:T(8,128)(2,1)S(1)}, bf16[8,128,128]{2,1,0:T(8,128)(2,1)S(1)}, u32[]{:S(2)}, u32[]{:S(2)}) collective-permute-start(bf16[8,128,128]{2,1,0:T(8,128)(2,1)S(1)} %get-tuple-element.34), channel_id=1, source_target_pairs={{0,12},{1,13},{2,14},{3,15},{4,8},{5,9},{6,10},{7,11},{8,4},{9,5},... | collective-permute-start | bytes 786440 | tf_op jit(solution)/shard_map/ppermute | solution.py:286
  59.1 19.3 %collective-permute-start.14 = (bf16[8,128,128]{2,1,0:T(8,128)(2,1)S(1)}, bf16[8,128,128]{2,1,0:T(8,128)(2,1)S(1)}, u32[]{:S(2)}, u32[]{:S(2)}) collective-permute-start(bf16[8,128,128]{2,1,0:T(8,128)(2,1)S(1)} %get-tuple-element.36), channel_id=1, source_target_pairs={{0,4},{1,5},{2,6},{3,7},{4,0},{5,1},{6,2},{7,3},{8,12},{9,13},{10,... | collective-permute-start | bytes 786440 | tf_op jit(solution)/shard_map/ppermute | solution.py:286
  61.6 36.7 %collective-permute-start.15 = (bf16[8,128,128]{2,1,0:T(8,128)(2,1)S(1)}, bf16[8,128,128]{2,1,0:T(8,128)(2,1)S(1)}, u32[]{:S(2)}, u32[]{:S(2)}) collective-permute-start(bf16[8,128,128]{2,1,0:T(8,128)(2,1)S(1)} %get-tuple-element.37), channel_id=1, source_target_pairs={{0,8},{1,9},{2,10},{3,11},{4,12},{5,13},{6,14},{7,15},{8,0},{9,1},... | collective-permute-start | bytes 786440 | tf_op jit(solution)/shard_map/ppermute | solution.py:286
  62.5 35.8 %collective-permute-start.16 = (bf16[8,128,128]{2,1,0:T(8,128)(2,1)S(1)}, bf16[8,128,128]{2,1,0:T(8,128)(2,1)S(1)}, u32[]{:S(2)}, u32[]{:S(2)}) collective-permute-start(bf16[8,128,128]{2,1,0:T(8,128)(2,1)S(1)} %get-tuple-element.38), channel_id=1, source_target_pairs={{0,12},{1,13},{2,14},{3,15},{4,8},{5,9},{6,10},{7,11},{8,4},{9,5},... | collective-permute-start | bytes 786440 | tf_op jit(solution)/shard_map/ppermute | solution.py:286
  98.3 16.9 %copy-start.2 = (f32[128]{0:T(128)S(1)}, f32[128]{0:T(128)}, u32[]{:S(2)}) copy-start(f32[128]{0:T(128)} %param.9) | copy-start | bytes 1540
